TPU v7x, 32 devices: a whole 2x2x4 slice. The times are simulated.
32 devices in a mesh: front: 2 (over y), wide: 16 (over z, x, core).
Axes of the slice: x: 2, y: 2, z: 4, core: 2. Of those that a mesh axis runs over, the one named last changes fastest.
Arguments:
- updates: bfloat16 [2, 8192, 1024], P('front', 'wide'), may hold values from -6 to 6
- parent_panels: bfloat16 [2, 16384, 2048], P('front', 'wide'), may hold values from -6 to 6
- slot_parent: int32 [2, 64, 1], P('front', 'wide'), may hold values from 0 to 1; in each aligned block of 4 rows (0 to 3, 4 to 7, ..., all dimensions but the last counted through in order) at most 2 rows name the same one
- slot_row: int32 [2, 64], P('front', 'wide'), may hold values from 0 to 7
- slot_cols: int32 [2, 64, 8], P('front', 'wide'), may hold values from 0 to 15, as said below
- slot_mask: int32 [2, 64, 8], P('front', 'wide'), may hold values 0 or 1
Outputs:
- parent_grid: bfloat16 [2, 131072, 256], P('front', 'wide')
Inputs may be any that keep to these rules, and one draw needn't show every extreme that they name: `slot_parent`: among the 4 update block rows of one device no parent front is named more than 2 times; in every draw some device names some front exactly 2 times. `slot_cols`: the 8 block columns of one update block row are distinct.
All inputs are finite; a program needn't handle non-finite values. No bound on the sum of `slot_mask` on one device may be relied on, other than what follows from the above.
Results may differ from a plain program's by a relative error of at most 0.001.
Values may be sent and summed in bfloat16 or wider, within the bound.
No kernel may reach another device: no remote copies, remote signals or barrier semaphores. Data moves between devices by JAX's collectives and lax.ppermute only.
A program may use at most 64 MiB of HBM per device.

v0:
```python
import jax
import jax.numpy as jnp
from jax import lax
from jax.sharding import PartitionSpec as P

GRID_COLS = 8


def shifted(value, axis, steps):
    count = lax.axis_size(axis)
    pairs = [(source, (source + steps) % count) for source in range(count)]
    return lax.ppermute(value, axis, pairs)


def bucket_slots(updates, slot_parent, slot_row, slot_cols, slot_mask, groups):
    slot_count = slot_parent.shape[1]
    row_width = updates.shape[2]
    block_size = updates.shape[1] // slot_count
    columns = slot_cols.shape[2]
    capacity = max(slot_count // 4, slot_count // groups)
    targets = slot_parent[0, :, 0]
    onehot_group = (targets[:, None] == jnp.arange(groups, dtype=jnp.int32)[None, :]).astype(
        jnp.int32
    )
    running = jnp.cumsum(onehot_group, axis=0)
    position = jnp.sum(onehot_group * running, axis=1) - 1
    blocks_in = updates[0].reshape(slot_count, block_size, row_width)
    data_buffer = (
        jnp.zeros((groups, capacity, block_size, row_width), jnp.bfloat16)
        .at[targets, position]
        .set(blocks_in)
    )
    row_buffer = jnp.full((groups, capacity), -1, jnp.int32).at[targets, position].set(slot_row[0])
    column_buffer = (
        jnp.zeros((groups, capacity, columns), jnp.int32).at[targets, position].set(slot_cols[0])
    )
    pattern_buffer = (
        jnp.zeros((groups, capacity, columns), jnp.int32).at[targets, position].set(slot_mask[0])
    )
    return (data_buffer, row_buffer, column_buffer, pattern_buffer)


def local(updates, parent_panels, slot_parent, slot_row, slot_cols, slot_mask):
    groups = lax.axis_size("front")
    data_buffer, row_buffer, column_buffer, pattern_buffer = bucket_slots(
        updates, slot_parent, slot_row, slot_cols, slot_mask, groups
    )
    received, row_got, column_got, pattern_got = (
        lax.all_to_all(data_buffer, "front", split_axis=0, concat_axis=0, tiled=True),
        lax.all_to_all(row_buffer, "front", split_axis=0, concat_axis=0, tiled=True),
        lax.all_to_all(column_buffer, "front", split_axis=0, concat_axis=0, tiled=True),
        lax.all_to_all(pattern_buffer, "front", split_axis=0, concat_axis=0, tiled=True),
    )
    slot_total = received.shape[0] * received.shape[1]
    block_size = received.shape[2]
    columns = column_got.shape[2]
    panel_blocks = parent_panels.shape[1] // block_size
    window_blocks = parent_panels.shape[2] // block_size
    col_groups = window_blocks // GRID_COLS
    row_onehot = (
        row_got.reshape(slot_total)[:, None] == jnp.arange(panel_blocks, dtype=jnp.int32)[None, :]
    ).astype(jnp.bfloat16)
    column_match = (
        column_got.reshape(slot_total, columns)[:, :, None]
        == jnp.arange(window_blocks, dtype=jnp.int32)[None, None, :]
    )
    column_onehot = column_match.astype(jnp.bfloat16) * pattern_got.reshape(slot_total, columns)[
        :, :, None
    ].astype(jnp.bfloat16)
    column_onehot = column_onehot.reshape(slot_total, columns, col_groups, GRID_COLS)
    placement = row_onehot[:, None, :, None, None] * column_onehot[:, :, None, :, :]
    pieces = received.reshape(slot_total, block_size, columns, block_size)
    contribution = jnp.einsum(
        "qjtcd,qujv->dtucv", placement, pieces, preferred_element_type=jnp.float32
    )
    own_panel = parent_panels[0].reshape(
        panel_blocks, block_size, col_groups, GRID_COLS, block_size
    )
    own_panel = jnp.transpose(own_panel, (3, 0, 1, 2, 4))
    assembled = (contribution + own_panel.astype(jnp.float32)).astype(jnp.bfloat16)
    lane_count = lax.axis_size("wide")
    grid_rows = lane_count // GRID_COLS
    lane_index = lax.axis_index("wide")
    grid_column = lane_index // grid_rows
    outgoing = lax.dynamic_index_in_dim(assembled, grid_column, 0, keepdims=False)
    collected = jnp.zeros(
        (panel_blocks, GRID_COLS, block_size, col_groups, block_size), jnp.bfloat16
    )
    collected = lax.dynamic_update_index_in_dim(collected, outgoing, grid_column, 1)
    for offset in range(1, GRID_COLS):
        target_col = (grid_column + offset) % GRID_COLS
        outgoing = lax.dynamic_index_in_dim(assembled, target_col, 0, keepdims=False)
        arrived = shifted(outgoing, "wide", offset * grid_rows)
        source_col = (grid_column - offset) % GRID_COLS
        collected = lax.dynamic_update_index_in_dim(collected, arrived, source_col, 1)
    grid_block = collected
    grid_block = grid_block.reshape(panel_blocks * GRID_COLS * block_size, col_groups * block_size)
    return grid_block[None]


def solution(mesh):
    return jax.shard_map(
        local,
        mesh=mesh,
        in_specs=(
            P("front", "wide", None),
            P("front", "wide", None),
            P("front", "wide", None),
            P("front", "wide"),
            P("front", "wide", None),
            P("front", "wide", None),
        ),
        out_specs=P("front", "wide", None),
        check_vma=False,
    )
```

profile of v0, /device:TPU:26, one launch (start us, length us, event | category | flops | bytes accessed | tf_op | source)
XLA Modules:
  0.0 169.8 jit_solution(11801384170304271435)
XLA Ops:
  0.0 0.7 fusion.7
  0.8 0.7 select_reduce_fusion
  1.5 0.7 fusion.9
  2.2 0.5 broadcast.110
  2.7 1.9 %scatter_fusion.1 = s32[2,2]{1,0:T(2,128)} fusion(s32[2,2]{1,0:T(2,128)} %broadcast.110, s32[4]{0:T(128)S(1)} %fusion.9, s32[4]{0:T(128)} %bitcast.106), kind=kCustom, calls=%fused_computation.1 | custom fusion | bytes 80 | tf_op jit(solution)/shard_map/scatter | solution.py:33
  4.6 3.1 %all-to-all-start.1 = ((s32[2,1,2]{2,1,0:T(1,128)}), s32[2,1,2]{2,1,0:T(1,128)S(1)}, u32[]{:S(2)}, u32[]{:S(2)}) async-start(s32[2,1,2]{2,1,0:T(1,128)} %bitcast.9), calls=%async_computation.1 | async-start | bytes 2048 | tf_op jit(solution)/shard_map/all_to_all | solution.py:50
  7.9 3.2 %convert_bitcast_fusion = f32[128,8,16,128]{3,1,2,0:T(8,128)S(1)} fusion(bf16[1,1024,2048]{2,1,0:T(8,128)(2,1)} %param.7), kind=kLoop, calls=%fused_computation.6 | loop fusion | flops 2097152 | bytes 12582912
  11.2 5.2 %copy.70 = f32[128,8,16,128]{3,2,1,0:T(8,128)} copy(f32[128,8,16,128]{3,1,2,0:T(8,128)S(1)} %convert_bitcast_fusion) | data formatting | bytes 16777216
  16.4 0.6 broadcast.111.clone.1
  17.0 2.1 %scatter_fusion.3 = s32[2,2,8]{2,1,0:T(2,128)} fusion(s32[2,2,8]{2,1,0:T(2,128)} %broadcast.111.clone.1, s32[4]{0:T(128)S(1)} %fusion.9, s32[4,8]{1,0:T(4,128)S(1)} %bitcast.104), kind=kCustom, calls=%fused_computation.3 | custom fusion | bytes 416 | tf_op jit(solution)/shard_map/scatter | solution.py:38
  19.1 3.2 %all-to-all-start.3 = ((s32[2,2,8]{2,1,0:T(2,128)}), s32[2,2,8]{2,1,0:T(2,128)S(1)}, u32[]{:S(2)}, u32[]{:S(2)}) async-start(s32[2,2,8]{2,1,0:T(2,128)} %scatter_fusion.3), calls=%async_computation.3 | async-start | bytes 4096 | tf_op jit(solution)/shard_map/all_to_all | solution.py:52
  22.3 0.6 broadcast.111.clone
  22.9 2.0 %scatter_fusion.2 = s32[2,2,8]{2,1,0:T(2,128)} fusion(s32[2,2,8]{2,1,0:T(2,128)} %broadcast.111.clone, s32[4]{0:T(128)S(1)} %fusion.9, s32[4,8]{1,0:T(4,128)S(1)} %bitcast.105), kind=kCustom, calls=%fused_computation.2 | custom fusion | bytes 416 | tf_op jit(solution)/shard_map/scatter | solution.py:35
  24.9 1.2 all-to-all-done.3
  26.1 3.1 %all-to-all-start.2 = ((s32[2,2,8]{2,1,0:T(2,128)}), s32[2,2,8]{2,1,0:T(2,128)S(1)}, u32[]{:S(2)}, u32[]{:S(2)}) async-start(s32[2,2,8]{2,1,0:T(2,128)} %scatter_fusion.2), calls=%async_computation.2 | async-start | bytes 4096 | tf_op jit(solution)/shard_map/all_to_all | solution.py:51
  29.2 1.1 broadcast_in_dim.44
  30.3 2.8 %scatter_fusion = bf16[2,2,128,1024]{3,2,1,0:T(8,128)(2,1)} fusion(bf16[2,2,128,1024]{3,2,1,0:T(8,128)(2,1)} %broadcast_in_dim.44, s32[4]{0:T(128)S(1)} %fusion.9, bf16[4,128,1024]{2,1,0:T(8,128)(2,1)S(1)} %bitcast.91), kind=kCustom, calls=%fused_computation | custom fusion | bytes 3145760 | tf_op jit(solution)/shard_map/scatter | solution.py:31
  33.1 3.6 %all-to-all-start = ((bf16[2,2,128,1024]{3,2,1,0:T(8,128)(2,1)}), bf16[2,2,128,1024]{3,2,1,0:T(8,128)(2,1)S(1)}, u32[]{:S(2)}, u32[]{:S(2)}) async-start(bf16[2,2,128,1024]{3,2,1,0:T(8,128)(2,1)} %scatter_fusion), calls=%async_computation | async-start | bytes 2097152 | tf_op jit(solution)/shard_map/all_to_all | solution.py:49
  36.7 0.5 broadcast.187
  37.2 0.6 reduce.3
  38.0 11.4 %all-to-all-done = bf16[2,2,128,1024]{3,2,1,0:T(8,128)(2,1)S(1)} async-done(((bf16[2,2,128,1024]{3,2,1,0:T(8,128)(2,1)}), bf16[2,2,128,1024]{3,2,1,0:T(8,128)(2,1)S(1)}, u32[]{:S(2)}, u32[]{:S(2)}) %all-to-all-start) | async-done | bytes 1048608 | tf_op jit(solution)/shard_map/all_to_all | solution.py:49
  49.7 4.3 %fusion = bf16[8,8,128,2,128]{4,0,3,1,2:T(8,128)(2,1)S(1)} fusion(f32[8,128,2,8,128]{4,3,2,1,0:T(8,128)} %bitcast.87, bf16[4,8,2,8]{1,3,0,2:T(8,128)(2,1)S(1)} %compare_select_fusion, bf16[4,8]{0,1:T(8,128)(2,1)S(1)} %fusion.6, bf16[4,128,8,128]{3,2,1,0:T(8,128)(2,1)S(1)} %bitcast.90), kind=kOutput, calls=%fused_computation.5 | convolution fusion | flops 138428416 | bytes 13632576 | tf_op jit(solution)/shard_map/qjtcd,qujv->dtucv/dot_general | solution.py:73
  54.0 10.3 %constant_dynamic-slice_fusion = (bf16[1,8,128,2,128]{4,0,3,1,2:T(2,128)(2,1)S(1)}, bf16[1,8,128,2,128]{4,0,3,1,2:T(2,128)(2,1)S(1)}, bf16[1,8,128,2,128]{4,0,3,...) fusion(bf16[8,8,128,2,128]{4,0,3,1,2:T(8,128)(2,1)S(1)} %fusion, ...), kind=kLoop, calls=%fused_computation.31 | loop fusion | bytes 8388640 | tf_op jit(solution)/shard_map/jit(dynamic_index_in_dim)/dynamic_slice | solution.py:92
  64.3 1.1 copy.96
  65.4 1.2 copy.95
  66.6 1.8 %collective-permute-start.1 = (bf16[8,128,2,128]{3,1,2,0:T(8,128)(2,1)}, bf16[8,128,2,128]{3,1,2,0:T(8,128)(2,1)}, u32[]{:S(2)}, u32[]{:S(2)}) collective-permute-start(bf16[8,128,2,128]{3,1,2,0:T(8,128)(2,1)} %bitcast.81), channel_id=1, source_target_pairs={{0,4},{1,5},{2,6},{3,7},{4,8},{5,9},{6,10},{7,11},{8,12},{9,13},{1... | collective-permute-start | bytes 1572872 | tf_op jit(solution)/shard_map/ppermute | solution.py:12
  68.4 1.6 copy.97
  69.9 1.6 copy.94
  71.5 1.8 %collective-permute-start.2 = (bf16[8,128,2,128]{3,1,2,0:T(8,128)(2,1)S(1)}, bf16[8,128,2,128]{3,1,2,0:T(8,128)(2,1)S(1)}, u32[]{:S(2)}, u32[]{:S(2)}) collective-permute-start(bf16[8,128,2,128]{3,1,2,0:T(8,128)(2,1)S(1)} %bitcast.95), channel_id=1, source_target_pairs={{0,6},{1,7},{2,8},{3,9},{4,10},{5,11},{6,12},{7,13},{8,14},{9,15},... | collective-permute-start | bytes 1572872 | tf_op jit(solution)/shard_map/ppermute | solution.py:12
  73.3 1.6 copy.93
  74.9 1.3 collective-permute-start.3
  76.5 1.8 %collective-permute-start.4 = (bf16[8,128,2,128]{3,1,2,0:T(8,128)(2,1)S(1)}, bf16[8,128,2,128]{3,1,2,0:T(8,128)(2,1)S(1)}, u32[]{:S(2)}, u32[]{:S(2)}) collective-permute-start(bf16[8,128,2,128]{3,1,2,0:T(8,128)(2,1)S(1)} %bitcast.93), channel_id=1, source_target_pairs={{0,10},{1,11},{2,12},{3,13},{4,14},{5,15},{6,0},{7,1},{8,2},{9,3},... | collective-permute-start | bytes 1572872 | tf_op jit(solution)/shard_map/ppermute | solution.py:12
  78.4 6.0 %broadcast_in_dim.43 = bf16[8,8,128,2,128]{4,3,2,1,0:T(2,128)(2,1)} broadcast(bf16[]{:T(256)} %constant.141.clone.1), dimensions={} | broadcast | bytes 4194306 | tf_op jit(solution)/shard_map/broadcast_in_dim | solution.py:86
  84.4 1.4 copy_dynamic-update-slice_fusion.7
  86.1 0.3 copy.90
  86.4 1.4 collective-permute-start.5
  87.8 2.4 %copy_dynamic-update-slice_fusion.6 = bf16[8,8,128,2,128]{4,3,2,1,0:T(2,128)(2,1)} fusion(bf16[8,8,128,2,128]{4,3,2,1,0:T(2,128)(2,1)} %copy_dynamic-update-slice_fusion.7, s32[]{:T(128)S(6)} %select_n.144, bf16[8,1,128,2,128]{4,2,3,1,0:T(8,128)(2,1)} %bitcast.21), kind=kLoop, calls=%fused_computation.21 | loop fusion | bytes 1048580 | tf_op jit(solution)/shard_map/jit(dynamic_update_index_in_dim)/dynamic_update_slice | solution.py:95
  90.2 0.5 collective-permute-start.6
  90.7 2.4 %copy_dynamic-update-slice_fusion.5 = bf16[8,8,128,2,128]{4,3,2,1,0:T(2,128)(2,1)} fusion(bf16[8,8,128,2,128]{4,3,2,1,0:T(2,128)(2,1)} %copy_dynamic-update-slice_fusion.6, s32[]{:T(128)S(6)} %select_n.148, bf16[8,1,128,2,128]{4,2,3,1,0:T(8,128)(2,1)} %bitcast.23), kind=kLoop, calls=%fused_computation.19 | loop fusion | bytes 1048580 | tf_op jit(solution)/shard_map/jit(dynamic_update_index_in_dim)/dynamic_update_slice | solution.py:95
  93.1 7.5 %collective-permute-done.2 = bf16[8,128,2,128]{3,1,2,0:T(8,128)(2,1)S(1)} collective-permute-done((bf16[8,128,2,128]{3,1,2,0:T(8,128)(2,1)S(1)}, bf16[8,128,2,128]{3,1,2,0:T(8,128)(2,1)S(1)}, u32[]{:S(2)}, u32[]{:S(2)}) %collective-permute-start.2) | collective-permute-done | bytes 524320 | tf_op jit(solution)/shard_map/ppermute | solution.py:12
  100.6 1.4 copy_dynamic-update-slice_fusion.4
  102.0 53.7 %collective-permute-done.3 = bf16[8,128,2,128]{3,1,2,0:T(8,128)(2,1)S(1)} collective-permute-done((bf16[8,128,2,128]{3,1,2,0:T(8,128)(2,1)S(1)}, bf16[8,128,2,128]{3,1,2,0:T(8,128)(2,1)S(1)}, u32[]{:S(2)}, u32[]{:S(2)}) %collective-permute-start.3) | collective-permute-done | bytes 524320 | tf_op jit(solution)/shard_map/ppermute | solution.py:12
  155.7 1.4 copy_dynamic-update-slice_fusion.3
  157.1 1.0 collective-permute-done.4
  158.1 1.4 copy_dynamic-update-slice_fusion.2
  159.5 1.3 copy_dynamic-update-slice_fusion.1
  160.8 1.4 copy_dynamic-update-slice_fusion
  162.2 7.6 %broadcast_in_dim_reshape.2 = bf16[1,8192,256]{2,1,0:T(8,128)(2,1)} reshape(bf16[8,8,128,2,128]{4,3,2,1,0:T(2,128)(2,1)} %copy_dynamic-update-slice_fusion) | data formatting | bytes 8388608 | tf_op jit(solution)/shard_map/broadcast_in_dim;reshape | solution.py:98
  (22 shorter events, 1.3 us)
Async XLA Ops:
  4.6 14.5 %all-to-all-start.1 = ((s32[2,1,2]{2,1,0:T(1,128)}), s32[2,1,2]{2,1,0:T(1,128)S(1)}, u32[]{:S(2)}, u32[]{:S(2)}) async-start(s32[2,1,2]{2,1,0:T(1,128)} %bitcast.9), calls=%async_computation.1 | async-start | bytes 2048 | tf_op jit(solution)/shard_map/all_to_all | solution.py:50
  11.2 5.9 %copy-start.1 = (s32[1,4,8]{2,1,0:T(4,128)S(1)}, s32[1,4,8]{2,1,0:T(4,128)}, u32[]{:S(2)}) copy-start(s32[1,4,8]{2,1,0:T(4,128)} %param.11) | copy-start | bytes 388
  11.2 11.7 %copy-start.2 = (s32[1,4,8]{2,1,0:T(4,128)S(1)}, s32[1,4,8]{2,1,0:T(4,128)}, u32[]{:S(2)}) copy-start(s32[1,4,8]{2,1,0:T(4,128)} %param.10) | copy-start | bytes 388
  11.2 19.1 %copy-start = (bf16[1,512,1024]{2,1,0:T(8,128)(2,1)S(1)}, bf16[1,512,1024]{2,1,0:T(8,128)(2,1)}, u32[]{:S(2)}) copy-start(bf16[1,512,1024]{2,1,0:T(8,128)(2,1)} %param.6) | copy-start | bytes 3145732
  19.1 7.0 %all-to-all-start.3 = ((s32[2,2,8]{2,1,0:T(2,128)}), s32[2,2,8]{2,1,0:T(2,128)S(1)}, u32[]{:S(2)}, u32[]{:S(2)}) async-start(s32[2,2,8]{2,1,0:T(2,128)} %scatter_fusion.3), calls=%async_computation.3 | async-start | bytes 4096 | tf_op jit(solution)/shard_map/all_to_all | solution.py:52
  26.1 7.0 %all-to-all-start.2 = ((s32[2,2,8]{2,1,0:T(2,128)}), s32[2,2,8]{2,1,0:T(2,128)S(1)}, u32[]{:S(2)}, u32[]{:S(2)}) async-start(s32[2,2,8]{2,1,0:T(2,128)} %scatter_fusion.2), calls=%async_computation.2 | async-start | bytes 4096 | tf_op jit(solution)/shard_map/all_to_all | solution.py:51
  33.1 16.3 %all-to-all-start = ((bf16[2,2,128,1024]{3,2,1,0:T(8,128)(2,1)}), bf16[2,2,128,1024]{3,2,1,0:T(8,128)(2,1)S(1)}, u32[]{:S(2)}, u32[]{:S(2)}) async-start(bf16[2,2,128,1024]{3,2,1,0:T(8,128)(2,1)} %scatter_fusion), calls=%async_computation | async-start | bytes 2097152 | tf_op jit(solution)/shard_map/all_to_all | solution.py:49
  65.4 21.0 %collective-permute-start = (bf16[8,128,2,128]{3,1,2,0:T(8,128)(2,1)}, bf16[8,128,2,128]{3,1,2,0:T(8,128)(2,1)}, u32[]{:S(2)}, u32[]{:S(2)}) collective-permute-start(bf16[8,128,2,128]{3,1,2,0:T(8,128)(2,1)} %bitcast.82), channel_id=1, source_target_pairs={{0,2},{1,3},{2,4},{3,5},{4,6},{5,7},{6,8},{7,9},{8,10},{9,11},{10,... | collective-permute-start | bytes 1572872 | tf_op jit(solution)/shard_map/ppermute | solution.py:12
  66.6 23.6 %collective-permute-start.1 = (bf16[8,128,2,128]{3,1,2,0:T(8,128)(2,1)}, bf16[8,128,2,128]{3,1,2,0:T(8,128)(2,1)}, u32[]{:S(2)}, u32[]{:S(2)}) collective-permute-start(bf16[8,128,2,128]{3,1,2,0:T(8,128)(2,1)} %bitcast.81), channel_id=1, source_target_pairs={{0,4},{1,5},{2,6},{3,7},{4,8},{5,9},{6,10},{7,11},{8,12},{9,13},{1... | collective-permute-start | bytes 1572872 | tf_op jit(solution)/shard_map/ppermute | solution.py:12
  71.5 29.1 %collective-permute-start.2 = (bf16[8,128,2,128]{3,1,2,0:T(8,128)(2,1)S(1)}, bf16[8,128,2,128]{3,1,2,0:T(8,128)(2,1)S(1)}, u32[]{:S(2)}, u32[]{:S(2)}) collective-permute-start(bf16[8,128,2,128]{3,1,2,0:T(8,128)(2,1)S(1)} %bitcast.95), channel_id=1, source_target_pairs={{0,6},{1,7},{2,8},{3,9},{4,10},{5,11},{6,12},{7,13},{8,14},{9,15},... | collective-permute-start | bytes 1572872 | tf_op jit(solution)/shard_map/ppermute | solution.py:12
  74.9 80.8 %collective-permute-start.3 = (bf16[8,128,2,128]{3,1,2,0:T(8,128)(2,1)S(1)}, bf16[8,128,2,128]{3,1,2,0:T(8,128)(2,1)S(1)}, u32[]{:S(2)}, u32[]{:S(2)}) collective-permute-start(bf16[8,128,2,128]{3,1,2,0:T(8,128)(2,1)S(1)} %bitcast.94), channel_id=1, source_target_pairs={{0,8},{1,9},{2,10},{3,11},{4,12},{5,13},{6,14},{7,15},{8,0},{9,1},... | collective-permute-start | bytes 1572872 | tf_op jit(solution)/shard_map/ppermute | solution.py:12
  76.5 81.6 %collective-permute-start.4 = (bf16[8,128,2,128]{3,1,2,0:T(8,128)(2,1)S(1)}, bf16[8,128,2,128]{3,1,2,0:T(8,128)(2,1)S(1)}, u32[]{:S(2)}, u32[]{:S(2)}) collective-permute-start(bf16[8,128,2,128]{3,1,2,0:T(8,128)(2,1)S(1)} %bitcast.93), channel_id=1, source_target_pairs={{0,10},{1,11},{2,12},{3,13},{4,14},{5,15},{6,0},{7,1},{8,2},{9,3},... | collective-permute-start | bytes 1572872 | tf_op jit(solution)/shard_map/ppermute | solution.py:12
  86.4 73.1 %collective-permute-start.5 = (bf16[8,128,2,128]{3,1,2,0:T(8,128)(2,1)S(1)}, bf16[8,128,2,128]{3,1,2,0:T(8,128)(2,1)S(1)}, u32[]{:S(2)}, u32[]{:S(2)}) collective-permute-start(bf16[8,128,2,128]{3,1,2,0:T(8,128)(2,1)S(1)} %bitcast.96), channel_id=1, source_target_pairs={{0,12},{1,13},{2,14},{3,15},{4,0},{5,1},{6,2},{7,3},{8,4},{9,5},{1... | collective-permute-start | bytes 1572872 | tf_op jit(solution)/shard_map/ppermute | solution.py:12
  90.2 70.6 %collective-permute-start.6 = (bf16[8,128,2,128]{3,1,2,0:T(8,128)(2,1)S(1)}, bf16[8,128,2,128]{3,1,2,0:T(8,128)(2,1)S(1)}, u32[]{:S(2)}, u32[]{:S(2)}) collective-permute-start(bf16[8,128,2,128]{3,1,2,0:T(8,128)(2,1)S(1)} %bitcast.92), channel_id=1, source_target_pairs={{0,14},{1,15},{2,0},{3,1},{4,2},{5,3},{6,4},{7,5},{8,6},{9,7},{10,... | collective-permute-start | bytes 1572872 | tf_op jit(solution)/shard_map/ppermute | solution.py:12
where the time goes:
time: 171 us; the launch traced here: 170 us
  waiting for transfers between devices  74.8 us (44%)
  local copies, waits for them, and re-layouts  62.5 us (37%)
  starting transfers between devices  21.7 us (13%)
  other arithmetic  6.14 us (4%)
  matrix products  4.34 us (3%)
    ppermute x7, waiting for transfers between devices, shifted(): return lax.ppermute(value, axis, pairs)  62.3 us
    dynamic_slice x8, local copies, waits for them, and re-layouts, local(): lax.dynamic_index_in_dim(assembled, target_col, 0, keepdims=False)  16.7 us
    dynamic_update_slice x7, local copies, waits for them, and re-layouts, local(): lax.dynamic_update_index_in_dim(collected, arrived, source_col, 1)  11.6 us
    all_to_all x1, waiting for transfers between devices, local(): lax.all_to_all(data_buffer, 'front', split_axis=0, concat_axis=0, tiled=T...  11.4 us
    ppermute x7, starting transfers between devices, shifted(): return lax.ppermute(value, axis, pairs)  8.63 us
    another operation x1, local copies, waits for them, and re-layouts, local(): return grid_block[None]  7.58 us
    broadcast_in_dim x1, local copies, waits for them, and re-layouts, local(): jnp.zeros((panel_blocks, GRID_COLS, block_size, col_groups, block_size),...  5.98 us
    unnamed x8, local copies, waits for them, and re-layouts  5.52 us
  transfers between devices with their start and end apart: 11, of which 5 were waited for; matrix products, arithmetic and copies ran while one was open for 26% of the time, Pallas kernels for 0%

commit v1 on v0

v1 whole, which is shorter than its diff:
```python
import functools

import jax
import jax.numpy as jnp
from jax import lax
from jax.experimental import pallas as pl
from jax.experimental.pallas import tpu as pltpu
from jax.sharding import PartitionSpec as P

GRID_COLS = 8
NEAR = GRID_COLS // 2
TAG = 8

ANY = pl.BlockSpec(memory_space=pl.ANY)
HBM = pl.BlockSpec(memory_space=pltpu.HBM)
SMEM = pl.BlockSpec(memory_space=pltpu.SMEM)
VMEM = pl.BlockSpec(memory_space=pltpu.VMEM)


class Plan:
    def __init__(self, updates, panels, slot_cols):
        self.groups = lax.axis_size("front")
        self.lanes = lax.axis_size("wide")
        self.grid_rows = self.lanes // GRID_COLS
        self.slots = slot_cols.shape[1]
        self.columns = slot_cols.shape[2]
        self.block = updates.shape[1] // self.slots
        self.rows = panels.shape[1] // self.block
        self.window = panels.shape[2] // self.block
        self.col_groups = self.window // GRID_COLS
        self.width = self.col_groups * self.block
        self.capacity = max(self.slots // 4, self.slots // self.groups)
        self.first = max(0, self.rows - self.capacity * self.groups)
        self.second = self.rows - self.first


def params():
    return pltpu.CompilerParams(vmem_limit_bytes=48 << 20)


def at(start, size):
    return pl.ds(pl.multiple_of(start * size, size), size)


def parent_of(plan, codes, q):
    return codes[q, 0] // (plan.rows * 2 * plan.window)


def row_of(plan, codes, q):
    return (codes[q, 0] // (2 * plan.window)) % plan.rows


def first_set(plan, code_refs):
    me = lax.axis_index("front")
    touched = jnp.int32(0)
    for codes in code_refs:
        for q in range(plan.slots):
            bit = jnp.left_shift(jnp.int32(1), row_of(plan, codes, q))
            touched = touched | jnp.where(parent_of(plan, codes, q) == me, bit, 0)
    chosen, count = jnp.int32(0), jnp.int32(0)
    for t in range(plan.rows):
        free = (jnp.right_shift(touched, t) & 1) == 0
        take = jnp.logical_and(free, count < plan.first)
        chosen = chosen | jnp.where(take, 1 << t, 0)
        count = count + jnp.where(take, 1, 0)
    return chosen


def positions(plan, chosen):
    out, count = [], jnp.int32(0)
    for t in range(plan.rows):
        bit = jnp.right_shift(chosen, t) & 1
        out.append((bit, jnp.where(bit == 1, count, t - count)))
        count = count + bit
    return out


def run_all(copies):
    for copy in copies:
        copy.start()
    for copy in copies:
        copy.wait()


def bucket_kernel(plan, codes, updates, *refs):
    outs, sems = refs[:-1], refs[-1]
    me = lax.axis_index("front")

    def copies(act):
        for k in range(1, plan.groups):
            target = lax.rem(me + k, plan.groups)
            rank = jnp.int32(0)
            for q in range(plan.slots):
                named = parent_of(plan, codes, q) == target

                @pl.when(named)
                def _():
                    act(
                        pltpu.make_async_copy(
                            updates.at[0, pl.ds(q * plan.block, plan.block)],
                            outs[k - 1].at[rank],
                            sems.at[q],
                        )
                    )

                rank = rank + jnp.where(named, 1, 0)

    copies(lambda c: c.start())
    copies(lambda c: c.wait())


def pack_kernel(plan, *refs):
    groups = plan.groups
    code_refs, panel = refs[:groups], refs[groups]
    outs, order, sems = refs[groups + 1 : -2], refs[-2], refs[-1]
    column = lax.axis_index("wide") // plan.grid_rows
    chosen = first_set(plan, code_refs)
    for t, (bit, place) in enumerate(positions(plan, chosen)):

        @pl.when(bit == 1)
        def _():
            order[place] = t

    copies = []
    for i in range(NEAR):
        target = jnp.bitwise_xor(column, NEAR + i)
        for k in range(plan.first):
            t = order[k]
            for cc in range(plan.col_groups):
                copies.append(
                    pltpu.make_async_copy(
                        panel.at[0, at(t, plan.block), at(cc * GRID_COLS + target, plan.block)],
                        outs[i].at[
                            pl.ds(k * plan.block, plan.block), pl.ds(cc * plan.block, plan.block)
                        ],
                        sems.at[i, k, cc],
                    )
                )
    for copy in copies:
        copy.start()
    tag = jnp.full((TAG, plan.width), chosen.astype(jnp.float32), jnp.float32).astype(jnp.bfloat16)
    for i in range(NEAR):
        outs[i][plan.first * plan.block :, :] = tag
    for copy in copies:
        copy.wait()


def assemble_kernel(plan, *refs):
    groups, block = plan.groups, plan.block
    code_refs, refs = refs[:groups], refs[groups:]
    panel, updates, refs = refs[0], refs[1], refs[2:]
    got, refs = refs[: groups - 1], refs[groups - 1 :]
    far, near, refs = refs[:NEAR], refs[NEAR : 2 * NEAR], refs[2 * NEAR :]
    total, raw, moved, place_ref, row_sems, slot_sems = refs
    me = lax.axis_index("front")
    column = lax.axis_index("wide") // plan.grid_rows

    slot_copies = [
        pltpu.make_async_copy(
            updates.at[0, pl.ds(q * block, block)], moved.at[q], slot_sems.at[q]
        )
        for q in range(plan.slots)
    ]
    for k in range(1, groups):
        for c in range(plan.capacity):
            index = plan.slots + (k - 1) * plan.capacity + c
            slot_copies.append(
                pltpu.make_async_copy(got[k - 1].at[c], moved.at[index], slot_sems.at[index])
            )
    row_copies = [
        pltpu.make_async_copy(panel.at[0, pl.ds(t * block, block)], raw.at[t], row_sems.at[t])
        for t in range(plan.rows)
    ]
    for copy in row_copies + slot_copies:
        copy.start()

    chosen = first_set(plan, code_refs)
    for t, (bit, place) in enumerate(positions(plan, chosen)):
        place_ref[t] = jnp.where(bit == 1, -1, place)

    for t in range(plan.rows):
        row_copies[t].wait()
    for copy in slot_copies:
        copy.wait()

    def widen(t, carry):
        total[t] = raw[t].astype(jnp.float32)
        return carry

    lax.fori_loop(0, plan.rows, widen, 0)

    for s, codes in enumerate(code_refs):

        def add_slot(q, rank):
            named = parent_of(plan, codes, q) == me
            index = q if s == 0 else plan.slots + (s - 1) * plan.capacity + rank
            t = row_of(plan, codes, q)

            @pl.when(named)
            def _():
                for j in range(plan.columns):
                    code = codes[q, j]
                    col = code % plan.window

                    @pl.when((code // plan.window) % 2 == 1)
                    def _():
                        where = at(col, block)
                        total[t, :, where] += moved[
                            index, :, pl.ds(j * block, block)
                        ].astype(jnp.float32)

            return rank + jnp.where(named, 1, 0)

        lax.fori_loop(0, plan.slots, add_slot, jnp.int32(0))

    def pack(t, carry):
        place = place_ref[t]
        for o in range(GRID_COLS):
            target = jnp.bitwise_xor(column, o)

            def put(ref, row):
                for cc in range(plan.col_groups):
                    ref[at(row, block), pl.ds(cc * block, block)] = total[
                        t, :, at(cc * GRID_COLS + target, block)
                    ].astype(jnp.bfloat16)

            if o < NEAR:
                put(near[o], t)
            else:

                @pl.when(place >= 0)
                def _():
                    put(far[o - NEAR], place)

        return carry

    lax.fori_loop(0, plan.rows, pack, 0)


def place_first_kernel(plan, *refs):
    pieces, out, sets, refs = refs[:NEAR], refs[NEAR], refs[NEAR + 1], refs[NEAR + 2 :]
    tags, where, tag_sems, sems = refs
    column = lax.axis_index("wide") // plan.grid_rows
    block = plan.block
    run_all(
        [
            pltpu.make_async_copy(
                pieces[i].at[pl.ds(plan.first * block, TAG)], tags.at[i], tag_sems.at[i]
            )
            for i in range(NEAR)
        ]
    )
    copies = []
    for i in range(NEAR):
        source = jnp.bitwise_xor(column, NEAR + i)
        chosen = jnp.max(tags[i].astype(jnp.float32)).astype(jnp.int32)
        sets[i] = chosen
        for t, (bit, place) in enumerate(positions(plan, chosen)):

            @pl.when(bit == 1)
            def _():
                where[i, place] = t

        for k in range(plan.first):
            copies.append(
                pltpu.make_async_copy(
                    pieces[i].at[pl.ds(k * block, block)],
                    out.at[at(where[i, k] * GRID_COLS + source, block)],
                    sems.at[i, k],
                )
            )
            copies[-1].start()
    for copy in copies:
        copy.wait()


def place_near_kernel(plan, aliased, pieces, out, sems):
    column = lax.axis_index("wide") // plan.grid_rows
    block = plan.block
    copies = []
    for o in pieces:
        source = jnp.bitwise_xor(column, o)
        for t in range(plan.rows):
            copies.append(
                pltpu.make_async_copy(
                    pieces[o].at[pl.ds(t * block, block)],
                    out.at[at(t * GRID_COLS + source, block)],
                    sems.at[o, t],
                )
            )
    run_all(copies)


def place_far_kernel(plan, *refs):
    refs = refs[1:] if plan.first else refs
    sets = refs[0] if plan.first else None
    refs = refs[1:] if plan.first else refs
    pieces, out, where, sems = refs[:NEAR], refs[NEAR], refs[NEAR + 1], refs[NEAR + 2]
    column = lax.axis_index("wide") // plan.grid_rows
    block = plan.block
    copies = []
    for i in range(NEAR):
        source = jnp.bitwise_xor(column, NEAR + i)
        if plan.first:
            for t, (bit, place) in enumerate(positions(plan, sets[i])):

                @pl.when(bit == 0)
                def _():
                    where[i, place] = t

        for k in range(plan.second):
            t = where[i, k] if plan.first else k
            copies.append(
                pltpu.make_async_copy(
                    pieces[i].at[pl.ds(k * block, block)],
                    out.at[at(t * GRID_COLS + source, block)],
                    sems.at[i, k],
                )
            )
            copies[-1].start()
    for copy in copies:
        copy.wait()


def across(value, plan, offset):
    pairs = [
        (c * plan.grid_rows + r, (c ^ offset) * plan.grid_rows + r)
        for c in range(GRID_COLS)
        for r in range(plan.grid_rows)
    ]
    return lax.ppermute(value, "wide", pairs)


def along(value, plan, steps):
    return lax.ppermute(
        value, "front", [(f, (f + steps) % plan.groups) for f in range(plan.groups)]
    )


def local(updates, parent_panels, slot_parent, slot_row, slot_cols, slot_mask):
    plan = Plan(updates, parent_panels, slot_cols)
    block, width = plan.block, plan.width
    bf16 = jnp.bfloat16
    head = slot_parent[0, :, 0] * plan.rows + slot_row[0]
    codes = (head[:, None] * 2 + slot_mask[0]) * plan.window + slot_cols[0]
    all_codes = [codes] + [along(codes, plan, k) for k in range(1, plan.groups)]

    buckets = pl.pallas_call(
        functools.partial(bucket_kernel, plan),
        out_shape=[
            jax.ShapeDtypeStruct((plan.capacity, block, updates.shape[2]), bf16)
            for _ in range(1, plan.groups)
        ],
        in_specs=[SMEM, ANY],
        out_specs=[ANY] * (plan.groups - 1),
        scratch_shapes=[pltpu.SemaphoreType.DMA((plan.slots,))],
        name="bucket",
    )(codes, updates)

    far_first = []
    if plan.first:
        packed = pl.pallas_call(
            functools.partial(pack_kernel, plan),
            out_shape=[jax.ShapeDtypeStruct((plan.first * block + TAG, width), bf16)] * NEAR,
            in_specs=[SMEM] * plan.groups + [ANY],
            out_specs=[VMEM] * NEAR,
            scratch_shapes=[
                pltpu.SMEM((plan.rows,), jnp.int32),
                pltpu.SemaphoreType.DMA((NEAR, plan.first, plan.col_groups)),
            ],
            compiler_params=params(),
            name="pack_first",
        )(*all_codes, parent_panels)
        far_first = [across(packed[i], plan, NEAR + i) for i in range(NEAR)]

    got = [along(buckets[k - 1], plan, k) for k in range(1, plan.groups)]

    moved = plan.slots + (plan.groups - 1) * plan.capacity
    assembled = pl.pallas_call(
        functools.partial(assemble_kernel, plan),
        out_shape=[jax.ShapeDtypeStruct((plan.second * block, width), bf16)] * NEAR
        + [jax.ShapeDtypeStruct((plan.rows * block, width), bf16)] * NEAR,
        in_specs=[SMEM] * plan.groups + [ANY] * (1 + plan.groups),
        out_specs=[VMEM] * (2 * NEAR),
        scratch_shapes=[
            pltpu.VMEM((plan.rows, block, parent_panels.shape[2]), jnp.float32),
            pltpu.VMEM((plan.rows, block, parent_panels.shape[2]), bf16),
            pltpu.VMEM((moved, block, updates.shape[2]), bf16),
            pltpu.SMEM((plan.rows,), jnp.int32),
            pltpu.SemaphoreType.DMA((plan.rows,)),
            pltpu.SemaphoreType.DMA((moved,)),
        ],
        compiler_params=params(),
        name="assemble",
    )(*all_codes, parent_panels, updates, *got)
    far, near = assembled[:NEAR], assembled[NEAR:]
    far_second = [across(far[i], plan, NEAR + i) for i in range(NEAR)]
    near_all = [near[0]] + [across(near[o], plan, o) for o in range(1, NEAR)]

    out_shape = jax.ShapeDtypeStruct((plan.rows * GRID_COLS * block, width), bf16)
    out, sets = None, None
    if plan.first:
        out, sets = pl.pallas_call(
            functools.partial(place_first_kernel, plan),
            out_shape=[out_shape, jax.ShapeDtypeStruct((NEAR,), jnp.int32)],
            in_specs=[ANY] * NEAR,
            out_specs=[HBM, SMEM],
            scratch_shapes=[
                pltpu.VMEM((NEAR, TAG, width), bf16),
                pltpu.SMEM((NEAR, plan.rows), jnp.int32),
                pltpu.SemaphoreType.DMA((NEAR,)),
                pltpu.SemaphoreType.DMA((NEAR, plan.first)),
            ],
            compiler_params=params(),
            name="place_first",
        )(*far_first)

    def near_body(*refs):
        refs = list(refs)
        if plan.first:
            refs = refs[1:]
        place_near_kernel(plan, None, dict(enumerate(refs[:NEAR])), refs[NEAR], refs[NEAR + 1])

    held = [out] if plan.first else []
    out = pl.pallas_call(
        near_body,
        out_shape=out_shape,
        in_specs=[HBM] * len(held) + [ANY] * NEAR,
        out_specs=HBM,
        input_output_aliases={0: 0} if held else {},
        scratch_shapes=[pltpu.SemaphoreType.DMA((NEAR, plan.rows))],
        compiler_params=params(),
        name="place_near",
    )(*held, *near_all)

    extra = [sets] if plan.first else []

    def far_body(*refs):
        refs = list(refs)[1:]
        sets_ref = [refs.pop(0)] if plan.first else []
        lead = [None] if plan.first else []
        place_far_kernel(plan, *(lead + sets_ref + refs))

    out = pl.pallas_call(
        far_body,
        out_shape=out_shape,
        in_specs=[HBM] + [SMEM] * len(extra) + [ANY] * NEAR,
        out_specs=HBM,
        input_output_aliases={0: 0},
        scratch_shapes=[
            pltpu.SMEM((NEAR, plan.rows), jnp.int32),
            pltpu.SemaphoreType.DMA((NEAR, plan.second)),
        ],
        compiler_params=params(),
        name="place_far",
    )(out, *extra, *far_second)
    return out[None]


def solution(mesh):
    return jax.shard_map(
        local,
        mesh=mesh,
        in_specs=(
            P("front", "wide", None),
            P("front", "wide", None),
            P("front", "wide", None),
            P("front", "wide"),
            P("front", "wide", None),
            P("front", "wide", None),
        ),
        out_specs=P("front", "wide", None),
        check_vma=False,
    )
```

time: 171 us -> 136 us (0.80)
  the two profiles are of different devices: /device:TPU:26 before, /device:TPU:17 now
where the time goes in v1:
time: 136 us
  waiting for transfers between devices  73.6 us (54%)
  Pallas kernels  29.7 us (22%)
  starting transfers between devices  27.6 us (20%)
  local copies, waits for them, and re-layouts  2.87 us (2%)
  other arithmetic  2.12 us (2%)
    ppermute x11, waiting for transfers between devices, across(): return lax.ppermute(value, 'wide', pairs)  62 us
    ppermute x11, starting transfers between devices, across(): return lax.ppermute(value, 'wide', pairs)  26 us
    pallas_call x1, Pallas kernels, local(): pl.pallas_call(functools.partial(bucket_kernel, plan), out_shape=[jax.Sha...  17.7 us
    ppermute x2, waiting for transfers between devices, along(): lax.ppermute(value, 'front', [(f, (f + steps) % plan.groups) for f in ran...  11.6 us
    pallas_call x1, Pallas kernels, local(): pl.pallas_call(functools.partial(assemble_kernel, plan), out_shape=[jax.S...  5.46 us
    unnamed x6, local copies, waits for them, and re-layouts  2.87 us
  transfers between devices with their start and end apart: 13, of which 8 were waited for; matrix products, arithmetic and copies ran while one was open for 0% of the time, Pallas kernels for 8%

profile of v1, /device:TPU:17, one launch (start us, length us, event | category | flops | bytes accessed | tf_op | source)
XLA Modules:
  0.0 136.0 jit_solution(4698747932614535264)
XLA Ops:
  0.0 0.0 copy-start.1
  0.0 0.8 fusion.1
  0.8 1.4 bitcast_add_fusion.refs_0_.codes
  2.1 17.7 %bucket.1 = bf16[2,128,1024]{2,1,0:T(8,128)(2,1)} custom-call(s32[4,8]{1,0:T(4,128)} %bitcast_add_fusion.refs_0_.codes, bf16[1,512,1024]{2,1,0:T(8,128)(2,1)} %refs_3_.1), custom_call_target="tpu_custom_call" | custom-call | tf_op jit(solution)/shard_map/bucket/pallas_call | solution.py:348
  19.9 1.3 collective-permute-start.5
  21.2 0.2 collective-permute-start
  21.4 11.6 %collective-permute-done.refs_1_ = s32[4,8]{1,0:T(4,128)S(1)} collective-permute-done((s32[4,8]{1,0:T(4,128)}, s32[4,8]{1,0:T(4,128)S(1)}, u32[]{:S(2)}, u32[]{:S(2)}) %collective-permute-start) | collective-permute-done | bytes 160 | tf_op jit(solution)/shard_map/ppermute | solution.py:335
  33.0 0.0 copy-start
  33.0 2.2 %copy-done = bf16[1,1024,2048]{2,1,0:T(8,128)(2,1)S(1)} copy-done((bf16[1,1024,2048]{2,1,0:T(8,128)(2,1)S(1)}, bf16[1,1024,2048]{2,1,0:T(8,128)(2,1)}, u32[]{:S(2)}) %copy-start) | copy-done | bytes 4194328
  35.2 0.0 copy-start.2
  35.2 0.7 copy-done.2
  35.8 1.4 %pack_first.1 = (bf16[520,256]{1,0:T(8,128)(2,1)S(1)}, bf16[520,256]{1,0:T(8,128)(2,1)S(1)}, bf16[520,256]{1,0:T(8,128)(2,1)S(1)}, bf16[520,256]{1,0:T(8,128)(2,1)S(1)}) custom-call(s32[4,8]{1,0:T(4,128)S(1)} %copy-done.2, s32[4,8]{1,0:T(4,128)S(1)} %collective-permute-done.refs_1_, bf16[1,1024,2048]{2,1,0:T(8,128)(2,1)S(1)} %copy-done), custom_call_target="tpu_custom_call" | custom-call | tf_op jit(solution)/shard_map/pack_first/pallas_call | solution.py:362
  37.3 0.2 collective-permute-start.1
  37.5 3.1 %collective-permute-start.2 = (bf16[520,256]{1,0:T(8,128)(2,1)S(1)}, bf16[520,256]{1,0:T(8,128)(2,1)S(1)}, u32[]{:S(2)}, u32[]{:S(2)}) collective-permute-start(bf16[520,256]{1,0:T(8,128)(2,1)S(1)} %get-tuple-element.20), channel_id=1, source_target_pairs={{0,10},{1,11},{2,8},{3,9},{4,14},{5,15},{6,12},{7,13},{8,2},{9,3},... | collective-permute-start | bytes 798728 | tf_op jit(solution)/shard_map/ppermute | solution.py:331
  40.6 0.0 collective-permute-done.5.refs_4_
  40.6 0.0 copy-done.1
  40.6 5.5 %assemble.1 = (bf16[512,256]{1,0:T(8,128)(2,1)S(1)}, bf16[512,256]{1,0:T(8,128)(2,1)S(1)}, bf16[512,256]{1,0:T(8,128)(2,1)S(1)}, bf16[512,256]{1,0:T(8,128)(2,1)...) custom-call(s32[4,8]{1,0:T(4,128)S(1)} %copy-done.2, ...), custom_call_target="tpu_custom_call" | custom-call | tf_op jit(solution)/shard_map/assemble/pallas_call | solution.py:379
  46.1 0.4 collective-permute-start.6
  46.4 1.3 collective-permute-start.7
  47.7 0.0 collective-permute-start.3
  47.7 6.4 %collective-permute-done.1.refs_0_ = bf16[520,256]{1,0:T(8,128)(2,1)S(1)} collective-permute-done((bf16[520,256]{1,0:T(8,128)(2,1)S(1)}, bf16[520,256]{1,0:T(8,128)(2,1)S(1)}, u32[]{:S(2)}, u32[]{:S(2)}) %collective-permute-start.1) | collective-permute-done | bytes 266272 | tf_op jit(solution)/shard_map/ppermute | solution.py:331
  54.1 4.1 %collective-permute-start.4 = (bf16[520,256]{1,0:T(8,128)(2,1)S(1)}, bf16[520,256]{1,0:T(8,128)(2,1)S(1)}, u32[]{:S(2)}, u32[]{:S(2)}) collective-permute-start(bf16[520,256]{1,0:T(8,128)(2,1)S(1)} %get-tuple-element.22), channel_id=1, source_target_pairs={{0,14},{1,15},{2,12},{3,13},{4,10},{5,11},{6,8},{7,9},{8,6},{9,7},... | collective-permute-start | bytes 798728 | tf_op jit(solution)/shard_map/ppermute | solution.py:331
  58.2 1.6 %collective-permute-done.2.refs_1_ = bf16[520,256]{1,0:T(8,128)(2,1)S(1)} collective-permute-done((bf16[520,256]{1,0:T(8,128)(2,1)S(1)}, bf16[520,256]{1,0:T(8,128)(2,1)S(1)}, u32[]{:S(2)}, u32[]{:S(2)}) %collective-permute-start.2) | collective-permute-done | bytes 266272 | tf_op jit(solution)/shard_map/ppermute | solution.py:331
  59.8 15.5 %collective-permute-start.8 = (bf16[1024,256]{1,0:T(8,128)(2,1)S(1)}, bf16[1024,256]{1,0:T(8,128)(2,1)S(1)}, u32[]{:S(2)}, u32[]{:S(2)}) collective-permute-start(bf16[1024,256]{1,0:T(8,128)(2,1)S(1)} %get-tuple-element.27), channel_id=1, source_target_pairs={{0,6},{1,7},{2,4},{3,5},{4,2},{5,3},{6,0},{7,1},{8,14},{9,15},{10,... | collective-permute-start | bytes 1572872 | tf_op jit(solution)/shard_map/ppermute | solution.py:331
  75.3 5.6 %collective-permute-done.3.refs_2_ = bf16[520,256]{1,0:T(8,128)(2,1)S(1)} collective-permute-done((bf16[520,256]{1,0:T(8,128)(2,1)S(1)}, bf16[520,256]{1,0:T(8,128)(2,1)S(1)}, u32[]{:S(2)}, u32[]{:S(2)}) %collective-permute-start.3) | collective-permute-done | bytes 266272 | tf_op jit(solution)/shard_map/ppermute | solution.py:331
  80.9 0.0 collective-permute-start.9
  80.9 11.9 %collective-permute-done.4.refs_3_ = bf16[520,256]{1,0:T(8,128)(2,1)S(1)} collective-permute-done((bf16[520,256]{1,0:T(8,128)(2,1)S(1)}, bf16[520,256]{1,0:T(8,128)(2,1)S(1)}, u32[]{:S(2)}, u32[]{:S(2)}) %collective-permute-start.4) | collective-permute-done | bytes 266272 | tf_op jit(solution)/shard_map/ppermute | solution.py:331
  92.8 0.0 collective-permute-start.10
  92.8 0.0 collective-permute-done.6.refs_2_
  92.8 0.0 collective-permute-start.11
  92.8 0.0 collective-permute-done.7.refs_3_
  92.8 1.5 %collective-permute-start.12 = (bf16[512,256]{1,0:T(8,128)(2,1)S(1)}, bf16[512,256]{1,0:T(8,128)(2,1)S(1)}, u32[]{:S(2)}, u32[]{:S(2)}) collective-permute-start(bf16[512,256]{1,0:T(8,128)(2,1)S(1)} %get-tuple-element.32), channel_id=1, source_target_pairs={{0,14},{1,15},{2,12},{3,13},{4,10},{5,11},{6,8},{7,9},{8,6},{9,7},... | collective-permute-start | bytes 786440 | tf_op jit(solution)/shard_map/ppermute | solution.py:331
  94.3 1.9 %place_first.1 = (bf16[8192,256]{1,0:T(8,128)(2,1)}, s32[4]{0:T(128)S(1)}) custom-call(bf16[520,256]{1,0:T(8,128)(2,1)S(1)} %collective-permute-done.1.refs_0_, bf16[520,256]{1,0:T(8,128)(2,1)S(1)} %collective-permute-done.2.refs_1_, bf16[520,256]{1,0:T(8,128)(2,1)S(1)} %collective-permute-done.3.refs_2_, bf16[520,256]{1,0:T(8,128)(2,1)S(1)} %collective-permute-done.4.refs_3_), custom_call_target="tpu_custom_call" | custom-call | tf_op jit(solution)/shard_map/place_first/pallas_call | solution.py:403
  96.2 0.0 collective-permute-done.8.refs_4_
  96.2 1.6 %place_near.1.refs_0_ = bf16[8192,256]{1,0:T(8,128)(2,1)} custom-call(bf16[8192,256]{1,0:T(8,128)(2,1)} %get-tuple-element.23.refs_0_, bf16[1024,256]{1,0:T(8,128)(2,1)S(1)} %get-tuple-element.24.refs_1_, bf16[1024,256]{1,0:T(8,128)(2,1)S(1)} %collective-permute-done.6.refs_2_, ...), custom_call_target="tpu_custom_call", output_to_operand_aliasing={{}: (0, {})} | custom-call | tf_op jit(solution)/shard_map/place_near/pallas_call | solution.py:425
  97.8 0.0 collective-permute-done.9.refs_2_
  97.8 22.0 %collective-permute-done.10.refs_3_ = bf16[512,256]{1,0:T(8,128)(2,1)S(1)} collective-permute-done((bf16[512,256]{1,0:T(8,128)(2,1)S(1)}, bf16[512,256]{1,0:T(8,128)(2,1)S(1)}, u32[]{:S(2)}, u32[]{:S(2)}) %collective-permute-start.10) | collective-permute-done | bytes 262176 | tf_op jit(solution)/shard_map/ppermute | solution.py:331
  119.8 7.9 %collective-permute-done.11.refs_4_ = bf16[512,256]{1,0:T(8,128)(2,1)S(1)} collective-permute-done((bf16[512,256]{1,0:T(8,128)(2,1)S(1)}, bf16[512,256]{1,0:T(8,128)(2,1)S(1)}, u32[]{:S(2)}, u32[]{:S(2)}) %collective-permute-start.11) | collective-permute-done | bytes 262176 | tf_op jit(solution)/shard_map/ppermute | solution.py:331
  127.7 6.6 %collective-permute-done.12.refs_5_ = bf16[512,256]{1,0:T(8,128)(2,1)S(1)} collective-permute-done((bf16[512,256]{1,0:T(8,128)(2,1)S(1)}, bf16[512,256]{1,0:T(8,128)(2,1)S(1)}, u32[]{:S(2)}, u32[]{:S(2)}) %collective-permute-start.12) | collective-permute-done | bytes 262176 | tf_op jit(solution)/shard_map/ppermute | solution.py:331
  134.3 1.7 %place_far.1 = bf16[8192,256]{1,0:T(8,128)(2,1)} custom-call(bf16[8192,256]{1,0:T(8,128)(2,1)} %place_near.1.refs_0_, s32[4]{0:T(128)S(1)} %get-tuple-element.28.refs_1_, bf16[512,256]{1,0:T(8,128)(2,1)S(1)} %collective-permute-done.9.refs_2_, bf16[512,256]{1,0:T(8,128)(2,1)S(1)} %collective-permute-done.10.refs_3_, ...), custom_call_target="tpu_custom_call", output_to_operand_aliasing={{}: (0, {})} | custom-call | tf_op jit(solution)/shard_map/place_far/pallas_call | solution.py:444
Async XLA Ops:
  0.0 40.6 %copy-start.1 = (bf16[1,512,1024]{2,1,0:T(8,128)(2,1)S(1)}, bf16[1,512,1024]{2,1,0:T(8,128)(2,1)}, u32[]{:S(2)}) copy-start(bf16[1,512,1024]{2,1,0:T(8,128)(2,1)} %refs_3_.1) | copy-start | bytes 3145732
  19.9 20.7 %collective-permute-start.5 = (bf16[2,128,1024]{2,1,0:T(8,128)(2,1)}, bf16[2,128,1024]{2,1,0:T(8,128)(2,1)S(1)}, u32[]{:S(2)}, u32[]{:S(2)}) collective-permute-start(bf16[2,128,1024]{2,1,0:T(8,128)(2,1)} %bucket.1), channel_id=1, source_target_pairs={{0,16},{16,0},{1,17},{17,1},{2,18},{18,2},{3,19},{19,3},{4,20},{20... | collective-permute-start | bytes 1572872 | tf_op jit(solution)/shard_map/ppermute | solution.py:335
  21.2 11.8 %collective-permute-start = (s32[4,8]{1,0:T(4,128)}, s32[4,8]{1,0:T(4,128)S(1)}, u32[]{:S(2)}, u32[]{:S(2)}) collective-permute-start(s32[4,8]{1,0:T(4,128)} %bitcast_add_fusion.refs_0_.codes), channel_id=1, source_target_pairs={{0,16},{16,0},{1,17},{17,1},{2,18},{18,2},{3,19},{19,3},{4,20},{20... | collective-permute-start | bytes 392 | tf_op jit(solution)/shard_map/ppermute | solution.py:335
  33.0 2.2 %copy-start = (bf16[1,1024,2048]{2,1,0:T(8,128)(2,1)S(1)}, bf16[1,1024,2048]{2,1,0:T(8,128)(2,1)}, u32[]{:S(2)}) copy-start(bf16[1,1024,2048]{2,1,0:T(8,128)(2,1)} %refs_2_.3) | copy-start | bytes 12582916
  35.2 0.7 copy-start.2
  37.3 16.8 %collective-permute-start.1 = (bf16[520,256]{1,0:T(8,128)(2,1)S(1)}, bf16[520,256]{1,0:T(8,128)(2,1)S(1)}, u32[]{:S(2)}, u32[]{:S(2)}) collective-permute-start(bf16[520,256]{1,0:T(8,128)(2,1)S(1)} %get-tuple-element.19), channel_id=1, source_target_pairs={{0,8},{1,9},{2,10},{3,11},{4,12},{5,13},{6,14},{7,15},{8,0},{9,1},... | collective-permute-start | bytes 798728 | tf_op jit(solution)/shard_map/ppermute | solution.py:331
  37.5 22.3 %collective-permute-start.2 = (bf16[520,256]{1,0:T(8,128)(2,1)S(1)}, bf16[520,256]{1,0:T(8,128)(2,1)S(1)}, u32[]{:S(2)}, u32[]{:S(2)}) collective-permute-start(bf16[520,256]{1,0:T(8,128)(2,1)S(1)} %get-tuple-element.20), channel_id=1, source_target_pairs={{0,10},{1,11},{2,8},{3,9},{4,14},{5,15},{6,12},{7,13},{8,2},{9,3},... | collective-permute-start | bytes 798728 | tf_op jit(solution)/shard_map/ppermute | solution.py:331
  46.1 46.7 %collective-permute-start.6 = (bf16[1024,256]{1,0:T(8,128)(2,1)S(1)}, bf16[1024,256]{1,0:T(8,128)(2,1)S(1)}, u32[]{:S(2)}, u32[]{:S(2)}) collective-permute-start(bf16[1024,256]{1,0:T(8,128)(2,1)S(1)} %get-tuple-element.25), channel_id=1, source_target_pairs={{0,2},{1,3},{2,0},{3,1},{4,6},{5,7},{6,4},{7,5},{8,10},{9,11},{10,... | collective-permute-start | bytes 1572872 | tf_op jit(solution)/shard_map/ppermute | solution.py:331
  46.4 46.4 %collective-permute-start.7 = (bf16[1024,256]{1,0:T(8,128)(2,1)S(1)}, bf16[1024,256]{1,0:T(8,128)(2,1)S(1)}, u32[]{:S(2)}, u32[]{:S(2)}) collective-permute-start(bf16[1024,256]{1,0:T(8,128)(2,1)S(1)} %get-tuple-element.26), channel_id=1, source_target_pairs={{0,4},{1,5},{2,6},{3,7},{4,0},{5,1},{6,2},{7,3},{8,12},{9,13},{10,... | collective-permute-start | bytes 1572872 | tf_op jit(solution)/shard_map/ppermute | solution.py:331
  47.7 33.1 %collective-permute-start.3 = (bf16[520,256]{1,0:T(8,128)(2,1)S(1)}, bf16[520,256]{1,0:T(8,128)(2,1)S(1)}, u32[]{:S(2)}, u32[]{:S(2)}) collective-permute-start(bf16[520,256]{1,0:T(8,128)(2,1)S(1)} %get-tuple-element.21), channel_id=1, source_target_pairs={{0,12},{1,13},{2,14},{3,15},{4,8},{5,9},{6,10},{7,11},{8,4},{9,5},... | collective-permute-start | bytes 798728 | tf_op jit(solution)/shard_map/ppermute | solution.py:331
  54.1 38.7 %collective-permute-start.4 = (bf16[520,256]{1,0:T(8,128)(2,1)S(1)}, bf16[520,256]{1,0:T(8,128)(2,1)S(1)}, u32[]{:S(2)}, u32[]{:S(2)}) collective-permute-start(bf16[520,256]{1,0:T(8,128)(2,1)S(1)} %get-tuple-element.22), channel_id=1, source_target_pairs={{0,14},{1,15},{2,12},{3,13},{4,10},{5,11},{6,8},{7,9},{8,6},{9,7},... | collective-permute-start | bytes 798728 | tf_op jit(solution)/shard_map/ppermute | solution.py:331
  59.8 36.4 %collective-permute-start.8 = (bf16[1024,256]{1,0:T(8,128)(2,1)S(1)}, bf16[1024,256]{1,0:T(8,128)(2,1)S(1)}, u32[]{:S(2)}, u32[]{:S(2)}) collective-permute-start(bf16[1024,256]{1,0:T(8,128)(2,1)S(1)} %get-tuple-element.27), channel_id=1, source_target_pairs={{0,6},{1,7},{2,4},{3,5},{4,2},{5,3},{6,0},{7,1},{8,14},{9,15},{10,... | collective-permute-start | bytes 1572872 | tf_op jit(solution)/shard_map/ppermute | solution.py:331
  80.9 16.9 %collective-permute-start.9 = (bf16[512,256]{1,0:T(8,128)(2,1)S(1)}, bf16[512,256]{1,0:T(8,128)(2,1)S(1)}, u32[]{:S(2)}, u32[]{:S(2)}) collective-permute-start(bf16[512,256]{1,0:T(8,128)(2,1)S(1)} %get-tuple-element.29), channel_id=1, source_target_pairs={{0,8},{1,9},{2,10},{3,11},{4,12},{5,13},{6,14},{7,15},{8,0},{9,1},... | collective-permute-start | bytes 786440 | tf_op jit(solution)/shard_map/ppermute | solution.py:331
  92.8 27.0 %collective-permute-start.10 = (bf16[512,256]{1,0:T(8,128)(2,1)S(1)}, bf16[512,256]{1,0:T(8,128)(2,1)S(1)}, u32[]{:S(2)}, u32[]{:S(2)}) collective-permute-start(bf16[512,256]{1,0:T(8,128)(2,1)S(1)} %get-tuple-element.30), channel_id=1, source_target_pairs={{0,10},{1,11},{2,8},{3,9},{4,14},{5,15},{6,12},{7,13},{8,2},{9,3},... | collective-permute-start | bytes 786440 | tf_op jit(solution)/shard_map/ppermute | solution.py:331
  92.8 34.9 %collective-permute-start.11 = (bf16[512,256]{1,0:T(8,128)(2,1)S(1)}, bf16[512,256]{1,0:T(8,128)(2,1)S(1)}, u32[]{:S(2)}, u32[]{:S(2)}) collective-permute-start(bf16[512,256]{1,0:T(8,128)(2,1)S(1)} %get-tuple-element.31), channel_id=1, source_target_pairs={{0,12},{1,13},{2,14},{3,15},{4,8},{5,9},{6,10},{7,11},{8,4},{9,5},... | collective-permute-start | bytes 786440 | tf_op jit(solution)/shard_map/ppermute | solution.py:331
  92.8 41.5 %collective-permute-start.12 = (bf16[512,256]{1,0:T(8,128)(2,1)S(1)}, bf16[512,256]{1,0:T(8,128)(2,1)S(1)}, u32[]{:S(2)}, u32[]{:S(2)}) collective-permute-start(bf16[512,256]{1,0:T(8,128)(2,1)S(1)} %get-tuple-element.32), channel_id=1, source_target_pairs={{0,14},{1,15},{2,12},{3,13},{4,10},{5,11},{6,8},{7,9},{8,6},{9,7},... | collective-permute-start | bytes 786440 | tf_op jit(solution)/shard_map/ppermute | solution.py:331

commit v2 on v1

v2 whole, which is shorter than its diff:
```python
import functools

import jax
import jax.numpy as jnp
from jax import lax
from jax.experimental import pallas as pl
from jax.experimental.pallas import tpu as pltpu
from jax.sharding import PartitionSpec as P

GRID_COLS = 8
NEAR = GRID_COLS // 2
FAR = (5, 7, 4, 6)
TAG = 8

ANY = pl.BlockSpec(memory_space=pl.ANY)
HBM = pl.BlockSpec(memory_space=pltpu.HBM)
SMEM = pl.BlockSpec(memory_space=pltpu.SMEM)
VMEM = pl.BlockSpec(memory_space=pltpu.VMEM)


class Plan:
    def __init__(self, updates, panels, slot_cols):
        self.groups = lax.axis_size("front")
        self.lanes = lax.axis_size("wide")
        self.grid_rows = self.lanes // GRID_COLS
        self.slots = slot_cols.shape[1]
        self.columns = slot_cols.shape[2]
        self.block = updates.shape[1] // self.slots
        self.rows = panels.shape[1] // self.block
        self.window = panels.shape[2] // self.block
        self.col_groups = self.window // GRID_COLS
        self.width = self.col_groups * self.block
        self.capacity = max(self.slots // 4, self.slots // self.groups)
        self.first = max(0, self.rows - self.capacity * self.groups)
        self.early = {5: self.first, 7: self.first, 4: self.first, 6: 0}
        self.late = [(o, 0, self.rows) for o in range(NEAR)]
        for o in FAR:
            count = self.rows - self.early[o]
            cuts = [0, count // 2, count] if o == 6 else [0, count]
            self.late += [(o, lo, hi) for lo, hi in zip(cuts, cuts[1:])]


COST = pl.CostEstimate(flops=0, transcendentals=0, bytes_accessed=0)


def params():
    return pltpu.CompilerParams(vmem_limit_bytes=48 << 20)


def at(start, size):
    return pl.ds(pl.multiple_of(start * size, size), size)


def parent_of(plan, heads, q):
    return heads[q] // plan.rows


def row_of(plan, heads, q):
    return heads[q] % plan.rows


def touched_rows(plan, head_refs):
    me = lax.axis_index("front")
    touched = jnp.int32(0)
    for heads in head_refs:
        for q in range(plan.slots):
            bit = jnp.left_shift(jnp.int32(1), row_of(plan, heads, q))
            touched = touched | jnp.where(parent_of(plan, heads, q) == me, bit, 0)
    return touched


def first_rows(plan, touched, limit):
    chosen, count = jnp.int32(0), jnp.int32(0)
    for t in range(plan.rows):
        free = (jnp.right_shift(touched, t) & 1) == 0
        take = jnp.logical_and(free, count < limit)
        chosen = chosen | jnp.where(take, 1 << t, 0)
        count = count + jnp.where(take, 1, 0)
    return chosen


def positions(plan, chosen):
    out, count = [], jnp.int32(0)
    for t in range(plan.rows):
        bit = jnp.right_shift(chosen, t) & 1
        out.append((bit, jnp.where(bit == 1, count, t - count)))
        count = count + bit
    return out


def list_rows(plan, chosen, bit_wanted, where):
    for t, (bit, place) in enumerate(positions(plan, chosen)):

        @pl.when(bit == bit_wanted)
        def _():
            where[place] = t


def run_all(copies):
    for copy in copies:
        copy.start()
    for copy in copies:
        copy.wait()


def bucket_kernel(plan, heads, updates, *refs):
    outs, sems = refs[-plan.groups : -1], refs[-1]
    me = lax.axis_index("front")

    def copies(act):
        for k in range(1, plan.groups):
            target = lax.rem(me + k, plan.groups)
            rank = jnp.int32(0)
            for q in range(plan.slots):
                named = parent_of(plan, heads, q) == target

                @pl.when(named)
                def _():
                    act(
                        pltpu.make_async_copy(
                            updates.at[0, pl.ds(q * plan.block, plan.block)],
                            outs[k - 1].at[rank],
                            sems.at[q],
                        )
                    )

                rank = rank + jnp.where(named, 1, 0)

    copies(lambda c: c.start())
    copies(lambda c: c.wait())


def pack_kernel(plan, offsets, *refs):
    groups = plan.groups
    head_refs, panel = refs[:groups], refs[groups]
    outs, refs = refs[groups + 1 : groups + 1 + len(offsets)], refs[groups + 1 + len(offsets) :]
    touched_out, order, sems = refs
    column = lax.axis_index("wide") // plan.grid_rows
    block = plan.block
    touched = touched_rows(plan, head_refs)
    touched_out[0] = touched
    list_rows(plan, first_rows(plan, touched, plan.first), 1, order)
    copies = []
    for i, o in enumerate(offsets):
        target = jnp.bitwise_xor(column, o)
        for k in range(plan.early[o]):
            for cc in range(plan.col_groups):
                copies.append(
                    pltpu.make_async_copy(
                        panel.at[0, at(order[k], block), at(cc * GRID_COLS + target, block)],
                        outs[i].at[pl.ds(k * block, block), pl.ds(cc * block, block)],
                        sems.at[i, k, cc],
                    )
                )
                copies[-1].start()
    for i, o in enumerate(offsets):
        chosen = first_rows(plan, touched, plan.early[o]).astype(jnp.float32)
        tag = jnp.full((TAG, plan.width), chosen, jnp.float32).astype(jnp.bfloat16)
        outs[i][plan.early[o] * block :, :] = tag
    for copy in copies:
        copy.wait()


def assemble_kernel(plan, *refs):
    groups, block = plan.groups, plan.block
    head_refs, refs = refs[:groups], refs[groups:]
    code_refs, refs = refs[:groups], refs[groups:]
    panel, updates, refs = refs[0], refs[1], refs[2:]
    got, refs = refs[: groups - 1], refs[groups - 1 :]
    outs, refs = refs[: len(plan.late)], refs[len(plan.late) :]
    total, raw, moved, place_ref, row_sems, slot_sems = refs
    me = lax.axis_index("front")
    column = lax.axis_index("wide") // plan.grid_rows

    slot_copies = [
        pltpu.make_async_copy(
            updates.at[0, pl.ds(q * block, block)], moved.at[q], slot_sems.at[q]
        )
        for q in range(plan.slots)
    ]
    for k in range(1, groups):
        for c in range(plan.capacity):
            index = plan.slots + (k - 1) * plan.capacity + c
            slot_copies.append(
                pltpu.make_async_copy(got[k - 1].at[c], moved.at[index], slot_sems.at[index])
            )
    row_copies = [
        pltpu.make_async_copy(panel.at[0, pl.ds(t * block, block)], raw.at[t], row_sems.at[t])
        for t in range(plan.rows)
    ]
    for copy in row_copies + slot_copies:
        copy.start()

    touched = touched_rows(plan, head_refs)
    for o in FAR:
        for t, (bit, place) in enumerate(
            positions(plan, first_rows(plan, touched, plan.early[o]))
        ):
            place_ref[o, t] = jnp.where(bit == 1, -1, place)

    for t in range(plan.rows):
        row_copies[t].wait()
    for copy in slot_copies:
        copy.wait()

    def widen(t, carry):
        total[t] = raw[t].astype(jnp.float32)
        return carry

    lax.fori_loop(0, plan.rows, widen, 0)

    for s, (heads, codes) in enumerate(zip(head_refs, code_refs)):

        def add_slot(q, rank):
            named = parent_of(plan, heads, q) == me
            index = q if s == 0 else plan.slots + (s - 1) * plan.capacity + rank
            t = row_of(plan, heads, q)

            @pl.when(named)
            def _():
                for j in range(plan.columns):
                    code = codes[q, j]
                    col = code % plan.window

                    @pl.when(code >= plan.window)
                    def _():
                        where = at(col, block)
                        total[t, :, where] += moved[
                            index, :, pl.ds(j * block, block)
                        ].astype(jnp.float32)

            return rank + jnp.where(named, 1, 0)

        lax.fori_loop(0, plan.slots, add_slot, jnp.int32(0))

    def pack(t, carry):
        for ref, (o, lo, hi) in zip(outs, plan.late):
            target = jnp.bitwise_xor(column, o)

            def put(row):
                for cc in range(plan.col_groups):
                    ref[at(row, block), pl.ds(cc * block, block)] = total[
                        t, :, at(cc * GRID_COLS + target, block)
                    ].astype(jnp.bfloat16)

            if hi - lo == plan.rows:
                put(t)
            else:
                place = place_ref[o, t] if plan.early[o] else t
                pl.when(jnp.logical_and(place >= lo, place < hi))(lambda: put(place - lo))

        return carry

    lax.fori_loop(0, plan.rows, pack, 0)


def place_early_kernel(plan, offsets, *refs):
    count = len(offsets)
    pieces, out, sets, refs = refs[:count], refs[count], refs[count + 1], refs[count + 2 :]
    tags, where, tag_sems, sems = refs
    column = lax.axis_index("wide") // plan.grid_rows
    block = plan.block
    run_all(
        [
            pltpu.make_async_copy(
                pieces[i].at[pl.ds(plan.early[o] * block, TAG)], tags.at[i], tag_sems.at[i]
            )
            for i, o in enumerate(offsets)
        ]
    )
    copies = []
    for i, o in enumerate(offsets):
        source = jnp.bitwise_xor(column, o)
        chosen = jnp.max(tags[i].astype(jnp.float32)).astype(jnp.int32)
        sets[i] = chosen
        list_rows(plan, chosen, 1, where.at[i])
        for k in range(plan.early[o]):
            copies.append(
                pltpu.make_async_copy(
                    pieces[i].at[pl.ds(k * block, block)],
                    out.at[at(where[i, k] * GRID_COLS + source, block)],
                    sems.at[i, k],
                )
            )
            copies[-1].start()
    for copy in copies:
        copy.wait()


def place_late_kernel(plan, messages, early, sets, pieces, out, where, sems):
    column = lax.axis_index("wide") // plan.grid_rows
    block = plan.block
    copies = []
    for i, (o, lo, hi) in enumerate(messages):
        source = jnp.bitwise_xor(column, o)
        split = o in early
        if split:
            list_rows(plan, sets[early.index(o)], 0, where.at[i])
        for k in range(lo, hi):
            t = where[i, k] if split else k
            copies.append(
                pltpu.make_async_copy(
                    pieces[i].at[pl.ds((k - lo) * block, block)],
                    out.at[at(t * GRID_COLS + source, block)],
                    sems.at[i, k],
                )
            )
            copies[-1].start()
    for copy in copies:
        copy.wait()


def after(value, *others):
    return lax.optimization_barrier((value, *others))[0]


def across(value, plan, offset):
    pairs = [
        (c * plan.grid_rows + r, (c ^ offset) * plan.grid_rows + r)
        for c in range(GRID_COLS)
        for r in range(plan.grid_rows)
    ]
    return lax.ppermute(value, "wide", pairs)


def along(value, plan, steps):
    return lax.ppermute(
        value, "front", [(f, (f + steps) % plan.groups) for f in range(plan.groups)]
    )


def local(updates, parent_panels, slot_parent, slot_row, slot_cols, slot_mask):
    plan = Plan(updates, parent_panels, slot_cols)
    block, width = plan.block, plan.width
    bf16 = jnp.bfloat16
    heads = slot_parent[0, :, 0] * plan.rows + slot_row[0]
    all_heads = [heads] + [along(heads, plan, k) for k in range(1, plan.groups)]
    codes = slot_mask[0] * plan.window + slot_cols[0]
    panels = pltpu.with_memory_space_constraint(parent_panels, pltpu.HBM)


    early = [o for o in FAR if plan.early[o]]
    packed, touched = {}, []
    if early:
        *outs, touched_set = pl.pallas_call(
            functools.partial(pack_kernel, plan, early),
            out_shape=[
                jax.ShapeDtypeStruct((plan.early[o] * block + TAG, width), bf16) for o in early
            ]
            + [jax.ShapeDtypeStruct((1,), jnp.int32)],
            in_specs=[SMEM] * plan.groups + [HBM],
            out_specs=[VMEM] * len(early) + [SMEM],
            scratch_shapes=[
                pltpu.SMEM((plan.rows,), jnp.int32),
                pltpu.SemaphoreType.DMA((len(early), plan.first, plan.col_groups)),
            ],
            compiler_params=params(),
            cost_estimate=COST,
            name="pack_early",
        )(*all_heads, panels)
        packed = dict(zip(early, outs))
        touched = [touched_set]
        codes = after(codes, touched_set)

    buckets = pl.pallas_call(
        functools.partial(bucket_kernel, plan),
        out_shape=[
            jax.ShapeDtypeStruct((plan.capacity, block, updates.shape[2]), bf16)
            for _ in range(1, plan.groups)
        ],
        in_specs=[SMEM, HBM] + [SMEM] * len(touched),
        out_specs=[VMEM] * (plan.groups - 1),
        scratch_shapes=[pltpu.SemaphoreType.DMA((plan.slots,))],
        compiler_params=params(),
        cost_estimate=COST,
        name="bucket",
    )(heads, updates, *touched)

    all_codes = [codes] + [along(codes, plan, k) for k in range(1, plan.groups)]
    got = [along(buckets[k - 1], plan, k) for k in range(1, plan.groups)]

    moved = plan.slots + (plan.groups - 1) * plan.capacity
    assembled = pl.pallas_call(
        functools.partial(assemble_kernel, plan),
        out_shape=[
            jax.ShapeDtypeStruct(((hi - lo) * block, width), bf16) for o, lo, hi in plan.late
        ],
        in_specs=[SMEM] * (2 * plan.groups) + [HBM, HBM] + [ANY] * (plan.groups - 1),
        out_specs=[VMEM] * len(plan.late),
        scratch_shapes=[
            pltpu.VMEM((plan.rows, block, parent_panels.shape[2]), jnp.float32),
            pltpu.VMEM((plan.rows, block, parent_panels.shape[2]), bf16),
            pltpu.VMEM((moved, block, updates.shape[2]), bf16),
            pltpu.SMEM((GRID_COLS, plan.rows), jnp.int32),
            pltpu.SemaphoreType.DMA((plan.rows,)),
            pltpu.SemaphoreType.DMA((moved,)),
        ],
        compiler_params=params(),
        cost_estimate=COST,
        name="assemble",
    )(*all_heads, *all_codes, panels, updates, *got)

    ready = dict(zip(plan.late, assembled))

    def late(o, part=0):
        return [m for m in plan.late if m[0] == o][part]

    first = {o: across(packed[o], plan, o) for o in early}
    arrived = {late(0): ready[late(0)]}

    def send(message, *others):
        arrived[message] = across(after(ready[message], *others), plan, message[0])
        return arrived[message]

    gate = [first[o] for o in early]
    a = send(late(5), *gate)
    b = send(late(7), *gate)
    send(late(4), *gate)
    n1 = send(late(1), *gate)
    n2 = send(late(2), *gate)
    send(late(3), n1, n2)
    send(late(6, 0), a)
    send(late(6, 1), b)

    out_shape = jax.ShapeDtypeStruct((plan.rows * GRID_COLS * block, width), bf16)
    held, sets = [], []
    if early:
        out, sets = pl.pallas_call(
            functools.partial(place_early_kernel, plan, early),
            out_shape=[out_shape, jax.ShapeDtypeStruct((len(early),), jnp.int32)],
            in_specs=[ANY] * len(early),
            out_specs=[HBM, SMEM],
            scratch_shapes=[
                pltpu.VMEM((len(early), TAG, width), bf16),
                pltpu.SMEM((len(early), plan.rows), jnp.int32),
                pltpu.SemaphoreType.DMA((len(early),)),
                pltpu.SemaphoreType.DMA((len(early), plan.first)),
            ],
            compiler_params=params(),
            cost_estimate=COST,
            name="place_early",
        )(*[first[o] for o in early])
        held, sets = [out], [sets]

    def place(held, messages, name):
        def body(*refs):
            refs = list(refs)[len(held) :]
            sets_ref = refs.pop(0) if sets else None
            count = len(messages)
            place_late_kernel(plan, messages, early, sets_ref, refs[:count], *refs[count:])

        return [
            pl.pallas_call(
                body,
                out_shape=out_shape,
                in_specs=[HBM] * len(held) + [SMEM] * len(sets) + [ANY] * len(messages),
                out_specs=HBM,
                input_output_aliases={0: 0} if held else {},
                scratch_shapes=[
                    pltpu.SMEM((len(messages), plan.rows), jnp.int32),
                    pltpu.SemaphoreType.DMA((len(messages), plan.rows)),
                ],
                compiler_params=params(),
                cost_estimate=COST,
                name=name,
            )(*held, *sets, *[arrived[m] for m in messages])
        ]

    last = [late(4), late(6, 0), late(6, 1)]
    held = place(held, [m for m in plan.late if m not in last], "place_mid")
    held = place(held, last, "place_last")
    return held[0][None]


def solution(mesh):
    return jax.shard_map(
        local,
        mesh=mesh,
        in_specs=(
            P("front", "wide", None),
            P("front", "wide", None),
            P("front", "wide", None),
            P("front", "wide"),
            P("front", "wide", None),
            P("front", "wide", None),
        ),
        out_specs=P("front", "wide", None),
        check_vma=False,
    )
```

time: 136 us -> 118 us (0.87)
  the two profiles are of different devices: /device:TPU:17 before, /device:TPU:16 now
where the time goes in v2:
time: 118 us
  waiting for transfers between devices  71.5 us (61%)
  starting transfers between devices  30.2 us (26%)
  Pallas kernels  15.1 us (13%)
    ppermute x11, waiting for transfers between devices, across(): return lax.ppermute(value, 'wide', pairs)  64.2 us
    ppermute x11, starting transfers between devices, across(): return lax.ppermute(value, 'wide', pairs)  26.5 us
    ppermute x3, waiting for transfers between devices, along(): lax.ppermute(value, 'front', [(f, (f + steps) % plan.groups) for f in ran...  7.3 us
    pallas_call x1, Pallas kernels, local(): pl.pallas_call(functools.partial(assemble_kernel, plan), out_shape=[jax.S...  5.45 us
    pallas_call x2, Pallas kernels, place(): pl.pallas_call(body, out_shape=out_shape, in_specs=[HBM] * len(held) + [S...  4.09 us
    ppermute x3, starting transfers between devices, along(): lax.ppermute(value, 'front', [(f, (f + steps) % plan.groups) for f in ran...  3.68 us
    pallas_call x1, Pallas kernels, local(): pl.pallas_call(functools.partial(pack_kernel, plan, early), out_shape=[ja...  2.49 us
  transfers between devices with their start and end apart: 14, of which 10 were waited for; matrix products, arithmetic and copies ran while one was open for 0% of the time, Pallas kernels for 8%

profile of v2, /device:TPU:16, one launch (start us, length us, event | category | flops | bytes accessed | tf_op | source)
XLA Modules:
  0.0 117.7 jit_solution(3627912423947393934)
XLA Ops:
  0.0 0.0 copy-start
  0.0 0.0 copy-start.2
  0.0 0.0 copy-start.1
  0.0 0.8 bitcast_add_fusion.refs_0_.heads
  0.8 1.5 %collective-permute-start = (s32[4]{0:T(128)S(1)}, s32[4]{0:T(128)S(1)}, u32[]{:S(2)}, u32[]{:S(2)}) collective-permute-start(s32[4]{0:T(128)S(1)} %bitcast_add_fusion.refs_0_.heads), channel_id=1, source_target_pairs={{0,16},{16,0},{1,17},{17,1},{2,18},{18,2},{3,19},{19,3},{4,20},{20... | collective-permute-start | bytes 56 | tf_op jit(solution)/shard_map/ppermute | solution.py:327
  2.3 2.0 %collective-permute-done.refs_1_ = s32[4]{0:T(128)S(1)} collective-permute-done((s32[4]{0:T(128)S(1)}, s32[4]{0:T(128)S(1)}, u32[]{:S(2)}, u32[]{:S(2)}) %collective-permute-start) | collective-permute-done | bytes 48 | tf_op jit(solution)/shard_map/ppermute | solution.py:327
  4.3 2.5 %pack_early.1 = (bf16[520,256]{1,0:T(8,128)(2,1)S(1)}, bf16[520,256]{1,0:T(8,128)(2,1)S(1)}, bf16[520,256]{1,0:T(8,128)(2,1)S(1)}, s32[1]{0:T(128)}) custom-call(s32[4]{0:T(128)S(1)} %bitcast_add_fusion.refs_0_.heads, s32[4]{0:T(128)S(1)} %collective-permute-done.refs_1_, bf16[1,1024,2048]{2,1,0:T(8,128)(2,1)} %refs_4_.1), custom_call_target="tpu_custom_call" | custom-call | tf_op jit(solution)/shard_map/pack_early/pallas_call | solution.py:345
  6.8 0.0 copy-done
  6.8 1.4 %bucket.1 = bf16[2,128,1024]{2,1,0:T(8,128)(2,1)S(1)} custom-call(s32[4]{0:T(128)S(1)} %bitcast_add_fusion.refs_0_.heads, bf16[1,512,1024]{2,1,0:T(8,128)(2,1)S(1)} %copy-done, s32[1]{0:T(128)} %get-tuple-element.34.refs_0_), custom_call_target="tpu_custom_call" | custom-call | tf_op jit(solution)/shard_map/bucket/pallas_call | solution.py:365
  8.2 1.6 %collective-permute-start.5 = (bf16[2,128,1024]{2,1,0:T(8,128)(2,1)S(1)}, bf16[2,128,1024]{2,1,0:T(8,128)(2,1)S(1)}, u32[]{:S(2)}, u32[]{:S(2)}) collective-permute-start(bf16[2,128,1024]{2,1,0:T(8,128)(2,1)S(1)} %bucket.1), channel_id=1, source_target_pairs={{0,16},{16,0},{1,17},{17,1},{2,18},{18,2},{3,19},{19,3},{4,20},{20... | collective-permute-start | bytes 1572872 | tf_op jit(solution)/shard_map/ppermute | solution.py:327
  9.8 1.3 %collective-permute-start.1 = (bf16[520,256]{1,0:T(8,128)(2,1)S(1)}, bf16[520,256]{1,0:T(8,128)(2,1)S(1)}, u32[]{:S(2)}, u32[]{:S(2)}) collective-permute-start(bf16[520,256]{1,0:T(8,128)(2,1)S(1)} %get-tuple-element.29), channel_id=1, source_target_pairs={{0,10},{1,11},{2,8},{3,9},{4,14},{5,15},{6,12},{7,13},{8,2},{9,3},... | collective-permute-start | bytes 798728 | tf_op jit(solution)/shard_map/ppermute | solution.py:323
  11.0 2.7 %collective-permute-start.2 = (bf16[520,256]{1,0:T(8,128)(2,1)S(1)}, bf16[520,256]{1,0:T(8,128)(2,1)S(1)}, u32[]{:S(2)}, u32[]{:S(2)}) collective-permute-start(bf16[520,256]{1,0:T(8,128)(2,1)S(1)} %get-tuple-element.30), channel_id=1, source_target_pairs={{0,14},{1,15},{2,12},{3,13},{4,10},{5,11},{6,8},{7,9},{8,6},{9,7},... | collective-permute-start | bytes 798728 | tf_op jit(solution)/shard_map/ppermute | solution.py:323
  13.7 1.2 %collective-permute-start.3 = (bf16[520,256]{1,0:T(8,128)(2,1)S(1)}, bf16[520,256]{1,0:T(8,128)(2,1)S(1)}, u32[]{:S(2)}, u32[]{:S(2)}) collective-permute-start(bf16[520,256]{1,0:T(8,128)(2,1)S(1)} %get-tuple-element.31), channel_id=1, source_target_pairs={{0,8},{1,9},{2,10},{3,11},{4,12},{5,13},{6,14},{7,15},{8,0},{9,1},... | collective-permute-start | bytes 798728 | tf_op jit(solution)/shard_map/ppermute | solution.py:323
  15.0 0.0 copy-done.2
  15.0 0.0 copy-done.1
  15.0 0.6 collective-permute-start.4
  15.5 5.3 %collective-permute-done.4.refs_3_ = s32[4,8]{1,0:T(4,128)S(1)} collective-permute-done((s32[4,8]{1,0:T(4,128)S(1)}, s32[4,8]{1,0:T(4,128)S(1)}, u32[]{:S(2)}, u32[]{:S(2)}) %collective-permute-start.4) | collective-permute-done | bytes 160 | tf_op jit(solution)/shard_map/ppermute | solution.py:327
  20.8 0.0 collective-permute-done.5.refs_6_
  20.8 5.4 %assemble.1 = (bf16[1024,256]{1,0:T(8,128)(2,1)S(1)}, bf16[1024,256]{1,0:T(8,128)(2,1)S(1)}, bf16[1024,256]{1,0:T(8,128)(2,1)S(1)}, bf16[1024,256]{1,0:T(8,128)(...) custom-call(s32[4]{0:T(128)S(1)} %bitcast_add_fusion.refs_0_.heads, ...), custom_call_target="tpu_custom_call" | custom-call | tf_op jit(solution)/shard_map/assemble/pallas_call | solution.py:383
  26.3 7.3 %collective-permute-done.1.refs_0_ = bf16[520,256]{1,0:T(8,128)(2,1)S(1)} collective-permute-done((bf16[520,256]{1,0:T(8,128)(2,1)S(1)}, bf16[520,256]{1,0:T(8,128)(2,1)S(1)}, u32[]{:S(2)}, u32[]{:S(2)}) %collective-permute-start.1) | collective-permute-done | bytes 266272 | tf_op jit(solution)/shard_map/ppermute | solution.py:323
  33.6 7.6 %collective-permute-done.2.refs_1_ = bf16[520,256]{1,0:T(8,128)(2,1)S(1)} collective-permute-done((bf16[520,256]{1,0:T(8,128)(2,1)S(1)}, bf16[520,256]{1,0:T(8,128)(2,1)S(1)}, u32[]{:S(2)}, u32[]{:S(2)}) %collective-permute-start.2) | collective-permute-done | bytes 266272 | tf_op jit(solution)/shard_map/ppermute | solution.py:323
  41.2 2.6 %collective-permute-done.3.refs_2_ = bf16[520,256]{1,0:T(8,128)(2,1)S(1)} collective-permute-done((bf16[520,256]{1,0:T(8,128)(2,1)S(1)}, bf16[520,256]{1,0:T(8,128)(2,1)S(1)}, u32[]{:S(2)}, u32[]{:S(2)}) %collective-permute-start.3) | collective-permute-done | bytes 266272 | tf_op jit(solution)/shard_map/ppermute | solution.py:323
  43.8 4.5 %collective-permute-start.7 = (bf16[1024,256]{1,0:T(8,128)(2,1)S(1)}, bf16[1024,256]{1,0:T(8,128)(2,1)S(1)}, u32[]{:S(2)}, u32[]{:S(2)}) collective-permute-start(bf16[1024,256]{1,0:T(8,128)(2,1)S(1)} %get-tuple-element.40), channel_id=1, source_target_pairs={{0,4},{1,5},{2,6},{3,7},{4,0},{5,1},{6,2},{7,3},{8,12},{9,13},{10,... | collective-permute-start | bytes 1572872 | tf_op jit(solution)/shard_map/ppermute | solution.py:323
  48.3 0.5 collective-permute-start.6
  48.8 0.4 collective-permute-start.10
  49.2 16.1 %collective-permute-done.7.refs_4_ = bf16[1024,256]{1,0:T(8,128)(2,1)S(1)} collective-permute-done((bf16[1024,256]{1,0:T(8,128)(2,1)S(1)}, bf16[1024,256]{1,0:T(8,128)(2,1)S(1)}, u32[]{:S(2)}, u32[]{:S(2)}) %collective-permute-start.7) | collective-permute-done | bytes 524320 | tf_op jit(solution)/shard_map/ppermute | solution.py:323
  65.3 2.2 %collective-permute-done.6.refs_3_ = bf16[1024,256]{1,0:T(8,128)(2,1)S(1)} collective-permute-done((bf16[1024,256]{1,0:T(8,128)(2,1)S(1)}, bf16[1024,256]{1,0:T(8,128)(2,1)S(1)}, u32[]{:S(2)}, u32[]{:S(2)}) %collective-permute-start.6) | collective-permute-done | bytes 524320 | tf_op jit(solution)/shard_map/ppermute | solution.py:323
  67.5 0.2 collective-permute-start.8
  67.7 0.5 collective-permute-start.9
  68.2 3.4 %collective-permute-start.11 = (bf16[512,256]{1,0:T(8,128)(2,1)S(1)}, bf16[512,256]{1,0:T(8,128)(2,1)S(1)}, u32[]{:S(2)}, u32[]{:S(2)}) collective-permute-start(bf16[512,256]{1,0:T(8,128)(2,1)S(1)} %get-tuple-element.48), channel_id=1, source_target_pairs={{0,8},{1,9},{2,10},{3,11},{4,12},{5,13},{6,14},{7,15},{8,0},{9,1},... | collective-permute-start | bytes 786440 | tf_op jit(solution)/shard_map/ppermute | solution.py:323
  71.6 0.0 collective-permute-done.10.refs_7_
  71.6 0.3 collective-permute-start.13
  71.9 14.9 %collective-permute-done.9.refs_6_ = bf16[512,256]{1,0:T(8,128)(2,1)S(1)} collective-permute-done((bf16[512,256]{1,0:T(8,128)(2,1)S(1)}, bf16[512,256]{1,0:T(8,128)(2,1)S(1)}, u32[]{:S(2)}, u32[]{:S(2)}) %collective-permute-start.9) | collective-permute-done | bytes 262176 | tf_op jit(solution)/shard_map/ppermute | solution.py:323
  86.8 11.5 %collective-permute-start.12 = (bf16[512,256]{1,0:T(8,128)(2,1)S(1)}, bf16[512,256]{1,0:T(8,128)(2,1)S(1)}, u32[]{:S(2)}, u32[]{:S(2)}) collective-permute-start(bf16[512,256]{1,0:T(8,128)(2,1)S(1)} %get-tuple-element.50), channel_id=1, source_target_pairs={{0,12},{1,13},{2,14},{3,15},{4,8},{5,9},{6,10},{7,11},{8,4},{9,5},... | collective-permute-start | bytes 786440 | tf_op jit(solution)/shard_map/ppermute | solution.py:323
  98.3 1.7 %place_early.1 = (bf16[8192,256]{1,0:T(8,128)(2,1)}, s32[3]{0:T(128)S(1)}) custom-call(bf16[520,256]{1,0:T(8,128)(2,1)S(1)} %collective-permute-done.1.refs_0_, bf16[520,256]{1,0:T(8,128)(2,1)S(1)} %collective-permute-done.2.refs_1_, bf16[520,256]{1,0:T(8,128)(2,1)S(1)} %collective-permute-done.3.refs_2_), custom_call_target="tpu_custom_call" | custom-call | tf_op jit(solution)/shard_map/place_early/pallas_call | solution.py:428
  100.1 0.0 collective-permute-done.8.refs_5_
  100.1 2.4 %place_mid.1.refs_0_ = bf16[8192,256]{1,0:T(8,128)(2,1)} custom-call(bf16[8192,256]{1,0:T(8,128)(2,1)} %get-tuple-element.32.refs_0_, s32[3]{0:T(128)S(1)} %get-tuple-element.33.refs_1_, bf16[1024,256]{1,0:T(8,128)(2,1)S(1)} %get-tuple-element.36.refs_2_, bf16[1024,256]{1,0:T(8,128)(2,1)S(1)} %collective-permute-done.6.refs_3_, ...), custom_call_target="tpu_custom_call", output_to_operand_aliasing={{}: (0, {})} | custom-call | tf_op jit(solution)/shard_map/place_mid/pallas_call | solution.py:453
  102.5 0.0 collective-permute-done.11.refs_2_
  102.5 10.3 %collective-permute-done.13.refs_4_ = bf16[512,256]{1,0:T(8,128)(2,1)S(1)} collective-permute-done((bf16[512,256]{1,0:T(8,128)(2,1)S(1)}, bf16[512,256]{1,0:T(8,128)(2,1)S(1)}, u32[]{:S(2)}, u32[]{:S(2)}) %collective-permute-start.13) | collective-permute-done | bytes 262176 | tf_op jit(solution)/shard_map/ppermute | solution.py:323
  112.8 3.2 %collective-permute-done.12.refs_3_ = bf16[512,256]{1,0:T(8,128)(2,1)S(1)} collective-permute-done((bf16[512,256]{1,0:T(8,128)(2,1)S(1)}, bf16[512,256]{1,0:T(8,128)(2,1)S(1)}, u32[]{:S(2)}, u32[]{:S(2)}) %collective-permute-start.12) | collective-permute-done | bytes 262176 | tf_op jit(solution)/shard_map/ppermute | solution.py:323
  116.0 1.6 %place_last.1 = bf16[8192,256]{1,0:T(8,128)(2,1)} custom-call(bf16[8192,256]{1,0:T(8,128)(2,1)} %place_mid.1.refs_0_, s32[3]{0:T(128)S(1)} %get-tuple-element.33.refs_1_, bf16[512,256]{1,0:T(8,128)(2,1)S(1)} %collective-permute-done.11.refs_2_, bf16[512,256]{1,0:T(8,128)(2,1)S(1)} %collective-permute-done.12.refs_3_, ...), custom_call_target="tpu_custom_call", output_to_operand_aliasing={{}: (0, {})} | custom-call | tf_op jit(solution)/shard_map/place_last/pallas_call | solution.py:453
  (1 shorter events, 0.0 us)
Async XLA Ops:
  0.0 6.8 %copy-start = (bf16[1,512,1024]{2,1,0:T(8,128)(2,1)S(1)}, bf16[1,512,1024]{2,1,0:T(8,128)(2,1)}, u32[]{:S(2)}) copy-start(bf16[1,512,1024]{2,1,0:T(8,128)(2,1)} %refs_5_.1) | copy-start | bytes 3145732
  0.0 15.0 %copy-start.2 = (s32[1,4,8]{2,1,0:T(4,128)S(1)}, s32[1,4,8]{2,1,0:T(4,128)}, u32[]{:S(2)}) copy-start(s32[1,4,8]{2,1,0:T(4,128)} %param.11) | copy-start | bytes 388
  0.0 15.0 %copy-start.1 = (s32[1,4,8]{2,1,0:T(4,128)S(1)}, s32[1,4,8]{2,1,0:T(4,128)}, u32[]{:S(2)}) copy-start(s32[1,4,8]{2,1,0:T(4,128)} %param.10) | copy-start | bytes 388
  0.8 3.5 %collective-permute-start = (s32[4]{0:T(128)S(1)}, s32[4]{0:T(128)S(1)}, u32[]{:S(2)}, u32[]{:S(2)}) collective-permute-start(s32[4]{0:T(128)S(1)} %bitcast_add_fusion.refs_0_.heads), channel_id=1, source_target_pairs={{0,16},{16,0},{1,17},{17,1},{2,18},{18,2},{3,19},{19,3},{4,20},{20... | collective-permute-start | bytes 56 | tf_op jit(solution)/shard_map/ppermute | solution.py:327
  8.2 12.6 %collective-permute-start.5 = (bf16[2,128,1024]{2,1,0:T(8,128)(2,1)S(1)}, bf16[2,128,1024]{2,1,0:T(8,128)(2,1)S(1)}, u32[]{:S(2)}, u32[]{:S(2)}) collective-permute-start(bf16[2,128,1024]{2,1,0:T(8,128)(2,1)S(1)} %bucket.1), channel_id=1, source_target_pairs={{0,16},{16,0},{1,17},{17,1},{2,18},{18,2},{3,19},{19,3},{4,20},{20... | collective-permute-start | bytes 1572872 | tf_op jit(solution)/shard_map/ppermute | solution.py:327
  9.8 23.8 %collective-permute-start.1 = (bf16[520,256]{1,0:T(8,128)(2,1)S(1)}, bf16[520,256]{1,0:T(8,128)(2,1)S(1)}, u32[]{:S(2)}, u32[]{:S(2)}) collective-permute-start(bf16[520,256]{1,0:T(8,128)(2,1)S(1)} %get-tuple-element.29), channel_id=1, source_target_pairs={{0,10},{1,11},{2,8},{3,9},{4,14},{5,15},{6,12},{7,13},{8,2},{9,3},... | collective-permute-start | bytes 798728 | tf_op jit(solution)/shard_map/ppermute | solution.py:323
  11.0 30.2 %collective-permute-start.2 = (bf16[520,256]{1,0:T(8,128)(2,1)S(1)}, bf16[520,256]{1,0:T(8,128)(2,1)S(1)}, u32[]{:S(2)}, u32[]{:S(2)}) collective-permute-start(bf16[520,256]{1,0:T(8,128)(2,1)S(1)} %get-tuple-element.30), channel_id=1, source_target_pairs={{0,14},{1,15},{2,12},{3,13},{4,10},{5,11},{6,8},{7,9},{8,6},{9,7},... | collective-permute-start | bytes 798728 | tf_op jit(solution)/shard_map/ppermute | solution.py:323
  13.7 30.1 %collective-permute-start.3 = (bf16[520,256]{1,0:T(8,128)(2,1)S(1)}, bf16[520,256]{1,0:T(8,128)(2,1)S(1)}, u32[]{:S(2)}, u32[]{:S(2)}) collective-permute-start(bf16[520,256]{1,0:T(8,128)(2,1)S(1)} %get-tuple-element.31), channel_id=1, source_target_pairs={{0,8},{1,9},{2,10},{3,11},{4,12},{5,13},{6,14},{7,15},{8,0},{9,1},... | collective-permute-start | bytes 798728 | tf_op jit(solution)/shard_map/ppermute | solution.py:323
  15.0 5.9 %collective-permute-start.4 = (s32[4,8]{1,0:T(4,128)S(1)}, s32[4,8]{1,0:T(4,128)S(1)}, u32[]{:S(2)}, u32[]{:S(2)}) collective-permute-start(s32[4,8]{1,0:T(4,128)S(1)} %add_bitcast_fusion.refs_2_), channel_id=1, source_target_pairs={{0,16},{16,0},{1,17},{17,1},{2,18},{18,2},{3,19},{19,3},{4,20},{20... | collective-permute-start | bytes 392 | tf_op jit(solution)/shard_map/ppermute | solution.py:327
  43.8 21.5 %collective-permute-start.7 = (bf16[1024,256]{1,0:T(8,128)(2,1)S(1)}, bf16[1024,256]{1,0:T(8,128)(2,1)S(1)}, u32[]{:S(2)}, u32[]{:S(2)}) collective-permute-start(bf16[1024,256]{1,0:T(8,128)(2,1)S(1)} %get-tuple-element.40), channel_id=1, source_target_pairs={{0,4},{1,5},{2,6},{3,7},{4,0},{5,1},{6,2},{7,3},{8,12},{9,13},{10,... | collective-permute-start | bytes 1572872 | tf_op jit(solution)/shard_map/ppermute | solution.py:323
  48.3 19.2 %collective-permute-start.6 = (bf16[1024,256]{1,0:T(8,128)(2,1)S(1)}, bf16[1024,256]{1,0:T(8,128)(2,1)S(1)}, u32[]{:S(2)}, u32[]{:S(2)}) collective-permute-start(bf16[1024,256]{1,0:T(8,128)(2,1)S(1)} %get-tuple-element.38), channel_id=1, source_target_pairs={{0,2},{1,3},{2,0},{3,1},{4,6},{5,7},{6,4},{7,5},{8,10},{9,11},{10,... | collective-permute-start | bytes 1572872 | tf_op jit(solution)/shard_map/ppermute | solution.py:323
  48.8 22.8 %collective-permute-start.10 = (bf16[512,256]{1,0:T(8,128)(2,1)S(1)}, bf16[512,256]{1,0:T(8,128)(2,1)S(1)}, u32[]{:S(2)}, u32[]{:S(2)}) collective-permute-start(bf16[512,256]{1,0:T(8,128)(2,1)S(1)} %get-tuple-element.46), channel_id=1, source_target_pairs={{0,14},{1,15},{2,12},{3,13},{4,10},{5,11},{6,8},{7,9},{8,6},{9,7},... | collective-permute-start | bytes 786440 | tf_op jit(solution)/shard_map/ppermute | solution.py:323
  67.5 32.6 %collective-permute-start.8 = (bf16[1024,256]{1,0:T(8,128)(2,1)S(1)}, bf16[1024,256]{1,0:T(8,128)(2,1)S(1)}, u32[]{:S(2)}, u32[]{:S(2)}) collective-permute-start(bf16[1024,256]{1,0:T(8,128)(2,1)S(1)} %get-tuple-element.42), channel_id=1, source_target_pairs={{0,6},{1,7},{2,4},{3,5},{4,2},{5,3},{6,0},{7,1},{8,14},{9,15},{10,... | collective-permute-start | bytes 1572872 | tf_op jit(solution)/shard_map/ppermute | solution.py:323
  67.7 19.0 %collective-permute-start.9 = (bf16[512,256]{1,0:T(8,128)(2,1)S(1)}, bf16[512,256]{1,0:T(8,128)(2,1)S(1)}, u32[]{:S(2)}, u32[]{:S(2)}) collective-permute-start(bf16[512,256]{1,0:T(8,128)(2,1)S(1)} %get-tuple-element.44), channel_id=1, source_target_pairs={{0,10},{1,11},{2,8},{3,9},{4,14},{5,15},{6,12},{7,13},{8,2},{9,3},... | collective-permute-start | bytes 786440 | tf_op jit(solution)/shard_map/ppermute | solution.py:323
  68.2 34.3 %collective-permute-start.11 = (bf16[512,256]{1,0:T(8,128)(2,1)S(1)}, bf16[512,256]{1,0:T(8,128)(2,1)S(1)}, u32[]{:S(2)}, u32[]{:S(2)}) collective-permute-start(bf16[512,256]{1,0:T(8,128)(2,1)S(1)} %get-tuple-element.48), channel_id=1, source_target_pairs={{0,8},{1,9},{2,10},{3,11},{4,12},{5,13},{6,14},{7,15},{8,0},{9,1},... | collective-permute-start | bytes 786440 | tf_op jit(solution)/shard_map/ppermute | solution.py:323
  71.6 41.2 %collective-permute-start.13 = (bf16[512,256]{1,0:T(8,128)(2,1)S(1)}, bf16[512,256]{1,0:T(8,128)(2,1)S(1)}, u32[]{:S(2)}, u32[]{:S(2)}) collective-permute-start(bf16[512,256]{1,0:T(8,128)(2,1)S(1)} %get-tuple-element.52), channel_id=1, source_target_pairs={{0,12},{1,13},{2,14},{3,15},{4,8},{5,9},{6,10},{7,11},{8,4},{9,5},... | collective-permute-start | bytes 786440 | tf_op jit(solution)/shard_map/ppermute | solution.py:323
  86.8 29.2 %collective-permute-start.12 = (bf16[512,256]{1,0:T(8,128)(2,1)S(1)}, bf16[512,256]{1,0:T(8,128)(2,1)S(1)}, u32[]{:S(2)}, u32[]{:S(2)}) collective-permute-start(bf16[512,256]{1,0:T(8,128)(2,1)S(1)} %get-tuple-element.50), channel_id=1, source_target_pairs={{0,12},{1,13},{2,14},{3,15},{4,8},{5,9},{6,10},{7,11},{8,4},{9,5},... | collective-permute-start | bytes 786440 | tf_op jit(solution)/shard_map/ppermute | solution.py:323

commit v3 on v2

--- a/solution.py
+++ b/solution.py
@@ -9,7 +9,7 @@
 
 GRID_COLS = 8
 NEAR = GRID_COLS // 2
-FAR = (5, 7, 4, 6)
+FAR = (5, 4, 7, 6)
 TAG = 8
 
 ANY = pl.BlockSpec(memory_space=pl.ANY)
@@ -32,12 +32,13 @@
         self.width = self.col_groups * self.block
         self.capacity = max(self.slots // 4, self.slots // self.groups)
         self.first = max(0, self.rows - self.capacity * self.groups)
-        self.early = {5: self.first, 7: self.first, 4: self.first, 6: 0}
-        self.late = [(o, 0, self.rows) for o in range(NEAR)]
+        self.early = {5: self.first, 7: self.first, 4: self.first // 2, 6: 0}
+        half = self.rows // 2
+        self.late = [(o, 0, self.rows) for o in range(NEAR - 1)]
+        self.late += [(NEAR - 1, 0, half), (NEAR - 1, half, self.rows)]
         for o in FAR:
             count = self.rows - self.early[o]
-            cuts = [0, count // 2, count] if o == 6 else [0, count]
-            self.late += [(o, lo, hi) for lo, hi in zip(cuts, cuts[1:])]
+            self.late.append((o, 0, count))
 
 
 COST = pl.CostEstimate(flops=0, transcendentals=0, bytes_accessed=0)
@@ -104,7 +105,8 @@
 
 
 def bucket_kernel(plan, heads, updates, *refs):
-    outs, sems = refs[-plan.groups : -1], refs[-1]
+    outs, done, sems = refs[:-2], refs[-2], refs[-1]
+    done[0] = 0
     me = lax.axis_index("front")
 
     def copies(act):
@@ -132,8 +134,8 @@
 
 def pack_kernel(plan, offsets, *refs):
     groups = plan.groups
-    head_refs, panel = refs[:groups], refs[groups]
-    outs, refs = refs[groups + 1 : groups + 1 + len(offsets)], refs[groups + 1 + len(offsets) :]
+    head_refs, panel, refs = refs[:groups], refs[groups + 1], refs[groups + 2 :]
+    outs, refs = refs[: len(offsets)], refs[len(offsets) :]
     touched_out, order, sems = refs
     column = lax.axis_index("wide") // plan.grid_rows
     block = plan.block
@@ -246,7 +248,7 @@
             if hi - lo == plan.rows:
                 put(t)
             else:
-                place = place_ref[o, t] if plan.early[o] else t
+                place = place_ref[o, t] if plan.early.get(o) else t
                 pl.when(jnp.logical_and(place >= lo, place < hi))(lambda: put(place - lo))
 
         return carry
@@ -339,6 +341,21 @@
     panels = pltpu.with_memory_space_constraint(parent_panels, pltpu.HBM)
 
 
+    *buckets, done = pl.pallas_call(
+        functools.partial(bucket_kernel, plan),
+        out_shape=[
+            jax.ShapeDtypeStruct((plan.capacity, block, updates.shape[2]), bf16)
+            for _ in range(1, plan.groups)
+        ]
+        + [jax.ShapeDtypeStruct((1,), jnp.int32)],
+        in_specs=[SMEM, HBM],
+        out_specs=[VMEM] * (plan.groups - 1) + [SMEM],
+        scratch_shapes=[pltpu.SemaphoreType.DMA((plan.slots,))],
+        compiler_params=params(),
+        cost_estimate=COST,
+        name="bucket",
+    )(heads, updates)
+
     early = [o for o in FAR if plan.early[o]]
     packed, touched = {}, []
     if early:
@@ -348,7 +365,7 @@
                 jax.ShapeDtypeStruct((plan.early[o] * block + TAG, width), bf16) for o in early
             ]
             + [jax.ShapeDtypeStruct((1,), jnp.int32)],
-            in_specs=[SMEM] * plan.groups + [HBM],
+            in_specs=[SMEM] * (plan.groups + 1) + [HBM],
             out_specs=[VMEM] * len(early) + [SMEM],
             scratch_shapes=[
                 pltpu.SMEM((plan.rows,), jnp.int32),
@@ -357,24 +374,11 @@
             compiler_params=params(),
             cost_estimate=COST,
             name="pack_early",
-        )(*all_heads, panels)
+        )(*all_heads, done, panels)
         packed = dict(zip(early, outs))
         touched = [touched_set]
         codes = after(codes, touched_set)
-
-    buckets = pl.pallas_call(
-        functools.partial(bucket_kernel, plan),
-        out_shape=[
-            jax.ShapeDtypeStruct((plan.capacity, block, updates.shape[2]), bf16)
-            for _ in range(1, plan.groups)
-        ],
-        in_specs=[SMEM, HBM] + [SMEM] * len(touched),
-        out_specs=[VMEM] * (plan.groups - 1),
-        scratch_shapes=[pltpu.SemaphoreType.DMA((plan.slots,))],
-        compiler_params=params(),
-        cost_estimate=COST,
-        name="bucket",
-    )(heads, updates, *touched)
+        buckets = [after(x, touched_set) for x in buckets]
 
     all_codes = [codes] + [along(codes, plan, k) for k in range(1, plan.groups)]
     got = [along(buckets[k - 1], plan, k) for k in range(1, plan.groups)]
@@ -405,22 +409,24 @@
     def late(o, part=0):
         return [m for m in plan.late if m[0] == o][part]
 
-    first = {o: across(packed[o], plan, o) for o in early}
+    first = {}
+    for o in early:
+        lead = [first[4]] if o == 7 else []
+        first[o] = across(after(packed[o], *lead), plan, o)
     arrived = {late(0): ready[late(0)]}
 
     def send(message, *others):
         arrived[message] = across(after(ready[message], *others), plan, message[0])
         return arrived[message]
 
-    gate = [first[o] for o in early]
-    a = send(late(5), *gate)
-    b = send(late(7), *gate)
-    send(late(4), *gate)
-    n1 = send(late(1), *gate)
-    n2 = send(late(2), *gate)
-    send(late(3), n1, n2)
-    send(late(6, 0), a)
-    send(late(6, 1), b)
+    b5 = send(late(5), *[first[o] for o in early if o == 5])
+    b7 = send(late(7), *[first[o] for o in early if o == 7])
+    send(late(6), b5)
+    send(late(4), b7)
+    n1 = send(late(1), *[first[o] for o in early if o == 5])
+    send(late(2), *[first[o] for o in early if o == 7])
+    send(late(3, 0), n1)
+    send(late(3, 1), b7)
 
     out_shape = jax.ShapeDtypeStruct((plan.rows * GRID_COLS * block, width), bf16)
     held, sets = [], []
@@ -466,7 +472,7 @@
             )(*held, *sets, *[arrived[m] for m in messages])
         ]
 
-    last = [late(4), late(6, 0), late(6, 1)]
+    last = [late(4), late(6)]
     held = place(held, [m for m in plan.late if m not in last], "place_mid")
     held = place(held, last, "place_last")
     return held[0][None]

time: 118 us -> 105 us (0.89)
  the two profiles are of different devices: /device:TPU:16 before, /device:TPU:0 now
where the time goes in v3:
time: 105 us
  waiting for transfers between devices  44.5 us (42%)
  starting transfers between devices  42.4 us (40%)
  Pallas kernels  15.7 us (15%)
  local copies, waits for them, and re-layouts  1.24 us (1%)
    ppermute x11, waiting for transfers between devices, across(): return lax.ppermute(value, 'wide', pairs)  42.4 us
    ppermute x11, starting transfers between devices, across(): return lax.ppermute(value, 'wide', pairs)  36.7 us
    ppermute x3, starting transfers between devices, along(): lax.ppermute(value, 'front', [(f, (f + steps) % plan.groups) for f in ran...  5.68 us
    pallas_call x1, Pallas kernels, local(): pl.pallas_call(functools.partial(assemble_kernel, plan), out_shape=[jax.S...  5.54 us
    pallas_call x2, Pallas kernels, place(): pl.pallas_call(body, out_shape=out_shape, in_specs=[HBM] * len(held) + [S...  4.13 us
    pallas_call x1, Pallas kernels, local(): pl.pallas_call(functools.partial(pack_kernel, plan, early), out_shape=[ja...  3.1 us
  transfers between devices with their start and end apart: 14, of which 6 were waited for; matrix products, arithmetic and copies ran while one was open for 0% of the time, Pallas kernels for 10%

profile of v3, /device:TPU:0, one launch (start us, length us, event | category | flops | bytes accessed | tf_op | source)
XLA Modules:
  0.0 104.6 jit_solution(5979875902452015006)
XLA Ops:
  0.0 0.7 bitcast_add_fusion.heads.refs_0_
  0.7 3.0 %collective-permute-start = (s32[4]{0:T(128)S(1)}, s32[4]{0:T(128)S(1)}, u32[]{:S(2)}, u32[]{:S(2)}) collective-permute-start(s32[4]{0:T(128)S(1)} %bitcast_add_fusion.heads.refs_0_), channel_id=1, source_target_pairs={{0,16},{16,0},{1,17},{17,1},{2,18},{18,2},{3,19},{19,3},{4,20},{20... | collective-permute-start | bytes 56 | tf_op jit(solution)/shard_map/ppermute | solution.py:329
  3.6 0.0 copy-start
  3.6 1.2 %copy-done = bf16[1,512,1024]{2,1,0:T(8,128)(2,1)S(1)} copy-done((bf16[1,512,1024]{2,1,0:T(8,128)(2,1)S(1)}, bf16[1,512,1024]{2,1,0:T(8,128)(2,1)}, u32[]{:S(2)}) %copy-start) | copy-done | bytes 1048600
  4.9 0.0 copy-start.2
  4.9 0.0 copy-start.3
  4.9 0.0 copy-start.1
  4.9 1.2 %bucket.1 = (bf16[2,128,1024]{2,1,0:T(8,128)(2,1)S(1)}, s32[1]{0:T(128)}) custom-call(s32[4]{0:T(128)S(1)} %bitcast_add_fusion.heads.refs_0_, bf16[1,512,1024]{2,1,0:T(8,128)(2,1)S(1)} %copy-done), custom_call_target="tpu_custom_call" | custom-call | tf_op jit(solution)/shard_map/bucket/pallas_call | solution.py:344
  6.1 0.0 collective-permute-done.refs_1_
  6.1 3.1 %pack_early.1 = (bf16[520,256]{1,0:T(8,128)(2,1)S(1)}, bf16[264,256]{1,0:T(8,128)(2,1)S(1)}, bf16[520,256]{1,0:T(8,128)(2,1)S(1)}, s32[1]{0:T(128)}) custom-call(s32[4]{0:T(128)S(1)} %bitcast_add_fusion.heads.refs_0_, s32[4]{0:T(128)S(1)} %collective-permute-done.refs_1_, s32[1]{0:T(128)} %get-tuple-element.33.refs_2_, bf16[1,1024,2048]{2,1,0:T(8,128)(2,1)} %refs_4_.1), custom_call_target="tpu_custom_call" | custom-call | tf_op jit(solution)/shard_map/pack_early/pallas_call | solution.py:362
  9.2 1.1 %collective-permute-start.5 = (bf16[2,128,1024]{2,1,0:T(8,128)(2,1)S(1)}, bf16[2,128,1024]{2,1,0:T(8,128)(2,1)S(1)}, u32[]{:S(2)}, u32[]{:S(2)}) collective-permute-start(bf16[2,128,1024]{2,1,0:T(8,128)(2,1)S(1)} %get-tuple-element.43), channel_id=1, source_target_pairs={{0,16},{16,0},{1,17},{17,1},{2,18},{18,2},{3,19},{19,3},{4,20},{20... | collective-permute-start | bytes 1572872 | tf_op jit(solution)/shard_map/ppermute | solution.py:329
  10.4 2.6 %collective-permute-start.2 = (bf16[264,256]{1,0:T(8,128)(2,1)S(1)}, bf16[264,256]{1,0:T(8,128)(2,1)S(1)}, u32[]{:S(2)}, u32[]{:S(2)}) collective-permute-start(bf16[264,256]{1,0:T(8,128)(2,1)S(1)} %get-tuple-element.35), channel_id=1, source_target_pairs={{0,8},{1,9},{2,10},{3,11},{4,12},{5,13},{6,14},{7,15},{8,0},{9,1},... | collective-permute-start | bytes 405512 | tf_op jit(solution)/shard_map/ppermute | solution.py:325
  12.9 1.3 %collective-permute-start.1 = (bf16[520,256]{1,0:T(8,128)(2,1)S(1)}, bf16[520,256]{1,0:T(8,128)(2,1)S(1)}, u32[]{:S(2)}, u32[]{:S(2)}) collective-permute-start(bf16[520,256]{1,0:T(8,128)(2,1)S(1)} %get-tuple-element.34), channel_id=1, source_target_pairs={{0,10},{1,11},{2,8},{3,9},{4,14},{5,15},{6,12},{7,13},{8,2},{9,3},... | collective-permute-start | bytes 798728 | tf_op jit(solution)/shard_map/ppermute | solution.py:325
  14.2 10.9 %collective-permute-done.2.refs_1_ = bf16[264,256]{1,0:T(8,128)(2,1)S(1)} collective-permute-done((bf16[264,256]{1,0:T(8,128)(2,1)S(1)}, bf16[264,256]{1,0:T(8,128)(2,1)S(1)}, u32[]{:S(2)}, u32[]{:S(2)}) %collective-permute-start.2) | collective-permute-done | bytes 135200 | tf_op jit(solution)/shard_map/ppermute | solution.py:325
  25.1 3.5 %collective-permute-start.3 = (bf16[520,256]{1,0:T(8,128)(2,1)S(1)}, bf16[520,256]{1,0:T(8,128)(2,1)S(1)}, u32[]{:S(2)}, u32[]{:S(2)}) collective-permute-start(bf16[520,256]{1,0:T(8,128)(2,1)S(1)} %get-tuple-element.37), channel_id=1, source_target_pairs={{0,14},{1,15},{2,12},{3,13},{4,10},{5,11},{6,8},{7,9},{8,6},{9,7},... | collective-permute-start | bytes 798728 | tf_op jit(solution)/shard_map/ppermute | solution.py:325
  28.6 0.0 copy-done.2
  28.6 0.0 copy-done.3
  28.6 1.6 %collective-permute-start.4 = (s32[4,8]{1,0:T(4,128)S(1)}, s32[4,8]{1,0:T(4,128)S(1)}, u32[]{:S(2)}, u32[]{:S(2)}) collective-permute-start(s32[4,8]{1,0:T(4,128)S(1)} %add_bitcast_fusion.refs_2_), channel_id=1, source_target_pairs={{0,16},{16,0},{1,17},{17,1},{2,18},{18,2},{3,19},{19,3},{4,20},{20... | collective-permute-start | bytes 392 | tf_op jit(solution)/shard_map/ppermute | solution.py:329
  30.2 2.1 %collective-permute-done.4.refs_3_ = s32[4,8]{1,0:T(4,128)S(1)} collective-permute-done((s32[4,8]{1,0:T(4,128)S(1)}, s32[4,8]{1,0:T(4,128)S(1)}, u32[]{:S(2)}, u32[]{:S(2)}) %collective-permute-start.4) | collective-permute-done | bytes 160 | tf_op jit(solution)/shard_map/ppermute | solution.py:329
  32.2 0.0 collective-permute-done.5.refs_6_
  32.2 0.0 copy-done.1
  32.2 5.5 %assemble.1 = (bf16[1024,256]{1,0:T(8,128)(2,1)S(1)}, bf16[1024,256]{1,0:T(8,128)(2,1)S(1)}, bf16[1024,256]{1,0:T(8,128)(2,1)S(1)}, bf16[512,256]{1,0:T(8,128)(2...) custom-call(s32[4]{0:T(128)S(1)} %bitcast_add_fusion.heads.refs_0_, ...), custom_call_target="tpu_custom_call" | custom-call | tf_op jit(solution)/shard_map/assemble/pallas_call | solution.py:387
  37.8 0.0 collective-permute-done.1.refs_0_
  37.8 0.6 collective-permute-start.6
  38.4 0.0 collective-permute-start.11
  38.4 0.0 collective-permute-done.3.refs_2_
  38.4 3.1 %collective-permute-start.9 = (bf16[512,256]{1,0:T(8,128)(2,1)S(1)}, bf16[512,256]{1,0:T(8,128)(2,1)S(1)}, u32[]{:S(2)}, u32[]{:S(2)}) collective-permute-start(bf16[512,256]{1,0:T(8,128)(2,1)S(1)} %get-tuple-element.53), channel_id=1, source_target_pairs={{0,14},{1,15},{2,12},{3,13},{4,10},{5,11},{6,8},{7,9},{8,6},{9,7},... | collective-permute-start | bytes 786440 | tf_op jit(solution)/shard_map/ppermute | solution.py:325
  41.5 15.2 %collective-permute-start.7 = (bf16[1024,256]{1,0:T(8,128)(2,1)S(1)}, bf16[1024,256]{1,0:T(8,128)(2,1)S(1)}, u32[]{:S(2)}, u32[]{:S(2)}) collective-permute-start(bf16[1024,256]{1,0:T(8,128)(2,1)S(1)} %get-tuple-element.48), channel_id=1, source_target_pairs={{0,4},{1,5},{2,6},{3,7},{4,0},{5,1},{6,2},{7,3},{8,12},{9,13},{10,... | collective-permute-start | bytes 1572872 | tf_op jit(solution)/shard_map/ppermute | solution.py:325
  56.7 3.2 %collective-permute-done.11.refs_7_ = bf16[512,256]{1,0:T(8,128)(2,1)S(1)} collective-permute-done((bf16[512,256]{1,0:T(8,128)(2,1)S(1)}, bf16[512,256]{1,0:T(8,128)(2,1)S(1)}, u32[]{:S(2)}, u32[]{:S(2)}) %collective-permute-start.11) | collective-permute-done | bytes 262176 | tf_op jit(solution)/shard_map/ppermute | solution.py:325
  59.9 2.9 %collective-permute-start.13 = (bf16[1024,256]{1,0:T(8,128)(2,1)S(1)}, bf16[1024,256]{1,0:T(8,128)(2,1)S(1)}, u32[]{:S(2)}, u32[]{:S(2)}) collective-permute-start(bf16[1024,256]{1,0:T(8,128)(2,1)S(1)} %get-tuple-element.60), channel_id=1, source_target_pairs={{0,12},{1,13},{2,14},{3,15},{4,8},{5,9},{6,10},{7,11},{8,4},{9,5},... | collective-permute-start | bytes 1572872 | tf_op jit(solution)/shard_map/ppermute | solution.py:325
  62.7 0.0 collective-permute-done.9.refs_8_
  62.8 4.7 %collective-permute-start.12 = (bf16[768,256]{1,0:T(8,128)(2,1)S(1)}, bf16[768,256]{1,0:T(8,128)(2,1)S(1)}, u32[]{:S(2)}, u32[]{:S(2)}) collective-permute-start(bf16[768,256]{1,0:T(8,128)(2,1)S(1)} %get-tuple-element.58), channel_id=1, source_target_pairs={{0,8},{1,9},{2,10},{3,11},{4,12},{5,13},{6,14},{7,15},{8,0},{9,1},... | collective-permute-start | bytes 1179656 | tf_op jit(solution)/shard_map/ppermute | solution.py:325
  67.4 0.0 collective-permute-start.10
  67.4 0.0 collective-permute-done.6.refs_3_
  67.4 2.9 %collective-permute-start.8 = (bf16[512,256]{1,0:T(8,128)(2,1)S(1)}, bf16[512,256]{1,0:T(8,128)(2,1)S(1)}, u32[]{:S(2)}, u32[]{:S(2)}) collective-permute-start(bf16[512,256]{1,0:T(8,128)(2,1)S(1)} %get-tuple-element.50), channel_id=1, source_target_pairs={{0,6},{1,7},{2,4},{3,5},{4,2},{5,3},{6,0},{7,1},{8,14},{9,15},{10,... | collective-permute-start | bytes 786440 | tf_op jit(solution)/shard_map/ppermute | solution.py:325
  70.4 1.7 %place_early.1 = (bf16[8192,256]{1,0:T(8,128)(2,1)}, s32[3]{0:T(128)S(1)}) custom-call(bf16[520,256]{1,0:T(8,128)(2,1)S(1)} %collective-permute-done.1.refs_0_, bf16[264,256]{1,0:T(8,128)(2,1)S(1)} %collective-permute-done.2.refs_1_, bf16[520,256]{1,0:T(8,128)(2,1)S(1)} %collective-permute-done.3.refs_2_), custom_call_target="tpu_custom_call" | custom-call | tf_op jit(solution)/shard_map/place_early/pallas_call | solution.py:434
  72.1 22.3 %collective-permute-done.10.refs_6_ = bf16[512,256]{1,0:T(8,128)(2,1)S(1)} collective-permute-done((bf16[512,256]{1,0:T(8,128)(2,1)S(1)}, bf16[512,256]{1,0:T(8,128)(2,1)S(1)}, u32[]{:S(2)}, u32[]{:S(2)}) %collective-permute-start.10) | collective-permute-done | bytes 262176 | tf_op jit(solution)/shard_map/ppermute | solution.py:325
  94.3 0.0 collective-permute-done.7.refs_4_
  94.3 4.2 %collective-permute-done.8.refs_5_ = bf16[512,256]{1,0:T(8,128)(2,1)S(1)} collective-permute-done((bf16[512,256]{1,0:T(8,128)(2,1)S(1)}, bf16[512,256]{1,0:T(8,128)(2,1)S(1)}, u32[]{:S(2)}, u32[]{:S(2)}) %collective-permute-start.8) | collective-permute-done | bytes 262176 | tf_op jit(solution)/shard_map/ppermute | solution.py:325
  98.6 2.5 %place_mid.1.refs_0_ = bf16[8192,256]{1,0:T(8,128)(2,1)} custom-call(bf16[8192,256]{1,0:T(8,128)(2,1)} %get-tuple-element.38.refs_0_, s32[3]{0:T(128)S(1)} %get-tuple-element.39.refs_1_, bf16[1024,256]{1,0:T(8,128)(2,1)S(1)} %get-tuple-element.44.refs_2_, bf16[1024,256]{1,0:T(8,128)(2,1)S(1)} %collective-permute-done.6.refs_3_, ...), custom_call_target="tpu_custom_call", output_to_operand_aliasing={{}: (0, {})} | custom-call | tf_op jit(solution)/shard_map/place_mid/pallas_call | solution.py:459
  101.1 1.9 %collective-permute-done.12.refs_2_ = bf16[768,256]{1,0:T(8,128)(2,1)S(1)} collective-permute-done((bf16[768,256]{1,0:T(8,128)(2,1)S(1)}, bf16[768,256]{1,0:T(8,128)(2,1)S(1)}, u32[]{:S(2)}, u32[]{:S(2)}) %collective-permute-start.12) | collective-permute-done | bytes 393248 | tf_op jit(solution)/shard_map/ppermute | solution.py:325
  103.0 0.0 collective-permute-done.13.refs_3_
  103.0 1.6 %place_last.1 = bf16[8192,256]{1,0:T(8,128)(2,1)} custom-call(bf16[8192,256]{1,0:T(8,128)(2,1)} %place_mid.1.refs_0_, s32[3]{0:T(128)S(1)} %get-tuple-element.39.refs_1_, bf16[768,256]{1,0:T(8,128)(2,1)S(1)} %collective-permute-done.12.refs_2_, bf16[1024,256]{1,0:T(8,128)(2,1)S(1)} %collective-permute-done.13.refs_3_), custom_call_target="tpu_custom_call", output_to_operand_aliasing={{}: (0, {})} | custom-call | tf_op jit(solution)/shard_map/place_last/pallas_call | solution.py:459
  (1 shorter events, 0.0 us)
Async XLA Ops:
  0.7 5.4 %collective-permute-start = (s32[4]{0:T(128)S(1)}, s32[4]{0:T(128)S(1)}, u32[]{:S(2)}, u32[]{:S(2)}) collective-permute-start(s32[4]{0:T(128)S(1)} %bitcast_add_fusion.heads.refs_0_), channel_id=1, source_target_pairs={{0,16},{16,0},{1,17},{17,1},{2,18},{18,2},{3,19},{19,3},{4,20},{20... | collective-permute-start | bytes 56 | tf_op jit(solution)/shard_map/ppermute | solution.py:329
  3.6 1.2 %copy-start = (bf16[1,512,1024]{2,1,0:T(8,128)(2,1)S(1)}, bf16[1,512,1024]{2,1,0:T(8,128)(2,1)}, u32[]{:S(2)}) copy-start(bf16[1,512,1024]{2,1,0:T(8,128)(2,1)} %refs_5_.1) | copy-start | bytes 3145732
  4.9 23.7 %copy-start.2 = (s32[1,4,8]{2,1,0:T(4,128)S(1)}, s32[1,4,8]{2,1,0:T(4,128)}, u32[]{:S(2)}) copy-start(s32[1,4,8]{2,1,0:T(4,128)} %param.10) | copy-start | bytes 388
  4.9 23.7 %copy-start.3 = (s32[1,4,8]{2,1,0:T(4,128)S(1)}, s32[1,4,8]{2,1,0:T(4,128)}, u32[]{:S(2)}) copy-start(s32[1,4,8]{2,1,0:T(4,128)} %param.11) | copy-start | bytes 388
  4.9 27.4 %copy-start.1 = (bf16[1,512,1024]{2,1,0:T(8,128)(2,1)S(1)}, bf16[1,512,1024]{2,1,0:T(8,128)(2,1)}, u32[]{:S(2)}) copy-start(bf16[1,512,1024]{2,1,0:T(8,128)(2,1)} %refs_5_.1) | copy-start | bytes 3145732
  9.2 23.0 %collective-permute-start.5 = (bf16[2,128,1024]{2,1,0:T(8,128)(2,1)S(1)}, bf16[2,128,1024]{2,1,0:T(8,128)(2,1)S(1)}, u32[]{:S(2)}, u32[]{:S(2)}) collective-permute-start(bf16[2,128,1024]{2,1,0:T(8,128)(2,1)S(1)} %get-tuple-element.43), channel_id=1, source_target_pairs={{0,16},{16,0},{1,17},{17,1},{2,18},{18,2},{3,19},{19,3},{4,20},{20... | collective-permute-start | bytes 1572872 | tf_op jit(solution)/shard_map/ppermute | solution.py:329
  10.4 14.7 %collective-permute-start.2 = (bf16[264,256]{1,0:T(8,128)(2,1)S(1)}, bf16[264,256]{1,0:T(8,128)(2,1)S(1)}, u32[]{:S(2)}, u32[]{:S(2)}) collective-permute-start(bf16[264,256]{1,0:T(8,128)(2,1)S(1)} %get-tuple-element.35), channel_id=1, source_target_pairs={{0,8},{1,9},{2,10},{3,11},{4,12},{5,13},{6,14},{7,15},{8,0},{9,1},... | collective-permute-start | bytes 405512 | tf_op jit(solution)/shard_map/ppermute | solution.py:325
  12.9 24.8 %collective-permute-start.1 = (bf16[520,256]{1,0:T(8,128)(2,1)S(1)}, bf16[520,256]{1,0:T(8,128)(2,1)S(1)}, u32[]{:S(2)}, u32[]{:S(2)}) collective-permute-start(bf16[520,256]{1,0:T(8,128)(2,1)S(1)} %get-tuple-element.34), channel_id=1, source_target_pairs={{0,10},{1,11},{2,8},{3,9},{4,14},{5,15},{6,12},{7,13},{8,2},{9,3},... | collective-permute-start | bytes 798728 | tf_op jit(solution)/shard_map/ppermute | solution.py:325
  25.1 13.3 %collective-permute-start.3 = (bf16[520,256]{1,0:T(8,128)(2,1)S(1)}, bf16[520,256]{1,0:T(8,128)(2,1)S(1)}, u32[]{:S(2)}, u32[]{:S(2)}) collective-permute-start(bf16[520,256]{1,0:T(8,128)(2,1)S(1)} %get-tuple-element.37), channel_id=1, source_target_pairs={{0,14},{1,15},{2,12},{3,13},{4,10},{5,11},{6,8},{7,9},{8,6},{9,7},... | collective-permute-start | bytes 798728 | tf_op jit(solution)/shard_map/ppermute | solution.py:325
  28.6 3.7 %collective-permute-start.4 = (s32[4,8]{1,0:T(4,128)S(1)}, s32[4,8]{1,0:T(4,128)S(1)}, u32[]{:S(2)}, u32[]{:S(2)}) collective-permute-start(s32[4,8]{1,0:T(4,128)S(1)} %add_bitcast_fusion.refs_2_), channel_id=1, source_target_pairs={{0,16},{16,0},{1,17},{17,1},{2,18},{18,2},{3,19},{19,3},{4,20},{20... | collective-permute-start | bytes 392 | tf_op jit(solution)/shard_map/ppermute | solution.py:329
  37.8 29.6 %collective-permute-start.6 = (bf16[1024,256]{1,0:T(8,128)(2,1)S(1)}, bf16[1024,256]{1,0:T(8,128)(2,1)S(1)}, u32[]{:S(2)}, u32[]{:S(2)}) collective-permute-start(bf16[1024,256]{1,0:T(8,128)(2,1)S(1)} %get-tuple-element.46), channel_id=1, source_target_pairs={{0,2},{1,3},{2,0},{3,1},{4,6},{5,7},{6,4},{7,5},{8,10},{9,11},{10,... | collective-permute-start | bytes 1572872 | tf_op jit(solution)/shard_map/ppermute | solution.py:325
  38.4 21.5 %collective-permute-start.11 = (bf16[512,256]{1,0:T(8,128)(2,1)S(1)}, bf16[512,256]{1,0:T(8,128)(2,1)S(1)}, u32[]{:S(2)}, u32[]{:S(2)}) collective-permute-start(bf16[512,256]{1,0:T(8,128)(2,1)S(1)} %get-tuple-element.56), channel_id=1, source_target_pairs={{0,10},{1,11},{2,8},{3,9},{4,14},{5,15},{6,12},{7,13},{8,2},{9,3},... | collective-permute-start | bytes 786440 | tf_op jit(solution)/shard_map/ppermute | solution.py:325
  38.4 24.4 %collective-permute-start.9 = (bf16[512,256]{1,0:T(8,128)(2,1)S(1)}, bf16[512,256]{1,0:T(8,128)(2,1)S(1)}, u32[]{:S(2)}, u32[]{:S(2)}) collective-permute-start(bf16[512,256]{1,0:T(8,128)(2,1)S(1)} %get-tuple-element.53), channel_id=1, source_target_pairs={{0,14},{1,15},{2,12},{3,13},{4,10},{5,11},{6,8},{7,9},{8,6},{9,7},... | collective-permute-start | bytes 786440 | tf_op jit(solution)/shard_map/ppermute | solution.py:325
  41.5 52.9 %collective-permute-start.7 = (bf16[1024,256]{1,0:T(8,128)(2,1)S(1)}, bf16[1024,256]{1,0:T(8,128)(2,1)S(1)}, u32[]{:S(2)}, u32[]{:S(2)}) collective-permute-start(bf16[1024,256]{1,0:T(8,128)(2,1)S(1)} %get-tuple-element.48), channel_id=1, source_target_pairs={{0,4},{1,5},{2,6},{3,7},{4,0},{5,1},{6,2},{7,3},{8,12},{9,13},{10,... | collective-permute-start | bytes 1572872 | tf_op jit(solution)/shard_map/ppermute | solution.py:325
  59.9 43.1 %collective-permute-start.13 = (bf16[1024,256]{1,0:T(8,128)(2,1)S(1)}, bf16[1024,256]{1,0:T(8,128)(2,1)S(1)}, u32[]{:S(2)}, u32[]{:S(2)}) collective-permute-start(bf16[1024,256]{1,0:T(8,128)(2,1)S(1)} %get-tuple-element.60), channel_id=1, source_target_pairs={{0,12},{1,13},{2,14},{3,15},{4,8},{5,9},{6,10},{7,11},{8,4},{9,5},... | collective-permute-start | bytes 1572872 | tf_op jit(solution)/shard_map/ppermute | solution.py:325
  62.8 40.2 %collective-permute-start.12 = (bf16[768,256]{1,0:T(8,128)(2,1)S(1)}, bf16[768,256]{1,0:T(8,128)(2,1)S(1)}, u32[]{:S(2)}, u32[]{:S(2)}) collective-permute-start(bf16[768,256]{1,0:T(8,128)(2,1)S(1)} %get-tuple-element.58), channel_id=1, source_target_pairs={{0,8},{1,9},{2,10},{3,11},{4,12},{5,13},{6,14},{7,15},{8,0},{9,1},... | collective-permute-start | bytes 1179656 | tf_op jit(solution)/shard_map/ppermute | solution.py:325
  67.4 26.9 %collective-permute-start.10 = (bf16[512,256]{1,0:T(8,128)(2,1)S(1)}, bf16[512,256]{1,0:T(8,128)(2,1)S(1)}, u32[]{:S(2)}, u32[]{:S(2)}) collective-permute-start(bf16[512,256]{1,0:T(8,128)(2,1)S(1)} %get-tuple-element.54), channel_id=1, source_target_pairs={{0,6},{1,7},{2,4},{3,5},{4,2},{5,3},{6,0},{7,1},{8,14},{9,15},{10,... | collective-permute-start | bytes 786440 | tf_op jit(solution)/shard_map/ppermute | solution.py:325
  67.4 31.1 %collective-permute-start.8 = (bf16[512,256]{1,0:T(8,128)(2,1)S(1)}, bf16[512,256]{1,0:T(8,128)(2,1)S(1)}, u32[]{:S(2)}, u32[]{:S(2)}) collective-permute-start(bf16[512,256]{1,0:T(8,128)(2,1)S(1)} %get-tuple-element.50), channel_id=1, source_target_pairs={{0,6},{1,7},{2,4},{3,5},{4,2},{5,3},{6,0},{7,1},{8,14},{9,15},{10,... | collective-permute-start | bytes 786440 | tf_op jit(solution)/shard_map/ppermute | solution.py:325

commit v4 on v3

--- a/solution.py
+++ b/solution.py
@@ -33,7 +33,7 @@
         self.capacity = max(self.slots // 4, self.slots // self.groups)
         self.first = max(0, self.rows - self.capacity * self.groups)
         self.early = {5: self.first, 7: self.first, 4: self.first // 2, 6: 0}
-        half = self.rows // 2
+        half = max(1, 3 * self.rows // 8)
         self.late = [(o, 0, self.rows) for o in range(NEAR - 1)]
         self.late += [(NEAR - 1, 0, half), (NEAR - 1, half, self.rows)]
         for o in FAR:
@@ -41,6 +41,7 @@
             self.late.append((o, 0, count))
 
 
+MID = pl.CostEstimate(flops=0, transcendentals=0, bytes_accessed=0)
 COST = pl.CostEstimate(flops=0, transcendentals=0, bytes_accessed=0)
 
 
@@ -104,12 +105,14 @@
         copy.wait()
 
 
-def bucket_kernel(plan, heads, updates, *refs):
-    outs, done, sems = refs[:-2], refs[-2], refs[-1]
-    done[0] = 0
+def stage_kernel(plan, early, heads, updates, panel, *refs):
+    outs, refs = refs[: plan.groups - 1], refs[plan.groups - 1 :]
+    staged, (slot_sems, sems) = refs[: len(early)], refs[len(early) :]
     me = lax.axis_index("front")
-
-    def copies(act):
+    column = lax.axis_index("wide") // plan.grid_rows
+    block = plan.block
+
+    def buckets(act):
         for k in range(1, plan.groups):
             target = lax.rem(me + k, plan.groups)
             rank = jnp.int32(0)
@@ -120,47 +123,43 @@
                 def _():
                     act(
                         pltpu.make_async_copy(
-                            updates.at[0, pl.ds(q * plan.block, plan.block)],
+                            updates.at[0, pl.ds(q * block, block)],
                             outs[k - 1].at[rank],
-                            sems.at[q],
+                            slot_sems.at[q],
                         )
                     )
 
                 rank = rank + jnp.where(named, 1, 0)
 
-    copies(lambda c: c.start())
-    copies(lambda c: c.wait())
+    buckets(lambda c: c.start())
+    run_all(
+        [
+            pltpu.make_async_copy(
+                panel.at[0, :, at(cc * GRID_COLS + jnp.bitwise_xor(column, o), block)],
+                staged[i].at[:, pl.ds(cc * block, block)],
+                sems.at[i, cc],
+            )
+            for i, o in enumerate(early)
+            for cc in range(plan.col_groups)
+        ]
+    )
+    buckets(lambda c: c.wait())
 
 
 def pack_kernel(plan, offsets, *refs):
-    groups = plan.groups
-    head_refs, panel, refs = refs[:groups], refs[groups + 1], refs[groups + 2 :]
-    outs, refs = refs[: len(offsets)], refs[len(offsets) :]
-    touched_out, order, sems = refs
-    column = lax.axis_index("wide") // plan.grid_rows
+    groups, count = plan.groups, len(offsets)
+    head_refs, staged, refs = refs[:groups], refs[groups : groups + count], refs[groups + count :]
+    outs, (touched_out, order) = refs[:count], refs[count:]
     block = plan.block
     touched = touched_rows(plan, head_refs)
     touched_out[0] = touched
     list_rows(plan, first_rows(plan, touched, plan.first), 1, order)
-    copies = []
     for i, o in enumerate(offsets):
-        target = jnp.bitwise_xor(column, o)
         for k in range(plan.early[o]):
-            for cc in range(plan.col_groups):
-                copies.append(
-                    pltpu.make_async_copy(
-                        panel.at[0, at(order[k], block), at(cc * GRID_COLS + target, block)],
-                        outs[i].at[pl.ds(k * block, block), pl.ds(cc * block, block)],
-                        sems.at[i, k, cc],
-                    )
-                )
-                copies[-1].start()
-    for i, o in enumerate(offsets):
+            outs[i][pl.ds(k * block, block), :] = staged[i][at(order[k], block), :]
         chosen = first_rows(plan, touched, plan.early[o]).astype(jnp.float32)
         tag = jnp.full((TAG, plan.width), chosen, jnp.float32).astype(jnp.bfloat16)
         outs[i][plan.early[o] * block :, :] = tag
-    for copy in copies:
-        copy.wait()
 
 
 def assemble_kernel(plan, *refs):
@@ -289,25 +288,36 @@
         copy.wait()
 
 
-def place_late_kernel(plan, messages, early, sets, pieces, out, where, sems):
+def place_late_kernel(plan, messages, early, sets, pieces, out, held, where, set_sem, sems):
     column = lax.axis_index("wide") // plan.grid_rows
     block = plan.block
     copies = []
-    for i, (o, lo, hi) in enumerate(messages):
+
+    def place(i, rows):
+        o, lo, hi = messages[i]
         source = jnp.bitwise_xor(column, o)
-        split = o in early
-        if split:
-            list_rows(plan, sets[early.index(o)], 0, where.at[i])
         for k in range(lo, hi):
-            t = where[i, k] if split else k
             copies.append(
                 pltpu.make_async_copy(
                     pieces[i].at[pl.ds((k - lo) * block, block)],
-                    out.at[at(t * GRID_COLS + source, block)],
+                    out.at[at(rows[k] * GRID_COLS + source, block)],
                     sems.at[i, k],
                 )
             )
             copies[-1].start()
+
+    split = [i for i, m in enumerate(messages) if m[0] in early]
+    if split:
+        fetch = pltpu.make_async_copy(sets, held, set_sem)
+        fetch.start()
+    for i in range(len(messages)):
+        if i not in split:
+            place(i, range(plan.rows))
+    if split:
+        fetch.wait()
+    for i in split:
+        list_rows(plan, held[early.index(messages[i][0])], 0, where.at[i])
+        place(i, where.at[i])
     for copy in copies:
         copy.wait()
 
@@ -339,48 +349,48 @@
     all_heads = [heads] + [along(heads, plan, k) for k in range(1, plan.groups)]
     codes = slot_mask[0] * plan.window + slot_cols[0]
     panels = pltpu.with_memory_space_constraint(parent_panels, pltpu.HBM)
-
-
-    *buckets, done = pl.pallas_call(
-        functools.partial(bucket_kernel, plan),
+    moving = pltpu.with_memory_space_constraint(updates, pltpu.HBM)
+
+
+    early = [o for o in FAR if plan.early[o]]
+    staged = pl.pallas_call(
+        functools.partial(stage_kernel, plan, early),
         out_shape=[
             jax.ShapeDtypeStruct((plan.capacity, block, updates.shape[2]), bf16)
             for _ in range(1, plan.groups)
         ]
-        + [jax.ShapeDtypeStruct((1,), jnp.int32)],
-        in_specs=[SMEM, HBM],
-        out_specs=[VMEM] * (plan.groups - 1) + [SMEM],
-        scratch_shapes=[pltpu.SemaphoreType.DMA((plan.slots,))],
+        + [jax.ShapeDtypeStruct((plan.rows * block, width), bf16) for _ in early],
+        in_specs=[SMEM, HBM, HBM],
+        out_specs=[VMEM] * (plan.groups - 1 + len(early)),
+        scratch_shapes=[
+            pltpu.SemaphoreType.DMA((plan.slots,)),
+            pltpu.SemaphoreType.DMA((max(1, len(early)), plan.col_groups)),
+        ],
         compiler_params=params(),
         cost_estimate=COST,
-        name="bucket",
-    )(heads, updates)
-
-    early = [o for o in FAR if plan.early[o]]
-    packed, touched = {}, []
+        name="stage",
+    )(heads, moving, panels)
+    buckets, staged = staged[: plan.groups - 1], staged[plan.groups - 1 :]
+
+    packed = {}
     if early:
-        *outs, touched_set = pl.pallas_call(
+        *outs, touched = pl.pallas_call(
             functools.partial(pack_kernel, plan, early),
             out_shape=[
                 jax.ShapeDtypeStruct((plan.early[o] * block + TAG, width), bf16) for o in early
             ]
             + [jax.ShapeDtypeStruct((1,), jnp.int32)],
-            in_specs=[SMEM] * (plan.groups + 1) + [HBM],
+            in_specs=[SMEM] * plan.groups + [VMEM] * len(early),
             out_specs=[VMEM] * len(early) + [SMEM],
-            scratch_shapes=[
-                pltpu.SMEM((plan.rows,), jnp.int32),
-                pltpu.SemaphoreType.DMA((len(early), plan.first, plan.col_groups)),
-            ],
+            scratch_shapes=[pltpu.SMEM((plan.rows,), jnp.int32)],
             compiler_params=params(),
-            cost_estimate=COST,
+            cost_estimate=pl.CostEstimate(flops=0, transcendentals=0, bytes_accessed=0),
             name="pack_early",
-        )(*all_heads, done, panels)
+        )(*all_heads, *staged)
         packed = dict(zip(early, outs))
-        touched = [touched_set]
-        codes = after(codes, touched_set)
-        buckets = [after(x, touched_set) for x in buckets]
 
     all_codes = [codes] + [along(codes, plan, k) for k in range(1, plan.groups)]
+    buckets = [after(x, *all_heads, *all_codes) for x in buckets]
     got = [along(buckets[k - 1], plan, k) for k in range(1, plan.groups)]
 
     moved = plan.slots + (plan.groups - 1) * plan.capacity
@@ -402,7 +412,7 @@
         compiler_params=params(),
         cost_estimate=COST,
         name="assemble",
-    )(*all_heads, *all_codes, panels, updates, *got)
+    )(*all_heads, *all_codes, panels, moving, *got)
 
     ready = dict(zip(plan.late, assembled))
 
@@ -423,10 +433,10 @@
     b7 = send(late(7), *[first[o] for o in early if o == 7])
     send(late(6), b5)
     send(late(4), b7)
-    n1 = send(late(1), *[first[o] for o in early if o == 5])
-    send(late(2), *[first[o] for o in early if o == 7])
-    send(late(3, 0), n1)
-    send(late(3, 1), b7)
+    n2 = send(late(2))
+    send(late(3, 1), n2)
+    n3 = send(late(3, 0), *[first[o] for o in early if o == 5])
+    send(late(1), n3)
 
     out_shape = jax.ShapeDtypeStruct((plan.rows * GRID_COLS * block, width), bf16)
     held, sets = [], []
@@ -459,15 +469,17 @@
             pl.pallas_call(
                 body,
                 out_shape=out_shape,
-                in_specs=[HBM] * len(held) + [SMEM] * len(sets) + [ANY] * len(messages),
+                in_specs=[HBM] * len(held) + [ANY] * (len(sets) + len(messages)),
                 out_specs=HBM,
                 input_output_aliases={0: 0} if held else {},
                 scratch_shapes=[
+                    pltpu.SMEM((max(1, len(early)),), jnp.int32),
                     pltpu.SMEM((len(messages), plan.rows), jnp.int32),
+                    pltpu.SemaphoreType.DMA,
                     pltpu.SemaphoreType.DMA((len(messages), plan.rows)),
                 ],
                 compiler_params=params(),
-                cost_estimate=COST,
+                cost_estimate=MID if name == "place_mid" else COST,
                 name=name,
             )(*held, *sets, *[arrived[m] for m in messages])
         ]

time: 105 us -> 106 us (level)
  waiting for transfers between devices: 44.5 us -> 56.5 us
  starting transfers between devices: 42.4 us -> 33.1 us
  Pallas kernels: 15.7 us -> 14.3 us
  local copies, waits for them, and re-layouts: 1.24 us -> 0 us
    ppermute x11, waiting for transfers between devices: 42.4 us -> 55.2 us  [across(): return lax.ppermute(value, 'wide', pairs)]
    ppermute x11, starting transfers between devices: 36.7 us -> 29.4 us  [across(): return lax.ppermute(value, 'wide', pairs)]
    ppermute x3, starting transfers between devices: 5.68 us -> 3.7 us  [along(): lax.ppermute(value, 'front', [(f, (f + steps) % plan.groups) for f in ran...]
    pallas_call x1, Pallas kernels: 3.1 us -> 1.14 us  [local(): pl.pallas_call(functools.partial(pack_kernel, plan, early), out_shape=[ja...]
    unnamed x8 -> x0, local copies, waits for them, and re-layouts: 1.24 us -> none
  transfers between devices with their start and end apart: 14 -> 14, of which waited for: 6 -> 6; matrix products, arithmetic and copies ran while one was open for 0% -> 1% of each run, Pallas kernels for 10% -> 12%
where the time goes in v4:
time: 106 us; the launch traced here: 105 us
  waiting for transfers between devices  56.5 us (53%)
  starting transfers between devices  33.1 us (31%)
  Pallas kernels  14.3 us (13%)
  other arithmetic  1.38 us (1%)
    ppermute x11, waiting for transfers between devices, across(): return lax.ppermute(value, 'wide', pairs)  55.2 us
    ppermute x11, starting transfers between devices, across(): return lax.ppermute(value, 'wide', pairs)  29.4 us
    pallas_call x1, Pallas kernels, local(): pl.pallas_call(functools.partial(assemble_kernel, plan), out_shape=[jax.S...  5.82 us
    ppermute x3, starting transfers between devices, along(): lax.ppermute(value, 'front', [(f, (f + steps) % plan.groups) for f in ran...  3.7 us
    pallas_call x2, Pallas kernels, place(): pl.pallas_call(body, out_shape=out_shape, in_specs=[HBM] * len(held) + [A...  3.41 us
    pallas_call x1, Pallas kernels, local(): pl.pallas_call(functools.partial(stage_kernel, plan, early), out_shape=[j...  2.2 us
  transfers between devices with their start and end apart: 14, of which 6 were waited for; matrix products, arithmetic and copies ran while one was open for 1% of the time, Pallas kernels for 12%

profile of v4, /device:TPU:0, one launch (start us, length us, event | category | flops | bytes accessed | tf_op | source)
XLA Modules:
  0.0 105.4 jit_solution(15958704322437748806)
XLA Ops:
  0.0 0.7 bitcast_add_fusion.heads.refs_0_
  0.7 3.0 %collective-permute-start = (s32[4]{0:T(128)S(1)}, s32[4]{0:T(128)S(1)}, u32[]{:S(2)}, u32[]{:S(2)}) collective-permute-start(s32[4]{0:T(128)S(1)} %bitcast_add_fusion.heads.refs_0_), channel_id=1, source_target_pairs={{0,16},{16,0},{1,17},{17,1},{2,18},{18,2},{3,19},{19,3},{4,20},{20... | collective-permute-start | bytes 56 | tf_op jit(solution)/shard_map/ppermute | solution.py:339
  3.6 0.7 add_bitcast_fusion.refs_2_
  4.3 0.0 collective-permute-start.4
  4.3 2.2 %stage.1 = (bf16[2,128,1024]{2,1,0:T(8,128)(2,1)S(1)}, bf16[1024,256]{1,0:T(8,128)(2,1)S(1)}, bf16[1024,256]{1,0:T(8,128)(2,1)S(1)}, bf16[1024,256]{1,0:T(8,128)(2,1)S(1)}) custom-call(s32[4]{0:T(128)S(1)} %bitcast_add_fusion.heads.refs_0_, bf16[1,512,1024]{2,1,0:T(8,128)(2,1)} %refs_5_.1, bf16[1,1024,2048]{2,1,0:T(8,128)(2,1)} %refs_4_.1), custom_call_target="tpu_custom_call" | custom-call | tf_op jit(solution)/shard_map/stage/pallas_call | solution.py:356
  6.6 0.0 collective-permute-done.refs_1_
  6.6 1.4 %collective-permute-done.4.refs_3_ = s32[4,8]{1,0:T(4,128)S(1)} collective-permute-done((s32[4,8]{1,0:T(4,128)S(1)}, s32[4,8]{1,0:T(4,128)S(1)}, u32[]{:S(2)}, u32[]{:S(2)}) %collective-permute-start.4) | collective-permute-done | bytes 160 | tf_op jit(solution)/shard_map/ppermute | solution.py:339
  7.9 0.7 collective-permute-start.5
  8.7 1.1 %pack_early.1 = (bf16[520,256]{1,0:T(8,128)(2,1)S(1)}, bf16[264,256]{1,0:T(8,128)(2,1)S(1)}, bf16[520,256]{1,0:T(8,128)(2,1)S(1)}, s32[1]{0:T(128)}) custom-call(s32[4]{0:T(128)S(1)} %bitcast_add_fusion.heads.refs_0_, s32[4]{0:T(128)S(1)} %collective-permute-done.refs_1_, bf16[1024,256]{1,0:T(8,128)(2,1)S(1)} %get-tuple-element.32.refs_2_, ...), custom_call_target="tpu_custom_call" | custom-call | tf_op jit(solution)/shard_map/pack_early/pallas_call | solution.py:377
  9.8 2.7 %collective-permute-start.2 = (bf16[264,256]{1,0:T(8,128)(2,1)S(1)}, bf16[264,256]{1,0:T(8,128)(2,1)S(1)}, u32[]{:S(2)}, u32[]{:S(2)}) collective-permute-start(bf16[264,256]{1,0:T(8,128)(2,1)S(1)} %get-tuple-element.36), channel_id=1, source_target_pairs={{0,8},{1,9},{2,10},{3,11},{4,12},{5,13},{6,14},{7,15},{8,0},{9,1},... | collective-permute-start | bytes 405512 | tf_op jit(solution)/shard_map/ppermute | solution.py:335
  12.5 1.3 %collective-permute-start.1 = (bf16[520,256]{1,0:T(8,128)(2,1)S(1)}, bf16[520,256]{1,0:T(8,128)(2,1)S(1)}, u32[]{:S(2)}, u32[]{:S(2)}) collective-permute-start(bf16[520,256]{1,0:T(8,128)(2,1)S(1)} %get-tuple-element.35), channel_id=1, source_target_pairs={{0,10},{1,11},{2,8},{3,9},{4,14},{5,15},{6,12},{7,13},{8,2},{9,3},... | collective-permute-start | bytes 798728 | tf_op jit(solution)/shard_map/ppermute | solution.py:335
  13.7 11.3 %collective-permute-done.2.refs_1_ = bf16[264,256]{1,0:T(8,128)(2,1)S(1)} collective-permute-done((bf16[264,256]{1,0:T(8,128)(2,1)S(1)}, bf16[264,256]{1,0:T(8,128)(2,1)S(1)}, u32[]{:S(2)}, u32[]{:S(2)}) %collective-permute-start.2) | collective-permute-done | bytes 135200 | tf_op jit(solution)/shard_map/ppermute | solution.py:335
  25.0 3.3 %collective-permute-start.3 = (bf16[520,256]{1,0:T(8,128)(2,1)S(1)}, bf16[520,256]{1,0:T(8,128)(2,1)S(1)}, u32[]{:S(2)}, u32[]{:S(2)}) collective-permute-start(bf16[520,256]{1,0:T(8,128)(2,1)S(1)} %get-tuple-element.38), channel_id=1, source_target_pairs={{0,14},{1,15},{2,12},{3,13},{4,10},{5,11},{6,8},{7,9},{8,6},{9,7},... | collective-permute-start | bytes 798728 | tf_op jit(solution)/shard_map/ppermute | solution.py:335
  28.4 0.0 collective-permute-done.5.refs_6_
  28.4 5.8 %assemble.1 = (bf16[1024,256]{1,0:T(8,128)(2,1)S(1)}, bf16[1024,256]{1,0:T(8,128)(2,1)S(1)}, bf16[1024,256]{1,0:T(8,128)(2,1)S(1)}, bf16[384,256]{1,0:T(8,128)(2...) custom-call(s32[4]{0:T(128)S(1)} %bitcast_add_fusion.heads.refs_0_, ...), custom_call_target="tpu_custom_call" | custom-call | tf_op jit(solution)/shard_map/assemble/pallas_call | solution.py:397
  34.2 0.1 collective-permute-start.8
  34.3 3.1 %collective-permute-done.1.refs_0_ = bf16[520,256]{1,0:T(8,128)(2,1)S(1)} collective-permute-done((bf16[520,256]{1,0:T(8,128)(2,1)S(1)}, bf16[520,256]{1,0:T(8,128)(2,1)S(1)}, u32[]{:S(2)}, u32[]{:S(2)}) %collective-permute-start.1) | collective-permute-done | bytes 266272 | tf_op jit(solution)/shard_map/ppermute | solution.py:335
  37.4 0.0 collective-permute-start.10
  37.4 3.9 %collective-permute-start.6 = (bf16[384,256]{1,0:T(8,128)(2,1)S(1)}, bf16[384,256]{1,0:T(8,128)(2,1)S(1)}, u32[]{:S(2)}, u32[]{:S(2)}) collective-permute-start(bf16[384,256]{1,0:T(8,128)(2,1)S(1)} %get-tuple-element.46), channel_id=1, source_target_pairs={{0,6},{1,7},{2,4},{3,5},{4,2},{5,3},{6,0},{7,1},{8,14},{9,15},{10,... | collective-permute-start | bytes 589832 | tf_op jit(solution)/shard_map/ppermute | solution.py:335
  41.3 0.0 collective-permute-done.3.refs_2_
  41.3 1.3 %collective-permute-start.11 = (bf16[512,256]{1,0:T(8,128)(2,1)S(1)}, bf16[512,256]{1,0:T(8,128)(2,1)S(1)}, u32[]{:S(2)}, u32[]{:S(2)}) collective-permute-start(bf16[512,256]{1,0:T(8,128)(2,1)S(1)} %get-tuple-element.54), channel_id=1, source_target_pairs={{0,14},{1,15},{2,12},{3,13},{4,10},{5,11},{6,8},{7,9},{8,6},{9,7},... | collective-permute-start | bytes 786440 | tf_op jit(solution)/shard_map/ppermute | solution.py:335
  42.6 21.0 %collective-permute-done.6.refs_5_ = bf16[384,256]{1,0:T(8,128)(2,1)S(1)} collective-permute-done((bf16[384,256]{1,0:T(8,128)(2,1)S(1)}, bf16[384,256]{1,0:T(8,128)(2,1)S(1)}, u32[]{:S(2)}, u32[]{:S(2)}) %collective-permute-start.6) | collective-permute-done | bytes 196640 | tf_op jit(solution)/shard_map/ppermute | solution.py:335
  63.6 1.1 %collective-permute-start.7 = (bf16[1024,256]{1,0:T(8,128)(2,1)S(1)}, bf16[1024,256]{1,0:T(8,128)(2,1)S(1)}, u32[]{:S(2)}, u32[]{:S(2)}) collective-permute-start(bf16[1024,256]{1,0:T(8,128)(2,1)S(1)} %get-tuple-element.47), channel_id=1, source_target_pairs={{0,2},{1,3},{2,0},{3,1},{4,6},{5,7},{6,4},{7,5},{8,10},{9,11},{10,... | collective-permute-start | bytes 1572872 | tf_op jit(solution)/shard_map/ppermute | solution.py:335
  64.6 0.0 collective-permute-done.10.refs_7_
  64.7 0.0 collective-permute-start.13
  64.7 0.0 collective-permute-done.11.refs_8_
  64.7 15.8 %collective-permute-start.12 = (bf16[768,256]{1,0:T(8,128)(2,1)S(1)}, bf16[768,256]{1,0:T(8,128)(2,1)S(1)}, u32[]{:S(2)}, u32[]{:S(2)}) collective-permute-start(bf16[768,256]{1,0:T(8,128)(2,1)S(1)} %get-tuple-element.56), channel_id=1, source_target_pairs={{0,8},{1,9},{2,10},{3,11},{4,12},{5,13},{6,14},{7,15},{8,0},{9,1},... | collective-permute-start | bytes 1179656 | tf_op jit(solution)/shard_map/ppermute | solution.py:335
  80.5 0.0 collective-permute-done.8.refs_4_
  80.5 0.0 collective-permute-start.9
  80.5 1.7 %place_early.1 = (bf16[8192,256]{1,0:T(8,128)(2,1)}, s32[3]{0:T(128)S(1)}) custom-call(bf16[520,256]{1,0:T(8,128)(2,1)S(1)} %collective-permute-done.1.refs_0_, bf16[264,256]{1,0:T(8,128)(2,1)S(1)} %collective-permute-done.2.refs_1_, bf16[520,256]{1,0:T(8,128)(2,1)S(1)} %collective-permute-done.3.refs_2_), custom_call_target="tpu_custom_call" | custom-call | tf_op jit(solution)/shard_map/place_early/pallas_call | solution.py:444
  82.2 0.0 collective-permute-done.7.refs_3_
  82.2 13.8 %collective-permute-done.9.refs_6_ = bf16[640,256]{1,0:T(8,128)(2,1)S(1)} collective-permute-done((bf16[640,256]{1,0:T(8,128)(2,1)S(1)}, bf16[640,256]{1,0:T(8,128)(2,1)S(1)}, u32[]{:S(2)}, u32[]{:S(2)}) %collective-permute-start.9) | collective-permute-done | bytes 327712 | tf_op jit(solution)/shard_map/ppermute | solution.py:335
  96.0 2.0 %place_mid.1.refs_0_ = bf16[8192,256]{1,0:T(8,128)(2,1)} custom-call(bf16[8192,256]{1,0:T(8,128)(2,1)} %get-tuple-element.39.refs_0_, s32[3]{0:T(128)S(1)} %get-tuple-element.40.refs_1_, bf16[1024,256]{1,0:T(8,128)(2,1)S(1)} %get-tuple-element.43.refs_2_, bf16[1024,256]{1,0:T(8,128)(2,1)S(1)} %collective-permute-done.7.refs_3_, ...), custom_call_target="tpu_custom_call", output_to_operand_aliasing={{}: (0, {})} | custom-call | tf_op jit(solution)/shard_map/place_mid/pallas_call | solution.py:469
  98.0 6.0 %collective-permute-done.12.refs_2_ = bf16[768,256]{1,0:T(8,128)(2,1)S(1)} collective-permute-done((bf16[768,256]{1,0:T(8,128)(2,1)S(1)}, bf16[768,256]{1,0:T(8,128)(2,1)S(1)}, u32[]{:S(2)}, u32[]{:S(2)}) %collective-permute-start.12) | collective-permute-done | bytes 393248 | tf_op jit(solution)/shard_map/ppermute | solution.py:335
  104.0 0.0 collective-permute-done.13.refs_3_
  104.0 1.5 %place_last.1 = bf16[8192,256]{1,0:T(8,128)(2,1)} custom-call(bf16[8192,256]{1,0:T(8,128)(2,1)} %place_mid.1.refs_0_, s32[3]{0:T(128)S(1)} %get-tuple-element.40.refs_1_, bf16[768,256]{1,0:T(8,128)(2,1)S(1)} %collective-permute-done.12.refs_2_, bf16[1024,256]{1,0:T(8,128)(2,1)S(1)} %collective-permute-done.13.refs_3_), custom_call_target="tpu_custom_call", output_to_operand_aliasing={{}: (0, {})} | custom-call | tf_op jit(solution)/shard_map/place_last/pallas_call | solution.py:469
Async XLA Ops:
  0.7 5.9 %collective-permute-start = (s32[4]{0:T(128)S(1)}, s32[4]{0:T(128)S(1)}, u32[]{:S(2)}, u32[]{:S(2)}) collective-permute-start(s32[4]{0:T(128)S(1)} %bitcast_add_fusion.heads.refs_0_), channel_id=1, source_target_pairs={{0,16},{16,0},{1,17},{17,1},{2,18},{18,2},{3,19},{19,3},{4,20},{20... | collective-permute-start | bytes 56 | tf_op jit(solution)/shard_map/ppermute | solution.py:339
  4.3 3.6 %collective-permute-start.4 = (s32[4,8]{1,0:T(4,128)S(1)}, s32[4,8]{1,0:T(4,128)S(1)}, u32[]{:S(2)}, u32[]{:S(2)}) collective-permute-start(s32[4,8]{1,0:T(4,128)S(1)} %add_bitcast_fusion.refs_2_), channel_id=1, source_target_pairs={{0,16},{16,0},{1,17},{17,1},{2,18},{18,2},{3,19},{19,3},{4,20},{20... | collective-permute-start | bytes 392 | tf_op jit(solution)/shard_map/ppermute | solution.py:339
  7.9 20.4 %collective-permute-start.5 = (bf16[2,128,1024]{2,1,0:T(8,128)(2,1)S(1)}, bf16[2,128,1024]{2,1,0:T(8,128)(2,1)S(1)}, u32[]{:S(2)}, u32[]{:S(2)}) collective-permute-start(bf16[2,128,1024]{2,1,0:T(8,128)(2,1)S(1)} %get-tuple-element.42), channel_id=1, source_target_pairs={{0,16},{16,0},{1,17},{17,1},{2,18},{18,2},{3,19},{19,3},{4,20},{20... | collective-permute-start | bytes 1572872 | tf_op jit(solution)/shard_map/ppermute | solution.py:339
  9.8 15.2 %collective-permute-start.2 = (bf16[264,256]{1,0:T(8,128)(2,1)S(1)}, bf16[264,256]{1,0:T(8,128)(2,1)S(1)}, u32[]{:S(2)}, u32[]{:S(2)}) collective-permute-start(bf16[264,256]{1,0:T(8,128)(2,1)S(1)} %get-tuple-element.36), channel_id=1, source_target_pairs={{0,8},{1,9},{2,10},{3,11},{4,12},{5,13},{6,14},{7,15},{8,0},{9,1},... | collective-permute-start | bytes 405512 | tf_op jit(solution)/shard_map/ppermute | solution.py:335
  12.5 24.9 %collective-permute-start.1 = (bf16[520,256]{1,0:T(8,128)(2,1)S(1)}, bf16[520,256]{1,0:T(8,128)(2,1)S(1)}, u32[]{:S(2)}, u32[]{:S(2)}) collective-permute-start(bf16[520,256]{1,0:T(8,128)(2,1)S(1)} %get-tuple-element.35), channel_id=1, source_target_pairs={{0,10},{1,11},{2,8},{3,9},{4,14},{5,15},{6,12},{7,13},{8,2},{9,3},... | collective-permute-start | bytes 798728 | tf_op jit(solution)/shard_map/ppermute | solution.py:335
  25.0 16.3 %collective-permute-start.3 = (bf16[520,256]{1,0:T(8,128)(2,1)S(1)}, bf16[520,256]{1,0:T(8,128)(2,1)S(1)}, u32[]{:S(2)}, u32[]{:S(2)}) collective-permute-start(bf16[520,256]{1,0:T(8,128)(2,1)S(1)} %get-tuple-element.38), channel_id=1, source_target_pairs={{0,14},{1,15},{2,12},{3,13},{4,10},{5,11},{6,8},{7,9},{8,6},{9,7},... | collective-permute-start | bytes 798728 | tf_op jit(solution)/shard_map/ppermute | solution.py:335
  34.2 46.3 %collective-permute-start.8 = (bf16[1024,256]{1,0:T(8,128)(2,1)S(1)}, bf16[1024,256]{1,0:T(8,128)(2,1)S(1)}, u32[]{:S(2)}, u32[]{:S(2)}) collective-permute-start(bf16[1024,256]{1,0:T(8,128)(2,1)S(1)} %get-tuple-element.48), channel_id=1, source_target_pairs={{0,4},{1,5},{2,6},{3,7},{4,0},{5,1},{6,2},{7,3},{8,12},{9,13},{10,... | collective-permute-start | bytes 1572872 | tf_op jit(solution)/shard_map/ppermute | solution.py:335
  37.4 27.3 %collective-permute-start.10 = (bf16[512,256]{1,0:T(8,128)(2,1)S(1)}, bf16[512,256]{1,0:T(8,128)(2,1)S(1)}, u32[]{:S(2)}, u32[]{:S(2)}) collective-permute-start(bf16[512,256]{1,0:T(8,128)(2,1)S(1)} %get-tuple-element.52), channel_id=1, source_target_pairs={{0,10},{1,11},{2,8},{3,9},{4,14},{5,15},{6,12},{7,13},{8,2},{9,3},... | collective-permute-start | bytes 786440 | tf_op jit(solution)/shard_map/ppermute | solution.py:335
  37.4 26.2 %collective-permute-start.6 = (bf16[384,256]{1,0:T(8,128)(2,1)S(1)}, bf16[384,256]{1,0:T(8,128)(2,1)S(1)}, u32[]{:S(2)}, u32[]{:S(2)}) collective-permute-start(bf16[384,256]{1,0:T(8,128)(2,1)S(1)} %get-tuple-element.46), channel_id=1, source_target_pairs={{0,6},{1,7},{2,4},{3,5},{4,2},{5,3},{6,0},{7,1},{8,14},{9,15},{10,... | collective-permute-start | bytes 589832 | tf_op jit(solution)/shard_map/ppermute | solution.py:335
  41.3 23.4 %collective-permute-start.11 = (bf16[512,256]{1,0:T(8,128)(2,1)S(1)}, bf16[512,256]{1,0:T(8,128)(2,1)S(1)}, u32[]{:S(2)}, u32[]{:S(2)}) collective-permute-start(bf16[512,256]{1,0:T(8,128)(2,1)S(1)} %get-tuple-element.54), channel_id=1, source_target_pairs={{0,14},{1,15},{2,12},{3,13},{4,10},{5,11},{6,8},{7,9},{8,6},{9,7},... | collective-permute-start | bytes 786440 | tf_op jit(solution)/shard_map/ppermute | solution.py:335
  63.6 18.6 %collective-permute-start.7 = (bf16[1024,256]{1,0:T(8,128)(2,1)S(1)}, bf16[1024,256]{1,0:T(8,128)(2,1)S(1)}, u32[]{:S(2)}, u32[]{:S(2)}) collective-permute-start(bf16[1024,256]{1,0:T(8,128)(2,1)S(1)} %get-tuple-element.47), channel_id=1, source_target_pairs={{0,2},{1,3},{2,0},{3,1},{4,6},{5,7},{6,4},{7,5},{8,10},{9,11},{10,... | collective-permute-start | bytes 1572872 | tf_op jit(solution)/shard_map/ppermute | solution.py:335
  64.7 39.3 %collective-permute-start.13 = (bf16[1024,256]{1,0:T(8,128)(2,1)S(1)}, bf16[1024,256]{1,0:T(8,128)(2,1)S(1)}, u32[]{:S(2)}, u32[]{:S(2)}) collective-permute-start(bf16[1024,256]{1,0:T(8,128)(2,1)S(1)} %get-tuple-element.58), channel_id=1, source_target_pairs={{0,12},{1,13},{2,14},{3,15},{4,8},{5,9},{6,10},{7,11},{8,4},{9,5},... | collective-permute-start | bytes 1572872 | tf_op jit(solution)/shard_map/ppermute | solution.py:335
  64.7 39.3 %collective-permute-start.12 = (bf16[768,256]{1,0:T(8,128)(2,1)S(1)}, bf16[768,256]{1,0:T(8,128)(2,1)S(1)}, u32[]{:S(2)}, u32[]{:S(2)}) collective-permute-start(bf16[768,256]{1,0:T(8,128)(2,1)S(1)} %get-tuple-element.56), channel_id=1, source_target_pairs={{0,8},{1,9},{2,10},{3,11},{4,12},{5,13},{6,14},{7,15},{8,0},{9,1},... | collective-permute-start | bytes 1179656 | tf_op jit(solution)/shard_map/ppermute | solution.py:335
  80.5 15.5 %collective-permute-start.9 = (bf16[640,256]{1,0:T(8,128)(2,1)S(1)}, bf16[640,256]{1,0:T(8,128)(2,1)S(1)}, u32[]{:S(2)}, u32[]{:S(2)}) collective-permute-start(bf16[640,256]{1,0:T(8,128)(2,1)S(1)} %get-tuple-element.50), channel_id=1, source_target_pairs={{0,6},{1,7},{2,4},{3,5},{4,2},{5,3},{6,0},{7,1},{8,14},{9,15},{10,... | collective-permute-start | bytes 983048 | tf_op jit(solution)/shard_map/ppermute | solution.py:335

commit v5 on v4

--- a/solution.py
+++ b/solution.py
@@ -9,7 +9,6 @@
 
 GRID_COLS = 8
 NEAR = GRID_COLS // 2
-FAR = (5, 4, 7, 6)
 TAG = 8
 
 ANY = pl.BlockSpec(memory_space=pl.ANY)
@@ -32,13 +31,12 @@
         self.width = self.col_groups * self.block
         self.capacity = max(self.slots // 4, self.slots // self.groups)
         self.first = max(0, self.rows - self.capacity * self.groups)
-        self.early = {5: self.first, 7: self.first, 4: self.first // 2, 6: 0}
-        half = max(1, 3 * self.rows // 8)
-        self.late = [(o, 0, self.rows) for o in range(NEAR - 1)]
-        self.late += [(NEAR - 1, 0, half), (NEAR - 1, half, self.rows)]
-        for o in FAR:
-            count = self.rows - self.early[o]
-            self.late.append((o, 0, count))
+        self.early = {4: self.first // 2, 5: self.first, 7: self.first, 2: self.first}
+        self.late = []
+        for o in range(GRID_COLS):
+            count = self.rows - self.early.get(o, 0)
+            cuts = [0, count // 2, count] if o == 4 else [0, max(1, 5 * count // 8), count] if o == 6 else [0, count]
+            self.late += [(o, lo, hi) for lo, hi in zip(cuts, cuts[1:]) if lo < hi]
 
 
 MID = pl.CostEstimate(flops=0, transcendentals=0, bytes_accessed=0)
@@ -193,7 +191,7 @@
         copy.start()
 
     touched = touched_rows(plan, head_refs)
-    for o in FAR:
+    for o in plan.early:
         for t, (bit, place) in enumerate(
             positions(plan, first_rows(plan, touched, plan.early[o]))
         ):
@@ -352,7 +350,7 @@
     moving = pltpu.with_memory_space_constraint(updates, pltpu.HBM)
 
 
-    early = [o for o in FAR if plan.early[o]]
+    early = [o for o in plan.early if plan.early[o]]
     staged = pl.pallas_call(
         functools.partial(stage_kernel, plan, early),
         out_shape=[
@@ -390,7 +388,7 @@
         packed = dict(zip(early, outs))
 
     all_codes = [codes] + [along(codes, plan, k) for k in range(1, plan.groups)]
-    buckets = [after(x, *all_heads, *all_codes) for x in buckets]
+    buckets = [after(x, *all_heads) for x in buckets]
     got = [along(buckets[k - 1], plan, k) for k in range(1, plan.groups)]
 
     moved = plan.slots + (plan.groups - 1) * plan.capacity
@@ -419,24 +417,34 @@
     def late(o, part=0):
         return [m for m in plan.late if m[0] == o][part]
 
-    first = {}
-    for o in early:
-        lead = [first[4]] if o == 7 else []
-        first[o] = across(after(packed[o], *lead), plan, o)
     arrived = {late(0): ready[late(0)]}
 
     def send(message, *others):
         arrived[message] = across(after(ready[message], *others), plan, message[0])
         return arrived[message]
 
-    b5 = send(late(5), *[first[o] for o in early if o == 5])
-    b7 = send(late(7), *[first[o] for o in early if o == 7])
-    send(late(6), b5)
-    send(late(4), b7)
-    n2 = send(late(2))
-    send(late(3, 1), n2)
-    n3 = send(late(3, 0), *[first[o] for o in early if o == 5])
-    send(late(1), n3)
+    first = {}
+
+    def send_early(o, *others):
+        if o in packed:
+            first[o] = across(after(packed[o], *others), plan, o)
+
+    def came(*offsets):
+        return [first[o] for o in offsets if o in first]
+
+    send_early(4)
+    send_early(5)
+    send_early(2)
+    send_early(7, *came(4), *all_codes[1:])
+    b5 = send(late(5), *came(5))
+    b7 = send(late(7), *came(7))
+    b6 = send(late(6, 0), b5)
+    send(late(6, 1), b7)
+    n3 = send(late(3), *came(2))
+    n1 = send(late(1), *came(7))
+    b4 = send(late(4, 0), *came(5))
+    send(late(4, 1), b4)
+    send(late(2), b5)
 
     out_shape = jax.ShapeDtypeStruct((plan.rows * GRID_COLS * block, width), bf16)
     held, sets = [], []
@@ -484,7 +492,7 @@
             )(*held, *sets, *[arrived[m] for m in messages])
         ]
 
-    last = [late(4), late(6)]
+    last = [late(4, 1), late(6, 0), late(6, 1)]
     held = place(held, [m for m in plan.late if m not in last], "place_mid")
     held = place(held, last, "place_last")
     return held[0][None]

time: 106 us -> 105 us (level)
  starting transfers between devices: 33.1 us -> 30.9 us
    ppermute x3, waiting for transfers between devices: 1.37 us -> 6.27 us  [along(): lax.ppermute(value, 'front', [(f, (f + steps) % plan.groups) for f in ran...]
    ppermute x11 -> x13, waiting for transfers between devices: 55.2 us -> 50.8 us  [across(): return lax.ppermute(value, 'wide', pairs)]
    ppermute x11 -> x13, starting transfers between devices: 29.4 us -> 25.8 us  [across(): return lax.ppermute(value, 'wide', pairs)]
    ppermute x3, starting transfers between devices: 3.7 us -> 5.12 us  [along(): lax.ppermute(value, 'front', [(f, (f + steps) % plan.groups) for f in ran...]
  transfers between devices with their start and end apart: 14 -> 16, of which waited for: 6 -> 9; matrix products, arithmetic and copies ran while one was open for 1% -> 0% of each run, Pallas kernels for 12% -> 13%
where the time goes in v5:
time: 105 us; the launch traced here: 103 us
  waiting for transfers between devices  57.1 us (54%)
  starting transfers between devices  30.9 us (29%)
  Pallas kernels  14.7 us (14%)
    ppermute x13, waiting for transfers between devices, across(): return lax.ppermute(value, 'wide', pairs)  50.8 us
    ppermute x13, starting transfers between devices, across(): return lax.ppermute(value, 'wide', pairs)  25.8 us
    ppermute x3, waiting for transfers between devices, along(): lax.ppermute(value, 'front', [(f, (f + steps) % plan.groups) for f in ran...  6.27 us
    pallas_call x1, Pallas kernels, local(): pl.pallas_call(functools.partial(assemble_kernel, plan), out_shape=[jax.S...  5.84 us
    ppermute x3, starting transfers between devices, along(): lax.ppermute(value, 'front', [(f, (f + steps) % plan.groups) for f in ran...  5.12 us
    pallas_call x2, Pallas kernels, place(): pl.pallas_call(body, out_shape=out_shape, in_specs=[HBM] * len(held) + [A...  3.53 us
    pallas_call x1, Pallas kernels, local(): pl.pallas_call(functools.partial(stage_kernel, plan, early), out_shape=[j...  2.39 us
  transfers between devices with their start and end apart: 16, of which 9 were waited for; matrix products, arithmetic and copies ran while one was open for 0% of the time, Pallas kernels for 13%

profile of v5, /device:TPU:0, one launch (start us, length us, event | category | flops | bytes accessed | tf_op | source)
XLA Modules:
  0.0 103.5 jit_solution(16080887385491819953)
XLA Ops:
  0.0 0.0 copy-start.1
  0.0 0.0 copy-start
  0.0 0.7 bitcast_add_fusion.heads.refs_0_
  0.7 3.0 %collective-permute-start = (s32[4]{0:T(128)S(1)}, s32[4]{0:T(128)S(1)}, u32[]{:S(2)}, u32[]{:S(2)}) collective-permute-start(s32[4]{0:T(128)S(1)} %bitcast_add_fusion.heads.refs_0_), channel_id=1, source_target_pairs={{0,16},{16,0},{1,17},{17,1},{2,18},{18,2},{3,19},{19,3},{4,20},{20... | collective-permute-start | bytes 56 | tf_op jit(solution)/shard_map/ppermute | solution.py:337
  3.7 2.4 %stage.1 = (bf16[2,128,1024]{2,1,0:T(8,128)(2,1)S(1)}, bf16[1024,256]{1,0:T(8,128)(2,1)S(1)}, bf16[1024,256]{1,0:T(8,128)(2,1)S(1)}, bf16[1024,256]{1,0:T(8,128)(2,1)S(1)}, bf16[1024,256]{1,0:T(8,128)(2,1)S(1)}) custom-call(s32[4]{0:T(128)S(1)} %bitcast_add_fusion.heads.refs_0_, bf16[1,512,1024]{2,1,0:T(8,128)(2,1)} %refs_5_.1, bf16[1,1024,2048]{2,1,0:T(8,128)(2,1)} %refs_4_.1), custom_call_target="tpu_custom_call" | custom-call | tf_op jit(solution)/shard_map/stage/pallas_call | solution.py:354
  6.1 0.0 collective-permute-done.refs_1_
  6.1 1.1 %collective-permute-start.6 = (bf16[2,128,1024]{2,1,0:T(8,128)(2,1)S(1)}, bf16[2,128,1024]{2,1,0:T(8,128)(2,1)S(1)}, u32[]{:S(2)}, u32[]{:S(2)}) collective-permute-start(bf16[2,128,1024]{2,1,0:T(8,128)(2,1)S(1)} %get-tuple-element.49), channel_id=1, source_target_pairs={{0,16},{16,0},{1,17},{17,1},{2,18},{18,2},{3,19},{19,3},{4,20},{20... | collective-permute-start | bytes 1572872 | tf_op jit(solution)/shard_map/ppermute | solution.py:337
  7.2 1.1 %pack_early.1 = (bf16[264,256]{1,0:T(8,128)(2,1)S(1)}, bf16[520,256]{1,0:T(8,128)(2,1)S(1)}, bf16[520,256]{1,0:T(8,128)(2,1)S(1)}, bf16[520,256]{1,0:T(8,128)(2,1)S(1)}, s32[1]{0:T(128)}) custom-call(s32[4]{0:T(128)S(1)} %bitcast_add_fusion.heads.refs_0_, s32[4]{0:T(128)S(1)} %collective-permute-done.refs_1_, ...), custom_call_target="tpu_custom_call" | custom-call | tf_op jit(solution)/shard_map/pack_early/pallas_call | solution.py:375
  8.4 2.7 %collective-permute-start.1 = (bf16[264,256]{1,0:T(8,128)(2,1)S(1)}, bf16[264,256]{1,0:T(8,128)(2,1)S(1)}, u32[]{:S(2)}, u32[]{:S(2)}) collective-permute-start(bf16[264,256]{1,0:T(8,128)(2,1)S(1)} %get-tuple-element.41), channel_id=1, source_target_pairs={{0,8},{1,9},{2,10},{3,11},{4,12},{5,13},{6,14},{7,15},{8,0},{9,1},... | collective-permute-start | bytes 405512 | tf_op jit(solution)/shard_map/ppermute | solution.py:333
  11.0 1.3 %collective-permute-start.2 = (bf16[520,256]{1,0:T(8,128)(2,1)S(1)}, bf16[520,256]{1,0:T(8,128)(2,1)S(1)}, u32[]{:S(2)}, u32[]{:S(2)}) collective-permute-start(bf16[520,256]{1,0:T(8,128)(2,1)S(1)} %get-tuple-element.42), channel_id=1, source_target_pairs={{0,10},{1,11},{2,8},{3,9},{4,14},{5,15},{6,12},{7,13},{8,2},{9,3},... | collective-permute-start | bytes 798728 | tf_op jit(solution)/shard_map/ppermute | solution.py:333
  12.3 0.0 copy-done.1
  12.3 0.0 copy-done
  12.3 1.0 collective-permute-start.3
  13.3 6.3 %collective-permute-done.3.refs_3_ = s32[4,8]{1,0:T(4,128)S(1)} collective-permute-done((s32[4,8]{1,0:T(4,128)S(1)}, s32[4,8]{1,0:T(4,128)S(1)}, u32[]{:S(2)}, u32[]{:S(2)}) %collective-permute-start.3) | collective-permute-done | bytes 160 | tf_op jit(solution)/shard_map/ppermute | solution.py:337
  19.6 3.6 %collective-permute-done.1.refs_0_ = bf16[264,256]{1,0:T(8,128)(2,1)S(1)} collective-permute-done((bf16[264,256]{1,0:T(8,128)(2,1)S(1)}, bf16[264,256]{1,0:T(8,128)(2,1)S(1)}, u32[]{:S(2)}, u32[]{:S(2)}) %collective-permute-start.1) | collective-permute-done | bytes 135200 | tf_op jit(solution)/shard_map/ppermute | solution.py:333
  23.2 3.5 %collective-permute-start.4 = (bf16[520,256]{1,0:T(8,128)(2,1)S(1)}, bf16[520,256]{1,0:T(8,128)(2,1)S(1)}, u32[]{:S(2)}, u32[]{:S(2)}) collective-permute-start(bf16[520,256]{1,0:T(8,128)(2,1)S(1)} %get-tuple-element.44), channel_id=1, source_target_pairs={{0,14},{1,15},{2,12},{3,13},{4,10},{5,11},{6,8},{7,9},{8,6},{9,7},... | collective-permute-start | bytes 798728 | tf_op jit(solution)/shard_map/ppermute | solution.py:333
  26.6 0.0 collective-permute-start.5
  26.6 0.0 collective-permute-done.6.refs_6_
  26.6 5.8 %assemble.1 = (bf16[1024,256]{1,0:T(8,128)(2,1)S(1)}, bf16[1024,256]{1,0:T(8,128)(2,1)S(1)}, bf16[512,256]{1,0:T(8,128)(2,1)S(1)}, bf16[1024,256]{1,0:T(8,128)(2...) custom-call(s32[4]{0:T(128)S(1)} %bitcast_add_fusion.heads.refs_0_, ...), custom_call_target="tpu_custom_call" | custom-call | tf_op jit(solution)/shard_map/assemble/pallas_call | solution.py:395
  32.5 3.2 %collective-permute-done.2.refs_1_ = bf16[520,256]{1,0:T(8,128)(2,1)S(1)} collective-permute-done((bf16[520,256]{1,0:T(8,128)(2,1)S(1)}, bf16[520,256]{1,0:T(8,128)(2,1)S(1)}, u32[]{:S(2)}, u32[]{:S(2)}) %collective-permute-start.2) | collective-permute-done | bytes 266272 | tf_op jit(solution)/shard_map/ppermute | solution.py:333
  35.7 0.0 collective-permute-start.8
  35.7 0.0 collective-permute-done.4.refs_2_
  35.7 3.9 %collective-permute-done.5.refs_3_ = bf16[520,256]{1,0:T(8,128)(2,1)S(1)} collective-permute-done((bf16[520,256]{1,0:T(8,128)(2,1)S(1)}, bf16[520,256]{1,0:T(8,128)(2,1)S(1)}, u32[]{:S(2)}, u32[]{:S(2)}) %collective-permute-start.5) | collective-permute-done | bytes 266272 | tf_op jit(solution)/shard_map/ppermute | solution.py:333
  39.6 7.7 %collective-permute-start.10 = (bf16[1024,256]{1,0:T(8,128)(2,1)S(1)}, bf16[1024,256]{1,0:T(8,128)(2,1)S(1)}, u32[]{:S(2)}, u32[]{:S(2)}) collective-permute-start(bf16[1024,256]{1,0:T(8,128)(2,1)S(1)} %get-tuple-element.58), channel_id=1, source_target_pairs={{0,6},{1,7},{2,4},{3,5},{4,2},{5,3},{6,0},{7,1},{8,14},{9,15},{10,... | collective-permute-start | bytes 1572872 | tf_op jit(solution)/shard_map/ppermute | solution.py:333
  47.4 1.7 %collective-permute-start.7 = (bf16[1024,256]{1,0:T(8,128)(2,1)S(1)}, bf16[1024,256]{1,0:T(8,128)(2,1)S(1)}, u32[]{:S(2)}, u32[]{:S(2)}) collective-permute-start(bf16[1024,256]{1,0:T(8,128)(2,1)S(1)} %get-tuple-element.52), channel_id=1, source_target_pairs={{0,2},{1,3},{2,0},{3,1},{4,6},{5,7},{6,4},{7,5},{8,10},{9,11},{10,... | collective-permute-start | bytes 1572872 | tf_op jit(solution)/shard_map/ppermute | solution.py:333
  49.0 0.0 collective-permute-start.11
  49.1 2.4 %collective-permute-start.12 = (bf16[512,256]{1,0:T(8,128)(2,1)S(1)}, bf16[512,256]{1,0:T(8,128)(2,1)S(1)}, u32[]{:S(2)}, u32[]{:S(2)}) collective-permute-start(bf16[512,256]{1,0:T(8,128)(2,1)S(1)} %get-tuple-element.62), channel_id=1, source_target_pairs={{0,14},{1,15},{2,12},{3,13},{4,10},{5,11},{6,8},{7,9},{8,6},{9,7},... | collective-permute-start | bytes 786440 | tf_op jit(solution)/shard_map/ppermute | solution.py:333
  51.4 0.7 collective-permute-done.8.refs_7_
  52.1 0.2 collective-permute-start.9
  52.3 15.1 %collective-permute-done.11.refs_6_ = bf16[384,256]{1,0:T(8,128)(2,1)S(1)} collective-permute-done((bf16[384,256]{1,0:T(8,128)(2,1)S(1)}, bf16[384,256]{1,0:T(8,128)(2,1)S(1)}, u32[]{:S(2)}, u32[]{:S(2)}) %collective-permute-start.11) | collective-permute-done | bytes 196640 | tf_op jit(solution)/shard_map/ppermute | solution.py:333
  67.4 2.7 %collective-permute-start.14 = (bf16[640,256]{1,0:T(8,128)(2,1)S(1)}, bf16[640,256]{1,0:T(8,128)(2,1)S(1)}, u32[]{:S(2)}, u32[]{:S(2)}) collective-permute-start(bf16[640,256]{1,0:T(8,128)(2,1)S(1)} %get-tuple-element.66), channel_id=1, source_target_pairs={{0,12},{1,13},{2,14},{3,15},{4,8},{5,9},{6,10},{7,11},{8,4},{9,5},... | collective-permute-start | bytes 983048 | tf_op jit(solution)/shard_map/ppermute | solution.py:333
  70.2 5.7 %collective-permute-done.12.refs_8_ = bf16[512,256]{1,0:T(8,128)(2,1)S(1)} collective-permute-done((bf16[512,256]{1,0:T(8,128)(2,1)S(1)}, bf16[512,256]{1,0:T(8,128)(2,1)S(1)}, u32[]{:S(2)}, u32[]{:S(2)}) %collective-permute-start.12) | collective-permute-done | bytes 262176 | tf_op jit(solution)/shard_map/ppermute | solution.py:333
  75.9 0.0 collective-permute-start.13
  75.9 2.8 %collective-permute-done.9.refs_4_ = bf16[512,256]{1,0:T(8,128)(2,1)S(1)} collective-permute-done((bf16[512,256]{1,0:T(8,128)(2,1)S(1)}, bf16[512,256]{1,0:T(8,128)(2,1)S(1)}, u32[]{:S(2)}, u32[]{:S(2)}) %collective-permute-start.9) | collective-permute-done | bytes 262176 | tf_op jit(solution)/shard_map/ppermute | solution.py:333
  78.7 3.6 %collective-permute-start.15 = (bf16[384,256]{1,0:T(8,128)(2,1)S(1)}, bf16[384,256]{1,0:T(8,128)(2,1)S(1)}, u32[]{:S(2)}, u32[]{:S(2)}) collective-permute-start(bf16[384,256]{1,0:T(8,128)(2,1)S(1)} %get-tuple-element.68), channel_id=1, source_target_pairs={{0,12},{1,13},{2,14},{3,15},{4,8},{5,9},{6,10},{7,11},{8,4},{9,5},... | collective-permute-start | bytes 589832 | tf_op jit(solution)/shard_map/ppermute | solution.py:333
  82.3 1.8 %place_early.1 = (bf16[8192,256]{1,0:T(8,128)(2,1)}, s32[4]{0:T(128)S(1)}) custom-call(bf16[264,256]{1,0:T(8,128)(2,1)S(1)} %collective-permute-done.1.refs_0_, bf16[520,256]{1,0:T(8,128)(2,1)S(1)} %collective-permute-done.2.refs_1_, bf16[520,256]{1,0:T(8,128)(2,1)S(1)} %collective-permute-done.4.refs_2_, bf16[520,256]{1,0:T(8,128)(2,1)S(1)} %collective-permute-done.5.refs_3_), custom_call_target="tpu_custom_call" | custom-call | tf_op jit(solution)/shard_map/place_early/pallas_call | solution.py:452
  84.1 0.0 collective-permute-done.10.refs_5_
  84.1 0.0 collective-permute-done.7.refs_3_
  84.1 2.1 %place_mid.1.refs_0_ = bf16[8192,256]{1,0:T(8,128)(2,1)} custom-call(bf16[8192,256]{1,0:T(8,128)(2,1)} %get-tuple-element.46.refs_0_, s32[4]{0:T(128)S(1)} %get-tuple-element.47.refs_1_, bf16[1024,256]{1,0:T(8,128)(2,1)S(1)} %get-tuple-element.50.refs_2_, bf16[1024,256]{1,0:T(8,128)(2,1)S(1)} %collective-permute-done.7.refs_3_, ...), custom_call_target="tpu_custom_call", output_to_operand_aliasing={{}: (0, {})} | custom-call | tf_op jit(solution)/shard_map/place_mid/pallas_call | solution.py:477
  86.2 15.8 %collective-permute-done.13.refs_2_ = bf16[384,256]{1,0:T(8,128)(2,1)S(1)} collective-permute-done((bf16[384,256]{1,0:T(8,128)(2,1)S(1)}, bf16[384,256]{1,0:T(8,128)(2,1)S(1)}, u32[]{:S(2)}, u32[]{:S(2)}) %collective-permute-start.13) | collective-permute-done | bytes 196640 | tf_op jit(solution)/shard_map/ppermute | solution.py:333
  102.0 0.0 collective-permute-done.15.refs_4_
  102.0 0.0 collective-permute-done.14.refs_3_
  102.0 1.5 %place_last.1 = bf16[8192,256]{1,0:T(8,128)(2,1)} custom-call(bf16[8192,256]{1,0:T(8,128)(2,1)} %place_mid.1.refs_0_, s32[4]{0:T(128)S(1)} %get-tuple-element.47.refs_1_, bf16[384,256]{1,0:T(8,128)(2,1)S(1)} %collective-permute-done.13.refs_2_, bf16[640,256]{1,0:T(8,128)(2,1)S(1)} %collective-permute-done.14.refs_3_, ...), custom_call_target="tpu_custom_call", output_to_operand_aliasing={{}: (0, {})} | custom-call | tf_op jit(solution)/shard_map/place_last/pallas_call | solution.py:477
  (1 shorter events, 0.0 us)
Async XLA Ops:
  0.0 12.3 %copy-start.1 = (s32[1,4,8]{2,1,0:T(4,128)S(1)}, s32[1,4,8]{2,1,0:T(4,128)}, u32[]{:S(2)}) copy-start(s32[1,4,8]{2,1,0:T(4,128)} %param.11) | copy-start | bytes 388
  0.0 12.3 %copy-start = (s32[1,4,8]{2,1,0:T(4,128)S(1)}, s32[1,4,8]{2,1,0:T(4,128)}, u32[]{:S(2)}) copy-start(s32[1,4,8]{2,1,0:T(4,128)} %param.10) | copy-start | bytes 388
  0.7 5.4 %collective-permute-start = (s32[4]{0:T(128)S(1)}, s32[4]{0:T(128)S(1)}, u32[]{:S(2)}, u32[]{:S(2)}) collective-permute-start(s32[4]{0:T(128)S(1)} %bitcast_add_fusion.heads.refs_0_), channel_id=1, source_target_pairs={{0,16},{16,0},{1,17},{17,1},{2,18},{18,2},{3,19},{19,3},{4,20},{20... | collective-permute-start | bytes 56 | tf_op jit(solution)/shard_map/ppermute | solution.py:337
  6.1 20.6 %collective-permute-start.6 = (bf16[2,128,1024]{2,1,0:T(8,128)(2,1)S(1)}, bf16[2,128,1024]{2,1,0:T(8,128)(2,1)S(1)}, u32[]{:S(2)}, u32[]{:S(2)}) collective-permute-start(bf16[2,128,1024]{2,1,0:T(8,128)(2,1)S(1)} %get-tuple-element.49), channel_id=1, source_target_pairs={{0,16},{16,0},{1,17},{17,1},{2,18},{18,2},{3,19},{19,3},{4,20},{20... | collective-permute-start | bytes 1572872 | tf_op jit(solution)/shard_map/ppermute | solution.py:337
  8.4 14.8 %collective-permute-start.1 = (bf16[264,256]{1,0:T(8,128)(2,1)S(1)}, bf16[264,256]{1,0:T(8,128)(2,1)S(1)}, u32[]{:S(2)}, u32[]{:S(2)}) collective-permute-start(bf16[264,256]{1,0:T(8,128)(2,1)S(1)} %get-tuple-element.41), channel_id=1, source_target_pairs={{0,8},{1,9},{2,10},{3,11},{4,12},{5,13},{6,14},{7,15},{8,0},{9,1},... | collective-permute-start | bytes 405512 | tf_op jit(solution)/shard_map/ppermute | solution.py:333
  11.0 24.7 %collective-permute-start.2 = (bf16[520,256]{1,0:T(8,128)(2,1)S(1)}, bf16[520,256]{1,0:T(8,128)(2,1)S(1)}, u32[]{:S(2)}, u32[]{:S(2)}) collective-permute-start(bf16[520,256]{1,0:T(8,128)(2,1)S(1)} %get-tuple-element.42), channel_id=1, source_target_pairs={{0,10},{1,11},{2,8},{3,9},{4,14},{5,15},{6,12},{7,13},{8,2},{9,3},... | collective-permute-start | bytes 798728 | tf_op jit(solution)/shard_map/ppermute | solution.py:333
  12.3 7.3 %collective-permute-start.3 = (s32[4,8]{1,0:T(4,128)S(1)}, s32[4,8]{1,0:T(4,128)S(1)}, u32[]{:S(2)}, u32[]{:S(2)}) collective-permute-start(s32[4,8]{1,0:T(4,128)S(1)} %add_bitcast_fusion.refs_2_), channel_id=1, source_target_pairs={{0,16},{16,0},{1,17},{17,1},{2,18},{18,2},{3,19},{19,3},{4,20},{20... | collective-permute-start | bytes 392 | tf_op jit(solution)/shard_map/ppermute | solution.py:337
  23.2 12.5 %collective-permute-start.4 = (bf16[520,256]{1,0:T(8,128)(2,1)S(1)}, bf16[520,256]{1,0:T(8,128)(2,1)S(1)}, u32[]{:S(2)}, u32[]{:S(2)}) collective-permute-start(bf16[520,256]{1,0:T(8,128)(2,1)S(1)} %get-tuple-element.44), channel_id=1, source_target_pairs={{0,14},{1,15},{2,12},{3,13},{4,10},{5,11},{6,8},{7,9},{8,6},{9,7},... | collective-permute-start | bytes 798728 | tf_op jit(solution)/shard_map/ppermute | solution.py:333
  26.6 13.0 %collective-permute-start.5 = (bf16[520,256]{1,0:T(8,128)(2,1)S(1)}, bf16[520,256]{1,0:T(8,128)(2,1)S(1)}, u32[]{:S(2)}, u32[]{:S(2)}) collective-permute-start(bf16[520,256]{1,0:T(8,128)(2,1)S(1)} %get-tuple-element.45), channel_id=1, source_target_pairs={{0,4},{1,5},{2,6},{3,7},{4,0},{5,1},{6,2},{7,3},{8,12},{9,13},{10,... | collective-permute-start | bytes 798728 | tf_op jit(solution)/shard_map/ppermute | solution.py:333
  35.7 16.4 %collective-permute-start.8 = (bf16[512,256]{1,0:T(8,128)(2,1)S(1)}, bf16[512,256]{1,0:T(8,128)(2,1)S(1)}, u32[]{:S(2)}, u32[]{:S(2)}) collective-permute-start(bf16[512,256]{1,0:T(8,128)(2,1)S(1)} %get-tuple-element.55), channel_id=1, source_target_pairs={{0,10},{1,11},{2,8},{3,9},{4,14},{5,15},{6,12},{7,13},{8,2},{9,3},... | collective-permute-start | bytes 786440 | tf_op jit(solution)/shard_map/ppermute | solution.py:333
  39.6 44.5 %collective-permute-start.10 = (bf16[1024,256]{1,0:T(8,128)(2,1)S(1)}, bf16[1024,256]{1,0:T(8,128)(2,1)S(1)}, u32[]{:S(2)}, u32[]{:S(2)}) collective-permute-start(bf16[1024,256]{1,0:T(8,128)(2,1)S(1)} %get-tuple-element.58), channel_id=1, source_target_pairs={{0,6},{1,7},{2,4},{3,5},{4,2},{5,3},{6,0},{7,1},{8,14},{9,15},{10,... | collective-permute-start | bytes 1572872 | tf_op jit(solution)/shard_map/ppermute | solution.py:333
  47.4 36.8 %collective-permute-start.7 = (bf16[1024,256]{1,0:T(8,128)(2,1)S(1)}, bf16[1024,256]{1,0:T(8,128)(2,1)S(1)}, u32[]{:S(2)}, u32[]{:S(2)}) collective-permute-start(bf16[1024,256]{1,0:T(8,128)(2,1)S(1)} %get-tuple-element.52), channel_id=1, source_target_pairs={{0,2},{1,3},{2,0},{3,1},{4,6},{5,7},{6,4},{7,5},{8,10},{9,11},{10,... | collective-permute-start | bytes 1572872 | tf_op jit(solution)/shard_map/ppermute | solution.py:333
  49.0 18.4 %collective-permute-start.11 = (bf16[384,256]{1,0:T(8,128)(2,1)S(1)}, bf16[384,256]{1,0:T(8,128)(2,1)S(1)}, u32[]{:S(2)}, u32[]{:S(2)}) collective-permute-start(bf16[384,256]{1,0:T(8,128)(2,1)S(1)} %get-tuple-element.60), channel_id=1, source_target_pairs={{0,8},{1,9},{2,10},{3,11},{4,12},{5,13},{6,14},{7,15},{8,0},{9,1},... | collective-permute-start | bytes 589832 | tf_op jit(solution)/shard_map/ppermute | solution.py:333
  49.1 26.8 %collective-permute-start.12 = (bf16[512,256]{1,0:T(8,128)(2,1)S(1)}, bf16[512,256]{1,0:T(8,128)(2,1)S(1)}, u32[]{:S(2)}, u32[]{:S(2)}) collective-permute-start(bf16[512,256]{1,0:T(8,128)(2,1)S(1)} %get-tuple-element.62), channel_id=1, source_target_pairs={{0,14},{1,15},{2,12},{3,13},{4,10},{5,11},{6,8},{7,9},{8,6},{9,7},... | collective-permute-start | bytes 786440 | tf_op jit(solution)/shard_map/ppermute | solution.py:333
  52.1 26.6 %collective-permute-start.9 = (bf16[512,256]{1,0:T(8,128)(2,1)S(1)}, bf16[512,256]{1,0:T(8,128)(2,1)S(1)}, u32[]{:S(2)}, u32[]{:S(2)}) collective-permute-start(bf16[512,256]{1,0:T(8,128)(2,1)S(1)} %get-tuple-element.56), channel_id=1, source_target_pairs={{0,4},{1,5},{2,6},{3,7},{4,0},{5,1},{6,2},{7,3},{8,12},{9,13},{10,... | collective-permute-start | bytes 786440 | tf_op jit(solution)/shard_map/ppermute | solution.py:333
  67.4 34.6 %collective-permute-start.14 = (bf16[640,256]{1,0:T(8,128)(2,1)S(1)}, bf16[640,256]{1,0:T(8,128)(2,1)S(1)}, u32[]{:S(2)}, u32[]{:S(2)}) collective-permute-start(bf16[640,256]{1,0:T(8,128)(2,1)S(1)} %get-tuple-element.66), channel_id=1, source_target_pairs={{0,12},{1,13},{2,14},{3,15},{4,8},{5,9},{6,10},{7,11},{8,4},{9,5},... | collective-permute-start | bytes 983048 | tf_op jit(solution)/shard_map/ppermute | solution.py:333
  75.9 26.2 %collective-permute-start.13 = (bf16[384,256]{1,0:T(8,128)(2,1)S(1)}, bf16[384,256]{1,0:T(8,128)(2,1)S(1)}, u32[]{:S(2)}, u32[]{:S(2)}) collective-permute-start(bf16[384,256]{1,0:T(8,128)(2,1)S(1)} %get-tuple-element.64), channel_id=1, source_target_pairs={{0,8},{1,9},{2,10},{3,11},{4,12},{5,13},{6,14},{7,15},{8,0},{9,1},... | collective-permute-start | bytes 589832 | tf_op jit(solution)/shard_map/ppermute | solution.py:333
  78.7 23.4 %collective-permute-start.15 = (bf16[384,256]{1,0:T(8,128)(2,1)S(1)}, bf16[384,256]{1,0:T(8,128)(2,1)S(1)}, u32[]{:S(2)}, u32[]{:S(2)}) collective-permute-start(bf16[384,256]{1,0:T(8,128)(2,1)S(1)} %get-tuple-element.68), channel_id=1, source_target_pairs={{0,12},{1,13},{2,14},{3,15},{4,8},{5,9},{6,10},{7,11},{8,4},{9,5},... | collective-permute-start | bytes 589832 | tf_op jit(solution)/shard_map/ppermute | solution.py:333

commit v6 on v5

--- a/solution.py
+++ b/solution.py
@@ -31,11 +31,11 @@
         self.width = self.col_groups * self.block
         self.capacity = max(self.slots // 4, self.slots // self.groups)
         self.first = max(0, self.rows - self.capacity * self.groups)
-        self.early = {4: self.first // 2, 5: self.first, 7: self.first, 2: self.first}
+        self.early = {4: self.first // 2, 5: self.first, 7: self.first}
         self.late = []
         for o in range(GRID_COLS):
             count = self.rows - self.early.get(o, 0)
-            cuts = [0, count // 2, count] if o == 4 else [0, max(1, 5 * count // 8), count] if o == 6 else [0, count]
+            cuts = [0, count // 2, count] if o == 3 else [0, count]
             self.late += [(o, lo, hi) for lo, hi in zip(cuts, cuts[1:]) if lo < hi]
 
 
@@ -103,33 +103,10 @@
         copy.wait()
 
 
-def stage_kernel(plan, early, heads, updates, panel, *refs):
-    outs, refs = refs[: plan.groups - 1], refs[plan.groups - 1 :]
-    staged, (slot_sems, sems) = refs[: len(early)], refs[len(early) :]
-    me = lax.axis_index("front")
+def stage_kernel(plan, lead, panel, *refs):
+    staged, sems = refs[: len(lead)], refs[len(lead)]
     column = lax.axis_index("wide") // plan.grid_rows
     block = plan.block
-
-    def buckets(act):
-        for k in range(1, plan.groups):
-            target = lax.rem(me + k, plan.groups)
-            rank = jnp.int32(0)
-            for q in range(plan.slots):
-                named = parent_of(plan, heads, q) == target
-
-                @pl.when(named)
-                def _():
-                    act(
-                        pltpu.make_async_copy(
-                            updates.at[0, pl.ds(q * block, block)],
-                            outs[k - 1].at[rank],
-                            slot_sems.at[q],
-                        )
-                    )
-
-                rank = rank + jnp.where(named, 1, 0)
-
-    buckets(lambda c: c.start())
     run_all(
         [
             pltpu.make_async_copy(
@@ -137,27 +114,83 @@
                 staged[i].at[:, pl.ds(cc * block, block)],
                 sems.at[i, cc],
             )
-            for i, o in enumerate(early)
+            for i, o in enumerate(lead)
             for cc in range(plan.col_groups)
         ]
     )
-    buckets(lambda c: c.wait())
-
-
-def pack_kernel(plan, offsets, *refs):
-    groups, count = plan.groups, len(offsets)
+
+
+def put_tag(plan, touched, o, out):
+    chosen = first_rows(plan, touched, plan.early[o]).astype(jnp.float32)
+    tag = jnp.full((TAG, plan.width), chosen, jnp.float32).astype(jnp.bfloat16)
+    out[plan.early[o] * plan.block :, :] = tag
+
+
+def pack_kernel(plan, lead, *refs):
+    groups, count = plan.groups, len(lead)
     head_refs, staged, refs = refs[:groups], refs[groups : groups + count], refs[groups + count :]
     outs, (touched_out, order) = refs[:count], refs[count:]
     block = plan.block
     touched = touched_rows(plan, head_refs)
     touched_out[0] = touched
     list_rows(plan, first_rows(plan, touched, plan.first), 1, order)
-    for i, o in enumerate(offsets):
+    for i, o in enumerate(lead):
         for k in range(plan.early[o]):
             outs[i][pl.ds(k * block, block), :] = staged[i][at(order[k], block), :]
-        chosen = first_rows(plan, touched, plan.early[o]).astype(jnp.float32)
-        tag = jnp.full((TAG, plan.width), chosen, jnp.float32).astype(jnp.bfloat16)
-        outs[i][plan.early[o] * block :, :] = tag
+        put_tag(plan, touched, o, outs[i])
+
+
+def bucket_kernel(plan, tail, heads, *refs):
+    touched_ref, refs = (refs[0], refs[1:]) if tail else (None, refs)
+    updates, panel, refs = refs[0], refs[1], refs[2:]
+    count = (plan.groups - 1) * plan.capacity
+    outs, packed, refs = refs[:count], refs[count : count + len(tail)], refs[count + len(tail) :]
+    order, slot_sems, sems = refs
+    me = lax.axis_index("front")
+    column = lax.axis_index("wide") // plan.grid_rows
+    block = plan.block
+
+    def buckets(act):
+        for k in range(1, plan.groups):
+            target = lax.rem(me + k, plan.groups)
+            rank = jnp.int32(0)
+            for q in range(plan.slots):
+                named = parent_of(plan, heads, q) == target
+                for c in range(plan.capacity):
+
+                    @pl.when(jnp.logical_and(named, rank == c))
+                    def _():
+                        act(
+                            pltpu.make_async_copy(
+                                updates.at[0, pl.ds(q * block, block)],
+                                outs[(k - 1) * plan.capacity + c],
+                                slot_sems.at[q],
+                            )
+                        )
+
+                rank = rank + jnp.where(named, 1, 0)
+
+    buckets(lambda c: c.start())
+    copies = []
+    if tail:
+        touched = touched_ref[0]
+        list_rows(plan, first_rows(plan, touched, plan.first), 1, order)
+        for i, o in enumerate(tail):
+            target = jnp.bitwise_xor(column, o)
+            for k in range(plan.early[o]):
+                for cc in range(plan.col_groups):
+                    copies.append(
+                        pltpu.make_async_copy(
+                            panel.at[0, at(order[k], block), at(cc * GRID_COLS + target, block)],
+                            packed[i].at[pl.ds(k * block, block), pl.ds(cc * block, block)],
+                            sems.at[i, k, cc],
+                        )
+                    )
+                    copies[-1].start()
+            put_tag(plan, touched, o, packed[i])
+    for copy in copies:
+        copy.wait()
+    buckets(lambda c: c.wait())
 
 
 def assemble_kernel(plan, *refs):
@@ -165,7 +198,8 @@
     head_refs, refs = refs[:groups], refs[groups:]
     code_refs, refs = refs[:groups], refs[groups:]
     panel, updates, refs = refs[0], refs[1], refs[2:]
-    got, refs = refs[: groups - 1], refs[groups - 1 :]
+    count = (groups - 1) * plan.capacity
+    got, refs = refs[:count], refs[count:]
     outs, refs = refs[: len(plan.late)], refs[len(plan.late) :]
     total, raw, moved, place_ref, row_sems, slot_sems = refs
     me = lax.axis_index("front")
@@ -179,9 +213,10 @@
     ]
     for k in range(1, groups):
         for c in range(plan.capacity):
-            index = plan.slots + (k - 1) * plan.capacity + c
+            part = (k - 1) * plan.capacity + c
+            index = plan.slots + part
             slot_copies.append(
-                pltpu.make_async_copy(got[k - 1].at[c], moved.at[index], slot_sems.at[index])
+                pltpu.make_async_copy(got[part], moved.at[index], slot_sems.at[index])
             )
     row_copies = [
         pltpu.make_async_copy(panel.at[0, pl.ds(t * block, block)], raw.at[t], row_sems.at[t])
@@ -351,45 +386,61 @@
 
 
     early = [o for o in plan.early if plan.early[o]]
-    staged = pl.pallas_call(
-        functools.partial(stage_kernel, plan, early),
-        out_shape=[
-            jax.ShapeDtypeStruct((plan.capacity, block, updates.shape[2]), bf16)
-            for _ in range(1, plan.groups)
-        ]
-        + [jax.ShapeDtypeStruct((plan.rows * block, width), bf16) for _ in early],
-        in_specs=[SMEM, HBM, HBM],
-        out_specs=[VMEM] * (plan.groups - 1 + len(early)),
+    lead, tail = early[:2], early[2:]
+    packed, touched = {}, []
+
+    def early_shape(o):
+        return jax.ShapeDtypeStruct((plan.early[o] * block + TAG, width), bf16)
+
+    if lead:
+        staged = pl.pallas_call(
+            functools.partial(stage_kernel, plan, lead),
+            out_shape=[jax.ShapeDtypeStruct((plan.rows * block, width), bf16) for _ in lead],
+            in_specs=[HBM],
+            out_specs=[VMEM] * len(lead),
+            scratch_shapes=[pltpu.SemaphoreType.DMA((len(lead), plan.col_groups))],
+            compiler_params=params(),
+            cost_estimate=COST,
+            name="stage",
+        )(panels)
+        *outs, touched_set = pl.pallas_call(
+            functools.partial(pack_kernel, plan, lead),
+            out_shape=[early_shape(o) for o in lead] + [jax.ShapeDtypeStruct((1,), jnp.int32)],
+            in_specs=[SMEM] * plan.groups + [VMEM] * len(lead),
+            out_specs=[VMEM] * len(lead) + [SMEM],
+            scratch_shapes=[pltpu.SMEM((plan.rows,), jnp.int32)],
+            compiler_params=params(),
+            cost_estimate=COST,
+            name="pack_early",
+        )(*all_heads, *staged)
+        packed = dict(zip(lead, outs))
+        touched = [touched_set]
+
+    count = (plan.groups - 1) * plan.capacity
+    outs = pl.pallas_call(
+        functools.partial(bucket_kernel, plan, tail),
+        out_shape=[jax.ShapeDtypeStruct((block, updates.shape[2]), bf16)] * count
+        + [early_shape(o) for o in tail],
+        in_specs=[SMEM] * (1 + len(touched)) + [HBM, HBM],
+        out_specs=[VMEM] * (count + len(tail)),
         scratch_shapes=[
+            pltpu.SMEM((plan.rows,), jnp.int32),
             pltpu.SemaphoreType.DMA((plan.slots,)),
-            pltpu.SemaphoreType.DMA((max(1, len(early)), plan.col_groups)),
+            pltpu.SemaphoreType.DMA((max(1, len(tail)), max(1, plan.first), plan.col_groups)),
         ],
         compiler_params=params(),
         cost_estimate=COST,
-        name="stage",
-    )(heads, moving, panels)
-    buckets, staged = staged[: plan.groups - 1], staged[plan.groups - 1 :]
-
-    packed = {}
-    if early:
-        *outs, touched = pl.pallas_call(
-            functools.partial(pack_kernel, plan, early),
-            out_shape=[
-                jax.ShapeDtypeStruct((plan.early[o] * block + TAG, width), bf16) for o in early
-            ]
-            + [jax.ShapeDtypeStruct((1,), jnp.int32)],
-            in_specs=[SMEM] * plan.groups + [VMEM] * len(early),
-            out_specs=[VMEM] * len(early) + [SMEM],
-            scratch_shapes=[pltpu.SMEM((plan.rows,), jnp.int32)],
-            compiler_params=params(),
-            cost_estimate=pl.CostEstimate(flops=0, transcendentals=0, bytes_accessed=0),
-            name="pack_early",
-        )(*all_heads, *staged)
-        packed = dict(zip(early, outs))
-
-    all_codes = [codes] + [along(codes, plan, k) for k in range(1, plan.groups)]
-    buckets = [after(x, *all_heads) for x in buckets]
-    got = [along(buckets[k - 1], plan, k) for k in range(1, plan.groups)]
+        name="bucket",
+    )(heads, *touched, moving, panels)
+    packed.update(zip(tail, outs[count:]))
+
+    all_codes = [after(codes, *touched)]
+    all_codes += [along(all_codes[0], plan, k) for k in range(1, plan.groups)]
+    got = [
+        along(outs[(k - 1) * plan.capacity + c], plan, k)
+        for k in range(1, plan.groups)
+        for c in range(plan.capacity)
+    ]
 
     moved = plan.slots + (plan.groups - 1) * plan.capacity
     assembled = pl.pallas_call(
@@ -397,7 +448,7 @@
         out_shape=[
             jax.ShapeDtypeStruct(((hi - lo) * block, width), bf16) for o, lo, hi in plan.late
         ],
-        in_specs=[SMEM] * (2 * plan.groups) + [HBM, HBM] + [ANY] * (plan.groups - 1),
+        in_specs=[SMEM] * (2 * plan.groups) + [HBM, HBM] + [ANY] * len(got),
         out_specs=[VMEM] * len(plan.late),
         scratch_shapes=[
             pltpu.VMEM((plan.rows, block, parent_panels.shape[2]), jnp.float32),
@@ -434,17 +485,15 @@
 
     send_early(4)
     send_early(5)
-    send_early(2)
     send_early(7, *came(4), *all_codes[1:])
     b5 = send(late(5), *came(5))
     b7 = send(late(7), *came(7))
-    b6 = send(late(6, 0), b5)
-    send(late(6, 1), b7)
-    n3 = send(late(3), *came(2))
-    n1 = send(late(1), *came(7))
-    b4 = send(late(4, 0), *came(5))
-    send(late(4, 1), b4)
-    send(late(2), b5)
+    send(late(6), b5)
+    send(late(4), b7)
+    n1 = send(late(1), *came(5))
+    send(late(2), *came(7))
+    send(late(3, 0), n1)
+    send(late(3, 1), b7)
 
     out_shape = jax.ShapeDtypeStruct((plan.rows * GRID_COLS * block, width), bf16)
     held, sets = [], []
@@ -492,7 +541,7 @@
             )(*held, *sets, *[arrived[m] for m in messages])
         ]
 
-    last = [late(4, 1), late(6, 0), late(6, 1)]
+    last = [late(4), late(6)]
     held = place(held, [m for m in plan.late if m not in last], "place_mid")
     held = place(held, last, "place_last")
     return held[0][None]

time: 105 us -> 101 us (0.962); the launches traced: 103 us -> 101 us
  waiting for transfers between devices: 57.1 us -> 39.4 us
  starting transfers between devices: 30.9 us -> 45.2 us
  Pallas kernels: 14.7 us -> 15.8 us
    ppermute x13 -> x11, waiting for transfers between devices: 50.8 us -> 30.6 us  [across(): return lax.ppermute(value, 'wide', pairs)]
    ppermute x13 -> x11, starting transfers between devices: 25.8 us -> 38.5 us  [across(): return lax.ppermute(value, 'wide', pairs)]
    ppermute x3 -> x4, waiting for transfers between devices: 6.27 us -> 8.78 us  [along(): lax.ppermute(value, 'front', [(f, (f + steps) % plan.groups) for f in ran...]
    ppermute x3 -> x4, starting transfers between devices: 5.12 us -> 6.64 us  [along(): lax.ppermute(value, 'front', [(f, (f + steps) % plan.groups) for f in ran...]
    pallas_call x2 -> x3, Pallas kernels: 3.52 us -> 4.91 us  [the longest x1 2.53 us: local(): pl.pallas_call(functools.partial(bucket_kernel, plan, tail), out_shape=[j...]
  transfers between devices with their start and end apart: 16 -> 15, of which waited for: 9 -> 6; matrix products, arithmetic and copies ran while one was open for 0% -> 0% of each run, Pallas kernels for 13% -> 13%
where the time goes in v6:
time: 101 us
  starting transfers between devices  45.2 us (45%)
  waiting for transfers between devices  39.4 us (39%)
  Pallas kernels  15.8 us (16%)
    ppermute x11, starting transfers between devices, across(): return lax.ppermute(value, 'wide', pairs)  38.5 us
    ppermute x11, waiting for transfers between devices, across(): return lax.ppermute(value, 'wide', pairs)  30.6 us
    ppermute x4, waiting for transfers between devices, along(): lax.ppermute(value, 'front', [(f, (f + steps) % plan.groups) for f in ran...  8.78 us
    ppermute x4, starting transfers between devices, along(): lax.ppermute(value, 'front', [(f, (f + steps) % plan.groups) for f in ran...  6.64 us
    pallas_call x1, Pallas kernels, local(): pl.pallas_call(functools.partial(assemble_kernel, plan), out_shape=[jax.S...  5.79 us
    pallas_call x2, Pallas kernels, place(): pl.pallas_call(body, out_shape=out_shape, in_specs=[HBM] * len(held) + [A...  3.41 us
    pallas_call x1, Pallas kernels, local(): pl.pallas_call(functools.partial(bucket_kernel, plan, tail), out_shape=[j...  2.53 us
  transfers between devices with their start and end apart: 15, of which 6 were waited for; matrix products, arithmetic and copies ran while one was open for 0% of the time, Pallas kernels for 13%

profile of v6, /device:TPU:0, one launch (start us, length us, event | category | flops | bytes accessed | tf_op | source)
XLA Modules:
  0.0 101.2 jit_solution(3350011452033750365)
XLA Ops:
  0.0 0.7 bitcast_add_fusion.refs_0_.heads
  0.7 3.0 %collective-permute-start = (s32[4]{0:T(128)S(1)}, s32[4]{0:T(128)S(1)}, u32[]{:S(2)}, u32[]{:S(2)}) collective-permute-start(s32[4]{0:T(128)S(1)} %bitcast_add_fusion.refs_0_.heads), channel_id=1, source_target_pairs={{0,16},{16,0},{1,17},{17,1},{2,18},{18,2},{3,19},{19,3},{4,20},{20... | collective-permute-start | bytes 56 | tf_op jit(solution)/shard_map/ppermute | solution.py:372
  3.6 1.2 %stage.1 = (bf16[1024,256]{1,0:T(8,128)(2,1)S(1)}, bf16[1024,256]{1,0:T(8,128)(2,1)S(1)}) custom-call(bf16[1,1024,2048]{2,1,0:T(8,128)(2,1)} %refs_4_.1), custom_call_target="tpu_custom_call" | custom-call | tf_op jit(solution)/shard_map/stage/pallas_call | solution.py:396
  4.9 0.0 copy-start
  4.9 0.0 copy-start.1
  4.9 0.2 collective-permute-done.refs_1_
  5.2 1.1 %pack_early.1 = (bf16[264,256]{1,0:T(8,128)(2,1)S(1)}, bf16[520,256]{1,0:T(8,128)(2,1)S(1)}, s32[1]{0:T(128)}) custom-call(s32[4]{0:T(128)S(1)} %bitcast_add_fusion.refs_0_.heads, s32[4]{0:T(128)S(1)} %collective-permute-done.refs_1_, bf16[1024,256]{1,0:T(8,128)(2,1)S(1)} %get-tuple-element.34.refs_2_, bf16[1024,256]{1,0:T(8,128)(2,1)S(1)} %get-tuple-element.35.refs_3_), custom_call_target="tpu_custom_call" | custom-call | tf_op jit(solution)/shard_map/pack_early/pallas_call | solution.py:406
  6.3 3.2 %collective-permute-start.1 = (bf16[264,256]{1,0:T(8,128)(2,1)S(1)}, bf16[264,256]{1,0:T(8,128)(2,1)S(1)}, u32[]{:S(2)}, u32[]{:S(2)}) collective-permute-start(bf16[264,256]{1,0:T(8,128)(2,1)S(1)} %get-tuple-element.36), channel_id=1, source_target_pairs={{0,8},{1,9},{2,10},{3,11},{4,12},{5,13},{6,14},{7,15},{8,0},{9,1},... | collective-permute-start | bytes 405512 | tf_op jit(solution)/shard_map/ppermute | solution.py:368
  9.5 1.3 %collective-permute-start.2 = (bf16[520,256]{1,0:T(8,128)(2,1)S(1)}, bf16[520,256]{1,0:T(8,128)(2,1)S(1)}, u32[]{:S(2)}, u32[]{:S(2)}) collective-permute-start(bf16[520,256]{1,0:T(8,128)(2,1)S(1)} %get-tuple-element.37), channel_id=1, source_target_pairs={{0,10},{1,11},{2,8},{3,9},{4,14},{5,15},{6,12},{7,13},{8,2},{9,3},... | collective-permute-start | bytes 798728 | tf_op jit(solution)/shard_map/ppermute | solution.py:368
  10.7 2.5 %bucket.1 = (bf16[128,1024]{1,0:T(8,128)(2,1)S(1)}, bf16[128,1024]{1,0:T(8,128)(2,1)S(1)}, bf16[520,256]{1,0:T(8,128)(2,1)S(1)}) custom-call(s32[4]{0:T(128)S(1)} %bitcast_add_fusion.refs_0_.heads, s32[1]{0:T(128)} %get-tuple-element.38.refs_0_, bf16[1,512,1024]{2,1,0:T(8,128)(2,1)} %refs_5_.1, bf16[1,1024,2048]{2,1,0:T(8,128)(2,1)} %refs_4_.1), custom_call_target="tpu_custom_call" | custom-call | tf_op jit(solution)/shard_map/bucket/pallas_call | solution.py:420
  13.3 1.6 %collective-permute-start.5 = (bf16[128,1024]{1,0:T(8,128)(2,1)S(1)}, bf16[128,1024]{1,0:T(8,128)(2,1)S(1)}, u32[]{:S(2)}, u32[]{:S(2)}) collective-permute-start(bf16[128,1024]{1,0:T(8,128)(2,1)S(1)} %get-tuple-element.44), channel_id=1, source_target_pairs={{0,16},{16,0},{1,17},{17,1},{2,18},{18,2},{3,19},{19,3},{4,20},{20... | collective-permute-start | bytes 786440 | tf_op jit(solution)/shard_map/ppermute | solution.py:372
  14.9 0.5 collective-permute-start.6
  15.4 0.0 copy-done
  15.4 0.0 copy-done.1
  15.4 1.6 %collective-permute-start.3 = (s32[4,8]{1,0:T(4,128)S(1)}, s32[4,8]{1,0:T(4,128)S(1)}, u32[]{:S(2)}, u32[]{:S(2)}) collective-permute-start(s32[4,8]{1,0:T(4,128)S(1)} %add_bitcast_fusion.refs_2_), channel_id=1, source_target_pairs={{0,16},{16,0},{1,17},{17,1},{2,18},{18,2},{3,19},{19,3},{4,20},{20... | collective-permute-start | bytes 392 | tf_op jit(solution)/shard_map/ppermute | solution.py:372
  17.0 8.5 %collective-permute-done.3.refs_3_ = s32[4,8]{1,0:T(4,128)S(1)} collective-permute-done((s32[4,8]{1,0:T(4,128)S(1)}, s32[4,8]{1,0:T(4,128)S(1)}, u32[]{:S(2)}, u32[]{:S(2)}) %collective-permute-start.3) | collective-permute-done | bytes 160 | tf_op jit(solution)/shard_map/ppermute | solution.py:372
  25.5 0.0 collective-permute-done.1.refs_0_
  25.5 3.5 %collective-permute-start.4 = (bf16[520,256]{1,0:T(8,128)(2,1)S(1)}, bf16[520,256]{1,0:T(8,128)(2,1)S(1)}, u32[]{:S(2)}, u32[]{:S(2)}) collective-permute-start(bf16[520,256]{1,0:T(8,128)(2,1)S(1)} %get-tuple-element.41), channel_id=1, source_target_pairs={{0,14},{1,15},{2,12},{3,13},{4,10},{5,11},{6,8},{7,9},{8,6},{9,7},... | collective-permute-start | bytes 798728 | tf_op jit(solution)/shard_map/ppermute | solution.py:368
  29.0 0.0 collective-permute-done.5.refs_6_
  29.0 0.0 collective-permute-done.6.refs_7_
  29.0 5.8 %assemble.1 = (bf16[1024,256]{1,0:T(8,128)(2,1)S(1)}, bf16[1024,256]{1,0:T(8,128)(2,1)S(1)}, bf16[1024,256]{1,0:T(8,128)(2,1)S(1)}, bf16[512,256]{1,0:T(8,128)(2...) custom-call(s32[4]{0:T(128)S(1)} %bitcast_add_fusion.refs_0_.heads, ...), custom_call_target="tpu_custom_call" | custom-call | tf_op jit(solution)/shard_map/assemble/pallas_call | solution.py:446
  34.8 0.0 collective-permute-done.2.refs_1_
  34.8 1.5 %collective-permute-start.7 = (bf16[1024,256]{1,0:T(8,128)(2,1)S(1)}, bf16[1024,256]{1,0:T(8,128)(2,1)S(1)}, u32[]{:S(2)}, u32[]{:S(2)}) collective-permute-start(bf16[1024,256]{1,0:T(8,128)(2,1)S(1)} %get-tuple-element.48), channel_id=1, source_target_pairs={{0,2},{1,3},{2,0},{3,1},{4,6},{5,7},{6,4},{7,5},{8,10},{9,11},{10,... | collective-permute-start | bytes 1572872 | tf_op jit(solution)/shard_map/ppermute | solution.py:368
  36.3 0.0 collective-permute-start.12
  36.3 0.0 collective-permute-done.4.refs_2_
  36.3 2.9 %collective-permute-start.10 = (bf16[512,256]{1,0:T(8,128)(2,1)S(1)}, bf16[512,256]{1,0:T(8,128)(2,1)S(1)}, u32[]{:S(2)}, u32[]{:S(2)}) collective-permute-start(bf16[512,256]{1,0:T(8,128)(2,1)S(1)} %get-tuple-element.55), channel_id=1, source_target_pairs={{0,14},{1,15},{2,12},{3,13},{4,10},{5,11},{6,8},{7,9},{8,6},{9,7},... | collective-permute-start | bytes 786440 | tf_op jit(solution)/shard_map/ppermute | solution.py:368
  39.2 15.0 %collective-permute-start.8 = (bf16[1024,256]{1,0:T(8,128)(2,1)S(1)}, bf16[1024,256]{1,0:T(8,128)(2,1)S(1)}, u32[]{:S(2)}, u32[]{:S(2)}) collective-permute-start(bf16[1024,256]{1,0:T(8,128)(2,1)S(1)} %get-tuple-element.50), channel_id=1, source_target_pairs={{0,4},{1,5},{2,6},{3,7},{4,0},{5,1},{6,2},{7,3},{8,12},{9,13},{10,... | collective-permute-start | bytes 1572872 | tf_op jit(solution)/shard_map/ppermute | solution.py:368
  54.2 2.5 %collective-permute-done.12.refs_7_ = bf16[512,256]{1,0:T(8,128)(2,1)S(1)} collective-permute-done((bf16[512,256]{1,0:T(8,128)(2,1)S(1)}, bf16[512,256]{1,0:T(8,128)(2,1)S(1)}, u32[]{:S(2)}, u32[]{:S(2)}) %collective-permute-start.12) | collective-permute-done | bytes 262176 | tf_op jit(solution)/shard_map/ppermute | solution.py:368
  56.7 3.5 %collective-permute-start.14 = (bf16[1024,256]{1,0:T(8,128)(2,1)S(1)}, bf16[1024,256]{1,0:T(8,128)(2,1)S(1)}, u32[]{:S(2)}, u32[]{:S(2)}) collective-permute-start(bf16[1024,256]{1,0:T(8,128)(2,1)S(1)} %get-tuple-element.62), channel_id=1, source_target_pairs={{0,12},{1,13},{2,14},{3,15},{4,8},{5,9},{6,10},{7,11},{8,4},{9,5},... | collective-permute-start | bytes 1572872 | tf_op jit(solution)/shard_map/ppermute | solution.py:368
  60.2 0.0 collective-permute-done.10.refs_8_
  60.2 4.8 %collective-permute-start.13 = (bf16[768,256]{1,0:T(8,128)(2,1)S(1)}, bf16[768,256]{1,0:T(8,128)(2,1)S(1)}, u32[]{:S(2)}, u32[]{:S(2)}) collective-permute-start(bf16[768,256]{1,0:T(8,128)(2,1)S(1)} %get-tuple-element.60), channel_id=1, source_target_pairs={{0,8},{1,9},{2,10},{3,11},{4,12},{5,13},{6,14},{7,15},{8,0},{9,1},... | collective-permute-start | bytes 1179656 | tf_op jit(solution)/shard_map/ppermute | solution.py:368
  65.0 0.0 collective-permute-start.11
  65.0 0.0 collective-permute-done.7.refs_3_
  65.0 2.9 %collective-permute-start.9 = (bf16[512,256]{1,0:T(8,128)(2,1)S(1)}, bf16[512,256]{1,0:T(8,128)(2,1)S(1)}, u32[]{:S(2)}, u32[]{:S(2)}) collective-permute-start(bf16[512,256]{1,0:T(8,128)(2,1)S(1)} %get-tuple-element.52), channel_id=1, source_target_pairs={{0,6},{1,7},{2,4},{3,5},{4,2},{5,3},{6,0},{7,1},{8,14},{9,15},{10,... | collective-permute-start | bytes 786440 | tf_op jit(solution)/shard_map/ppermute | solution.py:368
  67.9 1.7 %place_early.1 = (bf16[8192,256]{1,0:T(8,128)(2,1)}, s32[3]{0:T(128)S(1)}) custom-call(bf16[264,256]{1,0:T(8,128)(2,1)S(1)} %collective-permute-done.1.refs_0_, bf16[520,256]{1,0:T(8,128)(2,1)S(1)} %collective-permute-done.2.refs_1_, bf16[520,256]{1,0:T(8,128)(2,1)S(1)} %collective-permute-done.4.refs_2_), custom_call_target="tpu_custom_call" | custom-call | tf_op jit(solution)/shard_map/place_early/pallas_call | solution.py:501
  69.6 21.9 %collective-permute-done.11.refs_6_ = bf16[512,256]{1,0:T(8,128)(2,1)S(1)} collective-permute-done((bf16[512,256]{1,0:T(8,128)(2,1)S(1)}, bf16[512,256]{1,0:T(8,128)(2,1)S(1)}, u32[]{:S(2)}, u32[]{:S(2)}) %collective-permute-start.11) | collective-permute-done | bytes 262176 | tf_op jit(solution)/shard_map/ppermute | solution.py:368
  91.6 0.0 collective-permute-done.8.refs_4_
  91.6 2.8 %collective-permute-done.9.refs_5_ = bf16[512,256]{1,0:T(8,128)(2,1)S(1)} collective-permute-done((bf16[512,256]{1,0:T(8,128)(2,1)S(1)}, bf16[512,256]{1,0:T(8,128)(2,1)S(1)}, u32[]{:S(2)}, u32[]{:S(2)}) %collective-permute-start.9) | collective-permute-done | bytes 262176 | tf_op jit(solution)/shard_map/ppermute | solution.py:368
  94.4 2.0 %place_mid.1.refs_0_ = bf16[8192,256]{1,0:T(8,128)(2,1)} custom-call(bf16[8192,256]{1,0:T(8,128)(2,1)} %get-tuple-element.42.refs_0_, s32[3]{0:T(128)S(1)} %get-tuple-element.43.refs_1_, bf16[1024,256]{1,0:T(8,128)(2,1)S(1)} %get-tuple-element.46.refs_2_, bf16[1024,256]{1,0:T(8,128)(2,1)S(1)} %collective-permute-done.7.refs_3_, ...), custom_call_target="tpu_custom_call", output_to_operand_aliasing={{}: (0, {})} | custom-call | tf_op jit(solution)/shard_map/place_mid/pallas_call | solution.py:526
  96.3 0.0 collective-permute-done.14.refs_3_
  96.3 3.4 %collective-permute-done.13.refs_2_ = bf16[768,256]{1,0:T(8,128)(2,1)S(1)} collective-permute-done((bf16[768,256]{1,0:T(8,128)(2,1)S(1)}, bf16[768,256]{1,0:T(8,128)(2,1)S(1)}, u32[]{:S(2)}, u32[]{:S(2)}) %collective-permute-start.13) | collective-permute-done | bytes 393248 | tf_op jit(solution)/shard_map/ppermute | solution.py:368
  99.7 1.5 %place_last.1 = bf16[8192,256]{1,0:T(8,128)(2,1)} custom-call(bf16[8192,256]{1,0:T(8,128)(2,1)} %place_mid.1.refs_0_, s32[3]{0:T(128)S(1)} %get-tuple-element.43.refs_1_, bf16[768,256]{1,0:T(8,128)(2,1)S(1)} %collective-permute-done.13.refs_2_, bf16[1024,256]{1,0:T(8,128)(2,1)S(1)} %collective-permute-done.14.refs_3_), custom_call_target="tpu_custom_call", output_to_operand_aliasing={{}: (0, {})} | custom-call | tf_op jit(solution)/shard_map/place_last/pallas_call | solution.py:526
  (1 shorter events, 0.0 us)
Async XLA Ops:
  0.7 4.5 %collective-permute-start = (s32[4]{0:T(128)S(1)}, s32[4]{0:T(128)S(1)}, u32[]{:S(2)}, u32[]{:S(2)}) collective-permute-start(s32[4]{0:T(128)S(1)} %bitcast_add_fusion.refs_0_.heads), channel_id=1, source_target_pairs={{0,16},{16,0},{1,17},{17,1},{2,18},{18,2},{3,19},{19,3},{4,20},{20... | collective-permute-start | bytes 56 | tf_op jit(solution)/shard_map/ppermute | solution.py:372
  4.9 10.5 %copy-start = (s32[1,4,8]{2,1,0:T(4,128)S(1)}, s32[1,4,8]{2,1,0:T(4,128)}, u32[]{:S(2)}) copy-start(s32[1,4,8]{2,1,0:T(4,128)} %param.10) | copy-start | bytes 388
  4.9 10.5 %copy-start.1 = (s32[1,4,8]{2,1,0:T(4,128)S(1)}, s32[1,4,8]{2,1,0:T(4,128)}, u32[]{:S(2)}) copy-start(s32[1,4,8]{2,1,0:T(4,128)} %param.11) | copy-start | bytes 388
  6.3 19.2 %collective-permute-start.1 = (bf16[264,256]{1,0:T(8,128)(2,1)S(1)}, bf16[264,256]{1,0:T(8,128)(2,1)S(1)}, u32[]{:S(2)}, u32[]{:S(2)}) collective-permute-start(bf16[264,256]{1,0:T(8,128)(2,1)S(1)} %get-tuple-element.36), channel_id=1, source_target_pairs={{0,8},{1,9},{2,10},{3,11},{4,12},{5,13},{6,14},{7,15},{8,0},{9,1},... | collective-permute-start | bytes 405512 | tf_op jit(solution)/shard_map/ppermute | solution.py:368
  9.5 25.4 %collective-permute-start.2 = (bf16[520,256]{1,0:T(8,128)(2,1)S(1)}, bf16[520,256]{1,0:T(8,128)(2,1)S(1)}, u32[]{:S(2)}, u32[]{:S(2)}) collective-permute-start(bf16[520,256]{1,0:T(8,128)(2,1)S(1)} %get-tuple-element.37), channel_id=1, source_target_pairs={{0,10},{1,11},{2,8},{3,9},{4,14},{5,15},{6,12},{7,13},{8,2},{9,3},... | collective-permute-start | bytes 798728 | tf_op jit(solution)/shard_map/ppermute | solution.py:368
  13.3 15.7 %collective-permute-start.5 = (bf16[128,1024]{1,0:T(8,128)(2,1)S(1)}, bf16[128,1024]{1,0:T(8,128)(2,1)S(1)}, u32[]{:S(2)}, u32[]{:S(2)}) collective-permute-start(bf16[128,1024]{1,0:T(8,128)(2,1)S(1)} %get-tuple-element.44), channel_id=1, source_target_pairs={{0,16},{16,0},{1,17},{17,1},{2,18},{18,2},{3,19},{19,3},{4,20},{20... | collective-permute-start | bytes 786440 | tf_op jit(solution)/shard_map/ppermute | solution.py:372
  14.9 14.2 %collective-permute-start.6 = (bf16[128,1024]{1,0:T(8,128)(2,1)S(1)}, bf16[128,1024]{1,0:T(8,128)(2,1)S(1)}, u32[]{:S(2)}, u32[]{:S(2)}) collective-permute-start(bf16[128,1024]{1,0:T(8,128)(2,1)S(1)} %get-tuple-element.45), channel_id=1, source_target_pairs={{0,16},{16,0},{1,17},{17,1},{2,18},{18,2},{3,19},{19,3},{4,20},{20... | collective-permute-start | bytes 786440 | tf_op jit(solution)/shard_map/ppermute | solution.py:372
  15.4 10.1 %collective-permute-start.3 = (s32[4,8]{1,0:T(4,128)S(1)}, s32[4,8]{1,0:T(4,128)S(1)}, u32[]{:S(2)}, u32[]{:S(2)}) collective-permute-start(s32[4,8]{1,0:T(4,128)S(1)} %add_bitcast_fusion.refs_2_), channel_id=1, source_target_pairs={{0,16},{16,0},{1,17},{17,1},{2,18},{18,2},{3,19},{19,3},{4,20},{20... | collective-permute-start | bytes 392 | tf_op jit(solution)/shard_map/ppermute | solution.py:372
  25.5 10.8 %collective-permute-start.4 = (bf16[520,256]{1,0:T(8,128)(2,1)S(1)}, bf16[520,256]{1,0:T(8,128)(2,1)S(1)}, u32[]{:S(2)}, u32[]{:S(2)}) collective-permute-start(bf16[520,256]{1,0:T(8,128)(2,1)S(1)} %get-tuple-element.41), channel_id=1, source_target_pairs={{0,14},{1,15},{2,12},{3,13},{4,10},{5,11},{6,8},{7,9},{8,6},{9,7},... | collective-permute-start | bytes 798728 | tf_op jit(solution)/shard_map/ppermute | solution.py:368
  34.8 30.2 %collective-permute-start.7 = (bf16[1024,256]{1,0:T(8,128)(2,1)S(1)}, bf16[1024,256]{1,0:T(8,128)(2,1)S(1)}, u32[]{:S(2)}, u32[]{:S(2)}) collective-permute-start(bf16[1024,256]{1,0:T(8,128)(2,1)S(1)} %get-tuple-element.48), channel_id=1, source_target_pairs={{0,2},{1,3},{2,0},{3,1},{4,6},{5,7},{6,4},{7,5},{8,10},{9,11},{10,... | collective-permute-start | bytes 1572872 | tf_op jit(solution)/shard_map/ppermute | solution.py:368
  36.3 20.4 %collective-permute-start.12 = (bf16[512,256]{1,0:T(8,128)(2,1)S(1)}, bf16[512,256]{1,0:T(8,128)(2,1)S(1)}, u32[]{:S(2)}, u32[]{:S(2)}) collective-permute-start(bf16[512,256]{1,0:T(8,128)(2,1)S(1)} %get-tuple-element.58), channel_id=1, source_target_pairs={{0,10},{1,11},{2,8},{3,9},{4,14},{5,15},{6,12},{7,13},{8,2},{9,3},... | collective-permute-start | bytes 786440 | tf_op jit(solution)/shard_map/ppermute | solution.py:368
  36.3 23.8 %collective-permute-start.10 = (bf16[512,256]{1,0:T(8,128)(2,1)S(1)}, bf16[512,256]{1,0:T(8,128)(2,1)S(1)}, u32[]{:S(2)}, u32[]{:S(2)}) collective-permute-start(bf16[512,256]{1,0:T(8,128)(2,1)S(1)} %get-tuple-element.55), channel_id=1, source_target_pairs={{0,14},{1,15},{2,12},{3,13},{4,10},{5,11},{6,8},{7,9},{8,6},{9,7},... | collective-permute-start | bytes 786440 | tf_op jit(solution)/shard_map/ppermute | solution.py:368
  39.2 52.4 %collective-permute-start.8 = (bf16[1024,256]{1,0:T(8,128)(2,1)S(1)}, bf16[1024,256]{1,0:T(8,128)(2,1)S(1)}, u32[]{:S(2)}, u32[]{:S(2)}) collective-permute-start(bf16[1024,256]{1,0:T(8,128)(2,1)S(1)} %get-tuple-element.50), channel_id=1, source_target_pairs={{0,4},{1,5},{2,6},{3,7},{4,0},{5,1},{6,2},{7,3},{8,12},{9,13},{10,... | collective-permute-start | bytes 1572872 | tf_op jit(solution)/shard_map/ppermute | solution.py:368
  56.7 39.6 %collective-permute-start.14 = (bf16[1024,256]{1,0:T(8,128)(2,1)S(1)}, bf16[1024,256]{1,0:T(8,128)(2,1)S(1)}, u32[]{:S(2)}, u32[]{:S(2)}) collective-permute-start(bf16[1024,256]{1,0:T(8,128)(2,1)S(1)} %get-tuple-element.62), channel_id=1, source_target_pairs={{0,12},{1,13},{2,14},{3,15},{4,8},{5,9},{6,10},{7,11},{8,4},{9,5},... | collective-permute-start | bytes 1572872 | tf_op jit(solution)/shard_map/ppermute | solution.py:368
  60.2 39.5 %collective-permute-start.13 = (bf16[768,256]{1,0:T(8,128)(2,1)S(1)}, bf16[768,256]{1,0:T(8,128)(2,1)S(1)}, u32[]{:S(2)}, u32[]{:S(2)}) collective-permute-start(bf16[768,256]{1,0:T(8,128)(2,1)S(1)} %get-tuple-element.60), channel_id=1, source_target_pairs={{0,8},{1,9},{2,10},{3,11},{4,12},{5,13},{6,14},{7,15},{8,0},{9,1},... | collective-permute-start | bytes 1179656 | tf_op jit(solution)/shard_map/ppermute | solution.py:368
  65.0 26.6 %collective-permute-start.11 = (bf16[512,256]{1,0:T(8,128)(2,1)S(1)}, bf16[512,256]{1,0:T(8,128)(2,1)S(1)}, u32[]{:S(2)}, u32[]{:S(2)}) collective-permute-start(bf16[512,256]{1,0:T(8,128)(2,1)S(1)} %get-tuple-element.56), channel_id=1, source_target_pairs={{0,6},{1,7},{2,4},{3,5},{4,2},{5,3},{6,0},{7,1},{8,14},{9,15},{10,... | collective-permute-start | bytes 786440 | tf_op jit(solution)/shard_map/ppermute | solution.py:368
  65.0 29.4 %collective-permute-start.9 = (bf16[512,256]{1,0:T(8,128)(2,1)S(1)}, bf16[512,256]{1,0:T(8,128)(2,1)S(1)}, u32[]{:S(2)}, u32[]{:S(2)}) collective-permute-start(bf16[512,256]{1,0:T(8,128)(2,1)S(1)} %get-tuple-element.52), channel_id=1, source_target_pairs={{0,6},{1,7},{2,4},{3,5},{4,2},{5,3},{6,0},{7,1},{8,14},{9,15},{10,... | collective-permute-start | bytes 786440 | tf_op jit(solution)/shard_map/ppermute | solution.py:368

commit v7 on v6

--- a/solution.py
+++ b/solution.py
@@ -51,12 +51,9 @@
     return pl.ds(pl.multiple_of(start * size, size), size)
 
 
-def parent_of(plan, heads, q):
-    return heads[q] // plan.rows
-
-
-def row_of(plan, heads, q):
-    return heads[q] % plan.rows
+def own_row(plan, heads, q, front):
+    row = heads[q] - front * plan.rows
+    return jnp.logical_and(row >= 0, row < plan.rows), row
 
 
 def touched_rows(plan, head_refs):
@@ -64,18 +61,20 @@
     touched = jnp.int32(0)
     for heads in head_refs:
         for q in range(plan.slots):
-            bit = jnp.left_shift(jnp.int32(1), row_of(plan, heads, q))
-            touched = touched | jnp.where(parent_of(plan, heads, q) == me, bit, 0)
+            named, row = own_row(plan, heads, q, me)
+            bit = jnp.left_shift(jnp.int32(1), jnp.where(named, row, 0))
+            touched = touched | jnp.where(named, bit, 0)
     return touched
 
 
-def first_rows(plan, touched, limit):
-    chosen, count = jnp.int32(0), jnp.int32(0)
+def first_rows(plan, touched, limits, order=None):
+    chosen, count = [jnp.int32(0) for _ in limits], jnp.int32(0)
     for t in range(plan.rows):
-        free = (jnp.right_shift(touched, t) & 1) == 0
-        take = jnp.logical_and(free, count < limit)
-        chosen = chosen | jnp.where(take, 1 << t, 0)
-        count = count + jnp.where(take, 1, 0)
+        free = 1 - (jnp.right_shift(touched, t) & 1)
+        chosen = [c | jnp.where(count < n, free << t, 0) for c, n in zip(chosen, limits)]
+        if order is not None:
+            order[count] = t
+        count = count + free
     return chosen
 
 
@@ -120,8 +119,8 @@
     )
 
 
-def put_tag(plan, touched, o, out):
-    chosen = first_rows(plan, touched, plan.early[o]).astype(jnp.float32)
+def put_tag(plan, chosen, o, out):
+    chosen = chosen.astype(jnp.float32)
     tag = jnp.full((TAG, plan.width), chosen, jnp.float32).astype(jnp.bfloat16)
     out[plan.early[o] * plan.block :, :] = tag
 
@@ -133,11 +132,11 @@
     block = plan.block
     touched = touched_rows(plan, head_refs)
     touched_out[0] = touched
-    list_rows(plan, first_rows(plan, touched, plan.first), 1, order)
+    chosen = first_rows(plan, touched, [plan.early[o] for o in lead], order)
     for i, o in enumerate(lead):
         for k in range(plan.early[o]):
             outs[i][pl.ds(k * block, block), :] = staged[i][at(order[k], block), :]
-        put_tag(plan, touched, o, outs[i])
+        put_tag(plan, chosen[i], o, outs[i])
 
 
 def bucket_kernel(plan, tail, heads, *refs):
@@ -155,7 +154,7 @@
             target = lax.rem(me + k, plan.groups)
             rank = jnp.int32(0)
             for q in range(plan.slots):
-                named = parent_of(plan, heads, q) == target
+                named, _ = own_row(plan, heads, q, target)
                 for c in range(plan.capacity):
 
                     @pl.when(jnp.logical_and(named, rank == c))
@@ -174,7 +173,7 @@
     copies = []
     if tail:
         touched = touched_ref[0]
-        list_rows(plan, first_rows(plan, touched, plan.first), 1, order)
+        chosen = first_rows(plan, touched, [plan.early[o] for o in tail], order)
         for i, o in enumerate(tail):
             target = jnp.bitwise_xor(column, o)
             for k in range(plan.early[o]):
@@ -187,7 +186,7 @@
                         )
                     )
                     copies[-1].start()
-            put_tag(plan, touched, o, packed[i])
+            put_tag(plan, chosen[i], o, packed[i])
     for copy in copies:
         copy.wait()
     buckets(lambda c: c.wait())
@@ -226,10 +225,9 @@
         copy.start()
 
     touched = touched_rows(plan, head_refs)
-    for o in plan.early:
-        for t, (bit, place) in enumerate(
-            positions(plan, first_rows(plan, touched, plan.early[o]))
-        ):
+    limits = list(plan.early.values())
+    for o, chosen in zip(plan.early, first_rows(plan, touched, limits)):
+        for t, (bit, place) in enumerate(positions(plan, chosen)):
             place_ref[o, t] = jnp.where(bit == 1, -1, place)
 
     for t in range(plan.rows):
@@ -246,9 +244,8 @@
     for s, (heads, codes) in enumerate(zip(head_refs, code_refs)):
 
         def add_slot(q, rank):
-            named = parent_of(plan, heads, q) == me
+            named, t = own_row(plan, heads, q, me)
             index = q if s == 0 else plan.slots + (s - 1) * plan.capacity + rank
-            t = row_of(plan, heads, q)
 
             @pl.when(named)
             def _():

time: 101 us -> 101 us (level)
  no operation moved by 1% of the time
where the time goes in v7:
time: 101 us
  starting transfers between devices  45.9 us (45%)
  waiting for transfers between devices  38.8 us (38%)
  Pallas kernels  15.6 us (15%)
    ppermute x11, starting transfers between devices, across(): return lax.ppermute(value, 'wide', pairs)  39.3 us
    ppermute x11, waiting for transfers between devices, across(): return lax.ppermute(value, 'wide', pairs)  30 us
    ppermute x4, waiting for transfers between devices, along(): lax.ppermute(value, 'front', [(f, (f + steps) % plan.groups) for f in ran...  8.78 us
    ppermute x4, starting transfers between devices, along(): lax.ppermute(value, 'front', [(f, (f + steps) % plan.groups) for f in ran...  6.64 us
    pallas_call x1, Pallas kernels, local(): pl.pallas_call(functools.partial(assemble_kernel, plan), out_shape=[jax.S...  5.67 us
    pallas_call x2, Pallas kernels, place(): pl.pallas_call(body, out_shape=out_shape, in_specs=[HBM] * len(held) + [A...  3.41 us
    pallas_call x1, Pallas kernels, local(): pl.pallas_call(functools.partial(bucket_kernel, plan, tail), out_shape=[j...  2.5 us
  transfers between devices with their start and end apart: 15, of which 6 were waited for; matrix products, arithmetic and copies ran while one was open for 0% of the time, Pallas kernels for 13%

profile of v7, /device:TPU:0, one launch (start us, length us, event | category | flops | bytes accessed | tf_op | source)
XLA Modules:
  0.0 101.2 jit_solution(10556127532316078219)
XLA Ops:
  0.0 0.7 bitcast_add_fusion.refs_0_.heads
  0.7 3.0 %collective-permute-start = (s32[4]{0:T(128)S(1)}, s32[4]{0:T(128)S(1)}, u32[]{:S(2)}, u32[]{:S(2)}) collective-permute-start(s32[4]{0:T(128)S(1)} %bitcast_add_fusion.refs_0_.heads), channel_id=1, source_target_pairs={{0,16},{16,0},{1,17},{17,1},{2,18},{18,2},{3,19},{19,3},{4,20},{20... | collective-permute-start | bytes 56 | tf_op jit(solution)/shard_map/ppermute | solution.py:369
  3.6 1.2 %stage.1 = (bf16[1024,256]{1,0:T(8,128)(2,1)S(1)}, bf16[1024,256]{1,0:T(8,128)(2,1)S(1)}) custom-call(bf16[1,1024,2048]{2,1,0:T(8,128)(2,1)} %refs_4_.1), custom_call_target="tpu_custom_call" | custom-call | tf_op jit(solution)/shard_map/stage/pallas_call | solution.py:393
  4.9 0.0 copy-start
  4.9 0.0 copy-start.1
  4.9 0.2 collective-permute-done.refs_1_
  5.2 1.1 %pack_early.1 = (bf16[264,256]{1,0:T(8,128)(2,1)S(1)}, bf16[520,256]{1,0:T(8,128)(2,1)S(1)}, s32[1]{0:T(128)}) custom-call(s32[4]{0:T(128)S(1)} %bitcast_add_fusion.refs_0_.heads, s32[4]{0:T(128)S(1)} %collective-permute-done.refs_1_, bf16[1024,256]{1,0:T(8,128)(2,1)S(1)} %get-tuple-element.34.refs_2_, bf16[1024,256]{1,0:T(8,128)(2,1)S(1)} %get-tuple-element.35.refs_3_), custom_call_target="tpu_custom_call" | custom-call | tf_op jit(solution)/shard_map/pack_early/pallas_call | solution.py:403
  6.3 3.2 %collective-permute-start.1 = (bf16[264,256]{1,0:T(8,128)(2,1)S(1)}, bf16[264,256]{1,0:T(8,128)(2,1)S(1)}, u32[]{:S(2)}, u32[]{:S(2)}) collective-permute-start(bf16[264,256]{1,0:T(8,128)(2,1)S(1)} %get-tuple-element.36), channel_id=1, source_target_pairs={{0,8},{1,9},{2,10},{3,11},{4,12},{5,13},{6,14},{7,15},{8,0},{9,1},... | collective-permute-start | bytes 405512 | tf_op jit(solution)/shard_map/ppermute | solution.py:365
  9.4 1.3 %collective-permute-start.2 = (bf16[520,256]{1,0:T(8,128)(2,1)S(1)}, bf16[520,256]{1,0:T(8,128)(2,1)S(1)}, u32[]{:S(2)}, u32[]{:S(2)}) collective-permute-start(bf16[520,256]{1,0:T(8,128)(2,1)S(1)} %get-tuple-element.37), channel_id=1, source_target_pairs={{0,10},{1,11},{2,8},{3,9},{4,14},{5,15},{6,12},{7,13},{8,2},{9,3},... | collective-permute-start | bytes 798728 | tf_op jit(solution)/shard_map/ppermute | solution.py:365
  10.7 2.5 %bucket.1 = (bf16[128,1024]{1,0:T(8,128)(2,1)S(1)}, bf16[128,1024]{1,0:T(8,128)(2,1)S(1)}, bf16[520,256]{1,0:T(8,128)(2,1)S(1)}) custom-call(s32[4]{0:T(128)S(1)} %bitcast_add_fusion.refs_0_.heads, s32[1]{0:T(128)} %get-tuple-element.38.refs_0_, bf16[1,512,1024]{2,1,0:T(8,128)(2,1)} %refs_5_.1, bf16[1,1024,2048]{2,1,0:T(8,128)(2,1)} %refs_4_.1), custom_call_target="tpu_custom_call" | custom-call | tf_op jit(solution)/shard_map/bucket/pallas_call | solution.py:417
  13.2 1.6 %collective-permute-start.5 = (bf16[128,1024]{1,0:T(8,128)(2,1)S(1)}, bf16[128,1024]{1,0:T(8,128)(2,1)S(1)}, u32[]{:S(2)}, u32[]{:S(2)}) collective-permute-start(bf16[128,1024]{1,0:T(8,128)(2,1)S(1)} %get-tuple-element.44), channel_id=1, source_target_pairs={{0,16},{16,0},{1,17},{17,1},{2,18},{18,2},{3,19},{19,3},{4,20},{20... | collective-permute-start | bytes 786440 | tf_op jit(solution)/shard_map/ppermute | solution.py:369
  14.8 0.5 collective-permute-start.6
  15.3 0.0 copy-done
  15.3 0.0 copy-done.1
  15.3 1.6 %collective-permute-start.3 = (s32[4,8]{1,0:T(4,128)S(1)}, s32[4,8]{1,0:T(4,128)S(1)}, u32[]{:S(2)}, u32[]{:S(2)}) collective-permute-start(s32[4,8]{1,0:T(4,128)S(1)} %add_bitcast_fusion.refs_2_), channel_id=1, source_target_pairs={{0,16},{16,0},{1,17},{17,1},{2,18},{18,2},{3,19},{19,3},{4,20},{20... | collective-permute-start | bytes 392 | tf_op jit(solution)/shard_map/ppermute | solution.py:369
  16.9 8.5 %collective-permute-done.3.refs_3_ = s32[4,8]{1,0:T(4,128)S(1)} collective-permute-done((s32[4,8]{1,0:T(4,128)S(1)}, s32[4,8]{1,0:T(4,128)S(1)}, u32[]{:S(2)}, u32[]{:S(2)}) %collective-permute-start.3) | collective-permute-done | bytes 160 | tf_op jit(solution)/shard_map/ppermute | solution.py:369
  25.4 0.0 collective-permute-done.1.refs_0_
  25.4 3.5 %collective-permute-start.4 = (bf16[520,256]{1,0:T(8,128)(2,1)S(1)}, bf16[520,256]{1,0:T(8,128)(2,1)S(1)}, u32[]{:S(2)}, u32[]{:S(2)}) collective-permute-start(bf16[520,256]{1,0:T(8,128)(2,1)S(1)} %get-tuple-element.41), channel_id=1, source_target_pairs={{0,14},{1,15},{2,12},{3,13},{4,10},{5,11},{6,8},{7,9},{8,6},{9,7},... | collective-permute-start | bytes 798728 | tf_op jit(solution)/shard_map/ppermute | solution.py:365
  29.0 0.0 collective-permute-done.5.refs_6_
  29.0 0.0 collective-permute-done.6.refs_7_
  29.0 5.7 %assemble.1 = (bf16[1024,256]{1,0:T(8,128)(2,1)S(1)}, bf16[1024,256]{1,0:T(8,128)(2,1)S(1)}, bf16[1024,256]{1,0:T(8,128)(2,1)S(1)}, bf16[512,256]{1,0:T(8,128)(2...) custom-call(s32[4]{0:T(128)S(1)} %bitcast_add_fusion.refs_0_.heads, ...), custom_call_target="tpu_custom_call" | custom-call | tf_op jit(solution)/shard_map/assemble/pallas_call | solution.py:443
  34.6 0.0 collective-permute-done.2.refs_1_
  34.7 1.6 %collective-permute-start.7 = (bf16[1024,256]{1,0:T(8,128)(2,1)S(1)}, bf16[1024,256]{1,0:T(8,128)(2,1)S(1)}, u32[]{:S(2)}, u32[]{:S(2)}) collective-permute-start(bf16[1024,256]{1,0:T(8,128)(2,1)S(1)} %get-tuple-element.48), channel_id=1, source_target_pairs={{0,2},{1,3},{2,0},{3,1},{4,6},{5,7},{6,4},{7,5},{8,10},{9,11},{10,... | collective-permute-start | bytes 1572872 | tf_op jit(solution)/shard_map/ppermute | solution.py:365
  36.3 0.0 collective-permute-start.12
  36.3 0.0 collective-permute-done.4.refs_2_
  36.3 2.7 %collective-permute-start.10 = (bf16[512,256]{1,0:T(8,128)(2,1)S(1)}, bf16[512,256]{1,0:T(8,128)(2,1)S(1)}, u32[]{:S(2)}, u32[]{:S(2)}) collective-permute-start(bf16[512,256]{1,0:T(8,128)(2,1)S(1)} %get-tuple-element.55), channel_id=1, source_target_pairs={{0,14},{1,15},{2,12},{3,13},{4,10},{5,11},{6,8},{7,9},{8,6},{9,7},... | collective-permute-start | bytes 786440 | tf_op jit(solution)/shard_map/ppermute | solution.py:365
  39.0 15.2 %collective-permute-start.8 = (bf16[1024,256]{1,0:T(8,128)(2,1)S(1)}, bf16[1024,256]{1,0:T(8,128)(2,1)S(1)}, u32[]{:S(2)}, u32[]{:S(2)}) collective-permute-start(bf16[1024,256]{1,0:T(8,128)(2,1)S(1)} %get-tuple-element.50), channel_id=1, source_target_pairs={{0,4},{1,5},{2,6},{3,7},{4,0},{5,1},{6,2},{7,3},{8,12},{9,13},{10,... | collective-permute-start | bytes 1572872 | tf_op jit(solution)/shard_map/ppermute | solution.py:365
  54.2 2.4 %collective-permute-done.12.refs_7_ = bf16[512,256]{1,0:T(8,128)(2,1)S(1)} collective-permute-done((bf16[512,256]{1,0:T(8,128)(2,1)S(1)}, bf16[512,256]{1,0:T(8,128)(2,1)S(1)}, u32[]{:S(2)}, u32[]{:S(2)}) %collective-permute-start.12) | collective-permute-done | bytes 262176 | tf_op jit(solution)/shard_map/ppermute | solution.py:365
  56.7 3.6 %collective-permute-start.14 = (bf16[1024,256]{1,0:T(8,128)(2,1)S(1)}, bf16[1024,256]{1,0:T(8,128)(2,1)S(1)}, u32[]{:S(2)}, u32[]{:S(2)}) collective-permute-start(bf16[1024,256]{1,0:T(8,128)(2,1)S(1)} %get-tuple-element.62), channel_id=1, source_target_pairs={{0,12},{1,13},{2,14},{3,15},{4,8},{5,9},{6,10},{7,11},{8,4},{9,5},... | collective-permute-start | bytes 1572872 | tf_op jit(solution)/shard_map/ppermute | solution.py:365
  60.3 0.0 collective-permute-done.10.refs_8_
  60.3 5.2 %collective-permute-start.13 = (bf16[768,256]{1,0:T(8,128)(2,1)S(1)}, bf16[768,256]{1,0:T(8,128)(2,1)S(1)}, u32[]{:S(2)}, u32[]{:S(2)}) collective-permute-start(bf16[768,256]{1,0:T(8,128)(2,1)S(1)} %get-tuple-element.60), channel_id=1, source_target_pairs={{0,8},{1,9},{2,10},{3,11},{4,12},{5,13},{6,14},{7,15},{8,0},{9,1},... | collective-permute-start | bytes 1179656 | tf_op jit(solution)/shard_map/ppermute | solution.py:365
  65.5 0.0 collective-permute-start.11
  65.5 0.0 collective-permute-done.7.refs_3_
  65.5 2.9 %collective-permute-start.9 = (bf16[512,256]{1,0:T(8,128)(2,1)S(1)}, bf16[512,256]{1,0:T(8,128)(2,1)S(1)}, u32[]{:S(2)}, u32[]{:S(2)}) collective-permute-start(bf16[512,256]{1,0:T(8,128)(2,1)S(1)} %get-tuple-element.52), channel_id=1, source_target_pairs={{0,6},{1,7},{2,4},{3,5},{4,2},{5,3},{6,0},{7,1},{8,14},{9,15},{10,... | collective-permute-start | bytes 786440 | tf_op jit(solution)/shard_map/ppermute | solution.py:365
  68.4 1.7 %place_early.1 = (bf16[8192,256]{1,0:T(8,128)(2,1)}, s32[3]{0:T(128)S(1)}) custom-call(bf16[264,256]{1,0:T(8,128)(2,1)S(1)} %collective-permute-done.1.refs_0_, bf16[520,256]{1,0:T(8,128)(2,1)S(1)} %collective-permute-done.2.refs_1_, bf16[520,256]{1,0:T(8,128)(2,1)S(1)} %collective-permute-done.4.refs_2_), custom_call_target="tpu_custom_call" | custom-call | tf_op jit(solution)/shard_map/place_early/pallas_call | solution.py:498
  70.1 21.4 %collective-permute-done.11.refs_6_ = bf16[512,256]{1,0:T(8,128)(2,1)S(1)} collective-permute-done((bf16[512,256]{1,0:T(8,128)(2,1)S(1)}, bf16[512,256]{1,0:T(8,128)(2,1)S(1)}, u32[]{:S(2)}, u32[]{:S(2)}) %collective-permute-start.11) | collective-permute-done | bytes 262176 | tf_op jit(solution)/shard_map/ppermute | solution.py:365
  91.5 0.0 collective-permute-done.8.refs_4_
  91.5 2.8 %collective-permute-done.9.refs_5_ = bf16[512,256]{1,0:T(8,128)(2,1)S(1)} collective-permute-done((bf16[512,256]{1,0:T(8,128)(2,1)S(1)}, bf16[512,256]{1,0:T(8,128)(2,1)S(1)}, u32[]{:S(2)}, u32[]{:S(2)}) %collective-permute-start.9) | collective-permute-done | bytes 262176 | tf_op jit(solution)/shard_map/ppermute | solution.py:365
  94.3 2.0 %place_mid.1.refs_0_ = bf16[8192,256]{1,0:T(8,128)(2,1)} custom-call(bf16[8192,256]{1,0:T(8,128)(2,1)} %get-tuple-element.42.refs_0_, s32[3]{0:T(128)S(1)} %get-tuple-element.43.refs_1_, bf16[1024,256]{1,0:T(8,128)(2,1)S(1)} %get-tuple-element.46.refs_2_, bf16[1024,256]{1,0:T(8,128)(2,1)S(1)} %collective-permute-done.7.refs_3_, ...), custom_call_target="tpu_custom_call", output_to_operand_aliasing={{}: (0, {})} | custom-call | tf_op jit(solution)/shard_map/place_mid/pallas_call | solution.py:523
  96.3 0.0 collective-permute-done.14.refs_3_
  96.3 3.4 %collective-permute-done.13.refs_2_ = bf16[768,256]{1,0:T(8,128)(2,1)S(1)} collective-permute-done((bf16[768,256]{1,0:T(8,128)(2,1)S(1)}, bf16[768,256]{1,0:T(8,128)(2,1)S(1)}, u32[]{:S(2)}, u32[]{:S(2)}) %collective-permute-start.13) | collective-permute-done | bytes 393248 | tf_op jit(solution)/shard_map/ppermute | solution.py:365
  99.7 1.5 %place_last.1 = bf16[8192,256]{1,0:T(8,128)(2,1)} custom-call(bf16[8192,256]{1,0:T(8,128)(2,1)} %place_mid.1.refs_0_, s32[3]{0:T(128)S(1)} %get-tuple-element.43.refs_1_, bf16[768,256]{1,0:T(8,128)(2,1)S(1)} %collective-permute-done.13.refs_2_, bf16[1024,256]{1,0:T(8,128)(2,1)S(1)} %collective-permute-done.14.refs_3_), custom_call_target="tpu_custom_call", output_to_operand_aliasing={{}: (0, {})} | custom-call | tf_op jit(solution)/shard_map/place_last/pallas_call | solution.py:523
  (1 shorter events, 0.0 us)
Async XLA Ops:
  0.7 4.5 %collective-permute-start = (s32[4]{0:T(128)S(1)}, s32[4]{0:T(128)S(1)}, u32[]{:S(2)}, u32[]{:S(2)}) collective-permute-start(s32[4]{0:T(128)S(1)} %bitcast_add_fusion.refs_0_.heads), channel_id=1, source_target_pairs={{0,16},{16,0},{1,17},{17,1},{2,18},{18,2},{3,19},{19,3},{4,20},{20... | collective-permute-start | bytes 56 | tf_op jit(solution)/shard_map/ppermute | solution.py:369
  4.9 10.4 %copy-start = (s32[1,4,8]{2,1,0:T(4,128)S(1)}, s32[1,4,8]{2,1,0:T(4,128)}, u32[]{:S(2)}) copy-start(s32[1,4,8]{2,1,0:T(4,128)} %param.10) | copy-start | bytes 388
  4.9 10.4 %copy-start.1 = (s32[1,4,8]{2,1,0:T(4,128)S(1)}, s32[1,4,8]{2,1,0:T(4,128)}, u32[]{:S(2)}) copy-start(s32[1,4,8]{2,1,0:T(4,128)} %param.11) | copy-start | bytes 388
  6.3 19.2 %collective-permute-start.1 = (bf16[264,256]{1,0:T(8,128)(2,1)S(1)}, bf16[264,256]{1,0:T(8,128)(2,1)S(1)}, u32[]{:S(2)}, u32[]{:S(2)}) collective-permute-start(bf16[264,256]{1,0:T(8,128)(2,1)S(1)} %get-tuple-element.36), channel_id=1, source_target_pairs={{0,8},{1,9},{2,10},{3,11},{4,12},{5,13},{6,14},{7,15},{8,0},{9,1},... | collective-permute-start | bytes 405512 | tf_op jit(solution)/shard_map/ppermute | solution.py:365
  9.4 25.2 %collective-permute-start.2 = (bf16[520,256]{1,0:T(8,128)(2,1)S(1)}, bf16[520,256]{1,0:T(8,128)(2,1)S(1)}, u32[]{:S(2)}, u32[]{:S(2)}) collective-permute-start(bf16[520,256]{1,0:T(8,128)(2,1)S(1)} %get-tuple-element.37), channel_id=1, source_target_pairs={{0,10},{1,11},{2,8},{3,9},{4,14},{5,15},{6,12},{7,13},{8,2},{9,3},... | collective-permute-start | bytes 798728 | tf_op jit(solution)/shard_map/ppermute | solution.py:365
  13.2 15.7 %collective-permute-start.5 = (bf16[128,1024]{1,0:T(8,128)(2,1)S(1)}, bf16[128,1024]{1,0:T(8,128)(2,1)S(1)}, u32[]{:S(2)}, u32[]{:S(2)}) collective-permute-start(bf16[128,1024]{1,0:T(8,128)(2,1)S(1)} %get-tuple-element.44), channel_id=1, source_target_pairs={{0,16},{16,0},{1,17},{17,1},{2,18},{18,2},{3,19},{19,3},{4,20},{20... | collective-permute-start | bytes 786440 | tf_op jit(solution)/shard_map/ppermute | solution.py:369
  14.8 14.2 %collective-permute-start.6 = (bf16[128,1024]{1,0:T(8,128)(2,1)S(1)}, bf16[128,1024]{1,0:T(8,128)(2,1)S(1)}, u32[]{:S(2)}, u32[]{:S(2)}) collective-permute-start(bf16[128,1024]{1,0:T(8,128)(2,1)S(1)} %get-tuple-element.45), channel_id=1, source_target_pairs={{0,16},{16,0},{1,17},{17,1},{2,18},{18,2},{3,19},{19,3},{4,20},{20... | collective-permute-start | bytes 786440 | tf_op jit(solution)/shard_map/ppermute | solution.py:369
  15.3 10.1 %collective-permute-start.3 = (s32[4,8]{1,0:T(4,128)S(1)}, s32[4,8]{1,0:T(4,128)S(1)}, u32[]{:S(2)}, u32[]{:S(2)}) collective-permute-start(s32[4,8]{1,0:T(4,128)S(1)} %add_bitcast_fusion.refs_2_), channel_id=1, source_target_pairs={{0,16},{16,0},{1,17},{17,1},{2,18},{18,2},{3,19},{19,3},{4,20},{20... | collective-permute-start | bytes 392 | tf_op jit(solution)/shard_map/ppermute | solution.py:369
  25.4 10.9 %collective-permute-start.4 = (bf16[520,256]{1,0:T(8,128)(2,1)S(1)}, bf16[520,256]{1,0:T(8,128)(2,1)S(1)}, u32[]{:S(2)}, u32[]{:S(2)}) collective-permute-start(bf16[520,256]{1,0:T(8,128)(2,1)S(1)} %get-tuple-element.41), channel_id=1, source_target_pairs={{0,14},{1,15},{2,12},{3,13},{4,10},{5,11},{6,8},{7,9},{8,6},{9,7},... | collective-permute-start | bytes 798728 | tf_op jit(solution)/shard_map/ppermute | solution.py:365
  34.7 30.9 %collective-permute-start.7 = (bf16[1024,256]{1,0:T(8,128)(2,1)S(1)}, bf16[1024,256]{1,0:T(8,128)(2,1)S(1)}, u32[]{:S(2)}, u32[]{:S(2)}) collective-permute-start(bf16[1024,256]{1,0:T(8,128)(2,1)S(1)} %get-tuple-element.48), channel_id=1, source_target_pairs={{0,2},{1,3},{2,0},{3,1},{4,6},{5,7},{6,4},{7,5},{8,10},{9,11},{10,... | collective-permute-start | bytes 1572872 | tf_op jit(solution)/shard_map/ppermute | solution.py:365
  36.3 20.4 %collective-permute-start.12 = (bf16[512,256]{1,0:T(8,128)(2,1)S(1)}, bf16[512,256]{1,0:T(8,128)(2,1)S(1)}, u32[]{:S(2)}, u32[]{:S(2)}) collective-permute-start(bf16[512,256]{1,0:T(8,128)(2,1)S(1)} %get-tuple-element.58), channel_id=1, source_target_pairs={{0,10},{1,11},{2,8},{3,9},{4,14},{5,15},{6,12},{7,13},{8,2},{9,3},... | collective-permute-start | bytes 786440 | tf_op jit(solution)/shard_map/ppermute | solution.py:365
  36.3 24.0 %collective-permute-start.10 = (bf16[512,256]{1,0:T(8,128)(2,1)S(1)}, bf16[512,256]{1,0:T(8,128)(2,1)S(1)}, u32[]{:S(2)}, u32[]{:S(2)}) collective-permute-start(bf16[512,256]{1,0:T(8,128)(2,1)S(1)} %get-tuple-element.55), channel_id=1, source_target_pairs={{0,14},{1,15},{2,12},{3,13},{4,10},{5,11},{6,8},{7,9},{8,6},{9,7},... | collective-permute-start | bytes 786440 | tf_op jit(solution)/shard_map/ppermute | solution.py:365
  39.0 52.5 %collective-permute-start.8 = (bf16[1024,256]{1,0:T(8,128)(2,1)S(1)}, bf16[1024,256]{1,0:T(8,128)(2,1)S(1)}, u32[]{:S(2)}, u32[]{:S(2)}) collective-permute-start(bf16[1024,256]{1,0:T(8,128)(2,1)S(1)} %get-tuple-element.50), channel_id=1, source_target_pairs={{0,4},{1,5},{2,6},{3,7},{4,0},{5,1},{6,2},{7,3},{8,12},{9,13},{10,... | collective-permute-start | bytes 1572872 | tf_op jit(solution)/shard_map/ppermute | solution.py:365
  56.7 39.6 %collective-permute-start.14 = (bf16[1024,256]{1,0:T(8,128)(2,1)S(1)}, bf16[1024,256]{1,0:T(8,128)(2,1)S(1)}, u32[]{:S(2)}, u32[]{:S(2)}) collective-permute-start(bf16[1024,256]{1,0:T(8,128)(2,1)S(1)} %get-tuple-element.62), channel_id=1, source_target_pairs={{0,12},{1,13},{2,14},{3,15},{4,8},{5,9},{6,10},{7,11},{8,4},{9,5},... | collective-permute-start | bytes 1572872 | tf_op jit(solution)/shard_map/ppermute | solution.py:365
  60.3 39.5 %collective-permute-start.13 = (bf16[768,256]{1,0:T(8,128)(2,1)S(1)}, bf16[768,256]{1,0:T(8,128)(2,1)S(1)}, u32[]{:S(2)}, u32[]{:S(2)}) collective-permute-start(bf16[768,256]{1,0:T(8,128)(2,1)S(1)} %get-tuple-element.60), channel_id=1, source_target_pairs={{0,8},{1,9},{2,10},{3,11},{4,12},{5,13},{6,14},{7,15},{8,0},{9,1},... | collective-permute-start | bytes 1179656 | tf_op jit(solution)/shard_map/ppermute | solution.py:365
  65.5 26.0 %collective-permute-start.11 = (bf16[512,256]{1,0:T(8,128)(2,1)S(1)}, bf16[512,256]{1,0:T(8,128)(2,1)S(1)}, u32[]{:S(2)}, u32[]{:S(2)}) collective-permute-start(bf16[512,256]{1,0:T(8,128)(2,1)S(1)} %get-tuple-element.56), channel_id=1, source_target_pairs={{0,6},{1,7},{2,4},{3,5},{4,2},{5,3},{6,0},{7,1},{8,14},{9,15},{10,... | collective-permute-start | bytes 786440 | tf_op jit(solution)/shard_map/ppermute | solution.py:365
  65.5 28.8 %collective-permute-start.9 = (bf16[512,256]{1,0:T(8,128)(2,1)S(1)}, bf16[512,256]{1,0:T(8,128)(2,1)S(1)}, u32[]{:S(2)}, u32[]{:S(2)}) collective-permute-start(bf16[512,256]{1,0:T(8,128)(2,1)S(1)} %get-tuple-element.52), channel_id=1, source_target_pairs={{0,6},{1,7},{2,4},{3,5},{4,2},{5,3},{6,0},{7,1},{8,14},{9,15},{10,... | collective-permute-start | bytes 786440 | tf_op jit(solution)/shard_map/ppermute | solution.py:365

commit v8 on v7

--- a/solution.py
+++ b/solution.py
@@ -35,7 +35,7 @@
         self.late = []
         for o in range(GRID_COLS):
             count = self.rows - self.early.get(o, 0)
-            cuts = [0, count // 2, count] if o == 3 else [0, count]
+            cuts = [0, count // 2, count] if o == 3 else [0, max(1, count - 2), count] if o in (4, 6) else [0, count]
             self.late += [(o, lo, hi) for lo, hi in zip(cuts, cuts[1:]) if lo < hi]
 
 
@@ -128,19 +128,39 @@
 def pack_kernel(plan, lead, *refs):
     groups, count = plan.groups, len(lead)
     head_refs, staged, refs = refs[:groups], refs[groups : groups + count], refs[groups + count :]
-    outs, (touched_out, order) = refs[:count], refs[count:]
+    outs, (order, tags, sems) = refs[:count], refs[count:]
     block = plan.block
     touched = touched_rows(plan, head_refs)
-    touched_out[0] = touched
     chosen = first_rows(plan, touched, [plan.early[o] for o in lead], order)
+    copies = []
     for i, o in enumerate(lead):
         for k in range(plan.early[o]):
-            outs[i][pl.ds(k * block, block), :] = staged[i][at(order[k], block), :]
-        put_tag(plan, chosen[i], o, outs[i])
-
-
-def bucket_kernel(plan, tail, heads, *refs):
-    touched_ref, refs = (refs[0], refs[1:]) if tail else (None, refs)
+            copies.append(
+                pltpu.make_async_copy(
+                    staged[i].at[at(order[k], block)],
+                    outs[i].at[pl.ds(k * block, block)],
+                    sems.at[i, k],
+                )
+            )
+            copies[-1].start()
+    for i, o in enumerate(lead):
+        tag = jnp.full((TAG, plan.width), chosen[i].astype(jnp.float32), jnp.float32)
+        tags[i] = tag.astype(jnp.bfloat16)
+        copies.append(
+            pltpu.make_async_copy(
+                tags.at[i],
+                outs[i].at[pl.ds(plan.early[o] * block, TAG)],
+                sems.at[i, plan.first],
+            )
+        )
+        copies[-1].start()
+    for copy in copies:
+        copy.wait()
+
+
+def bucket_kernel(plan, tail, *refs):
+    head_refs, refs = refs[: plan.groups], refs[plan.groups :]
+    heads = head_refs[0]
     updates, panel, refs = refs[0], refs[1], refs[2:]
     count = (plan.groups - 1) * plan.capacity
     outs, packed, refs = refs[:count], refs[count : count + len(tail)], refs[count + len(tail) :]
@@ -172,7 +192,7 @@
     buckets(lambda c: c.start())
     copies = []
     if tail:
-        touched = touched_ref[0]
+        touched = touched_rows(plan, head_refs)
         chosen = first_rows(plan, touched, [plan.early[o] for o in tail], order)
         for i, o in enumerate(tail):
             target = jnp.bitwise_xor(column, o)
@@ -384,7 +404,7 @@
 
     early = [o for o in plan.early if plan.early[o]]
     lead, tail = early[:2], early[2:]
-    packed, touched = {}, []
+    packed = {}
 
     def early_shape(o):
         return jax.ShapeDtypeStruct((plan.early[o] * block + TAG, width), bf16)
@@ -400,25 +420,28 @@
             cost_estimate=COST,
             name="stage",
         )(panels)
-        *outs, touched_set = pl.pallas_call(
+        outs = pl.pallas_call(
             functools.partial(pack_kernel, plan, lead),
-            out_shape=[early_shape(o) for o in lead] + [jax.ShapeDtypeStruct((1,), jnp.int32)],
-            in_specs=[SMEM] * plan.groups + [VMEM] * len(lead),
-            out_specs=[VMEM] * len(lead) + [SMEM],
-            scratch_shapes=[pltpu.SMEM((plan.rows,), jnp.int32)],
+            out_shape=[early_shape(o) for o in lead],
+            in_specs=[SMEM] * plan.groups + [ANY] * len(lead),
+            out_specs=[ANY] * len(lead),
+            scratch_shapes=[
+                pltpu.SMEM((plan.rows,), jnp.int32),
+                pltpu.VMEM((len(lead), TAG, width), bf16),
+                pltpu.SemaphoreType.DMA((len(lead), plan.first + 1)),
+            ],
             compiler_params=params(),
             cost_estimate=COST,
             name="pack_early",
         )(*all_heads, *staged)
         packed = dict(zip(lead, outs))
-        touched = [touched_set]
 
     count = (plan.groups - 1) * plan.capacity
     outs = pl.pallas_call(
         functools.partial(bucket_kernel, plan, tail),
         out_shape=[jax.ShapeDtypeStruct((block, updates.shape[2]), bf16)] * count
         + [early_shape(o) for o in tail],
-        in_specs=[SMEM] * (1 + len(touched)) + [HBM, HBM],
+        in_specs=[SMEM] * plan.groups + [HBM, HBM],
         out_specs=[VMEM] * (count + len(tail)),
         scratch_shapes=[
             pltpu.SMEM((plan.rows,), jnp.int32),
@@ -428,10 +451,10 @@
         compiler_params=params(),
         cost_estimate=COST,
         name="bucket",
-    )(heads, *touched, moving, panels)
+    )(after(heads, *packed.values()), *all_heads[1:], moving, panels)
     packed.update(zip(tail, outs[count:]))
 
-    all_codes = [after(codes, *touched)]
+    all_codes = [after(codes, *packed.values())]
     all_codes += [along(all_codes[0], plan, k) for k in range(1, plan.groups)]
     got = [
         along(outs[(k - 1) * plan.capacity + c], plan, k)
@@ -483,15 +506,18 @@
     send_early(4)
     send_early(5)
     send_early(7, *came(4), *all_codes[1:])
+
+    def parts(o):
+        return len([m for m in plan.late if m[0] == o])
+
     b5 = send(late(5), *came(5))
     b7 = send(late(7), *came(7))
-    send(late(6), b5)
-    send(late(4), b7)
+    b6 = send(late(6, 0), b5)
+    b4 = send(late(4, 0), b7)
     n1 = send(late(1), *came(5))
     send(late(2), *came(7))
     send(late(3, 0), n1)
     send(late(3, 1), b7)
-
     out_shape = jax.ShapeDtypeStruct((plan.rows * GRID_COLS * block, width), bf16)
     held, sets = [], []
     if early:
@@ -512,6 +538,12 @@
         )(*[first[o] for o in early])
         held, sets = [out], [sets]
 
+    if parts(6) > 1:
+        send(late(6, 1), b6, *sets)
+    if parts(4) > 1:
+        send(late(4, 1), b4)
+
+
     def place(held, messages, name):
         def body(*refs):
             refs = list(refs)[len(held) :]
@@ -538,7 +570,7 @@
             )(*held, *sets, *[arrived[m] for m in messages])
         ]
 
-    last = [late(4), late(6)]
+    last = [late(4, parts(4) - 1), late(6, parts(6) - 1)]
     held = place(held, [m for m in plan.late if m not in last], "place_mid")
     held = place(held, last, "place_last")
     return held[0][None]

time: 101 us -> 106 us (1.050)
  waiting for transfers between devices: 38.8 us -> 50.2 us
  starting transfers between devices: 45.9 us -> 39.1 us
    ppermute x11 -> x13, waiting for transfers between devices: 30 us -> 41.4 us  [across(): return lax.ppermute(value, 'wide', pairs)]
    ppermute x11 -> x13, starting transfers between devices: 39.3 us -> 32.5 us  [across(): return lax.ppermute(value, 'wide', pairs)]
  transfers between devices with their start and end apart: 15 -> 17, of which waited for: 6 -> 6; matrix products, arithmetic and copies ran while one was open for 0% -> 0% of each run, Pallas kernels for 13% -> 12%
where the time goes in v8:
time: 106 us
  waiting for transfers between devices  50.2 us (47%)
  starting transfers between devices  39.1 us (37%)
  Pallas kernels  15.6 us (15%)
    ppermute x13, waiting for transfers between devices, across(): return lax.ppermute(value, 'wide', pairs)  41.4 us
    ppermute x13, starting transfers between devices, across(): return lax.ppermute(value, 'wide', pairs)  32.5 us
    ppermute x4, waiting for transfers between devices, along(): lax.ppermute(value, 'front', [(f, (f + steps) % plan.groups) for f in ran...  8.78 us
    ppermute x4, starting transfers between devices, along(): lax.ppermute(value, 'front', [(f, (f + steps) % plan.groups) for f in ran...  6.64 us
    pallas_call x1, Pallas kernels, local(): pl.pallas_call(functools.partial(assemble_kernel, plan), out_shape=[jax.S...  5.85 us
    pallas_call x2, Pallas kernels, place(): pl.pallas_call(body, out_shape=out_shape, in_specs=[HBM] * len(held) + [A...  3.69 us
  transfers between devices with their start and end apart: 17, of which 6 were waited for; matrix products, arithmetic and copies ran while one was open for 0% of the time, Pallas kernels for 12%

profile of v8, /device:TPU:0, one launch (start us, length us, event | category | flops | bytes accessed | tf_op | source)
XLA Modules:
  0.0 105.7 jit_solution(17239888487868269132)
XLA Ops:
  0.0 0.7 bitcast_add_fusion.refs_0_
  0.7 3.0 %collective-permute-start = (s32[4]{0:T(128)S(1)}, s32[4]{0:T(128)S(1)}, u32[]{:S(2)}, u32[]{:S(2)}) collective-permute-start(s32[4]{0:T(128)S(1)} %bitcast_add_fusion.refs_0_), channel_id=1, source_target_pairs={{0,16},{16,0},{1,17},{17,1},{2,18},{18,2},{3,19},{19,3},{4,20},{20... | collective-permute-start | bytes 56 | tf_op jit(solution)/shard_map/ppermute | solution.py:389
  3.6 1.2 %stage.1 = (bf16[1024,256]{1,0:T(8,128)(2,1)S(1)}, bf16[1024,256]{1,0:T(8,128)(2,1)S(1)}) custom-call(bf16[1,1024,2048]{2,1,0:T(8,128)(2,1)} %refs_4_.1), custom_call_target="tpu_custom_call" | custom-call | tf_op jit(solution)/shard_map/stage/pallas_call | solution.py:413
  4.9 0.0 copy-start
  4.9 0.0 copy-start.1
  4.9 0.2 collective-permute-done.refs_1_
  5.2 1.2 %pack_early.1 = (bf16[264,256]{1,0:T(8,128)(2,1)S(1)}, bf16[520,256]{1,0:T(8,128)(2,1)S(1)}) custom-call(s32[4]{0:T(128)S(1)} %bitcast_add_fusion.refs_0_, s32[4]{0:T(128)S(1)} %collective-permute-done.refs_1_, bf16[1024,256]{1,0:T(8,128)(2,1)S(1)} %get-tuple-element.38.refs_2_, bf16[1024,256]{1,0:T(8,128)(2,1)S(1)} %get-tuple-element.39.refs_3_), custom_call_target="tpu_custom_call" | custom-call | tf_op jit(solution)/shard_map/pack_early/pallas_call | solution.py:423
  6.4 3.2 %collective-permute-start.1 = (bf16[264,256]{1,0:T(8,128)(2,1)S(1)}, bf16[264,256]{1,0:T(8,128)(2,1)S(1)}, u32[]{:S(2)}, u32[]{:S(2)}) collective-permute-start(bf16[264,256]{1,0:T(8,128)(2,1)S(1)} %get-tuple-element.40), channel_id=1, source_target_pairs={{0,8},{1,9},{2,10},{3,11},{4,12},{5,13},{6,14},{7,15},{8,0},{9,1},... | collective-permute-start | bytes 405512 | tf_op jit(solution)/shard_map/ppermute | solution.py:385
  9.6 1.3 %collective-permute-start.2 = (bf16[520,256]{1,0:T(8,128)(2,1)S(1)}, bf16[520,256]{1,0:T(8,128)(2,1)S(1)}, u32[]{:S(2)}, u32[]{:S(2)}) collective-permute-start(bf16[520,256]{1,0:T(8,128)(2,1)S(1)} %get-tuple-element.41), channel_id=1, source_target_pairs={{0,10},{1,11},{2,8},{3,9},{4,14},{5,15},{6,12},{7,13},{8,2},{9,3},... | collective-permute-start | bytes 798728 | tf_op jit(solution)/shard_map/ppermute | solution.py:385
  10.8 1.8 %bucket.1 = (bf16[128,1024]{1,0:T(8,128)(2,1)S(1)}, bf16[128,1024]{1,0:T(8,128)(2,1)S(1)}, bf16[520,256]{1,0:T(8,128)(2,1)S(1)}) custom-call(s32[4]{0:T(128)S(1)} %bitcast_add_fusion.refs_0_, s32[4]{0:T(128)S(1)} %collective-permute-done.refs_1_, bf16[1,512,1024]{2,1,0:T(8,128)(2,1)} %refs_5_.1, bf16[1,1024,2048]{2,1,0:T(8,128)(2,1)} %refs_4_.1), custom_call_target="tpu_custom_call" | custom-call | tf_op jit(solution)/shard_map/bucket/pallas_call | solution.py:440
  12.7 1.6 %collective-permute-start.5 = (bf16[128,1024]{1,0:T(8,128)(2,1)S(1)}, bf16[128,1024]{1,0:T(8,128)(2,1)S(1)}, u32[]{:S(2)}, u32[]{:S(2)}) collective-permute-start(bf16[128,1024]{1,0:T(8,128)(2,1)S(1)} %get-tuple-element.48), channel_id=1, source_target_pairs={{0,16},{16,0},{1,17},{17,1},{2,18},{18,2},{3,19},{19,3},{4,20},{20... | collective-permute-start | bytes 786440 | tf_op jit(solution)/shard_map/ppermute | solution.py:389
  14.3 0.5 collective-permute-start.6
  14.8 0.0 copy-done
  14.8 0.0 copy-done.1
  14.8 1.6 %collective-permute-start.3 = (s32[4,8]{1,0:T(4,128)S(1)}, s32[4,8]{1,0:T(4,128)S(1)}, u32[]{:S(2)}, u32[]{:S(2)}) collective-permute-start(s32[4,8]{1,0:T(4,128)S(1)} %add_bitcast_fusion.refs_2_), channel_id=1, source_target_pairs={{0,16},{16,0},{1,17},{17,1},{2,18},{18,2},{3,19},{19,3},{4,20},{20... | collective-permute-start | bytes 392 | tf_op jit(solution)/shard_map/ppermute | solution.py:389
  16.4 8.5 %collective-permute-done.3.refs_3_ = s32[4,8]{1,0:T(4,128)S(1)} collective-permute-done((s32[4,8]{1,0:T(4,128)S(1)}, s32[4,8]{1,0:T(4,128)S(1)}, u32[]{:S(2)}, u32[]{:S(2)}) %collective-permute-start.3) | collective-permute-done | bytes 160 | tf_op jit(solution)/shard_map/ppermute | solution.py:389
  24.9 0.0 collective-permute-done.1.refs_0_
  24.9 3.6 %collective-permute-start.4 = (bf16[520,256]{1,0:T(8,128)(2,1)S(1)}, bf16[520,256]{1,0:T(8,128)(2,1)S(1)}, u32[]{:S(2)}, u32[]{:S(2)}) collective-permute-start(bf16[520,256]{1,0:T(8,128)(2,1)S(1)} %get-tuple-element.45), channel_id=1, source_target_pairs={{0,14},{1,15},{2,12},{3,13},{4,10},{5,11},{6,8},{7,9},{8,6},{9,7},... | collective-permute-start | bytes 798728 | tf_op jit(solution)/shard_map/ppermute | solution.py:385
  28.5 0.0 collective-permute-done.5.refs_6_
  28.5 0.0 collective-permute-done.6.refs_7_
  28.5 5.9 %assemble.1 = (bf16[1024,256]{1,0:T(8,128)(2,1)S(1)}, bf16[1024,256]{1,0:T(8,128)(2,1)S(1)}, bf16[1024,256]{1,0:T(8,128)(2,1)S(1)}, bf16[512,256]{1,0:T(8,128)(2...) custom-call(s32[4]{0:T(128)S(1)} %bitcast_add_fusion.refs_0_, ...), custom_call_target="tpu_custom_call" | custom-call | tf_op jit(solution)/shard_map/assemble/pallas_call | solution.py:466
  34.4 0.0 collective-permute-done.2.refs_1_
  34.4 0.5 collective-permute-start.13
  34.9 1.1 %collective-permute-start.7 = (bf16[1024,256]{1,0:T(8,128)(2,1)S(1)}, bf16[1024,256]{1,0:T(8,128)(2,1)S(1)}, u32[]{:S(2)}, u32[]{:S(2)}) collective-permute-start(bf16[1024,256]{1,0:T(8,128)(2,1)S(1)} %get-tuple-element.52), channel_id=1, source_target_pairs={{0,2},{1,3},{2,0},{3,1},{4,6},{5,7},{6,4},{7,5},{8,10},{9,11},{10,... | collective-permute-start | bytes 1572872 | tf_op jit(solution)/shard_map/ppermute | solution.py:385
  36.0 0.0 collective-permute-done.4.refs_2_
  36.0 2.8 %collective-permute-start.10 = (bf16[512,256]{1,0:T(8,128)(2,1)S(1)}, bf16[512,256]{1,0:T(8,128)(2,1)S(1)}, u32[]{:S(2)}, u32[]{:S(2)}) collective-permute-start(bf16[512,256]{1,0:T(8,128)(2,1)S(1)} %get-tuple-element.59), channel_id=1, source_target_pairs={{0,14},{1,15},{2,12},{3,13},{4,10},{5,11},{6,8},{7,9},{8,6},{9,7},... | collective-permute-start | bytes 786440 | tf_op jit(solution)/shard_map/ppermute | solution.py:385
  38.8 17.5 %collective-permute-done.13.refs_8_ = bf16[512,256]{1,0:T(8,128)(2,1)S(1)} collective-permute-done((bf16[512,256]{1,0:T(8,128)(2,1)S(1)}, bf16[512,256]{1,0:T(8,128)(2,1)S(1)}, u32[]{:S(2)}, u32[]{:S(2)}) %collective-permute-start.13) | collective-permute-done | bytes 262176 | tf_op jit(solution)/shard_map/ppermute | solution.py:385
  56.3 3.2 %collective-permute-start.14 = (bf16[768,256]{1,0:T(8,128)(2,1)S(1)}, bf16[768,256]{1,0:T(8,128)(2,1)S(1)}, u32[]{:S(2)}, u32[]{:S(2)}) collective-permute-start(bf16[768,256]{1,0:T(8,128)(2,1)S(1)} %get-tuple-element.66), channel_id=1, source_target_pairs={{0,12},{1,13},{2,14},{3,15},{4,8},{5,9},{6,10},{7,11},{8,4},{9,5},... | collective-permute-start | bytes 1179656 | tf_op jit(solution)/shard_map/ppermute | solution.py:385
  59.5 0.0 collective-permute-start.8
  59.5 0.0 collective-permute-done.10.refs_10_
  59.5 13.1 %collective-permute-start.12 = (bf16[512,256]{1,0:T(8,128)(2,1)S(1)}, bf16[512,256]{1,0:T(8,128)(2,1)S(1)}, u32[]{:S(2)}, u32[]{:S(2)}) collective-permute-start(bf16[512,256]{1,0:T(8,128)(2,1)S(1)} %get-tuple-element.62), channel_id=1, source_target_pairs={{0,8},{1,9},{2,10},{3,11},{4,12},{5,13},{6,14},{7,15},{8,0},{9,1},... | collective-permute-start | bytes 786440 | tf_op jit(solution)/shard_map/ppermute | solution.py:385
  72.7 0.0 collective-permute-start.11
  72.7 0.0 collective-permute-done.7.refs_3_
  72.7 2.9 %collective-permute-start.9 = (bf16[512,256]{1,0:T(8,128)(2,1)S(1)}, bf16[512,256]{1,0:T(8,128)(2,1)S(1)}, u32[]{:S(2)}, u32[]{:S(2)}) collective-permute-start(bf16[512,256]{1,0:T(8,128)(2,1)S(1)} %get-tuple-element.56), channel_id=1, source_target_pairs={{0,6},{1,7},{2,4},{3,5},{4,2},{5,3},{6,0},{7,1},{8,14},{9,15},{10,... | collective-permute-start | bytes 786440 | tf_op jit(solution)/shard_map/ppermute | solution.py:385
  75.6 1.7 %place_early.1 = (bf16[8192,256]{1,0:T(8,128)(2,1)}, s32[3]{0:T(128)S(1)}) custom-call(bf16[264,256]{1,0:T(8,128)(2,1)S(1)} %collective-permute-done.1.refs_0_, bf16[520,256]{1,0:T(8,128)(2,1)S(1)} %collective-permute-done.2.refs_1_, bf16[520,256]{1,0:T(8,128)(2,1)S(1)} %collective-permute-done.4.refs_2_), custom_call_target="tpu_custom_call" | custom-call | tf_op jit(solution)/shard_map/place_early/pallas_call | solution.py:524
  77.3 0.0 collective-permute-done.14.refs_9_
  77.3 0.6 collective-permute-start.16
  78.0 11.3 %collective-permute-done.12.refs_7_ = bf16[512,256]{1,0:T(8,128)(2,1)S(1)} collective-permute-done((bf16[512,256]{1,0:T(8,128)(2,1)S(1)}, bf16[512,256]{1,0:T(8,128)(2,1)S(1)}, u32[]{:S(2)}, u32[]{:S(2)}) %collective-permute-start.12) | collective-permute-done | bytes 262176 | tf_op jit(solution)/shard_map/ppermute | solution.py:385
  89.2 0.1 collective-permute-start.15
  89.4 2.2 %collective-permute-done.11.refs_6_ = bf16[512,256]{1,0:T(8,128)(2,1)S(1)} collective-permute-done((bf16[512,256]{1,0:T(8,128)(2,1)S(1)}, bf16[512,256]{1,0:T(8,128)(2,1)S(1)}, u32[]{:S(2)}, u32[]{:S(2)}) %collective-permute-start.11) | collective-permute-done | bytes 262176 | tf_op jit(solution)/shard_map/ppermute | solution.py:385
  91.6 0.0 collective-permute-done.8.refs_4_
  91.6 10.4 %collective-permute-done.9.refs_5_ = bf16[512,256]{1,0:T(8,128)(2,1)S(1)} collective-permute-done((bf16[512,256]{1,0:T(8,128)(2,1)S(1)}, bf16[512,256]{1,0:T(8,128)(2,1)S(1)}, u32[]{:S(2)}, u32[]{:S(2)}) %collective-permute-start.9) | collective-permute-done | bytes 262176 | tf_op jit(solution)/shard_map/ppermute | solution.py:385
  102.0 2.3 %place_mid.1.refs_0_ = bf16[8192,256]{1,0:T(8,128)(2,1)} custom-call(bf16[8192,256]{1,0:T(8,128)(2,1)} %get-tuple-element.46.refs_0_, s32[3]{0:T(128)S(1)} %get-tuple-element.47.refs_1_, bf16[1024,256]{1,0:T(8,128)(2,1)S(1)} %get-tuple-element.50.refs_2_, bf16[1024,256]{1,0:T(8,128)(2,1)S(1)} %collective-permute-done.7.refs_3_, ...), custom_call_target="tpu_custom_call", output_to_operand_aliasing={{}: (0, {})} | custom-call | tf_op jit(solution)/shard_map/place_mid/pallas_call | solution.py:555
  104.3 0.0 collective-permute-done.16.refs_3_
  104.3 0.0 collective-permute-done.15.refs_2_
  104.3 1.4 %place_last.1 = bf16[8192,256]{1,0:T(8,128)(2,1)} custom-call(bf16[8192,256]{1,0:T(8,128)(2,1)} %place_mid.1.refs_0_, s32[3]{0:T(128)S(1)} %get-tuple-element.47.refs_1_, bf16[256,256]{1,0:T(8,128)(2,1)S(1)} %collective-permute-done.15.refs_2_, bf16[256,256]{1,0:T(8,128)(2,1)S(1)} %collective-permute-done.16.refs_3_), custom_call_target="tpu_custom_call", output_to_operand_aliasing={{}: (0, {})} | custom-call | tf_op jit(solution)/shard_map/place_last/pallas_call | solution.py:555
  (1 shorter events, 0.0 us)
Async XLA Ops:
  0.7 4.5 %collective-permute-start = (s32[4]{0:T(128)S(1)}, s32[4]{0:T(128)S(1)}, u32[]{:S(2)}, u32[]{:S(2)}) collective-permute-start(s32[4]{0:T(128)S(1)} %bitcast_add_fusion.refs_0_), channel_id=1, source_target_pairs={{0,16},{16,0},{1,17},{17,1},{2,18},{18,2},{3,19},{19,3},{4,20},{20... | collective-permute-start | bytes 56 | tf_op jit(solution)/shard_map/ppermute | solution.py:389
  4.9 9.9 %copy-start = (s32[1,4,8]{2,1,0:T(4,128)S(1)}, s32[1,4,8]{2,1,0:T(4,128)}, u32[]{:S(2)}) copy-start(s32[1,4,8]{2,1,0:T(4,128)} %param.10) | copy-start | bytes 388
  4.9 9.9 %copy-start.1 = (s32[1,4,8]{2,1,0:T(4,128)S(1)}, s32[1,4,8]{2,1,0:T(4,128)}, u32[]{:S(2)}) copy-start(s32[1,4,8]{2,1,0:T(4,128)} %param.11) | copy-start | bytes 388
  6.4 18.5 %collective-permute-start.1 = (bf16[264,256]{1,0:T(8,128)(2,1)S(1)}, bf16[264,256]{1,0:T(8,128)(2,1)S(1)}, u32[]{:S(2)}, u32[]{:S(2)}) collective-permute-start(bf16[264,256]{1,0:T(8,128)(2,1)S(1)} %get-tuple-element.40), channel_id=1, source_target_pairs={{0,8},{1,9},{2,10},{3,11},{4,12},{5,13},{6,14},{7,15},{8,0},{9,1},... | collective-permute-start | bytes 405512 | tf_op jit(solution)/shard_map/ppermute | solution.py:385
  9.6 24.8 %collective-permute-start.2 = (bf16[520,256]{1,0:T(8,128)(2,1)S(1)}, bf16[520,256]{1,0:T(8,128)(2,1)S(1)}, u32[]{:S(2)}, u32[]{:S(2)}) collective-permute-start(bf16[520,256]{1,0:T(8,128)(2,1)S(1)} %get-tuple-element.41), channel_id=1, source_target_pairs={{0,10},{1,11},{2,8},{3,9},{4,14},{5,15},{6,12},{7,13},{8,2},{9,3},... | collective-permute-start | bytes 798728 | tf_op jit(solution)/shard_map/ppermute | solution.py:385
  12.7 15.8 %collective-permute-start.5 = (bf16[128,1024]{1,0:T(8,128)(2,1)S(1)}, bf16[128,1024]{1,0:T(8,128)(2,1)S(1)}, u32[]{:S(2)}, u32[]{:S(2)}) collective-permute-start(bf16[128,1024]{1,0:T(8,128)(2,1)S(1)} %get-tuple-element.48), channel_id=1, source_target_pairs={{0,16},{16,0},{1,17},{17,1},{2,18},{18,2},{3,19},{19,3},{4,20},{20... | collective-permute-start | bytes 786440 | tf_op jit(solution)/shard_map/ppermute | solution.py:389
  14.3 14.2 %collective-permute-start.6 = (bf16[128,1024]{1,0:T(8,128)(2,1)S(1)}, bf16[128,1024]{1,0:T(8,128)(2,1)S(1)}, u32[]{:S(2)}, u32[]{:S(2)}) collective-permute-start(bf16[128,1024]{1,0:T(8,128)(2,1)S(1)} %get-tuple-element.49), channel_id=1, source_target_pairs={{0,16},{16,0},{1,17},{17,1},{2,18},{18,2},{3,19},{19,3},{4,20},{20... | collective-permute-start | bytes 786440 | tf_op jit(solution)/shard_map/ppermute | solution.py:389
  14.8 10.1 %collective-permute-start.3 = (s32[4,8]{1,0:T(4,128)S(1)}, s32[4,8]{1,0:T(4,128)S(1)}, u32[]{:S(2)}, u32[]{:S(2)}) collective-permute-start(s32[4,8]{1,0:T(4,128)S(1)} %add_bitcast_fusion.refs_2_), channel_id=1, source_target_pairs={{0,16},{16,0},{1,17},{17,1},{2,18},{18,2},{3,19},{19,3},{4,20},{20... | collective-permute-start | bytes 392 | tf_op jit(solution)/shard_map/ppermute | solution.py:389
  24.9 11.1 %collective-permute-start.4 = (bf16[520,256]{1,0:T(8,128)(2,1)S(1)}, bf16[520,256]{1,0:T(8,128)(2,1)S(1)}, u32[]{:S(2)}, u32[]{:S(2)}) collective-permute-start(bf16[520,256]{1,0:T(8,128)(2,1)S(1)} %get-tuple-element.45), channel_id=1, source_target_pairs={{0,14},{1,15},{2,12},{3,13},{4,10},{5,11},{6,8},{7,9},{8,6},{9,7},... | collective-permute-start | bytes 798728 | tf_op jit(solution)/shard_map/ppermute | solution.py:385
  34.4 21.9 %collective-permute-start.13 = (bf16[512,256]{1,0:T(8,128)(2,1)S(1)}, bf16[512,256]{1,0:T(8,128)(2,1)S(1)}, u32[]{:S(2)}, u32[]{:S(2)}) collective-permute-start(bf16[512,256]{1,0:T(8,128)(2,1)S(1)} %get-tuple-element.64), channel_id=1, source_target_pairs={{0,10},{1,11},{2,8},{3,9},{4,14},{5,15},{6,12},{7,13},{8,2},{9,3},... | collective-permute-start | bytes 786440 | tf_op jit(solution)/shard_map/ppermute | solution.py:385
  34.9 37.8 %collective-permute-start.7 = (bf16[1024,256]{1,0:T(8,128)(2,1)S(1)}, bf16[1024,256]{1,0:T(8,128)(2,1)S(1)}, u32[]{:S(2)}, u32[]{:S(2)}) collective-permute-start(bf16[1024,256]{1,0:T(8,128)(2,1)S(1)} %get-tuple-element.52), channel_id=1, source_target_pairs={{0,2},{1,3},{2,0},{3,1},{4,6},{5,7},{6,4},{7,5},{8,10},{9,11},{10,... | collective-permute-start | bytes 1572872 | tf_op jit(solution)/shard_map/ppermute | solution.py:385
  36.0 23.6 %collective-permute-start.10 = (bf16[512,256]{1,0:T(8,128)(2,1)S(1)}, bf16[512,256]{1,0:T(8,128)(2,1)S(1)}, u32[]{:S(2)}, u32[]{:S(2)}) collective-permute-start(bf16[512,256]{1,0:T(8,128)(2,1)S(1)} %get-tuple-element.59), channel_id=1, source_target_pairs={{0,14},{1,15},{2,12},{3,13},{4,10},{5,11},{6,8},{7,9},{8,6},{9,7},... | collective-permute-start | bytes 786440 | tf_op jit(solution)/shard_map/ppermute | solution.py:385
  56.3 21.0 %collective-permute-start.14 = (bf16[768,256]{1,0:T(8,128)(2,1)S(1)}, bf16[768,256]{1,0:T(8,128)(2,1)S(1)}, u32[]{:S(2)}, u32[]{:S(2)}) collective-permute-start(bf16[768,256]{1,0:T(8,128)(2,1)S(1)} %get-tuple-element.66), channel_id=1, source_target_pairs={{0,12},{1,13},{2,14},{3,15},{4,8},{5,9},{6,10},{7,11},{8,4},{9,5},... | collective-permute-start | bytes 1179656 | tf_op jit(solution)/shard_map/ppermute | solution.py:385
  59.5 32.1 %collective-permute-start.8 = (bf16[1024,256]{1,0:T(8,128)(2,1)S(1)}, bf16[1024,256]{1,0:T(8,128)(2,1)S(1)}, u32[]{:S(2)}, u32[]{:S(2)}) collective-permute-start(bf16[1024,256]{1,0:T(8,128)(2,1)S(1)} %get-tuple-element.54), channel_id=1, source_target_pairs={{0,4},{1,5},{2,6},{3,7},{4,0},{5,1},{6,2},{7,3},{8,12},{9,13},{10,... | collective-permute-start | bytes 1572872 | tf_op jit(solution)/shard_map/ppermute | solution.py:385
  59.5 29.7 %collective-permute-start.12 = (bf16[512,256]{1,0:T(8,128)(2,1)S(1)}, bf16[512,256]{1,0:T(8,128)(2,1)S(1)}, u32[]{:S(2)}, u32[]{:S(2)}) collective-permute-start(bf16[512,256]{1,0:T(8,128)(2,1)S(1)} %get-tuple-element.62), channel_id=1, source_target_pairs={{0,8},{1,9},{2,10},{3,11},{4,12},{5,13},{6,14},{7,15},{8,0},{9,1},... | collective-permute-start | bytes 786440 | tf_op jit(solution)/shard_map/ppermute | solution.py:385
  72.7 18.9 %collective-permute-start.11 = (bf16[512,256]{1,0:T(8,128)(2,1)S(1)}, bf16[512,256]{1,0:T(8,128)(2,1)S(1)}, u32[]{:S(2)}, u32[]{:S(2)}) collective-permute-start(bf16[512,256]{1,0:T(8,128)(2,1)S(1)} %get-tuple-element.60), channel_id=1, source_target_pairs={{0,6},{1,7},{2,4},{3,5},{4,2},{5,3},{6,0},{7,1},{8,14},{9,15},{10,... | collective-permute-start | bytes 786440 | tf_op jit(solution)/shard_map/ppermute | solution.py:385
  72.7 29.3 %collective-permute-start.9 = (bf16[512,256]{1,0:T(8,128)(2,1)S(1)}, bf16[512,256]{1,0:T(8,128)(2,1)S(1)}, u32[]{:S(2)}, u32[]{:S(2)}) collective-permute-start(bf16[512,256]{1,0:T(8,128)(2,1)S(1)} %get-tuple-element.56), channel_id=1, source_target_pairs={{0,6},{1,7},{2,4},{3,5},{4,2},{5,3},{6,0},{7,1},{8,14},{9,15},{10,... | collective-permute-start | bytes 786440 | tf_op jit(solution)/shard_map/ppermute | solution.py:385
  77.3 27.0 %collective-permute-start.16 = (bf16[256,256]{1,0:T(8,128)(2,1)S(1)}, bf16[256,256]{1,0:T(8,128)(2,1)S(1)}, u32[]{:S(2)}, u32[]{:S(2)}) collective-permute-start(bf16[256,256]{1,0:T(8,128)(2,1)S(1)} %get-tuple-element.70), channel_id=1, source_target_pairs={{0,12},{1,13},{2,14},{3,15},{4,8},{5,9},{6,10},{7,11},{8,4},{9,5},... | collective-permute-start | bytes 393224 | tf_op jit(solution)/shard_map/ppermute | solution.py:385
  89.2 15.1 %collective-permute-start.15 = (bf16[256,256]{1,0:T(8,128)(2,1)S(1)}, bf16[256,256]{1,0:T(8,128)(2,1)S(1)}, u32[]{:S(2)}, u32[]{:S(2)}) collective-permute-start(bf16[256,256]{1,0:T(8,128)(2,1)S(1)} %get-tuple-element.68), channel_id=1, source_target_pairs={{0,8},{1,9},{2,10},{3,11},{4,12},{5,13},{6,14},{7,15},{8,0},{9,1},... | collective-permute-start | bytes 393224 | tf_op jit(solution)/shard_map/ppermute | solution.py:385

commit v9 on v7

--- a/solution.py
+++ b/solution.py
@@ -309,7 +309,7 @@
             copies.append(
                 pltpu.make_async_copy(
                     pieces[i].at[pl.ds(k * block, block)],
-                    out.at[at(where[i, k] * GRID_COLS + source, block)],
+                    out.at[where[i, k], source],
                     sems.at[i, k],
                 )
             )
@@ -326,14 +326,12 @@
     def place(i, rows):
         o, lo, hi = messages[i]
         source = jnp.bitwise_xor(column, o)
-        for k in range(lo, hi):
-            copies.append(
-                pltpu.make_async_copy(
-                    pieces[i].at[pl.ds((k - lo) * block, block)],
-                    out.at[at(rows[k] * GRID_COLS + source, block)],
-                    sems.at[i, k],
-                )
-            )
+        if rows is None:
+            moves = [(pieces[i], out.at[pl.ds(lo, hi - lo), source])]
+        else:
+            moves = [(pieces[i].at[k - lo], out.at[rows[k], source]) for k in range(lo, hi)]
+        for k, (src, dst) in enumerate(moves):
+            copies.append(pltpu.make_async_copy(src, dst, sems.at[i, k]))
             copies[-1].start()
 
     split = [i for i, m in enumerate(messages) if m[0] in early]
@@ -342,7 +340,7 @@
         fetch.start()
     for i in range(len(messages)):
         if i not in split:
-            place(i, range(plan.rows))
+            place(i, None)
     if split:
         fetch.wait()
     for i in split:
@@ -492,7 +490,7 @@
     send(late(3, 0), n1)
     send(late(3, 1), b7)
 
-    out_shape = jax.ShapeDtypeStruct((plan.rows * GRID_COLS * block, width), bf16)
+    out_shape = jax.ShapeDtypeStruct((plan.rows, GRID_COLS, block, width), bf16)
     held, sets = [], []
     if early:
         out, sets = pl.pallas_call(
@@ -513,9 +511,11 @@
         held, sets = [out], [sets]
 
     def place(held, messages, name):
+        known = sets if any(m[0] in early for m in messages) else []
+
         def body(*refs):
             refs = list(refs)[len(held) :]
-            sets_ref = refs.pop(0) if sets else None
+            sets_ref = refs.pop(0) if known else None
             count = len(messages)
             place_late_kernel(plan, messages, early, sets_ref, refs[:count], *refs[count:])
 
@@ -523,7 +523,7 @@
             pl.pallas_call(
                 body,
                 out_shape=out_shape,
-                in_specs=[HBM] * len(held) + [ANY] * (len(sets) + len(messages)),
+                in_specs=[HBM] * len(held) + [ANY] * (len(known) + len(messages)),
                 out_specs=HBM,
                 input_output_aliases={0: 0} if held else {},
                 scratch_shapes=[
@@ -535,13 +535,14 @@
                 compiler_params=params(),
                 cost_estimate=MID if name == "place_mid" else COST,
                 name=name,
-            )(*held, *sets, *[arrived[m] for m in messages])
+            )(*held, *known, *[arrived[m].reshape(-1, block, width) for m in messages])
         ]
 
-    last = [late(4), late(6)]
+    last = [late(6), late(4)]
     held = place(held, [m for m in plan.late if m not in last], "place_mid")
-    held = place(held, last, "place_last")
-    return held[0][None]
+    for m in last:
+        held = place(held, [m], "place_last%d" % m[0])
+    return held[0].reshape(1, plan.rows * GRID_COLS * block, width)
 
 
 def solution(mesh):

time: 101 us -> 101 us (level)
    pallas_call x2 -> x3, Pallas kernels: 3.41 us -> 4.24 us  [place(): pl.pallas_call(body, out_shape=out_shape, in_specs=[HBM] * len(held) + [A...]
  transfers between devices with their start and end apart: 15 -> 15, of which waited for: 6 -> 6; matrix products, arithmetic and copies ran while one was open for 0% -> 0% of each run, Pallas kernels for 13% -> 14%
where the time goes in v9:
time: 101 us
  starting transfers between devices  45.7 us (45%)
  waiting for transfers between devices  38.1 us (38%)
  Pallas kernels  16.5 us (16%)
    ppermute x11, starting transfers between devices, across(): return lax.ppermute(value, 'wide', pairs)  39.2 us
    ppermute x11, waiting for transfers between devices, across(): return lax.ppermute(value, 'wide', pairs)  29.3 us
    ppermute x4, waiting for transfers between devices, along(): lax.ppermute(value, 'front', [(f, (f + steps) % plan.groups) for f in ran...  8.85 us
    ppermute x4, starting transfers between devices, along(): lax.ppermute(value, 'front', [(f, (f + steps) % plan.groups) for f in ran...  6.57 us
    pallas_call x1, Pallas kernels, local(): pl.pallas_call(functools.partial(assemble_kernel, plan), out_shape=[jax.S...  5.66 us
    pallas_call x3, Pallas kernels, place(): pl.pallas_call(body, out_shape=out_shape, in_specs=[HBM] * len(held) + [A...  4.24 us
    pallas_call x1, Pallas kernels, local(): pl.pallas_call(functools.partial(bucket_kernel, plan, tail), out_shape=[j...  2.5 us
  transfers between devices with their start and end apart: 15, of which 6 were waited for; matrix products, arithmetic and copies ran while one was open for 0% of the time, Pallas kernels for 14%

profile of v9, /device:TPU:0, one launch (start us, length us, event | category | flops | bytes accessed | tf_op | source)
XLA Modules:
  0.0 101.1 jit_solution(8073823201787041573)
XLA Ops:
  0.0 0.7 bitcast_add_fusion.refs_0_.heads
  0.7 3.0 %collective-permute-start = (s32[4]{0:T(128)S(1)}, s32[4]{0:T(128)S(1)}, u32[]{:S(2)}, u32[]{:S(2)}) collective-permute-start(s32[4]{0:T(128)S(1)} %bitcast_add_fusion.refs_0_.heads), channel_id=1, source_target_pairs={{0,16},{16,0},{1,17},{17,1},{2,18},{18,2},{3,19},{19,3},{4,20},{20... | collective-permute-start | bytes 56 | tf_op jit(solution)/shard_map/ppermute | solution.py:367
  3.6 1.2 %stage.1 = (bf16[1024,256]{1,0:T(8,128)(2,1)S(1)}, bf16[1024,256]{1,0:T(8,128)(2,1)S(1)}) custom-call(bf16[1,1024,2048]{2,1,0:T(8,128)(2,1)} %refs_4_.1), custom_call_target="tpu_custom_call" | custom-call | tf_op jit(solution)/shard_map/stage/pallas_call | solution.py:391
  4.9 0.0 copy-start
  4.9 0.0 copy-start.1
  4.9 0.2 collective-permute-done.refs_1_
  5.2 1.1 %pack_early.1 = (bf16[264,256]{1,0:T(8,128)(2,1)S(1)}, bf16[520,256]{1,0:T(8,128)(2,1)S(1)}, s32[1]{0:T(128)}) custom-call(s32[4]{0:T(128)S(1)} %bitcast_add_fusion.refs_0_.heads, s32[4]{0:T(128)S(1)} %collective-permute-done.refs_1_, bf16[1024,256]{1,0:T(8,128)(2,1)S(1)} %get-tuple-element.34.refs_2_, bf16[1024,256]{1,0:T(8,128)(2,1)S(1)} %get-tuple-element.35.refs_3_), custom_call_target="tpu_custom_call" | custom-call | tf_op jit(solution)/shard_map/pack_early/pallas_call | solution.py:401
  6.3 3.2 %collective-permute-start.1 = (bf16[264,256]{1,0:T(8,128)(2,1)S(1)}, bf16[264,256]{1,0:T(8,128)(2,1)S(1)}, u32[]{:S(2)}, u32[]{:S(2)}) collective-permute-start(bf16[264,256]{1,0:T(8,128)(2,1)S(1)} %get-tuple-element.36), channel_id=1, source_target_pairs={{0,8},{1,9},{2,10},{3,11},{4,12},{5,13},{6,14},{7,15},{8,0},{9,1},... | collective-permute-start | bytes 405512 | tf_op jit(solution)/shard_map/ppermute | solution.py:363
  9.4 1.3 %collective-permute-start.2 = (bf16[520,256]{1,0:T(8,128)(2,1)S(1)}, bf16[520,256]{1,0:T(8,128)(2,1)S(1)}, u32[]{:S(2)}, u32[]{:S(2)}) collective-permute-start(bf16[520,256]{1,0:T(8,128)(2,1)S(1)} %get-tuple-element.37), channel_id=1, source_target_pairs={{0,10},{1,11},{2,8},{3,9},{4,14},{5,15},{6,12},{7,13},{8,2},{9,3},... | collective-permute-start | bytes 798728 | tf_op jit(solution)/shard_map/ppermute | solution.py:363
  10.7 2.5 %bucket.1 = (bf16[128,1024]{1,0:T(8,128)(2,1)S(1)}, bf16[128,1024]{1,0:T(8,128)(2,1)S(1)}, bf16[520,256]{1,0:T(8,128)(2,1)S(1)}) custom-call(s32[4]{0:T(128)S(1)} %bitcast_add_fusion.refs_0_.heads, s32[1]{0:T(128)} %get-tuple-element.38.refs_0_, bf16[1,512,1024]{2,1,0:T(8,128)(2,1)} %refs_5_.1, bf16[1,1024,2048]{2,1,0:T(8,128)(2,1)} %refs_4_.1), custom_call_target="tpu_custom_call" | custom-call | tf_op jit(solution)/shard_map/bucket/pallas_call | solution.py:415
  13.2 1.5 %collective-permute-start.5 = (bf16[128,1024]{1,0:T(8,128)(2,1)S(1)}, bf16[128,1024]{1,0:T(8,128)(2,1)S(1)}, u32[]{:S(2)}, u32[]{:S(2)}) collective-permute-start(bf16[128,1024]{1,0:T(8,128)(2,1)S(1)} %get-tuple-element.44), channel_id=1, source_target_pairs={{0,16},{16,0},{1,17},{17,1},{2,18},{18,2},{3,19},{19,3},{4,20},{20... | collective-permute-start | bytes 786440 | tf_op jit(solution)/shard_map/ppermute | solution.py:367
  14.7 0.6 collective-permute-start.6
  15.3 0.0 copy-done
  15.3 0.0 copy-done.1
  15.3 1.5 %collective-permute-start.3 = (s32[4,8]{1,0:T(4,128)S(1)}, s32[4,8]{1,0:T(4,128)S(1)}, u32[]{:S(2)}, u32[]{:S(2)}) collective-permute-start(s32[4,8]{1,0:T(4,128)S(1)} %add_bitcast_fusion.refs_2_), channel_id=1, source_target_pairs={{0,16},{16,0},{1,17},{17,1},{2,18},{18,2},{3,19},{19,3},{4,20},{20... | collective-permute-start | bytes 392 | tf_op jit(solution)/shard_map/ppermute | solution.py:367
  16.8 8.6 %collective-permute-done.3.refs_3_ = s32[4,8]{1,0:T(4,128)S(1)} collective-permute-done((s32[4,8]{1,0:T(4,128)S(1)}, s32[4,8]{1,0:T(4,128)S(1)}, u32[]{:S(2)}, u32[]{:S(2)}) %collective-permute-start.3) | collective-permute-done | bytes 160 | tf_op jit(solution)/shard_map/ppermute | solution.py:367
  25.4 0.0 collective-permute-done.1.refs_0_
  25.4 3.6 %collective-permute-start.4 = (bf16[520,256]{1,0:T(8,128)(2,1)S(1)}, bf16[520,256]{1,0:T(8,128)(2,1)S(1)}, u32[]{:S(2)}, u32[]{:S(2)}) collective-permute-start(bf16[520,256]{1,0:T(8,128)(2,1)S(1)} %get-tuple-element.41), channel_id=1, source_target_pairs={{0,14},{1,15},{2,12},{3,13},{4,10},{5,11},{6,8},{7,9},{8,6},{9,7},... | collective-permute-start | bytes 798728 | tf_op jit(solution)/shard_map/ppermute | solution.py:363
  29.0 0.0 collective-permute-done.5.refs_6_
  29.0 0.0 collective-permute-done.6.refs_7_
  29.0 5.7 %assemble.1 = (bf16[1024,256]{1,0:T(8,128)(2,1)S(1)}, bf16[1024,256]{1,0:T(8,128)(2,1)S(1)}, bf16[1024,256]{1,0:T(8,128)(2,1)S(1)}, bf16[512,256]{1,0:T(8,128)(2...) custom-call(s32[4]{0:T(128)S(1)} %bitcast_add_fusion.refs_0_.heads, ...), custom_call_target="tpu_custom_call" | custom-call | tf_op jit(solution)/shard_map/assemble/pallas_call | solution.py:441
  34.7 0.0 collective-permute-done.2.refs_1_
  34.7 1.6 %collective-permute-start.7 = (bf16[1024,256]{1,0:T(8,128)(2,1)S(1)}, bf16[1024,256]{1,0:T(8,128)(2,1)S(1)}, u32[]{:S(2)}, u32[]{:S(2)}) collective-permute-start(bf16[1024,256]{1,0:T(8,128)(2,1)S(1)} %get-tuple-element.48), channel_id=1, source_target_pairs={{0,2},{1,3},{2,0},{3,1},{4,6},{5,7},{6,4},{7,5},{8,10},{9,11},{10,... | collective-permute-start | bytes 1572872 | tf_op jit(solution)/shard_map/ppermute | solution.py:363
  36.3 0.0 collective-permute-start.12
  36.3 0.0 collective-permute-done.4.refs_2_
  36.3 2.9 %collective-permute-start.10 = (bf16[512,256]{1,0:T(8,128)(2,1)S(1)}, bf16[512,256]{1,0:T(8,128)(2,1)S(1)}, u32[]{:S(2)}, u32[]{:S(2)}) collective-permute-start(bf16[512,256]{1,0:T(8,128)(2,1)S(1)} %get-tuple-element.55), channel_id=1, source_target_pairs={{0,14},{1,15},{2,12},{3,13},{4,10},{5,11},{6,8},{7,9},{8,6},{9,7},... | collective-permute-start | bytes 786440 | tf_op jit(solution)/shard_map/ppermute | solution.py:363
  39.2 15.1 %collective-permute-start.8 = (bf16[1024,256]{1,0:T(8,128)(2,1)S(1)}, bf16[1024,256]{1,0:T(8,128)(2,1)S(1)}, u32[]{:S(2)}, u32[]{:S(2)}) collective-permute-start(bf16[1024,256]{1,0:T(8,128)(2,1)S(1)} %get-tuple-element.50), channel_id=1, source_target_pairs={{0,4},{1,5},{2,6},{3,7},{4,0},{5,1},{6,2},{7,3},{8,12},{9,13},{10,... | collective-permute-start | bytes 1572872 | tf_op jit(solution)/shard_map/ppermute | solution.py:363
  54.2 2.4 %collective-permute-done.12 = bf16[512,256]{1,0:T(8,128)(2,1)S(1)} collective-permute-done((bf16[512,256]{1,0:T(8,128)(2,1)S(1)}, bf16[512,256]{1,0:T(8,128)(2,1)S(1)}, u32[]{:S(2)}, u32[]{:S(2)}) %collective-permute-start.12) | collective-permute-done | bytes 262176 | tf_op jit(solution)/shard_map/ppermute | solution.py:363
  56.7 3.6 %collective-permute-start.13 = (bf16[1024,256]{1,0:T(8,128)(2,1)S(1)}, bf16[1024,256]{1,0:T(8,128)(2,1)S(1)}, u32[]{:S(2)}, u32[]{:S(2)}) collective-permute-start(bf16[1024,256]{1,0:T(8,128)(2,1)S(1)} %get-tuple-element.60), channel_id=1, source_target_pairs={{0,12},{1,13},{2,14},{3,15},{4,8},{5,9},{6,10},{7,11},{8,4},{9,5},... | collective-permute-start | bytes 1572872 | tf_op jit(solution)/shard_map/ppermute | solution.py:363
  60.2 0.0 collective-permute-done.10
  60.2 5.1 %collective-permute-start.14 = (bf16[768,256]{1,0:T(8,128)(2,1)S(1)}, bf16[768,256]{1,0:T(8,128)(2,1)S(1)}, u32[]{:S(2)}, u32[]{:S(2)}) collective-permute-start(bf16[768,256]{1,0:T(8,128)(2,1)S(1)} %get-tuple-element.62), channel_id=1, source_target_pairs={{0,8},{1,9},{2,10},{3,11},{4,12},{5,13},{6,14},{7,15},{8,0},{9,1},... | collective-permute-start | bytes 1179656 | tf_op jit(solution)/shard_map/ppermute | solution.py:363
  65.4 0.0 collective-permute-start.11
  65.4 0.0 collective-permute-done.7
  65.4 2.9 %collective-permute-start.9 = (bf16[512,256]{1,0:T(8,128)(2,1)S(1)}, bf16[512,256]{1,0:T(8,128)(2,1)S(1)}, u32[]{:S(2)}, u32[]{:S(2)}) collective-permute-start(bf16[512,256]{1,0:T(8,128)(2,1)S(1)} %get-tuple-element.52), channel_id=1, source_target_pairs={{0,6},{1,7},{2,4},{3,5},{4,2},{5,3},{6,0},{7,1},{8,14},{9,15},{10,... | collective-permute-start | bytes 786440 | tf_op jit(solution)/shard_map/ppermute | solution.py:363
  68.3 1.7 %place_early.1 = (bf16[8,8,128,256]{3,2,1,0:T(8,128)(2,1)}, s32[3]{0:T(128)S(1)}) custom-call(bf16[264,256]{1,0:T(8,128)(2,1)S(1)} %collective-permute-done.1.refs_0_, bf16[520,256]{1,0:T(8,128)(2,1)S(1)} %collective-permute-done.2.refs_1_, bf16[520,256]{1,0:T(8,128)(2,1)S(1)} %collective-permute-done.4.refs_2_), custom_call_target="tpu_custom_call" | custom-call | tf_op jit(solution)/shard_map/place_early/pallas_call | solution.py:496
  70.0 21.5 %collective-permute-done.11 = bf16[512,256]{1,0:T(8,128)(2,1)S(1)} collective-permute-done((bf16[512,256]{1,0:T(8,128)(2,1)S(1)}, bf16[512,256]{1,0:T(8,128)(2,1)S(1)}, u32[]{:S(2)}, u32[]{:S(2)}) %collective-permute-start.11) | collective-permute-done | bytes 262176 | tf_op jit(solution)/shard_map/ppermute | solution.py:363
  91.5 0.0 collective-permute-done.8
  91.5 2.8 %collective-permute-done.9 = bf16[512,256]{1,0:T(8,128)(2,1)S(1)} collective-permute-done((bf16[512,256]{1,0:T(8,128)(2,1)S(1)}, bf16[512,256]{1,0:T(8,128)(2,1)S(1)}, u32[]{:S(2)}, u32[]{:S(2)}) %collective-permute-start.9) | collective-permute-done | bytes 262176 | tf_op jit(solution)/shard_map/ppermute | solution.py:363
  94.3 2.0 %place_mid.1.refs_0_ = bf16[8,8,128,256]{3,2,1,0:T(8,128)(2,1)} custom-call(bf16[8,8,128,256]{3,2,1,0:T(8,128)(2,1)} %get-tuple-element.42.refs_0_, s32[3]{0:T(128)S(1)} %get-tuple-element.43.refs_1_, bf16[8,128,256]{2,1,0:T(8,128)(2,1)S(1)} %bitcast.16, bf16[8,128,256]{2,1,0:T(8,128)(2,1)S(1)} %bitcast.17, ...), custom_call_target="tpu_custom_call", output_to_operand_aliasing={{}: (0, {})} | custom-call | tf_op jit(solution)/shard_map/place_mid/pallas_call | solution.py:523
  96.3 0.0 collective-permute-done.13
  96.3 0.9 place_last6.1.refs_0_
  97.2 2.5 %collective-permute-done.14 = bf16[768,256]{1,0:T(8,128)(2,1)S(1)} collective-permute-done((bf16[768,256]{1,0:T(8,128)(2,1)S(1)}, bf16[768,256]{1,0:T(8,128)(2,1)S(1)}, u32[]{:S(2)}, u32[]{:S(2)}) %collective-permute-start.14) | collective-permute-done | bytes 393248 | tf_op jit(solution)/shard_map/ppermute | solution.py:363
  99.7 1.4 %place_last4.1 = bf16[8,8,128,256]{3,2,1,0:T(8,128)(2,1)} custom-call(bf16[8,8,128,256]{3,2,1,0:T(8,128)(2,1)} %place_last6.1.refs_0_, s32[3]{0:T(128)S(1)} %get-tuple-element.43.refs_1_, bf16[6,128,256]{2,1,0:T(8,128)(2,1)S(1)} %bitcast.20), custom_call_target="tpu_custom_call", output_to_operand_aliasing={{}: (0, {})} | custom-call | tf_op jit(solution)/shard_map/place_last4/pallas_call | solution.py:523
  (1 shorter events, 0.0 us)
Async XLA Ops:
  0.7 4.5 %collective-permute-start = (s32[4]{0:T(128)S(1)}, s32[4]{0:T(128)S(1)}, u32[]{:S(2)}, u32[]{:S(2)}) collective-permute-start(s32[4]{0:T(128)S(1)} %bitcast_add_fusion.refs_0_.heads), channel_id=1, source_target_pairs={{0,16},{16,0},{1,17},{17,1},{2,18},{18,2},{3,19},{19,3},{4,20},{20... | collective-permute-start | bytes 56 | tf_op jit(solution)/shard_map/ppermute | solution.py:367
  4.9 10.4 %copy-start = (s32[1,4,8]{2,1,0:T(4,128)S(1)}, s32[1,4,8]{2,1,0:T(4,128)}, u32[]{:S(2)}) copy-start(s32[1,4,8]{2,1,0:T(4,128)} %param.10) | copy-start | bytes 388
  4.9 10.4 %copy-start.1 = (s32[1,4,8]{2,1,0:T(4,128)S(1)}, s32[1,4,8]{2,1,0:T(4,128)}, u32[]{:S(2)}) copy-start(s32[1,4,8]{2,1,0:T(4,128)} %param.11) | copy-start | bytes 388
  6.3 19.2 %collective-permute-start.1 = (bf16[264,256]{1,0:T(8,128)(2,1)S(1)}, bf16[264,256]{1,0:T(8,128)(2,1)S(1)}, u32[]{:S(2)}, u32[]{:S(2)}) collective-permute-start(bf16[264,256]{1,0:T(8,128)(2,1)S(1)} %get-tuple-element.36), channel_id=1, source_target_pairs={{0,8},{1,9},{2,10},{3,11},{4,12},{5,13},{6,14},{7,15},{8,0},{9,1},... | collective-permute-start | bytes 405512 | tf_op jit(solution)/shard_map/ppermute | solution.py:363
  9.4 25.2 %collective-permute-start.2 = (bf16[520,256]{1,0:T(8,128)(2,1)S(1)}, bf16[520,256]{1,0:T(8,128)(2,1)S(1)}, u32[]{:S(2)}, u32[]{:S(2)}) collective-permute-start(bf16[520,256]{1,0:T(8,128)(2,1)S(1)} %get-tuple-element.37), channel_id=1, source_target_pairs={{0,10},{1,11},{2,8},{3,9},{4,14},{5,15},{6,12},{7,13},{8,2},{9,3},... | collective-permute-start | bytes 798728 | tf_op jit(solution)/shard_map/ppermute | solution.py:363
  13.2 15.8 %collective-permute-start.5 = (bf16[128,1024]{1,0:T(8,128)(2,1)S(1)}, bf16[128,1024]{1,0:T(8,128)(2,1)S(1)}, u32[]{:S(2)}, u32[]{:S(2)}) collective-permute-start(bf16[128,1024]{1,0:T(8,128)(2,1)S(1)} %get-tuple-element.44), channel_id=1, source_target_pairs={{0,16},{16,0},{1,17},{17,1},{2,18},{18,2},{3,19},{19,3},{4,20},{20... | collective-permute-start | bytes 786440 | tf_op jit(solution)/shard_map/ppermute | solution.py:367
  14.7 14.3 %collective-permute-start.6 = (bf16[128,1024]{1,0:T(8,128)(2,1)S(1)}, bf16[128,1024]{1,0:T(8,128)(2,1)S(1)}, u32[]{:S(2)}, u32[]{:S(2)}) collective-permute-start(bf16[128,1024]{1,0:T(8,128)(2,1)S(1)} %get-tuple-element.45), channel_id=1, source_target_pairs={{0,16},{16,0},{1,17},{17,1},{2,18},{18,2},{3,19},{19,3},{4,20},{20... | collective-permute-start | bytes 786440 | tf_op jit(solution)/shard_map/ppermute | solution.py:367
  15.3 10.1 %collective-permute-start.3 = (s32[4,8]{1,0:T(4,128)S(1)}, s32[4,8]{1,0:T(4,128)S(1)}, u32[]{:S(2)}, u32[]{:S(2)}) collective-permute-start(s32[4,8]{1,0:T(4,128)S(1)} %add_bitcast_fusion.refs_2_), channel_id=1, source_target_pairs={{0,16},{16,0},{1,17},{17,1},{2,18},{18,2},{3,19},{19,3},{4,20},{20... | collective-permute-start | bytes 392 | tf_op jit(solution)/shard_map/ppermute | solution.py:367
  25.4 10.9 %collective-permute-start.4 = (bf16[520,256]{1,0:T(8,128)(2,1)S(1)}, bf16[520,256]{1,0:T(8,128)(2,1)S(1)}, u32[]{:S(2)}, u32[]{:S(2)}) collective-permute-start(bf16[520,256]{1,0:T(8,128)(2,1)S(1)} %get-tuple-element.41), channel_id=1, source_target_pairs={{0,14},{1,15},{2,12},{3,13},{4,10},{5,11},{6,8},{7,9},{8,6},{9,7},... | collective-permute-start | bytes 798728 | tf_op jit(solution)/shard_map/ppermute | solution.py:363
  34.7 30.7 %collective-permute-start.7 = (bf16[1024,256]{1,0:T(8,128)(2,1)S(1)}, bf16[1024,256]{1,0:T(8,128)(2,1)S(1)}, u32[]{:S(2)}, u32[]{:S(2)}) collective-permute-start(bf16[1024,256]{1,0:T(8,128)(2,1)S(1)} %get-tuple-element.48), channel_id=1, source_target_pairs={{0,2},{1,3},{2,0},{3,1},{4,6},{5,7},{6,4},{7,5},{8,10},{9,11},{10,... | collective-permute-start | bytes 1572872 | tf_op jit(solution)/shard_map/ppermute | solution.py:363
  36.3 20.4 %collective-permute-start.12 = (bf16[512,256]{1,0:T(8,128)(2,1)S(1)}, bf16[512,256]{1,0:T(8,128)(2,1)S(1)}, u32[]{:S(2)}, u32[]{:S(2)}) collective-permute-start(bf16[512,256]{1,0:T(8,128)(2,1)S(1)} %get-tuple-element.58), channel_id=1, source_target_pairs={{0,10},{1,11},{2,8},{3,9},{4,14},{5,15},{6,12},{7,13},{8,2},{9,3},... | collective-permute-start | bytes 786440 | tf_op jit(solution)/shard_map/ppermute | solution.py:363
  36.3 23.9 %collective-permute-start.10 = (bf16[512,256]{1,0:T(8,128)(2,1)S(1)}, bf16[512,256]{1,0:T(8,128)(2,1)S(1)}, u32[]{:S(2)}, u32[]{:S(2)}) collective-permute-start(bf16[512,256]{1,0:T(8,128)(2,1)S(1)} %get-tuple-element.55), channel_id=1, source_target_pairs={{0,14},{1,15},{2,12},{3,13},{4,10},{5,11},{6,8},{7,9},{8,6},{9,7},... | collective-permute-start | bytes 786440 | tf_op jit(solution)/shard_map/ppermute | solution.py:363
  39.2 52.3 %collective-permute-start.8 = (bf16[1024,256]{1,0:T(8,128)(2,1)S(1)}, bf16[1024,256]{1,0:T(8,128)(2,1)S(1)}, u32[]{:S(2)}, u32[]{:S(2)}) collective-permute-start(bf16[1024,256]{1,0:T(8,128)(2,1)S(1)} %get-tuple-element.50), channel_id=1, source_target_pairs={{0,4},{1,5},{2,6},{3,7},{4,0},{5,1},{6,2},{7,3},{8,12},{9,13},{10,... | collective-permute-start | bytes 1572872 | tf_op jit(solution)/shard_map/ppermute | solution.py:363
  56.7 39.6 %collective-permute-start.13 = (bf16[1024,256]{1,0:T(8,128)(2,1)S(1)}, bf16[1024,256]{1,0:T(8,128)(2,1)S(1)}, u32[]{:S(2)}, u32[]{:S(2)}) collective-permute-start(bf16[1024,256]{1,0:T(8,128)(2,1)S(1)} %get-tuple-element.60), channel_id=1, source_target_pairs={{0,12},{1,13},{2,14},{3,15},{4,8},{5,9},{6,10},{7,11},{8,4},{9,5},... | collective-permute-start | bytes 1572872 | tf_op jit(solution)/shard_map/ppermute | solution.py:363
  60.2 39.5 %collective-permute-start.14 = (bf16[768,256]{1,0:T(8,128)(2,1)S(1)}, bf16[768,256]{1,0:T(8,128)(2,1)S(1)}, u32[]{:S(2)}, u32[]{:S(2)}) collective-permute-start(bf16[768,256]{1,0:T(8,128)(2,1)S(1)} %get-tuple-element.62), channel_id=1, source_target_pairs={{0,8},{1,9},{2,10},{3,11},{4,12},{5,13},{6,14},{7,15},{8,0},{9,1},... | collective-permute-start | bytes 1179656 | tf_op jit(solution)/shard_map/ppermute | solution.py:363
  65.4 26.1 %collective-permute-start.11 = (bf16[512,256]{1,0:T(8,128)(2,1)S(1)}, bf16[512,256]{1,0:T(8,128)(2,1)S(1)}, u32[]{:S(2)}, u32[]{:S(2)}) collective-permute-start(bf16[512,256]{1,0:T(8,128)(2,1)S(1)} %get-tuple-element.56), channel_id=1, source_target_pairs={{0,6},{1,7},{2,4},{3,5},{4,2},{5,3},{6,0},{7,1},{8,14},{9,15},{10,... | collective-permute-start | bytes 786440 | tf_op jit(solution)/shard_map/ppermute | solution.py:363
  65.4 28.9 %collective-permute-start.9 = (bf16[512,256]{1,0:T(8,128)(2,1)S(1)}, bf16[512,256]{1,0:T(8,128)(2,1)S(1)}, u32[]{:S(2)}, u32[]{:S(2)}) collective-permute-start(bf16[512,256]{1,0:T(8,128)(2,1)S(1)} %get-tuple-element.52), channel_id=1, source_target_pairs={{0,6},{1,7},{2,4},{3,5},{4,2},{5,3},{6,0},{7,1},{8,14},{9,15},{10,... | collective-permute-start | bytes 786440 | tf_op jit(solution)/shard_map/ppermute | solution.py:363

commit v10 on v9

--- a/solution.py
+++ b/solution.py
@@ -31,7 +31,7 @@
         self.width = self.col_groups * self.block
         self.capacity = max(self.slots // 4, self.slots // self.groups)
         self.first = max(0, self.rows - self.capacity * self.groups)
-        self.early = {4: self.first // 2, 5: self.first, 7: self.first}
+        self.early = {6: self.first // 2, 5: self.first, 7: self.first}
         self.late = []
         for o in range(GRID_COLS):
             count = self.rows - self.early.get(o, 0)
@@ -478,13 +478,13 @@
     def came(*offsets):
         return [first[o] for o in offsets if o in first]
 
-    send_early(4)
+    send_early(6)
     send_early(5)
-    send_early(7, *came(4), *all_codes[1:])
+    send_early(7, *came(6), *all_codes[1:])
     b5 = send(late(5), *came(5))
     b7 = send(late(7), *came(7))
-    send(late(6), b5)
-    send(late(4), b7)
+    send(late(4), b5)
+    send(late(6), b7)
     n1 = send(late(1), *came(5))
     send(late(2), *came(7))
     send(late(3, 0), n1)

time: 101 us -> 102 us (level)
  waiting for transfers between devices: 38.1 us -> 42.5 us
  starting transfers between devices: 45.7 us -> 42.4 us
    ppermute x11, waiting for transfers between devices: 29.3 us -> 33.7 us  [across(): return lax.ppermute(value, 'wide', pairs)]
    ppermute x11, starting transfers between devices: 39.2 us -> 35.7 us  [across(): return lax.ppermute(value, 'wide', pairs)]
  transfers between devices with their start and end apart: 15 -> 15, of which waited for: 6 -> 5; matrix products, arithmetic and copies ran while one was open for 0% -> 0% of each run, Pallas kernels for 14% -> 14%
where the time goes in v10:
time: 102 us
  waiting for transfers between devices  42.5 us (42%)
  starting transfers between devices  42.4 us (42%)
  Pallas kernels  16.5 us (16%)
    ppermute x11, starting transfers between devices, across(): return lax.ppermute(value, 'wide', pairs)  35.7 us
    ppermute x11, waiting for transfers between devices, across(): return lax.ppermute(value, 'wide', pairs)  33.7 us
    ppermute x4, waiting for transfers between devices, along(): lax.ppermute(value, 'front', [(f, (f + steps) % plan.groups) for f in ran...  8.76 us
    ppermute x4, starting transfers between devices, along(): lax.ppermute(value, 'front', [(f, (f + steps) % plan.groups) for f in ran...  6.64 us
    pallas_call x1, Pallas kernels, local(): pl.pallas_call(functools.partial(assemble_kernel, plan), out_shape=[jax.S...  5.7 us
    pallas_call x3, Pallas kernels, place(): pl.pallas_call(body, out_shape=out_shape, in_specs=[HBM] * len(held) + [A...  4.25 us
    pallas_call x1, Pallas kernels, local(): pl.pallas_call(functools.partial(bucket_kernel, plan, tail), out_shape=[j...  2.5 us
  transfers between devices with their start and end apart: 15, of which 5 were waited for; matrix products, arithmetic and copies ran while one was open for 0% of the time, Pallas kernels for 14%

profile of v10, /device:TPU:0, one launch (start us, length us, event | category | flops | bytes accessed | tf_op | source)
XLA Modules:
  0.0 102.2 jit_solution(1734973259650229914)
XLA Ops:
  0.0 0.7 bitcast_add_fusion.refs_0_.heads
  0.7 3.0 %collective-permute-start = (s32[4]{0:T(128)S(1)}, s32[4]{0:T(128)S(1)}, u32[]{:S(2)}, u32[]{:S(2)}) collective-permute-start(s32[4]{0:T(128)S(1)} %bitcast_add_fusion.refs_0_.heads), channel_id=1, source_target_pairs={{0,16},{16,0},{1,17},{17,1},{2,18},{18,2},{3,19},{19,3},{4,20},{20... | collective-permute-start | bytes 56 | tf_op jit(solution)/shard_map/ppermute | solution.py:367
  3.6 1.2 %stage.1 = (bf16[1024,256]{1,0:T(8,128)(2,1)S(1)}, bf16[1024,256]{1,0:T(8,128)(2,1)S(1)}) custom-call(bf16[1,1024,2048]{2,1,0:T(8,128)(2,1)} %refs_4_.1), custom_call_target="tpu_custom_call" | custom-call | tf_op jit(solution)/shard_map/stage/pallas_call | solution.py:391
  4.9 0.0 copy-start
  4.9 0.0 copy-start.1
  4.9 0.2 collective-permute-done.refs_1_
  5.2 1.1 %pack_early.1 = (bf16[264,256]{1,0:T(8,128)(2,1)S(1)}, bf16[520,256]{1,0:T(8,128)(2,1)S(1)}, s32[1]{0:T(128)}) custom-call(s32[4]{0:T(128)S(1)} %bitcast_add_fusion.refs_0_.heads, s32[4]{0:T(128)S(1)} %collective-permute-done.refs_1_, bf16[1024,256]{1,0:T(8,128)(2,1)S(1)} %get-tuple-element.34.refs_2_, bf16[1024,256]{1,0:T(8,128)(2,1)S(1)} %get-tuple-element.35.refs_3_), custom_call_target="tpu_custom_call" | custom-call | tf_op jit(solution)/shard_map/pack_early/pallas_call | solution.py:401
  6.3 4.2 %collective-permute-start.1 = (bf16[264,256]{1,0:T(8,128)(2,1)S(1)}, bf16[264,256]{1,0:T(8,128)(2,1)S(1)}, u32[]{:S(2)}, u32[]{:S(2)}) collective-permute-start(bf16[264,256]{1,0:T(8,128)(2,1)S(1)} %get-tuple-element.36), channel_id=1, source_target_pairs={{0,12},{1,13},{2,14},{3,15},{4,8},{5,9},{6,10},{7,11},{8,4},{9,5},... | collective-permute-start | bytes 405512 | tf_op jit(solution)/shard_map/ppermute | solution.py:363
  10.5 0.4 collective-permute-start.2
  10.8 2.5 %bucket.1 = (bf16[128,1024]{1,0:T(8,128)(2,1)S(1)}, bf16[128,1024]{1,0:T(8,128)(2,1)S(1)}, bf16[520,256]{1,0:T(8,128)(2,1)S(1)}) custom-call(s32[4]{0:T(128)S(1)} %bitcast_add_fusion.refs_0_.heads, s32[1]{0:T(128)} %get-tuple-element.38.refs_0_, bf16[1,512,1024]{2,1,0:T(8,128)(2,1)} %refs_5_.1, bf16[1,1024,2048]{2,1,0:T(8,128)(2,1)} %refs_4_.1), custom_call_target="tpu_custom_call" | custom-call | tf_op jit(solution)/shard_map/bucket/pallas_call | solution.py:415
  13.3 1.6 %collective-permute-start.5 = (bf16[128,1024]{1,0:T(8,128)(2,1)S(1)}, bf16[128,1024]{1,0:T(8,128)(2,1)S(1)}, u32[]{:S(2)}, u32[]{:S(2)}) collective-permute-start(bf16[128,1024]{1,0:T(8,128)(2,1)S(1)} %get-tuple-element.44), channel_id=1, source_target_pairs={{0,16},{16,0},{1,17},{17,1},{2,18},{18,2},{3,19},{19,3},{4,20},{20... | collective-permute-start | bytes 786440 | tf_op jit(solution)/shard_map/ppermute | solution.py:367
  14.9 0.5 collective-permute-start.6
  15.4 0.0 copy-done
  15.4 0.0 copy-done.1
  15.4 1.6 %collective-permute-start.3 = (s32[4,8]{1,0:T(4,128)S(1)}, s32[4,8]{1,0:T(4,128)S(1)}, u32[]{:S(2)}, u32[]{:S(2)}) collective-permute-start(s32[4,8]{1,0:T(4,128)S(1)} %add_bitcast_fusion.refs_2_), channel_id=1, source_target_pairs={{0,16},{16,0},{1,17},{17,1},{2,18},{18,2},{3,19},{19,3},{4,20},{20... | collective-permute-start | bytes 392 | tf_op jit(solution)/shard_map/ppermute | solution.py:367
  17.0 8.5 %collective-permute-done.3.refs_3_ = s32[4,8]{1,0:T(4,128)S(1)} collective-permute-done((s32[4,8]{1,0:T(4,128)S(1)}, s32[4,8]{1,0:T(4,128)S(1)}, u32[]{:S(2)}, u32[]{:S(2)}) %collective-permute-start.3) | collective-permute-done | bytes 160 | tf_op jit(solution)/shard_map/ppermute | solution.py:367
  25.5 0.0 collective-permute-done.1.refs_0_
  25.5 2.4 %collective-permute-start.4 = (bf16[520,256]{1,0:T(8,128)(2,1)S(1)}, bf16[520,256]{1,0:T(8,128)(2,1)S(1)}, u32[]{:S(2)}, u32[]{:S(2)}) collective-permute-start(bf16[520,256]{1,0:T(8,128)(2,1)S(1)} %get-tuple-element.41), channel_id=1, source_target_pairs={{0,14},{1,15},{2,12},{3,13},{4,10},{5,11},{6,8},{7,9},{8,6},{9,7},... | collective-permute-start | bytes 798728 | tf_op jit(solution)/shard_map/ppermute | solution.py:363
  28.0 0.0 collective-permute-done.5.refs_6_
  28.0 0.0 collective-permute-done.6.refs_7_
  28.0 5.7 %assemble.1 = (bf16[1024,256]{1,0:T(8,128)(2,1)S(1)}, bf16[1024,256]{1,0:T(8,128)(2,1)S(1)}, bf16[1024,256]{1,0:T(8,128)(2,1)S(1)}, bf16[512,256]{1,0:T(8,128)(2...) custom-call(s32[4]{0:T(128)S(1)} %bitcast_add_fusion.refs_0_.heads, ...), custom_call_target="tpu_custom_call" | custom-call | tf_op jit(solution)/shard_map/assemble/pallas_call | solution.py:441
  33.7 0.0 collective-permute-done.2.refs_1_
  33.7 1.6 %collective-permute-start.7 = (bf16[1024,256]{1,0:T(8,128)(2,1)S(1)}, bf16[1024,256]{1,0:T(8,128)(2,1)S(1)}, u32[]{:S(2)}, u32[]{:S(2)}) collective-permute-start(bf16[1024,256]{1,0:T(8,128)(2,1)S(1)} %get-tuple-element.48), channel_id=1, source_target_pairs={{0,2},{1,3},{2,0},{3,1},{4,6},{5,7},{6,4},{7,5},{8,10},{9,11},{10,... | collective-permute-start | bytes 1572872 | tf_op jit(solution)/shard_map/ppermute | solution.py:363
  35.3 1.0 collective-permute-start.12
  36.3 0.0 collective-permute-done.4.refs_2_
  36.3 3.7 %collective-permute-start.10 = (bf16[512,256]{1,0:T(8,128)(2,1)S(1)}, bf16[512,256]{1,0:T(8,128)(2,1)S(1)}, u32[]{:S(2)}, u32[]{:S(2)}) collective-permute-start(bf16[512,256]{1,0:T(8,128)(2,1)S(1)} %get-tuple-element.55), channel_id=1, source_target_pairs={{0,14},{1,15},{2,12},{3,13},{4,10},{5,11},{6,8},{7,9},{8,6},{9,7},... | collective-permute-start | bytes 786440 | tf_op jit(solution)/shard_map/ppermute | solution.py:363
  40.0 13.9 %collective-permute-start.8 = (bf16[1024,256]{1,0:T(8,128)(2,1)S(1)}, bf16[1024,256]{1,0:T(8,128)(2,1)S(1)}, u32[]{:S(2)}, u32[]{:S(2)}) collective-permute-start(bf16[1024,256]{1,0:T(8,128)(2,1)S(1)} %get-tuple-element.50), channel_id=1, source_target_pairs={{0,4},{1,5},{2,6},{3,7},{4,0},{5,1},{6,2},{7,3},{8,12},{9,13},{10,... | collective-permute-start | bytes 1572872 | tf_op jit(solution)/shard_map/ppermute | solution.py:363
  53.9 2.8 %collective-permute-done.12 = bf16[512,256]{1,0:T(8,128)(2,1)S(1)} collective-permute-done((bf16[512,256]{1,0:T(8,128)(2,1)S(1)}, bf16[512,256]{1,0:T(8,128)(2,1)S(1)}, u32[]{:S(2)}, u32[]{:S(2)}) %collective-permute-start.12) | collective-permute-done | bytes 262176 | tf_op jit(solution)/shard_map/ppermute | solution.py:363
  56.7 0.0 collective-permute-start.14
  56.7 0.0 collective-permute-done.10
  56.7 3.3 %collective-permute-start.13 = (bf16[768,256]{1,0:T(8,128)(2,1)S(1)}, bf16[768,256]{1,0:T(8,128)(2,1)S(1)}, u32[]{:S(2)}, u32[]{:S(2)}) collective-permute-start(bf16[768,256]{1,0:T(8,128)(2,1)S(1)} %get-tuple-element.60), channel_id=1, source_target_pairs={{0,12},{1,13},{2,14},{3,15},{4,8},{5,9},{6,10},{7,11},{8,4},{9,5},... | collective-permute-start | bytes 1179656 | tf_op jit(solution)/shard_map/ppermute | solution.py:363
  60.0 5.2 %collective-permute-start.11 = (bf16[512,256]{1,0:T(8,128)(2,1)S(1)}, bf16[512,256]{1,0:T(8,128)(2,1)S(1)}, u32[]{:S(2)}, u32[]{:S(2)}) collective-permute-start(bf16[512,256]{1,0:T(8,128)(2,1)S(1)} %get-tuple-element.56), channel_id=1, source_target_pairs={{0,6},{1,7},{2,4},{3,5},{4,2},{5,3},{6,0},{7,1},{8,14},{9,15},{10,... | collective-permute-start | bytes 786440 | tf_op jit(solution)/shard_map/ppermute | solution.py:363
  65.2 0.0 collective-permute-done.7
  65.2 0.0 collective-permute-start.9
  65.2 1.7 %place_early.1 = (bf16[8,8,128,256]{3,2,1,0:T(8,128)(2,1)}, s32[3]{0:T(128)S(1)}) custom-call(bf16[264,256]{1,0:T(8,128)(2,1)S(1)} %collective-permute-done.1.refs_0_, bf16[520,256]{1,0:T(8,128)(2,1)S(1)} %collective-permute-done.2.refs_1_, bf16[520,256]{1,0:T(8,128)(2,1)S(1)} %collective-permute-done.4.refs_2_), custom_call_target="tpu_custom_call" | custom-call | tf_op jit(solution)/shard_map/place_early/pallas_call | solution.py:496
  66.9 26.1 %collective-permute-done.11 = bf16[512,256]{1,0:T(8,128)(2,1)S(1)} collective-permute-done((bf16[512,256]{1,0:T(8,128)(2,1)S(1)}, bf16[512,256]{1,0:T(8,128)(2,1)S(1)}, u32[]{:S(2)}, u32[]{:S(2)}) %collective-permute-start.11) | collective-permute-done | bytes 262176 | tf_op jit(solution)/shard_map/ppermute | solution.py:363
  93.0 0.0 collective-permute-done.8
  93.0 4.9 %collective-permute-done.9 = bf16[512,256]{1,0:T(8,128)(2,1)S(1)} collective-permute-done((bf16[512,256]{1,0:T(8,128)(2,1)S(1)}, bf16[512,256]{1,0:T(8,128)(2,1)S(1)}, u32[]{:S(2)}, u32[]{:S(2)}) %collective-permute-start.9) | collective-permute-done | bytes 262176 | tf_op jit(solution)/shard_map/ppermute | solution.py:363
  97.9 2.0 %place_mid.1.refs_0_ = bf16[8,8,128,256]{3,2,1,0:T(8,128)(2,1)} custom-call(bf16[8,8,128,256]{3,2,1,0:T(8,128)(2,1)} %get-tuple-element.42.refs_0_, s32[3]{0:T(128)S(1)} %get-tuple-element.43.refs_1_, bf16[8,128,256]{2,1,0:T(8,128)(2,1)S(1)} %bitcast.16, bf16[8,128,256]{2,1,0:T(8,128)(2,1)S(1)} %bitcast.17, ...), custom_call_target="tpu_custom_call", output_to_operand_aliasing={{}: (0, {})} | custom-call | tf_op jit(solution)/shard_map/place_mid/pallas_call | solution.py:523
  99.9 0.0 collective-permute-done.13
  99.9 1.4 %place_last6.1.refs_0_ = bf16[8,8,128,256]{3,2,1,0:T(8,128)(2,1)} custom-call(bf16[8,8,128,256]{3,2,1,0:T(8,128)(2,1)} %place_mid.1.refs_0_, s32[3]{0:T(128)S(1)} %get-tuple-element.43.refs_1_, bf16[6,128,256]{2,1,0:T(8,128)(2,1)S(1)} %bitcast.20), custom_call_target="tpu_custom_call", output_to_operand_aliasing={{}: (0, {})} | custom-call | tf_op jit(solution)/shard_map/place_last6/pallas_call | solution.py:523
  101.3 0.0 collective-permute-done.14
  101.3 0.9 place_last4.1
  (1 shorter events, 0.0 us)
Async XLA Ops:
  0.7 4.5 %collective-permute-start = (s32[4]{0:T(128)S(1)}, s32[4]{0:T(128)S(1)}, u32[]{:S(2)}, u32[]{:S(2)}) collective-permute-start(s32[4]{0:T(128)S(1)} %bitcast_add_fusion.refs_0_.heads), channel_id=1, source_target_pairs={{0,16},{16,0},{1,17},{17,1},{2,18},{18,2},{3,19},{19,3},{4,20},{20... | collective-permute-start | bytes 56 | tf_op jit(solution)/shard_map/ppermute | solution.py:367
  4.9 10.5 %copy-start = (s32[1,4,8]{2,1,0:T(4,128)S(1)}, s32[1,4,8]{2,1,0:T(4,128)}, u32[]{:S(2)}) copy-start(s32[1,4,8]{2,1,0:T(4,128)} %param.10) | copy-start | bytes 388
  4.9 10.5 %copy-start.1 = (s32[1,4,8]{2,1,0:T(4,128)S(1)}, s32[1,4,8]{2,1,0:T(4,128)}, u32[]{:S(2)}) copy-start(s32[1,4,8]{2,1,0:T(4,128)} %param.11) | copy-start | bytes 388
  6.3 19.2 %collective-permute-start.1 = (bf16[264,256]{1,0:T(8,128)(2,1)S(1)}, bf16[264,256]{1,0:T(8,128)(2,1)S(1)}, u32[]{:S(2)}, u32[]{:S(2)}) collective-permute-start(bf16[264,256]{1,0:T(8,128)(2,1)S(1)} %get-tuple-element.36), channel_id=1, source_target_pairs={{0,12},{1,13},{2,14},{3,15},{4,8},{5,9},{6,10},{7,11},{8,4},{9,5},... | collective-permute-start | bytes 405512 | tf_op jit(solution)/shard_map/ppermute | solution.py:363
  10.5 23.2 %collective-permute-start.2 = (bf16[520,256]{1,0:T(8,128)(2,1)S(1)}, bf16[520,256]{1,0:T(8,128)(2,1)S(1)}, u32[]{:S(2)}, u32[]{:S(2)}) collective-permute-start(bf16[520,256]{1,0:T(8,128)(2,1)S(1)} %get-tuple-element.37), channel_id=1, source_target_pairs={{0,10},{1,11},{2,8},{3,9},{4,14},{5,15},{6,12},{7,13},{8,2},{9,3},... | collective-permute-start | bytes 798728 | tf_op jit(solution)/shard_map/ppermute | solution.py:363
  13.3 14.7 %collective-permute-start.5 = (bf16[128,1024]{1,0:T(8,128)(2,1)S(1)}, bf16[128,1024]{1,0:T(8,128)(2,1)S(1)}, u32[]{:S(2)}, u32[]{:S(2)}) collective-permute-start(bf16[128,1024]{1,0:T(8,128)(2,1)S(1)} %get-tuple-element.44), channel_id=1, source_target_pairs={{0,16},{16,0},{1,17},{17,1},{2,18},{18,2},{3,19},{19,3},{4,20},{20... | collective-permute-start | bytes 786440 | tf_op jit(solution)/shard_map/ppermute | solution.py:367
  14.9 13.1 %collective-permute-start.6 = (bf16[128,1024]{1,0:T(8,128)(2,1)S(1)}, bf16[128,1024]{1,0:T(8,128)(2,1)S(1)}, u32[]{:S(2)}, u32[]{:S(2)}) collective-permute-start(bf16[128,1024]{1,0:T(8,128)(2,1)S(1)} %get-tuple-element.45), channel_id=1, source_target_pairs={{0,16},{16,0},{1,17},{17,1},{2,18},{18,2},{3,19},{19,3},{4,20},{20... | collective-permute-start | bytes 786440 | tf_op jit(solution)/shard_map/ppermute | solution.py:367
  15.4 10.1 %collective-permute-start.3 = (s32[4,8]{1,0:T(4,128)S(1)}, s32[4,8]{1,0:T(4,128)S(1)}, u32[]{:S(2)}, u32[]{:S(2)}) collective-permute-start(s32[4,8]{1,0:T(4,128)S(1)} %add_bitcast_fusion.refs_2_), channel_id=1, source_target_pairs={{0,16},{16,0},{1,17},{17,1},{2,18},{18,2},{3,19},{19,3},{4,20},{20... | collective-permute-start | bytes 392 | tf_op jit(solution)/shard_map/ppermute | solution.py:367
  25.5 10.8 %collective-permute-start.4 = (bf16[520,256]{1,0:T(8,128)(2,1)S(1)}, bf16[520,256]{1,0:T(8,128)(2,1)S(1)}, u32[]{:S(2)}, u32[]{:S(2)}) collective-permute-start(bf16[520,256]{1,0:T(8,128)(2,1)S(1)} %get-tuple-element.41), channel_id=1, source_target_pairs={{0,14},{1,15},{2,12},{3,13},{4,10},{5,11},{6,8},{7,9},{8,6},{9,7},... | collective-permute-start | bytes 798728 | tf_op jit(solution)/shard_map/ppermute | solution.py:363
  33.7 31.5 %collective-permute-start.7 = (bf16[1024,256]{1,0:T(8,128)(2,1)S(1)}, bf16[1024,256]{1,0:T(8,128)(2,1)S(1)}, u32[]{:S(2)}, u32[]{:S(2)}) collective-permute-start(bf16[1024,256]{1,0:T(8,128)(2,1)S(1)} %get-tuple-element.48), channel_id=1, source_target_pairs={{0,2},{1,3},{2,0},{3,1},{4,6},{5,7},{6,4},{7,5},{8,10},{9,11},{10,... | collective-permute-start | bytes 1572872 | tf_op jit(solution)/shard_map/ppermute | solution.py:363
  35.3 21.4 %collective-permute-start.12 = (bf16[512,256]{1,0:T(8,128)(2,1)S(1)}, bf16[512,256]{1,0:T(8,128)(2,1)S(1)}, u32[]{:S(2)}, u32[]{:S(2)}) collective-permute-start(bf16[512,256]{1,0:T(8,128)(2,1)S(1)} %get-tuple-element.58), channel_id=1, source_target_pairs={{0,10},{1,11},{2,8},{3,9},{4,14},{5,15},{6,12},{7,13},{8,2},{9,3},... | collective-permute-start | bytes 786440 | tf_op jit(solution)/shard_map/ppermute | solution.py:363
  36.3 20.4 %collective-permute-start.10 = (bf16[512,256]{1,0:T(8,128)(2,1)S(1)}, bf16[512,256]{1,0:T(8,128)(2,1)S(1)}, u32[]{:S(2)}, u32[]{:S(2)}) collective-permute-start(bf16[512,256]{1,0:T(8,128)(2,1)S(1)} %get-tuple-element.55), channel_id=1, source_target_pairs={{0,14},{1,15},{2,12},{3,13},{4,10},{5,11},{6,8},{7,9},{8,6},{9,7},... | collective-permute-start | bytes 786440 | tf_op jit(solution)/shard_map/ppermute | solution.py:363
  40.0 53.0 %collective-permute-start.8 = (bf16[1024,256]{1,0:T(8,128)(2,1)S(1)}, bf16[1024,256]{1,0:T(8,128)(2,1)S(1)}, u32[]{:S(2)}, u32[]{:S(2)}) collective-permute-start(bf16[1024,256]{1,0:T(8,128)(2,1)S(1)} %get-tuple-element.50), channel_id=1, source_target_pairs={{0,4},{1,5},{2,6},{3,7},{4,0},{5,1},{6,2},{7,3},{8,12},{9,13},{10,... | collective-permute-start | bytes 1572872 | tf_op jit(solution)/shard_map/ppermute | solution.py:363
  56.7 44.6 %collective-permute-start.14 = (bf16[1024,256]{1,0:T(8,128)(2,1)S(1)}, bf16[1024,256]{1,0:T(8,128)(2,1)S(1)}, u32[]{:S(2)}, u32[]{:S(2)}) collective-permute-start(bf16[1024,256]{1,0:T(8,128)(2,1)S(1)} %get-tuple-element.62), channel_id=1, source_target_pairs={{0,8},{1,9},{2,10},{3,11},{4,12},{5,13},{6,14},{7,15},{8,0},{9,1},... | collective-permute-start | bytes 1572872 | tf_op jit(solution)/shard_map/ppermute | solution.py:363
  56.7 43.2 %collective-permute-start.13 = (bf16[768,256]{1,0:T(8,128)(2,1)S(1)}, bf16[768,256]{1,0:T(8,128)(2,1)S(1)}, u32[]{:S(2)}, u32[]{:S(2)}) collective-permute-start(bf16[768,256]{1,0:T(8,128)(2,1)S(1)} %get-tuple-element.60), channel_id=1, source_target_pairs={{0,12},{1,13},{2,14},{3,15},{4,8},{5,9},{6,10},{7,11},{8,4},{9,5},... | collective-permute-start | bytes 1179656 | tf_op jit(solution)/shard_map/ppermute | solution.py:363
  60.0 33.0 %collective-permute-start.11 = (bf16[512,256]{1,0:T(8,128)(2,1)S(1)}, bf16[512,256]{1,0:T(8,128)(2,1)S(1)}, u32[]{:S(2)}, u32[]{:S(2)}) collective-permute-start(bf16[512,256]{1,0:T(8,128)(2,1)S(1)} %get-tuple-element.56), channel_id=1, source_target_pairs={{0,6},{1,7},{2,4},{3,5},{4,2},{5,3},{6,0},{7,1},{8,14},{9,15},{10,... | collective-permute-start | bytes 786440 | tf_op jit(solution)/shard_map/ppermute | solution.py:363
  65.2 32.7 %collective-permute-start.9 = (bf16[512,256]{1,0:T(8,128)(2,1)S(1)}, bf16[512,256]{1,0:T(8,128)(2,1)S(1)}, u32[]{:S(2)}, u32[]{:S(2)}) collective-permute-start(bf16[512,256]{1,0:T(8,128)(2,1)S(1)} %get-tuple-element.52), channel_id=1, source_target_pairs={{0,6},{1,7},{2,4},{3,5},{4,2},{5,3},{6,0},{7,1},{8,14},{9,15},{10,... | collective-permute-start | bytes 786440 | tf_op jit(solution)/shard_map/ppermute | solution.py:363

commit v11 on v9

--- a/solution.py
+++ b/solution.py
@@ -35,7 +35,7 @@
         self.late = []
         for o in range(GRID_COLS):
             count = self.rows - self.early.get(o, 0)
-            cuts = [0, count // 2, count] if o == 3 else [0, count]
+            cuts = [0, count // 2, count] if o == 1 else [0, count]
             self.late += [(o, lo, hi) for lo, hi in zip(cuts, cuts[1:]) if lo < hi]
 
 
@@ -485,10 +485,10 @@
     b7 = send(late(7), *came(7))
     send(late(6), b5)
     send(late(4), b7)
-    n1 = send(late(1), *came(5))
-    send(late(2), *came(7))
-    send(late(3, 0), n1)
-    send(late(3, 1), b7)
+    n2 = send(late(2), *came(5))
+    send(late(3), *came(7))
+    send(late(1, 0), n2)
+    send(late(1, 1), b7)
 
     out_shape = jax.ShapeDtypeStruct((plan.rows, GRID_COLS, block, width), bf16)
     held, sets = [], []
@@ -538,10 +538,9 @@
             )(*held, *known, *[arrived[m].reshape(-1, block, width) for m in messages])
         ]
 
-    last = [late(6), late(4)]
+    last = [late(4), late(6)]
     held = place(held, [m for m in plan.late if m not in last], "place_mid")
-    for m in last:
-        held = place(held, [m], "place_last%d" % m[0])
+    held = place(held, last, "place_last")
     return held[0].reshape(1, plan.rows * GRID_COLS * block, width)
 
 

time: 101 us -> 101 us (level)
  waiting for transfers between devices: 38.1 us -> 53 us
  starting transfers between devices: 45.7 us -> 31.8 us
    ppermute x11, waiting for transfers between devices: 29.3 us -> 44.2 us  [across(): return lax.ppermute(value, 'wide', pairs)]
    ppermute x11, starting transfers between devices: 39.2 us -> 25.1 us  [across(): return lax.ppermute(value, 'wide', pairs)]
    pallas_call x3 -> x2, Pallas kernels: 4.24 us -> 3.43 us  [place(): pl.pallas_call(body, out_shape=out_shape, in_specs=[HBM] * len(held) + [A...]
  transfers between devices with their start and end apart: 15 -> 15, of which waited for: 6 -> 8; matrix products, arithmetic and copies ran while one was open for 0% -> 0% of each run, Pallas kernels for 14% -> 13%
where the time goes in v11:
time: 101 us
  waiting for transfers between devices  53 us (52%)
  starting transfers between devices  31.8 us (31%)
  Pallas kernels  15.6 us (15%)
    ppermute x11, waiting for transfers between devices, across(): return lax.ppermute(value, 'wide', pairs)  44.2 us
    ppermute x11, starting transfers between devices, across(): return lax.ppermute(value, 'wide', pairs)  25.1 us
    ppermute x4, waiting for transfers between devices, along(): lax.ppermute(value, 'front', [(f, (f + steps) % plan.groups) for f in ran...  8.78 us
    ppermute x4, starting transfers between devices, along(): lax.ppermute(value, 'front', [(f, (f + steps) % plan.groups) for f in ran...  6.71 us
    pallas_call x1, Pallas kernels, local(): pl.pallas_call(functools.partial(assemble_kernel, plan), out_shape=[jax.S...  5.69 us
    pallas_call x2, Pallas kernels, place(): pl.pallas_call(body, out_shape=out_shape, in_specs=[HBM] * len(held) + [A...  3.43 us
    pallas_call x1, Pallas kernels, local(): pl.pallas_call(functools.partial(bucket_kernel, plan, tail), out_shape=[j...  2.43 us
  transfers between devices with their start and end apart: 15, of which 8 were waited for; matrix products, arithmetic and copies ran while one was open for 0% of the time, Pallas kernels for 13%

profile of v11, /device:TPU:0, one launch (start us, length us, event | category | flops | bytes accessed | tf_op | source)
XLA Modules:
  0.0 101.2 jit_solution(11409195834212727694)
XLA Ops:
  0.0 0.7 bitcast_add_fusion.refs_0_.heads
  0.7 3.0 %collective-permute-start = (s32[4]{0:T(128)S(1)}, s32[4]{0:T(128)S(1)}, u32[]{:S(2)}, u32[]{:S(2)}) collective-permute-start(s32[4]{0:T(128)S(1)} %bitcast_add_fusion.refs_0_.heads), channel_id=1, source_target_pairs={{0,16},{16,0},{1,17},{17,1},{2,18},{18,2},{3,19},{19,3},{4,20},{20... | collective-permute-start | bytes 56 | tf_op jit(solution)/shard_map/ppermute | solution.py:367
  3.6 1.2 %stage.1 = (bf16[1024,256]{1,0:T(8,128)(2,1)S(1)}, bf16[1024,256]{1,0:T(8,128)(2,1)S(1)}) custom-call(bf16[1,1024,2048]{2,1,0:T(8,128)(2,1)} %refs_4_.1), custom_call_target="tpu_custom_call" | custom-call | tf_op jit(solution)/shard_map/stage/pallas_call | solution.py:391
  4.9 0.0 copy-start
  4.9 0.0 copy-start.1
  4.9 0.2 collective-permute-done.refs_1_
  5.2 1.1 %pack_early.1 = (bf16[264,256]{1,0:T(8,128)(2,1)S(1)}, bf16[520,256]{1,0:T(8,128)(2,1)S(1)}, s32[1]{0:T(128)}) custom-call(s32[4]{0:T(128)S(1)} %bitcast_add_fusion.refs_0_.heads, s32[4]{0:T(128)S(1)} %collective-permute-done.refs_1_, bf16[1024,256]{1,0:T(8,128)(2,1)S(1)} %get-tuple-element.34.refs_2_, bf16[1024,256]{1,0:T(8,128)(2,1)S(1)} %get-tuple-element.35.refs_3_), custom_call_target="tpu_custom_call" | custom-call | tf_op jit(solution)/shard_map/pack_early/pallas_call | solution.py:401
  6.3 3.2 %collective-permute-start.1 = (bf16[264,256]{1,0:T(8,128)(2,1)S(1)}, bf16[264,256]{1,0:T(8,128)(2,1)S(1)}, u32[]{:S(2)}, u32[]{:S(2)}) collective-permute-start(bf16[264,256]{1,0:T(8,128)(2,1)S(1)} %get-tuple-element.36), channel_id=1, source_target_pairs={{0,8},{1,9},{2,10},{3,11},{4,12},{5,13},{6,14},{7,15},{8,0},{9,1},... | collective-permute-start | bytes 405512 | tf_op jit(solution)/shard_map/ppermute | solution.py:363
  9.4 1.3 %collective-permute-start.2 = (bf16[520,256]{1,0:T(8,128)(2,1)S(1)}, bf16[520,256]{1,0:T(8,128)(2,1)S(1)}, u32[]{:S(2)}, u32[]{:S(2)}) collective-permute-start(bf16[520,256]{1,0:T(8,128)(2,1)S(1)} %get-tuple-element.37), channel_id=1, source_target_pairs={{0,10},{1,11},{2,8},{3,9},{4,14},{5,15},{6,12},{7,13},{8,2},{9,3},... | collective-permute-start | bytes 798728 | tf_op jit(solution)/shard_map/ppermute | solution.py:363
  10.7 2.4 %bucket.1 = (bf16[128,1024]{1,0:T(8,128)(2,1)S(1)}, bf16[128,1024]{1,0:T(8,128)(2,1)S(1)}, bf16[520,256]{1,0:T(8,128)(2,1)S(1)}) custom-call(s32[4]{0:T(128)S(1)} %bitcast_add_fusion.refs_0_.heads, s32[1]{0:T(128)} %get-tuple-element.38.refs_0_, bf16[1,512,1024]{2,1,0:T(8,128)(2,1)} %refs_5_.1, bf16[1,1024,2048]{2,1,0:T(8,128)(2,1)} %refs_4_.1), custom_call_target="tpu_custom_call" | custom-call | tf_op jit(solution)/shard_map/bucket/pallas_call | solution.py:415
  13.1 1.7 %collective-permute-start.5 = (bf16[128,1024]{1,0:T(8,128)(2,1)S(1)}, bf16[128,1024]{1,0:T(8,128)(2,1)S(1)}, u32[]{:S(2)}, u32[]{:S(2)}) collective-permute-start(bf16[128,1024]{1,0:T(8,128)(2,1)S(1)} %get-tuple-element.44), channel_id=1, source_target_pairs={{0,16},{16,0},{1,17},{17,1},{2,18},{18,2},{3,19},{19,3},{4,20},{20... | collective-permute-start | bytes 786440 | tf_op jit(solution)/shard_map/ppermute | solution.py:367
  14.8 0.4 collective-permute-start.6
  15.2 0.0 copy-done
  15.2 0.0 copy-done.1
  15.2 1.7 %collective-permute-start.3 = (s32[4,8]{1,0:T(4,128)S(1)}, s32[4,8]{1,0:T(4,128)S(1)}, u32[]{:S(2)}, u32[]{:S(2)}) collective-permute-start(s32[4,8]{1,0:T(4,128)S(1)} %add_bitcast_fusion.refs_2_), channel_id=1, source_target_pairs={{0,16},{16,0},{1,17},{17,1},{2,18},{18,2},{3,19},{19,3},{4,20},{20... | collective-permute-start | bytes 392 | tf_op jit(solution)/shard_map/ppermute | solution.py:367
  16.9 8.5 %collective-permute-done.3.refs_3_ = s32[4,8]{1,0:T(4,128)S(1)} collective-permute-done((s32[4,8]{1,0:T(4,128)S(1)}, s32[4,8]{1,0:T(4,128)S(1)}, u32[]{:S(2)}, u32[]{:S(2)}) %collective-permute-start.3) | collective-permute-done | bytes 160 | tf_op jit(solution)/shard_map/ppermute | solution.py:367
  25.4 0.0 collective-permute-done.1.refs_0_
  25.4 3.6 %collective-permute-start.4 = (bf16[520,256]{1,0:T(8,128)(2,1)S(1)}, bf16[520,256]{1,0:T(8,128)(2,1)S(1)}, u32[]{:S(2)}, u32[]{:S(2)}) collective-permute-start(bf16[520,256]{1,0:T(8,128)(2,1)S(1)} %get-tuple-element.41), channel_id=1, source_target_pairs={{0,14},{1,15},{2,12},{3,13},{4,10},{5,11},{6,8},{7,9},{8,6},{9,7},... | collective-permute-start | bytes 798728 | tf_op jit(solution)/shard_map/ppermute | solution.py:363
  29.0 0.0 collective-permute-done.5.refs_6_
  29.0 0.0 collective-permute-done.6.refs_7_
  29.0 5.7 %assemble.1 = (bf16[1024,256]{1,0:T(8,128)(2,1)S(1)}, bf16[512,256]{1,0:T(8,128)(2,1)S(1)}, bf16[512,256]{1,0:T(8,128)(2,1)S(1)}, bf16[1024,256]{1,0:T(8,128)(2,...) custom-call(s32[4]{0:T(128)S(1)} %bitcast_add_fusion.refs_0_.heads, ...), custom_call_target="tpu_custom_call" | custom-call | tf_op jit(solution)/shard_map/assemble/pallas_call | solution.py:441
  34.7 0.0 collective-permute-done.2.refs_1_
  34.7 0.1 collective-permute-start.7
  34.8 1.7 %collective-permute-start.12 = (bf16[512,256]{1,0:T(8,128)(2,1)S(1)}, bf16[512,256]{1,0:T(8,128)(2,1)S(1)}, u32[]{:S(2)}, u32[]{:S(2)}) collective-permute-start(bf16[512,256]{1,0:T(8,128)(2,1)S(1)} %get-tuple-element.58), channel_id=1, source_target_pairs={{0,10},{1,11},{2,8},{3,9},{4,14},{5,15},{6,12},{7,13},{8,2},{9,3},... | collective-permute-start | bytes 786440 | tf_op jit(solution)/shard_map/ppermute | solution.py:363
  36.5 0.0 collective-permute-done.4.refs_2_
  36.5 3.6 %collective-permute-start.9 = (bf16[512,256]{1,0:T(8,128)(2,1)S(1)}, bf16[512,256]{1,0:T(8,128)(2,1)S(1)}, u32[]{:S(2)}, u32[]{:S(2)}) collective-permute-start(bf16[512,256]{1,0:T(8,128)(2,1)S(1)} %get-tuple-element.53), channel_id=1, source_target_pairs={{0,14},{1,15},{2,12},{3,13},{4,10},{5,11},{6,8},{7,9},{8,6},{9,7},... | collective-permute-start | bytes 786440 | tf_op jit(solution)/shard_map/ppermute | solution.py:363
  40.1 3.8 %collective-permute-start.11 = (bf16[1024,256]{1,0:T(8,128)(2,1)S(1)}, bf16[1024,256]{1,0:T(8,128)(2,1)S(1)}, u32[]{:S(2)}, u32[]{:S(2)}) collective-permute-start(bf16[1024,256]{1,0:T(8,128)(2,1)S(1)} %get-tuple-element.56), channel_id=1, source_target_pairs={{0,6},{1,7},{2,4},{3,5},{4,2},{5,3},{6,0},{7,1},{8,14},{9,15},{10,... | collective-permute-start | bytes 1572872 | tf_op jit(solution)/shard_map/ppermute | solution.py:363
  43.8 9.0 %collective-permute-done.12 = bf16[512,256]{1,0:T(8,128)(2,1)S(1)} collective-permute-done((bf16[512,256]{1,0:T(8,128)(2,1)S(1)}, bf16[512,256]{1,0:T(8,128)(2,1)S(1)}, u32[]{:S(2)}, u32[]{:S(2)}) %collective-permute-start.12) | collective-permute-done | bytes 262176 | tf_op jit(solution)/shard_map/ppermute | solution.py:363
  52.8 0.9 collective-permute-start.14
  53.7 7.0 %collective-permute-done.9 = bf16[512,256]{1,0:T(8,128)(2,1)S(1)} collective-permute-done((bf16[512,256]{1,0:T(8,128)(2,1)S(1)}, bf16[512,256]{1,0:T(8,128)(2,1)S(1)}, u32[]{:S(2)}, u32[]{:S(2)}) %collective-permute-start.9) | collective-permute-done | bytes 262176 | tf_op jit(solution)/shard_map/ppermute | solution.py:363
  60.7 5.1 %collective-permute-start.13 = (bf16[768,256]{1,0:T(8,128)(2,1)S(1)}, bf16[768,256]{1,0:T(8,128)(2,1)S(1)}, u32[]{:S(2)}, u32[]{:S(2)}) collective-permute-start(bf16[768,256]{1,0:T(8,128)(2,1)S(1)} %get-tuple-element.60), channel_id=1, source_target_pairs={{0,8},{1,9},{2,10},{3,11},{4,12},{5,13},{6,14},{7,15},{8,0},{9,1},... | collective-permute-start | bytes 1179656 | tf_op jit(solution)/shard_map/ppermute | solution.py:363
  65.7 0.6 collective-permute-start.10
  66.3 0.0 collective-permute-done.7
  66.3 1.5 %collective-permute-start.8 = (bf16[512,256]{1,0:T(8,128)(2,1)S(1)}, bf16[512,256]{1,0:T(8,128)(2,1)S(1)}, u32[]{:S(2)}, u32[]{:S(2)}) collective-permute-start(bf16[512,256]{1,0:T(8,128)(2,1)S(1)} %get-tuple-element.50), channel_id=1, source_target_pairs={{0,2},{1,3},{2,0},{3,1},{4,6},{5,7},{6,4},{7,5},{8,10},{9,11},{10,... | collective-permute-start | bytes 786440 | tf_op jit(solution)/shard_map/ppermute | solution.py:363
  67.8 1.7 %place_early.1 = (bf16[8,8,128,256]{3,2,1,0:T(8,128)(2,1)}, s32[3]{0:T(128)S(1)}) custom-call(bf16[264,256]{1,0:T(8,128)(2,1)S(1)} %collective-permute-done.1.refs_0_, bf16[520,256]{1,0:T(8,128)(2,1)S(1)} %collective-permute-done.2.refs_1_, bf16[520,256]{1,0:T(8,128)(2,1)S(1)} %collective-permute-done.4.refs_2_), custom_call_target="tpu_custom_call" | custom-call | tf_op jit(solution)/shard_map/place_early/pallas_call | solution.py:496
  69.5 6.5 %collective-permute-done.10 = bf16[512,256]{1,0:T(8,128)(2,1)S(1)} collective-permute-done((bf16[512,256]{1,0:T(8,128)(2,1)S(1)}, bf16[512,256]{1,0:T(8,128)(2,1)S(1)}, u32[]{:S(2)}, u32[]{:S(2)}) %collective-permute-start.10) | collective-permute-done | bytes 262176 | tf_op jit(solution)/shard_map/ppermute | solution.py:363
  76.0 0.0 collective-permute-done.11
  76.0 4.3 %collective-permute-done.8 = bf16[512,256]{1,0:T(8,128)(2,1)S(1)} collective-permute-done((bf16[512,256]{1,0:T(8,128)(2,1)S(1)}, bf16[512,256]{1,0:T(8,128)(2,1)S(1)}, u32[]{:S(2)}, u32[]{:S(2)}) %collective-permute-start.8) | collective-permute-done | bytes 262176 | tf_op jit(solution)/shard_map/ppermute | solution.py:363
  80.2 2.0 %place_mid.1.refs_0_ = bf16[8,8,128,256]{3,2,1,0:T(8,128)(2,1)} custom-call(bf16[8,8,128,256]{3,2,1,0:T(8,128)(2,1)} %get-tuple-element.42.refs_0_, s32[3]{0:T(128)S(1)} %get-tuple-element.43.refs_1_, bf16[8,128,256]{2,1,0:T(8,128)(2,1)S(1)} %bitcast.16, bf16[4,128,256]{2,1,0:T(8,128)(2,1)S(1)} %bitcast.24, ...), custom_call_target="tpu_custom_call", output_to_operand_aliasing={{}: (0, {})} | custom-call | tf_op jit(solution)/shard_map/place_mid/pallas_call | solution.py:523
  82.2 2.0 %collective-permute-done.14 = bf16[1024,256]{1,0:T(8,128)(2,1)S(1)} collective-permute-done((bf16[1024,256]{1,0:T(8,128)(2,1)S(1)}, bf16[1024,256]{1,0:T(8,128)(2,1)S(1)}, u32[]{:S(2)}, u32[]{:S(2)}) %collective-permute-start.14) | collective-permute-done | bytes 524320 | tf_op jit(solution)/shard_map/ppermute | solution.py:363
  84.2 15.5 %collective-permute-done.13 = bf16[768,256]{1,0:T(8,128)(2,1)S(1)} collective-permute-done((bf16[768,256]{1,0:T(8,128)(2,1)S(1)}, bf16[768,256]{1,0:T(8,128)(2,1)S(1)}, u32[]{:S(2)}, u32[]{:S(2)}) %collective-permute-start.13) | collective-permute-done | bytes 393248 | tf_op jit(solution)/shard_map/ppermute | solution.py:363
  99.7 1.5 %place_last.1 = bf16[8,8,128,256]{3,2,1,0:T(8,128)(2,1)} custom-call(bf16[8,8,128,256]{3,2,1,0:T(8,128)(2,1)} %place_mid.1.refs_0_, s32[3]{0:T(128)S(1)} %get-tuple-element.43.refs_1_, bf16[6,128,256]{2,1,0:T(8,128)(2,1)S(1)} %bitcast.20, bf16[8,128,256]{2,1,0:T(8,128)(2,1)S(1)} %bitcast.18), custom_call_target="tpu_custom_call", output_to_operand_aliasing={{}: (0, {})} | custom-call | tf_op jit(solution)/shard_map/place_last/pallas_call | solution.py:523
  (1 shorter events, 0.0 us)
Async XLA Ops:
  0.7 4.5 %collective-permute-start = (s32[4]{0:T(128)S(1)}, s32[4]{0:T(128)S(1)}, u32[]{:S(2)}, u32[]{:S(2)}) collective-permute-start(s32[4]{0:T(128)S(1)} %bitcast_add_fusion.refs_0_.heads), channel_id=1, source_target_pairs={{0,16},{16,0},{1,17},{17,1},{2,18},{18,2},{3,19},{19,3},{4,20},{20... | collective-permute-start | bytes 56 | tf_op jit(solution)/shard_map/ppermute | solution.py:367
  4.9 10.3 %copy-start = (s32[1,4,8]{2,1,0:T(4,128)S(1)}, s32[1,4,8]{2,1,0:T(4,128)}, u32[]{:S(2)}) copy-start(s32[1,4,8]{2,1,0:T(4,128)} %param.10) | copy-start | bytes 388
  4.9 10.3 %copy-start.1 = (s32[1,4,8]{2,1,0:T(4,128)S(1)}, s32[1,4,8]{2,1,0:T(4,128)}, u32[]{:S(2)}) copy-start(s32[1,4,8]{2,1,0:T(4,128)} %param.11) | copy-start | bytes 388
  6.3 19.2 %collective-permute-start.1 = (bf16[264,256]{1,0:T(8,128)(2,1)S(1)}, bf16[264,256]{1,0:T(8,128)(2,1)S(1)}, u32[]{:S(2)}, u32[]{:S(2)}) collective-permute-start(bf16[264,256]{1,0:T(8,128)(2,1)S(1)} %get-tuple-element.36), channel_id=1, source_target_pairs={{0,8},{1,9},{2,10},{3,11},{4,12},{5,13},{6,14},{7,15},{8,0},{9,1},... | collective-permute-start | bytes 405512 | tf_op jit(solution)/shard_map/ppermute | solution.py:363
  9.4 25.3 %collective-permute-start.2 = (bf16[520,256]{1,0:T(8,128)(2,1)S(1)}, bf16[520,256]{1,0:T(8,128)(2,1)S(1)}, u32[]{:S(2)}, u32[]{:S(2)}) collective-permute-start(bf16[520,256]{1,0:T(8,128)(2,1)S(1)} %get-tuple-element.37), channel_id=1, source_target_pairs={{0,10},{1,11},{2,8},{3,9},{4,14},{5,15},{6,12},{7,13},{8,2},{9,3},... | collective-permute-start | bytes 798728 | tf_op jit(solution)/shard_map/ppermute | solution.py:363
  13.1 15.9 %collective-permute-start.5 = (bf16[128,1024]{1,0:T(8,128)(2,1)S(1)}, bf16[128,1024]{1,0:T(8,128)(2,1)S(1)}, u32[]{:S(2)}, u32[]{:S(2)}) collective-permute-start(bf16[128,1024]{1,0:T(8,128)(2,1)S(1)} %get-tuple-element.44), channel_id=1, source_target_pairs={{0,16},{16,0},{1,17},{17,1},{2,18},{18,2},{3,19},{19,3},{4,20},{20... | collective-permute-start | bytes 786440 | tf_op jit(solution)/shard_map/ppermute | solution.py:367
  14.8 14.2 %collective-permute-start.6 = (bf16[128,1024]{1,0:T(8,128)(2,1)S(1)}, bf16[128,1024]{1,0:T(8,128)(2,1)S(1)}, u32[]{:S(2)}, u32[]{:S(2)}) collective-permute-start(bf16[128,1024]{1,0:T(8,128)(2,1)S(1)} %get-tuple-element.45), channel_id=1, source_target_pairs={{0,16},{16,0},{1,17},{17,1},{2,18},{18,2},{3,19},{19,3},{4,20},{20... | collective-permute-start | bytes 786440 | tf_op jit(solution)/shard_map/ppermute | solution.py:367
  15.2 10.2 %collective-permute-start.3 = (s32[4,8]{1,0:T(4,128)S(1)}, s32[4,8]{1,0:T(4,128)S(1)}, u32[]{:S(2)}, u32[]{:S(2)}) collective-permute-start(s32[4,8]{1,0:T(4,128)S(1)} %add_bitcast_fusion.refs_2_), channel_id=1, source_target_pairs={{0,16},{16,0},{1,17},{17,1},{2,18},{18,2},{3,19},{19,3},{4,20},{20... | collective-permute-start | bytes 392 | tf_op jit(solution)/shard_map/ppermute | solution.py:367
  25.4 11.0 %collective-permute-start.4 = (bf16[520,256]{1,0:T(8,128)(2,1)S(1)}, bf16[520,256]{1,0:T(8,128)(2,1)S(1)}, u32[]{:S(2)}, u32[]{:S(2)}) collective-permute-start(bf16[520,256]{1,0:T(8,128)(2,1)S(1)} %get-tuple-element.41), channel_id=1, source_target_pairs={{0,14},{1,15},{2,12},{3,13},{4,10},{5,11},{6,8},{7,9},{8,6},{9,7},... | collective-permute-start | bytes 798728 | tf_op jit(solution)/shard_map/ppermute | solution.py:363
  34.7 31.6 %collective-permute-start.7 = (bf16[1024,256]{1,0:T(8,128)(2,1)S(1)}, bf16[1024,256]{1,0:T(8,128)(2,1)S(1)}, u32[]{:S(2)}, u32[]{:S(2)}) collective-permute-start(bf16[1024,256]{1,0:T(8,128)(2,1)S(1)} %get-tuple-element.49), channel_id=1, source_target_pairs={{0,4},{1,5},{2,6},{3,7},{4,0},{5,1},{6,2},{7,3},{8,12},{9,13},{10,... | collective-permute-start | bytes 1572872 | tf_op jit(solution)/shard_map/ppermute | solution.py:363
  34.8 18.0 %collective-permute-start.12 = (bf16[512,256]{1,0:T(8,128)(2,1)S(1)}, bf16[512,256]{1,0:T(8,128)(2,1)S(1)}, u32[]{:S(2)}, u32[]{:S(2)}) collective-permute-start(bf16[512,256]{1,0:T(8,128)(2,1)S(1)} %get-tuple-element.58), channel_id=1, source_target_pairs={{0,10},{1,11},{2,8},{3,9},{4,14},{5,15},{6,12},{7,13},{8,2},{9,3},... | collective-permute-start | bytes 786440 | tf_op jit(solution)/shard_map/ppermute | solution.py:363
  36.5 24.2 %collective-permute-start.9 = (bf16[512,256]{1,0:T(8,128)(2,1)S(1)}, bf16[512,256]{1,0:T(8,128)(2,1)S(1)}, u32[]{:S(2)}, u32[]{:S(2)}) collective-permute-start(bf16[512,256]{1,0:T(8,128)(2,1)S(1)} %get-tuple-element.53), channel_id=1, source_target_pairs={{0,14},{1,15},{2,12},{3,13},{4,10},{5,11},{6,8},{7,9},{8,6},{9,7},... | collective-permute-start | bytes 786440 | tf_op jit(solution)/shard_map/ppermute | solution.py:363
  40.1 35.9 %collective-permute-start.11 = (bf16[1024,256]{1,0:T(8,128)(2,1)S(1)}, bf16[1024,256]{1,0:T(8,128)(2,1)S(1)}, u32[]{:S(2)}, u32[]{:S(2)}) collective-permute-start(bf16[1024,256]{1,0:T(8,128)(2,1)S(1)} %get-tuple-element.56), channel_id=1, source_target_pairs={{0,6},{1,7},{2,4},{3,5},{4,2},{5,3},{6,0},{7,1},{8,14},{9,15},{10,... | collective-permute-start | bytes 1572872 | tf_op jit(solution)/shard_map/ppermute | solution.py:363
  52.8 31.4 %collective-permute-start.14 = (bf16[1024,256]{1,0:T(8,128)(2,1)S(1)}, bf16[1024,256]{1,0:T(8,128)(2,1)S(1)}, u32[]{:S(2)}, u32[]{:S(2)}) collective-permute-start(bf16[1024,256]{1,0:T(8,128)(2,1)S(1)} %get-tuple-element.62), channel_id=1, source_target_pairs={{0,12},{1,13},{2,14},{3,15},{4,8},{5,9},{6,10},{7,11},{8,4},{9,5},... | collective-permute-start | bytes 1572872 | tf_op jit(solution)/shard_map/ppermute | solution.py:363
  60.7 39.0 %collective-permute-start.13 = (bf16[768,256]{1,0:T(8,128)(2,1)S(1)}, bf16[768,256]{1,0:T(8,128)(2,1)S(1)}, u32[]{:S(2)}, u32[]{:S(2)}) collective-permute-start(bf16[768,256]{1,0:T(8,128)(2,1)S(1)} %get-tuple-element.60), channel_id=1, source_target_pairs={{0,8},{1,9},{2,10},{3,11},{4,12},{5,13},{6,14},{7,15},{8,0},{9,1},... | collective-permute-start | bytes 1179656 | tf_op jit(solution)/shard_map/ppermute | solution.py:363
  65.7 10.2 %collective-permute-start.10 = (bf16[512,256]{1,0:T(8,128)(2,1)S(1)}, bf16[512,256]{1,0:T(8,128)(2,1)S(1)}, u32[]{:S(2)}, u32[]{:S(2)}) collective-permute-start(bf16[512,256]{1,0:T(8,128)(2,1)S(1)} %get-tuple-element.54), channel_id=1, source_target_pairs={{0,2},{1,3},{2,0},{3,1},{4,6},{5,7},{6,4},{7,5},{8,10},{9,11},{10,... | collective-permute-start | bytes 786440 | tf_op jit(solution)/shard_map/ppermute | solution.py:363
  66.3 13.9 %collective-permute-start.8 = (bf16[512,256]{1,0:T(8,128)(2,1)S(1)}, bf16[512,256]{1,0:T(8,128)(2,1)S(1)}, u32[]{:S(2)}, u32[]{:S(2)}) collective-permute-start(bf16[512,256]{1,0:T(8,128)(2,1)S(1)} %get-tuple-element.50), channel_id=1, source_target_pairs={{0,2},{1,3},{2,0},{3,1},{4,6},{5,7},{6,4},{7,5},{8,10},{9,11},{10,... | collective-permute-start | bytes 786440 | tf_op jit(solution)/shard_map/ppermute | solution.py:363

commit v12 on v11

--- a/solution.py
+++ b/solution.py
@@ -31,7 +31,7 @@
         self.width = self.col_groups * self.block
         self.capacity = max(self.slots // 4, self.slots // self.groups)
         self.first = max(0, self.rows - self.capacity * self.groups)
-        self.early = {4: self.first // 2, 5: self.first, 7: self.first}
+        self.early = {4: 3 * self.first // 4, 5: self.first, 7: self.first}
         self.late = []
         for o in range(GRID_COLS):
             count = self.rows - self.early.get(o, 0)

time: 101 us -> 101 us (level)
  waiting for transfers between devices: 53 us -> 51.4 us
  starting transfers between devices: 31.8 us -> 33.4 us
    ppermute x11, starting transfers between devices: 25.1 us -> 26.7 us  [across(): return lax.ppermute(value, 'wide', pairs)]
    ppermute x11, waiting for transfers between devices: 44.2 us -> 42.5 us  [across(): return lax.ppermute(value, 'wide', pairs)]
  transfers between devices with their start and end apart: 15 -> 15, of which waited for: 8 -> 9; matrix products, arithmetic and copies ran while one was open for 0% -> 0% of each run, Pallas kernels for 13% -> 13%
where the time goes in v12:
time: 101 us
  waiting for transfers between devices  51.4 us (51%)
  starting transfers between devices  33.4 us (33%)
  Pallas kernels  15.5 us (15%)
    ppermute x11, waiting for transfers between devices, across(): return lax.ppermute(value, 'wide', pairs)  42.5 us
    ppermute x11, starting transfers between devices, across(): return lax.ppermute(value, 'wide', pairs)  26.7 us
    ppermute x4, waiting for transfers between devices, along(): lax.ppermute(value, 'front', [(f, (f + steps) % plan.groups) for f in ran...  8.82 us
    ppermute x4, starting transfers between devices, along(): lax.ppermute(value, 'front', [(f, (f + steps) % plan.groups) for f in ran...  6.64 us
    pallas_call x1, Pallas kernels, local(): pl.pallas_call(functools.partial(assemble_kernel, plan), out_shape=[jax.S...  5.58 us
    pallas_call x2, Pallas kernels, place(): pl.pallas_call(body, out_shape=out_shape, in_specs=[HBM] * len(held) + [A...  3.4 us
    pallas_call x1, Pallas kernels, local(): pl.pallas_call(functools.partial(bucket_kernel, plan, tail), out_shape=[j...  2.47 us
  transfers between devices with their start and end apart: 15, of which 9 were waited for; matrix products, arithmetic and copies ran while one was open for 0% of the time, Pallas kernels for 13%

profile of v12, /device:TPU:0, one launch (start us, length us, event | category | flops | bytes accessed | tf_op | source)
XLA Modules:
  0.0 101.1 jit_solution(5964545293264281119)
XLA Ops:
  0.0 0.7 bitcast_add_fusion.refs_0_.heads
  0.7 3.0 %collective-permute-start = (s32[4]{0:T(128)S(1)}, s32[4]{0:T(128)S(1)}, u32[]{:S(2)}, u32[]{:S(2)}) collective-permute-start(s32[4]{0:T(128)S(1)} %bitcast_add_fusion.refs_0_.heads), channel_id=1, source_target_pairs={{0,16},{16,0},{1,17},{17,1},{2,18},{18,2},{3,19},{19,3},{4,20},{20... | collective-permute-start | bytes 56 | tf_op jit(solution)/shard_map/ppermute | solution.py:367
  3.6 1.2 %stage.1 = (bf16[1024,256]{1,0:T(8,128)(2,1)S(1)}, bf16[1024,256]{1,0:T(8,128)(2,1)S(1)}) custom-call(bf16[1,1024,2048]{2,1,0:T(8,128)(2,1)} %refs_4_.1), custom_call_target="tpu_custom_call" | custom-call | tf_op jit(solution)/shard_map/stage/pallas_call | solution.py:391
  4.9 0.0 copy-start
  4.9 0.0 copy-start.1
  4.9 0.2 collective-permute-done.refs_1_
  5.2 1.1 %pack_early.1 = (bf16[392,256]{1,0:T(8,128)(2,1)S(1)}, bf16[520,256]{1,0:T(8,128)(2,1)S(1)}, s32[1]{0:T(128)}) custom-call(s32[4]{0:T(128)S(1)} %bitcast_add_fusion.refs_0_.heads, s32[4]{0:T(128)S(1)} %collective-permute-done.refs_1_, bf16[1024,256]{1,0:T(8,128)(2,1)S(1)} %get-tuple-element.34.refs_2_, bf16[1024,256]{1,0:T(8,128)(2,1)S(1)} %get-tuple-element.35.refs_3_), custom_call_target="tpu_custom_call" | custom-call | tf_op jit(solution)/shard_map/pack_early/pallas_call | solution.py:401
  6.3 3.2 %collective-permute-start.1 = (bf16[392,256]{1,0:T(8,128)(2,1)S(1)}, bf16[392,256]{1,0:T(8,128)(2,1)S(1)}, u32[]{:S(2)}, u32[]{:S(2)}) collective-permute-start(bf16[392,256]{1,0:T(8,128)(2,1)S(1)} %get-tuple-element.36), channel_id=1, source_target_pairs={{0,8},{1,9},{2,10},{3,11},{4,12},{5,13},{6,14},{7,15},{8,0},{9,1},... | collective-permute-start | bytes 602120 | tf_op jit(solution)/shard_map/ppermute | solution.py:363
  9.4 1.3 %collective-permute-start.2 = (bf16[520,256]{1,0:T(8,128)(2,1)S(1)}, bf16[520,256]{1,0:T(8,128)(2,1)S(1)}, u32[]{:S(2)}, u32[]{:S(2)}) collective-permute-start(bf16[520,256]{1,0:T(8,128)(2,1)S(1)} %get-tuple-element.37), channel_id=1, source_target_pairs={{0,10},{1,11},{2,8},{3,9},{4,14},{5,15},{6,12},{7,13},{8,2},{9,3},... | collective-permute-start | bytes 798728 | tf_op jit(solution)/shard_map/ppermute | solution.py:363
  10.7 2.5 %bucket.1 = (bf16[128,1024]{1,0:T(8,128)(2,1)S(1)}, bf16[128,1024]{1,0:T(8,128)(2,1)S(1)}, bf16[520,256]{1,0:T(8,128)(2,1)S(1)}) custom-call(s32[4]{0:T(128)S(1)} %bitcast_add_fusion.refs_0_.heads, s32[1]{0:T(128)} %get-tuple-element.38.refs_0_, bf16[1,512,1024]{2,1,0:T(8,128)(2,1)} %refs_5_.1, bf16[1,1024,2048]{2,1,0:T(8,128)(2,1)} %refs_4_.1), custom_call_target="tpu_custom_call" | custom-call | tf_op jit(solution)/shard_map/bucket/pallas_call | solution.py:415
  13.2 1.6 %collective-permute-start.5 = (bf16[128,1024]{1,0:T(8,128)(2,1)S(1)}, bf16[128,1024]{1,0:T(8,128)(2,1)S(1)}, u32[]{:S(2)}, u32[]{:S(2)}) collective-permute-start(bf16[128,1024]{1,0:T(8,128)(2,1)S(1)} %get-tuple-element.44), channel_id=1, source_target_pairs={{0,16},{16,0},{1,17},{17,1},{2,18},{18,2},{3,19},{19,3},{4,20},{20... | collective-permute-start | bytes 786440 | tf_op jit(solution)/shard_map/ppermute | solution.py:367
  14.8 0.5 collective-permute-start.6
  15.3 0.0 copy-done
  15.3 0.0 copy-done.1
  15.3 1.6 %collective-permute-start.3 = (s32[4,8]{1,0:T(4,128)S(1)}, s32[4,8]{1,0:T(4,128)S(1)}, u32[]{:S(2)}, u32[]{:S(2)}) collective-permute-start(s32[4,8]{1,0:T(4,128)S(1)} %add_bitcast_fusion.refs_2_), channel_id=1, source_target_pairs={{0,16},{16,0},{1,17},{17,1},{2,18},{18,2},{3,19},{19,3},{4,20},{20... | collective-permute-start | bytes 392 | tf_op jit(solution)/shard_map/ppermute | solution.py:367
  16.9 8.6 %collective-permute-done.3.refs_3_ = s32[4,8]{1,0:T(4,128)S(1)} collective-permute-done((s32[4,8]{1,0:T(4,128)S(1)}, s32[4,8]{1,0:T(4,128)S(1)}, u32[]{:S(2)}, u32[]{:S(2)}) %collective-permute-start.3) | collective-permute-done | bytes 160 | tf_op jit(solution)/shard_map/ppermute | solution.py:367
  25.4 0.0 collective-permute-done.1.refs_0_
  25.4 3.5 %collective-permute-start.4 = (bf16[520,256]{1,0:T(8,128)(2,1)S(1)}, bf16[520,256]{1,0:T(8,128)(2,1)S(1)}, u32[]{:S(2)}, u32[]{:S(2)}) collective-permute-start(bf16[520,256]{1,0:T(8,128)(2,1)S(1)} %get-tuple-element.41), channel_id=1, source_target_pairs={{0,14},{1,15},{2,12},{3,13},{4,10},{5,11},{6,8},{7,9},{8,6},{9,7},... | collective-permute-start | bytes 798728 | tf_op jit(solution)/shard_map/ppermute | solution.py:363
  29.0 0.0 collective-permute-done.5.refs_6_
  29.0 0.0 collective-permute-done.6.refs_7_
  29.0 5.6 %assemble.1 = (bf16[1024,256]{1,0:T(8,128)(2,1)S(1)}, bf16[512,256]{1,0:T(8,128)(2,1)S(1)}, bf16[512,256]{1,0:T(8,128)(2,1)S(1)}, bf16[1024,256]{1,0:T(8,128)(2,...) custom-call(s32[4]{0:T(128)S(1)} %bitcast_add_fusion.refs_0_.heads, ...), custom_call_target="tpu_custom_call" | custom-call | tf_op jit(solution)/shard_map/assemble/pallas_call | solution.py:441
  34.6 2.4 %collective-permute-done.2.refs_1_ = bf16[520,256]{1,0:T(8,128)(2,1)S(1)} collective-permute-done((bf16[520,256]{1,0:T(8,128)(2,1)S(1)}, bf16[520,256]{1,0:T(8,128)(2,1)S(1)}, u32[]{:S(2)}, u32[]{:S(2)}) %collective-permute-start.2) | collective-permute-done | bytes 266272 | tf_op jit(solution)/shard_map/ppermute | solution.py:363
  37.0 0.0 collective-permute-start.7
  37.0 2.9 %collective-permute-start.12 = (bf16[512,256]{1,0:T(8,128)(2,1)S(1)}, bf16[512,256]{1,0:T(8,128)(2,1)S(1)}, u32[]{:S(2)}, u32[]{:S(2)}) collective-permute-start(bf16[512,256]{1,0:T(8,128)(2,1)S(1)} %get-tuple-element.58), channel_id=1, source_target_pairs={{0,10},{1,11},{2,8},{3,9},{4,14},{5,15},{6,12},{7,13},{8,2},{9,3},... | collective-permute-start | bytes 786440 | tf_op jit(solution)/shard_map/ppermute | solution.py:363
  39.9 0.0 collective-permute-done.4.refs_2_
  39.9 2.3 %collective-permute-start.9 = (bf16[512,256]{1,0:T(8,128)(2,1)S(1)}, bf16[512,256]{1,0:T(8,128)(2,1)S(1)}, u32[]{:S(2)}, u32[]{:S(2)}) collective-permute-start(bf16[512,256]{1,0:T(8,128)(2,1)S(1)} %get-tuple-element.53), channel_id=1, source_target_pairs={{0,14},{1,15},{2,12},{3,13},{4,10},{5,11},{6,8},{7,9},{8,6},{9,7},... | collective-permute-start | bytes 786440 | tf_op jit(solution)/shard_map/ppermute | solution.py:363
  42.3 3.4 %collective-permute-start.11 = (bf16[1024,256]{1,0:T(8,128)(2,1)S(1)}, bf16[1024,256]{1,0:T(8,128)(2,1)S(1)}, u32[]{:S(2)}, u32[]{:S(2)}) collective-permute-start(bf16[1024,256]{1,0:T(8,128)(2,1)S(1)} %get-tuple-element.56), channel_id=1, source_target_pairs={{0,6},{1,7},{2,4},{3,5},{4,2},{5,3},{6,0},{7,1},{8,14},{9,15},{10,... | collective-permute-start | bytes 1572872 | tf_op jit(solution)/shard_map/ppermute | solution.py:363
  45.7 9.4 %collective-permute-done.12 = bf16[512,256]{1,0:T(8,128)(2,1)S(1)} collective-permute-done((bf16[512,256]{1,0:T(8,128)(2,1)S(1)}, bf16[512,256]{1,0:T(8,128)(2,1)S(1)}, u32[]{:S(2)}, u32[]{:S(2)}) %collective-permute-start.12) | collective-permute-done | bytes 262176 | tf_op jit(solution)/shard_map/ppermute | solution.py:363
  55.0 2.3 %collective-permute-start.14 = (bf16[1024,256]{1,0:T(8,128)(2,1)S(1)}, bf16[1024,256]{1,0:T(8,128)(2,1)S(1)}, u32[]{:S(2)}, u32[]{:S(2)}) collective-permute-start(bf16[1024,256]{1,0:T(8,128)(2,1)S(1)} %get-tuple-element.62), channel_id=1, source_target_pairs={{0,12},{1,13},{2,14},{3,15},{4,8},{5,9},{6,10},{7,11},{8,4},{9,5},... | collective-permute-start | bytes 1572872 | tf_op jit(solution)/shard_map/ppermute | solution.py:363
  57.4 6.1 %collective-permute-done.9 = bf16[512,256]{1,0:T(8,128)(2,1)S(1)} collective-permute-done((bf16[512,256]{1,0:T(8,128)(2,1)S(1)}, bf16[512,256]{1,0:T(8,128)(2,1)S(1)}, u32[]{:S(2)}, u32[]{:S(2)}) %collective-permute-start.9) | collective-permute-done | bytes 262176 | tf_op jit(solution)/shard_map/ppermute | solution.py:363
  63.4 5.8 %collective-permute-start.13 = (bf16[640,256]{1,0:T(8,128)(2,1)S(1)}, bf16[640,256]{1,0:T(8,128)(2,1)S(1)}, u32[]{:S(2)}, u32[]{:S(2)}) collective-permute-start(bf16[640,256]{1,0:T(8,128)(2,1)S(1)} %get-tuple-element.60), channel_id=1, source_target_pairs={{0,8},{1,9},{2,10},{3,11},{4,12},{5,13},{6,14},{7,15},{8,0},{9,1},... | collective-permute-start | bytes 983048 | tf_op jit(solution)/shard_map/ppermute | solution.py:363
  69.2 0.0 collective-permute-start.10
  69.2 0.0 collective-permute-done.7
  69.2 2.0 %collective-permute-start.8 = (bf16[512,256]{1,0:T(8,128)(2,1)S(1)}, bf16[512,256]{1,0:T(8,128)(2,1)S(1)}, u32[]{:S(2)}, u32[]{:S(2)}) collective-permute-start(bf16[512,256]{1,0:T(8,128)(2,1)S(1)} %get-tuple-element.50), channel_id=1, source_target_pairs={{0,2},{1,3},{2,0},{3,1},{4,6},{5,7},{6,4},{7,5},{8,10},{9,11},{10,... | collective-permute-start | bytes 786440 | tf_op jit(solution)/shard_map/ppermute | solution.py:363
  71.3 1.7 %place_early.1 = (bf16[8,8,128,256]{3,2,1,0:T(8,128)(2,1)}, s32[3]{0:T(128)S(1)}) custom-call(bf16[392,256]{1,0:T(8,128)(2,1)S(1)} %collective-permute-done.1.refs_0_, bf16[520,256]{1,0:T(8,128)(2,1)S(1)} %collective-permute-done.2.refs_1_, bf16[520,256]{1,0:T(8,128)(2,1)S(1)} %collective-permute-done.4.refs_2_), custom_call_target="tpu_custom_call" | custom-call | tf_op jit(solution)/shard_map/place_early/pallas_call | solution.py:496
  73.0 5.5 %collective-permute-done.10 = bf16[512,256]{1,0:T(8,128)(2,1)S(1)} collective-permute-done((bf16[512,256]{1,0:T(8,128)(2,1)S(1)}, bf16[512,256]{1,0:T(8,128)(2,1)S(1)}, u32[]{:S(2)}, u32[]{:S(2)}) %collective-permute-start.10) | collective-permute-done | bytes 262176 | tf_op jit(solution)/shard_map/ppermute | solution.py:363
  78.5 0.0 collective-permute-done.11
  78.5 3.9 %collective-permute-done.8 = bf16[512,256]{1,0:T(8,128)(2,1)S(1)} collective-permute-done((bf16[512,256]{1,0:T(8,128)(2,1)S(1)}, bf16[512,256]{1,0:T(8,128)(2,1)S(1)}, u32[]{:S(2)}, u32[]{:S(2)}) %collective-permute-start.8) | collective-permute-done | bytes 262176 | tf_op jit(solution)/shard_map/ppermute | solution.py:363
  82.4 2.0 %place_mid.1.refs_0_ = bf16[8,8,128,256]{3,2,1,0:T(8,128)(2,1)} custom-call(bf16[8,8,128,256]{3,2,1,0:T(8,128)(2,1)} %get-tuple-element.42.refs_0_, s32[3]{0:T(128)S(1)} %get-tuple-element.43.refs_1_, bf16[8,128,256]{2,1,0:T(8,128)(2,1)S(1)} %bitcast.16, bf16[4,128,256]{2,1,0:T(8,128)(2,1)S(1)} %bitcast.24, ...), custom_call_target="tpu_custom_call", output_to_operand_aliasing={{}: (0, {})} | custom-call | tf_op jit(solution)/shard_map/place_mid/pallas_call | solution.py:523
  84.4 3.4 %collective-permute-done.14 = bf16[1024,256]{1,0:T(8,128)(2,1)S(1)} collective-permute-done((bf16[1024,256]{1,0:T(8,128)(2,1)S(1)}, bf16[1024,256]{1,0:T(8,128)(2,1)S(1)}, u32[]{:S(2)}, u32[]{:S(2)}) %collective-permute-start.14) | collective-permute-done | bytes 524320 | tf_op jit(solution)/shard_map/ppermute | solution.py:363
  87.8 11.9 %collective-permute-done.13 = bf16[640,256]{1,0:T(8,128)(2,1)S(1)} collective-permute-done((bf16[640,256]{1,0:T(8,128)(2,1)S(1)}, bf16[640,256]{1,0:T(8,128)(2,1)S(1)}, u32[]{:S(2)}, u32[]{:S(2)}) %collective-permute-start.13) | collective-permute-done | bytes 327712 | tf_op jit(solution)/shard_map/ppermute | solution.py:363
  99.6 1.4 %place_last.1 = bf16[8,8,128,256]{3,2,1,0:T(8,128)(2,1)} custom-call(bf16[8,8,128,256]{3,2,1,0:T(8,128)(2,1)} %place_mid.1.refs_0_, s32[3]{0:T(128)S(1)} %get-tuple-element.43.refs_1_, bf16[5,128,256]{2,1,0:T(8,128)(2,1)S(1)} %bitcast.20, bf16[8,128,256]{2,1,0:T(8,128)(2,1)S(1)} %bitcast.18), custom_call_target="tpu_custom_call", output_to_operand_aliasing={{}: (0, {})} | custom-call | tf_op jit(solution)/shard_map/place_last/pallas_call | solution.py:523
  (1 shorter events, 0.0 us)
Async XLA Ops:
  0.7 4.5 %collective-permute-start = (s32[4]{0:T(128)S(1)}, s32[4]{0:T(128)S(1)}, u32[]{:S(2)}, u32[]{:S(2)}) collective-permute-start(s32[4]{0:T(128)S(1)} %bitcast_add_fusion.refs_0_.heads), channel_id=1, source_target_pairs={{0,16},{16,0},{1,17},{17,1},{2,18},{18,2},{3,19},{19,3},{4,20},{20... | collective-permute-start | bytes 56 | tf_op jit(solution)/shard_map/ppermute | solution.py:367
  4.9 10.4 %copy-start = (s32[1,4,8]{2,1,0:T(4,128)S(1)}, s32[1,4,8]{2,1,0:T(4,128)}, u32[]{:S(2)}) copy-start(s32[1,4,8]{2,1,0:T(4,128)} %param.10) | copy-start | bytes 388
  4.9 10.4 %copy-start.1 = (s32[1,4,8]{2,1,0:T(4,128)S(1)}, s32[1,4,8]{2,1,0:T(4,128)}, u32[]{:S(2)}) copy-start(s32[1,4,8]{2,1,0:T(4,128)} %param.11) | copy-start | bytes 388
  6.3 19.2 %collective-permute-start.1 = (bf16[392,256]{1,0:T(8,128)(2,1)S(1)}, bf16[392,256]{1,0:T(8,128)(2,1)S(1)}, u32[]{:S(2)}, u32[]{:S(2)}) collective-permute-start(bf16[392,256]{1,0:T(8,128)(2,1)S(1)} %get-tuple-element.36), channel_id=1, source_target_pairs={{0,8},{1,9},{2,10},{3,11},{4,12},{5,13},{6,14},{7,15},{8,0},{9,1},... | collective-permute-start | bytes 602120 | tf_op jit(solution)/shard_map/ppermute | solution.py:363
  9.4 27.5 %collective-permute-start.2 = (bf16[520,256]{1,0:T(8,128)(2,1)S(1)}, bf16[520,256]{1,0:T(8,128)(2,1)S(1)}, u32[]{:S(2)}, u32[]{:S(2)}) collective-permute-start(bf16[520,256]{1,0:T(8,128)(2,1)S(1)} %get-tuple-element.37), channel_id=1, source_target_pairs={{0,10},{1,11},{2,8},{3,9},{4,14},{5,15},{6,12},{7,13},{8,2},{9,3},... | collective-permute-start | bytes 798728 | tf_op jit(solution)/shard_map/ppermute | solution.py:363
  13.2 15.8 %collective-permute-start.5 = (bf16[128,1024]{1,0:T(8,128)(2,1)S(1)}, bf16[128,1024]{1,0:T(8,128)(2,1)S(1)}, u32[]{:S(2)}, u32[]{:S(2)}) collective-permute-start(bf16[128,1024]{1,0:T(8,128)(2,1)S(1)} %get-tuple-element.44), channel_id=1, source_target_pairs={{0,16},{16,0},{1,17},{17,1},{2,18},{18,2},{3,19},{19,3},{4,20},{20... | collective-permute-start | bytes 786440 | tf_op jit(solution)/shard_map/ppermute | solution.py:367
  14.8 14.2 %collective-permute-start.6 = (bf16[128,1024]{1,0:T(8,128)(2,1)S(1)}, bf16[128,1024]{1,0:T(8,128)(2,1)S(1)}, u32[]{:S(2)}, u32[]{:S(2)}) collective-permute-start(bf16[128,1024]{1,0:T(8,128)(2,1)S(1)} %get-tuple-element.45), channel_id=1, source_target_pairs={{0,16},{16,0},{1,17},{17,1},{2,18},{18,2},{3,19},{19,3},{4,20},{20... | collective-permute-start | bytes 786440 | tf_op jit(solution)/shard_map/ppermute | solution.py:367
  15.3 10.2 %collective-permute-start.3 = (s32[4,8]{1,0:T(4,128)S(1)}, s32[4,8]{1,0:T(4,128)S(1)}, u32[]{:S(2)}, u32[]{:S(2)}) collective-permute-start(s32[4,8]{1,0:T(4,128)S(1)} %add_bitcast_fusion.refs_2_), channel_id=1, source_target_pairs={{0,16},{16,0},{1,17},{17,1},{2,18},{18,2},{3,19},{19,3},{4,20},{20... | collective-permute-start | bytes 392 | tf_op jit(solution)/shard_map/ppermute | solution.py:367
  25.4 14.5 %collective-permute-start.4 = (bf16[520,256]{1,0:T(8,128)(2,1)S(1)}, bf16[520,256]{1,0:T(8,128)(2,1)S(1)}, u32[]{:S(2)}, u32[]{:S(2)}) collective-permute-start(bf16[520,256]{1,0:T(8,128)(2,1)S(1)} %get-tuple-element.41), channel_id=1, source_target_pairs={{0,14},{1,15},{2,12},{3,13},{4,10},{5,11},{6,8},{7,9},{8,6},{9,7},... | collective-permute-start | bytes 798728 | tf_op jit(solution)/shard_map/ppermute | solution.py:363
  37.0 32.2 %collective-permute-start.7 = (bf16[1024,256]{1,0:T(8,128)(2,1)S(1)}, bf16[1024,256]{1,0:T(8,128)(2,1)S(1)}, u32[]{:S(2)}, u32[]{:S(2)}) collective-permute-start(bf16[1024,256]{1,0:T(8,128)(2,1)S(1)} %get-tuple-element.49), channel_id=1, source_target_pairs={{0,4},{1,5},{2,6},{3,7},{4,0},{5,1},{6,2},{7,3},{8,12},{9,13},{10,... | collective-permute-start | bytes 1572872 | tf_op jit(solution)/shard_map/ppermute | solution.py:363
  37.0 18.0 %collective-permute-start.12 = (bf16[512,256]{1,0:T(8,128)(2,1)S(1)}, bf16[512,256]{1,0:T(8,128)(2,1)S(1)}, u32[]{:S(2)}, u32[]{:S(2)}) collective-permute-start(bf16[512,256]{1,0:T(8,128)(2,1)S(1)} %get-tuple-element.58), channel_id=1, source_target_pairs={{0,10},{1,11},{2,8},{3,9},{4,14},{5,15},{6,12},{7,13},{8,2},{9,3},... | collective-permute-start | bytes 786440 | tf_op jit(solution)/shard_map/ppermute | solution.py:363
  39.9 23.5 %collective-permute-start.9 = (bf16[512,256]{1,0:T(8,128)(2,1)S(1)}, bf16[512,256]{1,0:T(8,128)(2,1)S(1)}, u32[]{:S(2)}, u32[]{:S(2)}) collective-permute-start(bf16[512,256]{1,0:T(8,128)(2,1)S(1)} %get-tuple-element.53), channel_id=1, source_target_pairs={{0,14},{1,15},{2,12},{3,13},{4,10},{5,11},{6,8},{7,9},{8,6},{9,7},... | collective-permute-start | bytes 786440 | tf_op jit(solution)/shard_map/ppermute | solution.py:363
  42.3 36.2 %collective-permute-start.11 = (bf16[1024,256]{1,0:T(8,128)(2,1)S(1)}, bf16[1024,256]{1,0:T(8,128)(2,1)S(1)}, u32[]{:S(2)}, u32[]{:S(2)}) collective-permute-start(bf16[1024,256]{1,0:T(8,128)(2,1)S(1)} %get-tuple-element.56), channel_id=1, source_target_pairs={{0,6},{1,7},{2,4},{3,5},{4,2},{5,3},{6,0},{7,1},{8,14},{9,15},{10,... | collective-permute-start | bytes 1572872 | tf_op jit(solution)/shard_map/ppermute | solution.py:363
  55.0 32.7 %collective-permute-start.14 = (bf16[1024,256]{1,0:T(8,128)(2,1)S(1)}, bf16[1024,256]{1,0:T(8,128)(2,1)S(1)}, u32[]{:S(2)}, u32[]{:S(2)}) collective-permute-start(bf16[1024,256]{1,0:T(8,128)(2,1)S(1)} %get-tuple-element.62), channel_id=1, source_target_pairs={{0,12},{1,13},{2,14},{3,15},{4,8},{5,9},{6,10},{7,11},{8,4},{9,5},... | collective-permute-start | bytes 1572872 | tf_op jit(solution)/shard_map/ppermute | solution.py:363
  63.4 36.2 %collective-permute-start.13 = (bf16[640,256]{1,0:T(8,128)(2,1)S(1)}, bf16[640,256]{1,0:T(8,128)(2,1)S(1)}, u32[]{:S(2)}, u32[]{:S(2)}) collective-permute-start(bf16[640,256]{1,0:T(8,128)(2,1)S(1)} %get-tuple-element.60), channel_id=1, source_target_pairs={{0,8},{1,9},{2,10},{3,11},{4,12},{5,13},{6,14},{7,15},{8,0},{9,1},... | collective-permute-start | bytes 983048 | tf_op jit(solution)/shard_map/ppermute | solution.py:363
  69.2 9.2 %collective-permute-start.10 = (bf16[512,256]{1,0:T(8,128)(2,1)S(1)}, bf16[512,256]{1,0:T(8,128)(2,1)S(1)}, u32[]{:S(2)}, u32[]{:S(2)}) collective-permute-start(bf16[512,256]{1,0:T(8,128)(2,1)S(1)} %get-tuple-element.54), channel_id=1, source_target_pairs={{0,2},{1,3},{2,0},{3,1},{4,6},{5,7},{6,4},{7,5},{8,10},{9,11},{10,... | collective-permute-start | bytes 786440 | tf_op jit(solution)/shard_map/ppermute | solution.py:363
  69.2 13.2 %collective-permute-start.8 = (bf16[512,256]{1,0:T(8,128)(2,1)S(1)}, bf16[512,256]{1,0:T(8,128)(2,1)S(1)}, u32[]{:S(2)}, u32[]{:S(2)}) collective-permute-start(bf16[512,256]{1,0:T(8,128)(2,1)S(1)} %get-tuple-element.50), channel_id=1, source_target_pairs={{0,2},{1,3},{2,0},{3,1},{4,6},{5,7},{6,4},{7,5},{8,10},{9,11},{10,... | collective-permute-start | bytes 786440 | tf_op jit(solution)/shard_map/ppermute | solution.py:363

commit v13 on v12

--- a/solution.py
+++ b/solution.py
@@ -31,11 +31,11 @@
         self.width = self.col_groups * self.block
         self.capacity = max(self.slots // 4, self.slots // self.groups)
         self.first = max(0, self.rows - self.capacity * self.groups)
-        self.early = {4: 3 * self.first // 4, 5: self.first, 7: self.first}
+        self.early = {6: self.first // 2, 5: self.first, 7: self.first}
         self.late = []
         for o in range(GRID_COLS):
             count = self.rows - self.early.get(o, 0)
-            cuts = [0, count // 2, count] if o == 1 else [0, count]
+            cuts = [0, max(1, 5 * count // 8), count] if o == 1 else [0, count]
             self.late += [(o, lo, hi) for lo, hi in zip(cuts, cuts[1:]) if lo < hi]
 
 
@@ -478,9 +478,9 @@
     def came(*offsets):
         return [first[o] for o in offsets if o in first]
 
-    send_early(4)
+    send_early(6)
     send_early(5)
-    send_early(7, *came(4), *all_codes[1:])
+    send_early(7, *came(6), *all_codes[1:])
     b5 = send(late(5), *came(5))
     b7 = send(late(7), *came(7))
     send(late(6), b5)
@@ -538,7 +538,7 @@
             )(*held, *known, *[arrived[m].reshape(-1, block, width) for m in messages])
         ]
 
-    last = [late(4), late(6)]
+    last = [late(4)]
     held = place(held, [m for m in plan.late if m not in last], "place_mid")
     held = place(held, last, "place_last")
     return held[0].reshape(1, plan.rows * GRID_COLS * block, width)

time: 101 us -> 105 us (1.040)
  the two profiles are of different devices: /device:TPU:0 before, /device:TPU:8 now
where the time goes in v13:
time: 105 us
  waiting for transfers between devices  67.6 us (64%)
  starting transfers between devices  20.9 us (20%)
  Pallas kernels  15.3 us (15%)
    ppermute x11, waiting for transfers between devices, across(): return lax.ppermute(value, 'wide', pairs)  58.1 us
    ppermute x11, starting transfers between devices, across(): return lax.ppermute(value, 'wide', pairs)  15.8 us
    ppermute x4, waiting for transfers between devices, along(): lax.ppermute(value, 'front', [(f, (f + steps) % plan.groups) for f in ran...  9.47 us
    pallas_call x1, Pallas kernels, local(): pl.pallas_call(functools.partial(assemble_kernel, plan), out_shape=[jax.S...  5.7 us
    ppermute x4, starting transfers between devices, along(): lax.ppermute(value, 'front', [(f, (f + steps) % plan.groups) for f in ran...  5.16 us
    pallas_call x2, Pallas kernels, place(): pl.pallas_call(body, out_shape=out_shape, in_specs=[HBM] * len(held) + [A...  3.06 us
    pallas_call x1, Pallas kernels, local(): pl.pallas_call(functools.partial(bucket_kernel, plan, tail), out_shape=[j...  2.47 us
  transfers between devices with their start and end apart: 15, of which 7 were waited for; matrix products, arithmetic and copies ran while one was open for 0% of the time, Pallas kernels for 13%

profile of v13, /device:TPU:8, one launch (start us, length us, event | category | flops | bytes accessed | tf_op | source)
XLA Modules:
  0.0 104.6 jit_solution(1155387315650222222)
XLA Ops:
  0.0 0.7 bitcast_add_fusion.refs_0_.heads
  0.7 1.5 %collective-permute-start = (s32[4]{0:T(128)S(1)}, s32[4]{0:T(128)S(1)}, u32[]{:S(2)}, u32[]{:S(2)}) collective-permute-start(s32[4]{0:T(128)S(1)} %bitcast_add_fusion.refs_0_.heads), channel_id=1, source_target_pairs={{0,16},{16,0},{1,17},{17,1},{2,18},{18,2},{3,19},{19,3},{4,20},{20... | collective-permute-start | bytes 56 | tf_op jit(solution)/shard_map/ppermute | solution.py:367
  2.2 1.2 %stage.1 = (bf16[1024,256]{1,0:T(8,128)(2,1)S(1)}, bf16[1024,256]{1,0:T(8,128)(2,1)S(1)}) custom-call(bf16[1,1024,2048]{2,1,0:T(8,128)(2,1)} %refs_4_.1), custom_call_target="tpu_custom_call" | custom-call | tf_op jit(solution)/shard_map/stage/pallas_call | solution.py:391
  3.4 0.0 copy-start
  3.5 0.0 copy-start.1
  3.5 0.7 collective-permute-done.refs_1_
  4.2 1.1 %pack_early.1 = (bf16[264,256]{1,0:T(8,128)(2,1)S(1)}, bf16[520,256]{1,0:T(8,128)(2,1)S(1)}, s32[1]{0:T(128)}) custom-call(s32[4]{0:T(128)S(1)} %bitcast_add_fusion.refs_0_.heads, s32[4]{0:T(128)S(1)} %collective-permute-done.refs_1_, bf16[1024,256]{1,0:T(8,128)(2,1)S(1)} %get-tuple-element.34.refs_2_, bf16[1024,256]{1,0:T(8,128)(2,1)S(1)} %get-tuple-element.35.refs_3_), custom_call_target="tpu_custom_call" | custom-call | tf_op jit(solution)/shard_map/pack_early/pallas_call | solution.py:401
  5.3 1.6 %collective-permute-start.1 = (bf16[264,256]{1,0:T(8,128)(2,1)S(1)}, bf16[264,256]{1,0:T(8,128)(2,1)S(1)}, u32[]{:S(2)}, u32[]{:S(2)}) collective-permute-start(bf16[264,256]{1,0:T(8,128)(2,1)S(1)} %get-tuple-element.36), channel_id=1, source_target_pairs={{0,12},{1,13},{2,14},{3,15},{4,8},{5,9},{6,10},{7,11},{8,4},{9,5},... | collective-permute-start | bytes 405512 | tf_op jit(solution)/shard_map/ppermute | solution.py:363
  7.0 2.2 %collective-permute-start.2 = (bf16[520,256]{1,0:T(8,128)(2,1)S(1)}, bf16[520,256]{1,0:T(8,128)(2,1)S(1)}, u32[]{:S(2)}, u32[]{:S(2)}) collective-permute-start(bf16[520,256]{1,0:T(8,128)(2,1)S(1)} %get-tuple-element.37), channel_id=1, source_target_pairs={{0,10},{1,11},{2,8},{3,9},{4,14},{5,15},{6,12},{7,13},{8,2},{9,3},... | collective-permute-start | bytes 798728 | tf_op jit(solution)/shard_map/ppermute | solution.py:363
  9.1 2.5 %bucket.1 = (bf16[128,1024]{1,0:T(8,128)(2,1)S(1)}, bf16[128,1024]{1,0:T(8,128)(2,1)S(1)}, bf16[520,256]{1,0:T(8,128)(2,1)S(1)}) custom-call(s32[4]{0:T(128)S(1)} %bitcast_add_fusion.refs_0_.heads, s32[1]{0:T(128)} %get-tuple-element.38.refs_0_, bf16[1,512,1024]{2,1,0:T(8,128)(2,1)} %refs_5_.1, bf16[1,1024,2048]{2,1,0:T(8,128)(2,1)} %refs_4_.1), custom_call_target="tpu_custom_call" | custom-call | tf_op jit(solution)/shard_map/bucket/pallas_call | solution.py:415
  11.6 1.6 %collective-permute-start.5 = (bf16[128,1024]{1,0:T(8,128)(2,1)S(1)}, bf16[128,1024]{1,0:T(8,128)(2,1)S(1)}, u32[]{:S(2)}, u32[]{:S(2)}) collective-permute-start(bf16[128,1024]{1,0:T(8,128)(2,1)S(1)} %get-tuple-element.44), channel_id=1, source_target_pairs={{0,16},{16,0},{1,17},{17,1},{2,18},{18,2},{3,19},{19,3},{4,20},{20... | collective-permute-start | bytes 786440 | tf_op jit(solution)/shard_map/ppermute | solution.py:367
  13.2 0.5 collective-permute-start.6
  13.7 0.0 copy-done
  13.7 0.0 copy-done.1
  13.7 1.6 %collective-permute-start.3 = (s32[4,8]{1,0:T(4,128)S(1)}, s32[4,8]{1,0:T(4,128)S(1)}, u32[]{:S(2)}, u32[]{:S(2)}) collective-permute-start(s32[4,8]{1,0:T(4,128)S(1)} %add_bitcast_fusion.refs_2_), channel_id=1, source_target_pairs={{0,16},{16,0},{1,17},{17,1},{2,18},{18,2},{3,19},{19,3},{4,20},{20... | collective-permute-start | bytes 392 | tf_op jit(solution)/shard_map/ppermute | solution.py:367
  15.3 8.7 %collective-permute-done.3.refs_3_ = s32[4,8]{1,0:T(4,128)S(1)} collective-permute-done((s32[4,8]{1,0:T(4,128)S(1)}, s32[4,8]{1,0:T(4,128)S(1)}, u32[]{:S(2)}, u32[]{:S(2)}) %collective-permute-start.3) | collective-permute-done | bytes 160 | tf_op jit(solution)/shard_map/ppermute | solution.py:367
  24.0 0.0 collective-permute-done.1.refs_0_
  24.0 2.5 %collective-permute-start.4 = (bf16[520,256]{1,0:T(8,128)(2,1)S(1)}, bf16[520,256]{1,0:T(8,128)(2,1)S(1)}, u32[]{:S(2)}, u32[]{:S(2)}) collective-permute-start(bf16[520,256]{1,0:T(8,128)(2,1)S(1)} %get-tuple-element.41), channel_id=1, source_target_pairs={{0,14},{1,15},{2,12},{3,13},{4,10},{5,11},{6,8},{7,9},{8,6},{9,7},... | collective-permute-start | bytes 798728 | tf_op jit(solution)/shard_map/ppermute | solution.py:363
  26.5 0.0 collective-permute-done.5.refs_6_
  26.5 0.0 collective-permute-done.6.refs_7_
  26.5 5.7 %assemble.1 = (bf16[1024,256]{1,0:T(8,128)(2,1)S(1)}, bf16[640,256]{1,0:T(8,128)(2,1)S(1)}, bf16[384,256]{1,0:T(8,128)(2,1)S(1)}, bf16[1024,256]{1,0:T(8,128)(2,...) custom-call(s32[4]{0:T(128)S(1)} %bitcast_add_fusion.refs_0_.heads, ...), custom_call_target="tpu_custom_call" | custom-call | tf_op jit(solution)/shard_map/assemble/pallas_call | solution.py:441
  32.2 0.0 collective-permute-done.2.refs_1_
  32.2 0.5 collective-permute-start.7
  32.7 3.7 %collective-permute-done.4.refs_2_ = bf16[520,256]{1,0:T(8,128)(2,1)S(1)} collective-permute-done((bf16[520,256]{1,0:T(8,128)(2,1)S(1)}, bf16[520,256]{1,0:T(8,128)(2,1)S(1)}, u32[]{:S(2)}, u32[]{:S(2)}) %collective-permute-start.4) | collective-permute-done | bytes 266272 | tf_op jit(solution)/shard_map/ppermute | solution.py:363
  36.4 2.3 %collective-permute-start.9 = (bf16[512,256]{1,0:T(8,128)(2,1)S(1)}, bf16[512,256]{1,0:T(8,128)(2,1)S(1)}, u32[]{:S(2)}, u32[]{:S(2)}) collective-permute-start(bf16[512,256]{1,0:T(8,128)(2,1)S(1)} %get-tuple-element.53), channel_id=1, source_target_pairs={{0,14},{1,15},{2,12},{3,13},{4,10},{5,11},{6,8},{7,9},{8,6},{9,7},... | collective-permute-start | bytes 786440 | tf_op jit(solution)/shard_map/ppermute | solution.py:363
  38.7 0.0 collective-permute-start.12
  38.7 2.8 %collective-permute-start.11 = (bf16[1024,256]{1,0:T(8,128)(2,1)S(1)}, bf16[1024,256]{1,0:T(8,128)(2,1)S(1)}, u32[]{:S(2)}, u32[]{:S(2)}) collective-permute-start(bf16[1024,256]{1,0:T(8,128)(2,1)S(1)} %get-tuple-element.56), channel_id=1, source_target_pairs={{0,6},{1,7},{2,4},{3,5},{4,2},{5,3},{6,0},{7,1},{8,14},{9,15},{10,... | collective-permute-start | bytes 1572872 | tf_op jit(solution)/shard_map/ppermute | solution.py:363
  41.4 16.3 %collective-permute-done.9 = bf16[512,256]{1,0:T(8,128)(2,1)S(1)} collective-permute-done((bf16[512,256]{1,0:T(8,128)(2,1)S(1)}, bf16[512,256]{1,0:T(8,128)(2,1)S(1)}, u32[]{:S(2)}, u32[]{:S(2)}) %collective-permute-start.9) | collective-permute-done | bytes 262176 | tf_op jit(solution)/shard_map/ppermute | solution.py:363
  57.7 0.0 collective-permute-start.14
  57.7 3.8 %collective-permute-done.12 = bf16[512,256]{1,0:T(8,128)(2,1)S(1)} collective-permute-done((bf16[512,256]{1,0:T(8,128)(2,1)S(1)}, bf16[512,256]{1,0:T(8,128)(2,1)S(1)}, u32[]{:S(2)}, u32[]{:S(2)}) %collective-permute-start.12) | collective-permute-done | bytes 262176 | tf_op jit(solution)/shard_map/ppermute | solution.py:363
  61.5 1.9 %collective-permute-start.13 = (bf16[768,256]{1,0:T(8,128)(2,1)S(1)}, bf16[768,256]{1,0:T(8,128)(2,1)S(1)}, u32[]{:S(2)}, u32[]{:S(2)}) collective-permute-start(bf16[768,256]{1,0:T(8,128)(2,1)S(1)} %get-tuple-element.60), channel_id=1, source_target_pairs={{0,12},{1,13},{2,14},{3,15},{4,8},{5,9},{6,10},{7,11},{8,4},{9,5},... | collective-permute-start | bytes 1179656 | tf_op jit(solution)/shard_map/ppermute | solution.py:363
  63.4 0.0 collective-permute-done.7
  63.4 0.0 collective-permute-start.8
  63.4 2.0 %collective-permute-start.10 = (bf16[384,256]{1,0:T(8,128)(2,1)S(1)}, bf16[384,256]{1,0:T(8,128)(2,1)S(1)}, u32[]{:S(2)}, u32[]{:S(2)}) collective-permute-start(bf16[384,256]{1,0:T(8,128)(2,1)S(1)} %get-tuple-element.54), channel_id=1, source_target_pairs={{0,2},{1,3},{2,0},{3,1},{4,6},{5,7},{6,4},{7,5},{8,10},{9,11},{10,... | collective-permute-start | bytes 589832 | tf_op jit(solution)/shard_map/ppermute | solution.py:363
  65.4 1.7 %place_early.1 = (bf16[8,8,128,256]{3,2,1,0:T(8,128)(2,1)}, s32[3]{0:T(128)S(1)}) custom-call(bf16[264,256]{1,0:T(8,128)(2,1)S(1)} %collective-permute-done.1.refs_0_, bf16[520,256]{1,0:T(8,128)(2,1)S(1)} %collective-permute-done.2.refs_1_, bf16[520,256]{1,0:T(8,128)(2,1)S(1)} %collective-permute-done.4.refs_2_), custom_call_target="tpu_custom_call" | custom-call | tf_op jit(solution)/shard_map/place_early/pallas_call | solution.py:496
  67.1 11.0 %collective-permute-done.10 = bf16[384,256]{1,0:T(8,128)(2,1)S(1)} collective-permute-done((bf16[384,256]{1,0:T(8,128)(2,1)S(1)}, bf16[384,256]{1,0:T(8,128)(2,1)S(1)}, u32[]{:S(2)}, u32[]{:S(2)}) %collective-permute-start.10) | collective-permute-done | bytes 196640 | tf_op jit(solution)/shard_map/ppermute | solution.py:363
  78.2 23.3 %collective-permute-done.13 = bf16[768,256]{1,0:T(8,128)(2,1)S(1)} collective-permute-done((bf16[768,256]{1,0:T(8,128)(2,1)S(1)}, bf16[768,256]{1,0:T(8,128)(2,1)S(1)}, u32[]{:S(2)}, u32[]{:S(2)}) %collective-permute-start.13) | collective-permute-done | bytes 393248 | tf_op jit(solution)/shard_map/ppermute | solution.py:363
  101.5 0.0 collective-permute-done.11
  101.5 0.0 collective-permute-done.8
  101.5 2.2 %place_mid.1.refs_0_ = bf16[8,8,128,256]{3,2,1,0:T(8,128)(2,1)} custom-call(bf16[8,8,128,256]{3,2,1,0:T(8,128)(2,1)} %get-tuple-element.42.refs_0_, s32[3]{0:T(128)S(1)} %get-tuple-element.43.refs_1_, bf16[8,128,256]{2,1,0:T(8,128)(2,1)S(1)} %bitcast.16, bf16[5,128,256]{2,1,0:T(8,128)(2,1)S(1)} %bitcast.21, ...), custom_call_target="tpu_custom_call", output_to_operand_aliasing={{}: (0, {})} | custom-call | tf_op jit(solution)/shard_map/place_mid/pallas_call | solution.py:523
  103.7 0.0 collective-permute-done.14
  103.7 0.9 place_last.1
  (1 shorter events, 0.0 us)
Async XLA Ops:
  0.7 3.5 %collective-permute-start = (s32[4]{0:T(128)S(1)}, s32[4]{0:T(128)S(1)}, u32[]{:S(2)}, u32[]{:S(2)}) collective-permute-start(s32[4]{0:T(128)S(1)} %bitcast_add_fusion.refs_0_.heads), channel_id=1, source_target_pairs={{0,16},{16,0},{1,17},{17,1},{2,18},{18,2},{3,19},{19,3},{4,20},{20... | collective-permute-start | bytes 56 | tf_op jit(solution)/shard_map/ppermute | solution.py:367
  3.4 10.3 %copy-start = (s32[1,4,8]{2,1,0:T(4,128)S(1)}, s32[1,4,8]{2,1,0:T(4,128)}, u32[]{:S(2)}) copy-start(s32[1,4,8]{2,1,0:T(4,128)} %param.10) | copy-start | bytes 388
  3.5 10.3 %copy-start.1 = (s32[1,4,8]{2,1,0:T(4,128)S(1)}, s32[1,4,8]{2,1,0:T(4,128)}, u32[]{:S(2)}) copy-start(s32[1,4,8]{2,1,0:T(4,128)} %param.11) | copy-start | bytes 388
  5.3 18.7 %collective-permute-start.1 = (bf16[264,256]{1,0:T(8,128)(2,1)S(1)}, bf16[264,256]{1,0:T(8,128)(2,1)S(1)}, u32[]{:S(2)}, u32[]{:S(2)}) collective-permute-start(bf16[264,256]{1,0:T(8,128)(2,1)S(1)} %get-tuple-element.36), channel_id=1, source_target_pairs={{0,12},{1,13},{2,14},{3,15},{4,8},{5,9},{6,10},{7,11},{8,4},{9,5},... | collective-permute-start | bytes 405512 | tf_op jit(solution)/shard_map/ppermute | solution.py:363
  7.0 25.2 %collective-permute-start.2 = (bf16[520,256]{1,0:T(8,128)(2,1)S(1)}, bf16[520,256]{1,0:T(8,128)(2,1)S(1)}, u32[]{:S(2)}, u32[]{:S(2)}) collective-permute-start(bf16[520,256]{1,0:T(8,128)(2,1)S(1)} %get-tuple-element.37), channel_id=1, source_target_pairs={{0,10},{1,11},{2,8},{3,9},{4,14},{5,15},{6,12},{7,13},{8,2},{9,3},... | collective-permute-start | bytes 798728 | tf_op jit(solution)/shard_map/ppermute | solution.py:363
  11.6 14.9 %collective-permute-start.5 = (bf16[128,1024]{1,0:T(8,128)(2,1)S(1)}, bf16[128,1024]{1,0:T(8,128)(2,1)S(1)}, u32[]{:S(2)}, u32[]{:S(2)}) collective-permute-start(bf16[128,1024]{1,0:T(8,128)(2,1)S(1)} %get-tuple-element.44), channel_id=1, source_target_pairs={{0,16},{16,0},{1,17},{17,1},{2,18},{18,2},{3,19},{19,3},{4,20},{20... | collective-permute-start | bytes 786440 | tf_op jit(solution)/shard_map/ppermute | solution.py:367
  13.2 13.3 %collective-permute-start.6 = (bf16[128,1024]{1,0:T(8,128)(2,1)S(1)}, bf16[128,1024]{1,0:T(8,128)(2,1)S(1)}, u32[]{:S(2)}, u32[]{:S(2)}) collective-permute-start(bf16[128,1024]{1,0:T(8,128)(2,1)S(1)} %get-tuple-element.45), channel_id=1, source_target_pairs={{0,16},{16,0},{1,17},{17,1},{2,18},{18,2},{3,19},{19,3},{4,20},{20... | collective-permute-start | bytes 786440 | tf_op jit(solution)/shard_map/ppermute | solution.py:367
  13.7 10.3 %collective-permute-start.3 = (s32[4,8]{1,0:T(4,128)S(1)}, s32[4,8]{1,0:T(4,128)S(1)}, u32[]{:S(2)}, u32[]{:S(2)}) collective-permute-start(s32[4,8]{1,0:T(4,128)S(1)} %add_bitcast_fusion.refs_2_), channel_id=1, source_target_pairs={{0,16},{16,0},{1,17},{17,1},{2,18},{18,2},{3,19},{19,3},{4,20},{20... | collective-permute-start | bytes 392 | tf_op jit(solution)/shard_map/ppermute | solution.py:367
  24.0 12.4 %collective-permute-start.4 = (bf16[520,256]{1,0:T(8,128)(2,1)S(1)}, bf16[520,256]{1,0:T(8,128)(2,1)S(1)}, u32[]{:S(2)}, u32[]{:S(2)}) collective-permute-start(bf16[520,256]{1,0:T(8,128)(2,1)S(1)} %get-tuple-element.41), channel_id=1, source_target_pairs={{0,14},{1,15},{2,12},{3,13},{4,10},{5,11},{6,8},{7,9},{8,6},{9,7},... | collective-permute-start | bytes 798728 | tf_op jit(solution)/shard_map/ppermute | solution.py:363
  32.2 31.2 %collective-permute-start.7 = (bf16[1024,256]{1,0:T(8,128)(2,1)S(1)}, bf16[1024,256]{1,0:T(8,128)(2,1)S(1)}, u32[]{:S(2)}, u32[]{:S(2)}) collective-permute-start(bf16[1024,256]{1,0:T(8,128)(2,1)S(1)} %get-tuple-element.49), channel_id=1, source_target_pairs={{0,4},{1,5},{2,6},{3,7},{4,0},{5,1},{6,2},{7,3},{8,12},{9,13},{10,... | collective-permute-start | bytes 1572872 | tf_op jit(solution)/shard_map/ppermute | solution.py:363
  36.4 21.3 %collective-permute-start.9 = (bf16[512,256]{1,0:T(8,128)(2,1)S(1)}, bf16[512,256]{1,0:T(8,128)(2,1)S(1)}, u32[]{:S(2)}, u32[]{:S(2)}) collective-permute-start(bf16[512,256]{1,0:T(8,128)(2,1)S(1)} %get-tuple-element.53), channel_id=1, source_target_pairs={{0,14},{1,15},{2,12},{3,13},{4,10},{5,11},{6,8},{7,9},{8,6},{9,7},... | collective-permute-start | bytes 786440 | tf_op jit(solution)/shard_map/ppermute | solution.py:363
  38.7 22.9 %collective-permute-start.12 = (bf16[512,256]{1,0:T(8,128)(2,1)S(1)}, bf16[512,256]{1,0:T(8,128)(2,1)S(1)}, u32[]{:S(2)}, u32[]{:S(2)}) collective-permute-start(bf16[512,256]{1,0:T(8,128)(2,1)S(1)} %get-tuple-element.58), channel_id=1, source_target_pairs={{0,10},{1,11},{2,8},{3,9},{4,14},{5,15},{6,12},{7,13},{8,2},{9,3},... | collective-permute-start | bytes 786440 | tf_op jit(solution)/shard_map/ppermute | solution.py:363
  38.7 62.8 %collective-permute-start.11 = (bf16[1024,256]{1,0:T(8,128)(2,1)S(1)}, bf16[1024,256]{1,0:T(8,128)(2,1)S(1)}, u32[]{:S(2)}, u32[]{:S(2)}) collective-permute-start(bf16[1024,256]{1,0:T(8,128)(2,1)S(1)} %get-tuple-element.56), channel_id=1, source_target_pairs={{0,6},{1,7},{2,4},{3,5},{4,2},{5,3},{6,0},{7,1},{8,14},{9,15},{10,... | collective-permute-start | bytes 1572872 | tf_op jit(solution)/shard_map/ppermute | solution.py:363
  57.7 46.0 %collective-permute-start.14 = (bf16[1024,256]{1,0:T(8,128)(2,1)S(1)}, bf16[1024,256]{1,0:T(8,128)(2,1)S(1)}, u32[]{:S(2)}, u32[]{:S(2)}) collective-permute-start(bf16[1024,256]{1,0:T(8,128)(2,1)S(1)} %get-tuple-element.62), channel_id=1, source_target_pairs={{0,8},{1,9},{2,10},{3,11},{4,12},{5,13},{6,14},{7,15},{8,0},{9,1},... | collective-permute-start | bytes 1572872 | tf_op jit(solution)/shard_map/ppermute | solution.py:363
  61.5 39.9 %collective-permute-start.13 = (bf16[768,256]{1,0:T(8,128)(2,1)S(1)}, bf16[768,256]{1,0:T(8,128)(2,1)S(1)}, u32[]{:S(2)}, u32[]{:S(2)}) collective-permute-start(bf16[768,256]{1,0:T(8,128)(2,1)S(1)} %get-tuple-element.60), channel_id=1, source_target_pairs={{0,12},{1,13},{2,14},{3,15},{4,8},{5,9},{6,10},{7,11},{8,4},{9,5},... | collective-permute-start | bytes 1179656 | tf_op jit(solution)/shard_map/ppermute | solution.py:363
  63.4 38.1 %collective-permute-start.8 = (bf16[640,256]{1,0:T(8,128)(2,1)S(1)}, bf16[640,256]{1,0:T(8,128)(2,1)S(1)}, u32[]{:S(2)}, u32[]{:S(2)}) collective-permute-start(bf16[640,256]{1,0:T(8,128)(2,1)S(1)} %get-tuple-element.50), channel_id=1, source_target_pairs={{0,2},{1,3},{2,0},{3,1},{4,6},{5,7},{6,4},{7,5},{8,10},{9,11},{10,... | collective-permute-start | bytes 983048 | tf_op jit(solution)/shard_map/ppermute | solution.py:363
  63.4 14.7 %collective-permute-start.10 = (bf16[384,256]{1,0:T(8,128)(2,1)S(1)}, bf16[384,256]{1,0:T(8,128)(2,1)S(1)}, u32[]{:S(2)}, u32[]{:S(2)}) collective-permute-start(bf16[384,256]{1,0:T(8,128)(2,1)S(1)} %get-tuple-element.54), channel_id=1, source_target_pairs={{0,2},{1,3},{2,0},{3,1},{4,6},{5,7},{6,4},{7,5},{8,10},{9,11},{10,... | collective-permute-start | bytes 589832 | tf_op jit(solution)/shard_map/ppermute | solution.py:363

commit v14 on v13

--- a/solution.py
+++ b/solution.py
@@ -31,7 +31,7 @@
         self.width = self.col_groups * self.block
         self.capacity = max(self.slots // 4, self.slots // self.groups)
         self.first = max(0, self.rows - self.capacity * self.groups)
-        self.early = {6: self.first // 2, 5: self.first, 7: self.first}
+        self.early = {6: 3 * self.first // 4, 5: self.first, 7: self.first}
         self.late = []
         for o in range(GRID_COLS):
             count = self.rows - self.early.get(o, 0)

time: 105 us -> 105 us (level)
  the two profiles are of different devices: /device:TPU:8 before, /device:TPU:16 now
where the time goes in v14:
time: 105 us; the launch traced here: 104 us
  waiting for transfers between devices  63.6 us (61%)
  starting transfers between devices  24.8 us (24%)
  Pallas kernels  15.4 us (15%)
    ppermute x11, waiting for transfers between devices, across(): return lax.ppermute(value, 'wide', pairs)  54.3 us
    ppermute x11, starting transfers between devices, across(): return lax.ppermute(value, 'wide', pairs)  19.6 us
    ppermute x4, waiting for transfers between devices, along(): lax.ppermute(value, 'front', [(f, (f + steps) % plan.groups) for f in ran...  9.27 us
    pallas_call x1, Pallas kernels, local(): pl.pallas_call(functools.partial(assemble_kernel, plan), out_shape=[jax.S...  5.71 us
    ppermute x4, starting transfers between devices, along(): lax.ppermute(value, 'front', [(f, (f + steps) % plan.groups) for f in ran...  5.2 us
    pallas_call x2, Pallas kernels, place(): pl.pallas_call(body, out_shape=out_shape, in_specs=[HBM] * len(held) + [A...  3.06 us
    pallas_call x1, Pallas kernels, local(): pl.pallas_call(functools.partial(bucket_kernel, plan, tail), out_shape=[j...  2.5 us
  transfers between devices with their start and end apart: 15, of which 7 were waited for; matrix products, arithmetic and copies ran while one was open for 0% of the time, Pallas kernels for 13%

profile of v14, /device:TPU:16, one launch (start us, length us, event | category | flops | bytes accessed | tf_op | source)
XLA Modules:
  0.0 104.5 jit_solution(2834322852967649351)
XLA Ops:
  0.0 0.7 bitcast_add_fusion.refs_0_.heads
  0.7 1.5 %collective-permute-start = (s32[4]{0:T(128)S(1)}, s32[4]{0:T(128)S(1)}, u32[]{:S(2)}, u32[]{:S(2)}) collective-permute-start(s32[4]{0:T(128)S(1)} %bitcast_add_fusion.refs_0_.heads), channel_id=1, source_target_pairs={{0,16},{16,0},{1,17},{17,1},{2,18},{18,2},{3,19},{19,3},{4,20},{20... | collective-permute-start | bytes 56 | tf_op jit(solution)/shard_map/ppermute | solution.py:367
  2.2 1.2 %stage.1 = (bf16[1024,256]{1,0:T(8,128)(2,1)S(1)}, bf16[1024,256]{1,0:T(8,128)(2,1)S(1)}) custom-call(bf16[1,1024,2048]{2,1,0:T(8,128)(2,1)} %refs_4_.1), custom_call_target="tpu_custom_call" | custom-call | tf_op jit(solution)/shard_map/stage/pallas_call | solution.py:391
  3.4 0.0 copy-start
  3.5 0.0 copy-start.1
  3.5 0.7 collective-permute-done.refs_1_
  4.2 1.1 %pack_early.1 = (bf16[392,256]{1,0:T(8,128)(2,1)S(1)}, bf16[520,256]{1,0:T(8,128)(2,1)S(1)}, s32[1]{0:T(128)}) custom-call(s32[4]{0:T(128)S(1)} %bitcast_add_fusion.refs_0_.heads, s32[4]{0:T(128)S(1)} %collective-permute-done.refs_1_, bf16[1024,256]{1,0:T(8,128)(2,1)S(1)} %get-tuple-element.34.refs_2_, bf16[1024,256]{1,0:T(8,128)(2,1)S(1)} %get-tuple-element.35.refs_3_), custom_call_target="tpu_custom_call" | custom-call | tf_op jit(solution)/shard_map/pack_early/pallas_call | solution.py:401
  5.3 0.5 collective-permute-start.1
  5.9 4.4 %collective-permute-start.2 = (bf16[520,256]{1,0:T(8,128)(2,1)S(1)}, bf16[520,256]{1,0:T(8,128)(2,1)S(1)}, u32[]{:S(2)}, u32[]{:S(2)}) collective-permute-start(bf16[520,256]{1,0:T(8,128)(2,1)S(1)} %get-tuple-element.37), channel_id=1, source_target_pairs={{0,10},{1,11},{2,8},{3,9},{4,14},{5,15},{6,12},{7,13},{8,2},{9,3},... | collective-permute-start | bytes 798728 | tf_op jit(solution)/shard_map/ppermute | solution.py:363
  10.3 2.5 %bucket.1 = (bf16[128,1024]{1,0:T(8,128)(2,1)S(1)}, bf16[128,1024]{1,0:T(8,128)(2,1)S(1)}, bf16[520,256]{1,0:T(8,128)(2,1)S(1)}) custom-call(s32[4]{0:T(128)S(1)} %bitcast_add_fusion.refs_0_.heads, s32[1]{0:T(128)} %get-tuple-element.38.refs_0_, bf16[1,512,1024]{2,1,0:T(8,128)(2,1)} %refs_5_.1, bf16[1,1024,2048]{2,1,0:T(8,128)(2,1)} %refs_4_.1), custom_call_target="tpu_custom_call" | custom-call | tf_op jit(solution)/shard_map/bucket/pallas_call | solution.py:415
  12.8 1.6 %collective-permute-start.5 = (bf16[128,1024]{1,0:T(8,128)(2,1)S(1)}, bf16[128,1024]{1,0:T(8,128)(2,1)S(1)}, u32[]{:S(2)}, u32[]{:S(2)}) collective-permute-start(bf16[128,1024]{1,0:T(8,128)(2,1)S(1)} %get-tuple-element.44), channel_id=1, source_target_pairs={{0,16},{16,0},{1,17},{17,1},{2,18},{18,2},{3,19},{19,3},{4,20},{20... | collective-permute-start | bytes 786440 | tf_op jit(solution)/shard_map/ppermute | solution.py:367
  14.4 0.5 collective-permute-start.6
  14.9 0.0 copy-done
  14.9 0.0 copy-done.1
  14.9 1.6 %collective-permute-start.3 = (s32[4,8]{1,0:T(4,128)S(1)}, s32[4,8]{1,0:T(4,128)S(1)}, u32[]{:S(2)}, u32[]{:S(2)}) collective-permute-start(s32[4,8]{1,0:T(4,128)S(1)} %add_bitcast_fusion.refs_2_), channel_id=1, source_target_pairs={{0,16},{16,0},{1,17},{17,1},{2,18},{18,2},{3,19},{19,3},{4,20},{20... | collective-permute-start | bytes 392 | tf_op jit(solution)/shard_map/ppermute | solution.py:367
  16.5 8.5 %collective-permute-done.3.refs_3_ = s32[4,8]{1,0:T(4,128)S(1)} collective-permute-done((s32[4,8]{1,0:T(4,128)S(1)}, s32[4,8]{1,0:T(4,128)S(1)}, u32[]{:S(2)}, u32[]{:S(2)}) %collective-permute-start.3) | collective-permute-done | bytes 160 | tf_op jit(solution)/shard_map/ppermute | solution.py:367
  25.0 0.0 collective-permute-done.1.refs_0_
  25.0 0.0 collective-permute-start.4
  25.0 0.0 collective-permute-done.5.refs_6_
  25.0 0.0 collective-permute-done.6.refs_7_
  25.0 5.7 %assemble.1 = (bf16[1024,256]{1,0:T(8,128)(2,1)S(1)}, bf16[640,256]{1,0:T(8,128)(2,1)S(1)}, bf16[384,256]{1,0:T(8,128)(2,1)S(1)}, bf16[1024,256]{1,0:T(8,128)(2,...) custom-call(s32[4]{0:T(128)S(1)} %bitcast_add_fusion.refs_0_.heads, ...), custom_call_target="tpu_custom_call" | custom-call | tf_op jit(solution)/shard_map/assemble/pallas_call | solution.py:441
  30.7 0.8 collective-permute-done.2.refs_1_
  31.5 5.3 %collective-permute-start.7 = (bf16[1024,256]{1,0:T(8,128)(2,1)S(1)}, bf16[1024,256]{1,0:T(8,128)(2,1)S(1)}, u32[]{:S(2)}, u32[]{:S(2)}) collective-permute-start(bf16[1024,256]{1,0:T(8,128)(2,1)S(1)} %get-tuple-element.49), channel_id=1, source_target_pairs={{0,4},{1,5},{2,6},{3,7},{4,0},{5,1},{6,2},{7,3},{8,12},{9,13},{10,... | collective-permute-start | bytes 1572872 | tf_op jit(solution)/shard_map/ppermute | solution.py:363
  36.8 2.7 %collective-permute-done.4.refs_2_ = bf16[520,256]{1,0:T(8,128)(2,1)S(1)} collective-permute-done((bf16[520,256]{1,0:T(8,128)(2,1)S(1)}, bf16[520,256]{1,0:T(8,128)(2,1)S(1)}, u32[]{:S(2)}, u32[]{:S(2)}) %collective-permute-start.4) | collective-permute-done | bytes 266272 | tf_op jit(solution)/shard_map/ppermute | solution.py:363
  39.5 2.3 %collective-permute-start.9 = (bf16[512,256]{1,0:T(8,128)(2,1)S(1)}, bf16[512,256]{1,0:T(8,128)(2,1)S(1)}, u32[]{:S(2)}, u32[]{:S(2)}) collective-permute-start(bf16[512,256]{1,0:T(8,128)(2,1)S(1)} %get-tuple-element.53), channel_id=1, source_target_pairs={{0,14},{1,15},{2,12},{3,13},{4,10},{5,11},{6,8},{7,9},{8,6},{9,7},... | collective-permute-start | bytes 786440 | tf_op jit(solution)/shard_map/ppermute | solution.py:363
  41.8 0.0 collective-permute-start.12
  41.8 3.0 %collective-permute-start.11 = (bf16[1024,256]{1,0:T(8,128)(2,1)S(1)}, bf16[1024,256]{1,0:T(8,128)(2,1)S(1)}, u32[]{:S(2)}, u32[]{:S(2)}) collective-permute-start(bf16[1024,256]{1,0:T(8,128)(2,1)S(1)} %get-tuple-element.56), channel_id=1, source_target_pairs={{0,6},{1,7},{2,4},{3,5},{4,2},{5,3},{6,0},{7,1},{8,14},{9,15},{10,... | collective-permute-start | bytes 1572872 | tf_op jit(solution)/shard_map/ppermute | solution.py:363
  44.8 11.7 %collective-permute-done.9 = bf16[512,256]{1,0:T(8,128)(2,1)S(1)} collective-permute-done((bf16[512,256]{1,0:T(8,128)(2,1)S(1)}, bf16[512,256]{1,0:T(8,128)(2,1)S(1)}, u32[]{:S(2)}, u32[]{:S(2)}) %collective-permute-start.9) | collective-permute-done | bytes 262176 | tf_op jit(solution)/shard_map/ppermute | solution.py:363
  56.5 0.0 collective-permute-start.14
  56.5 8.5 %collective-permute-done.12 = bf16[512,256]{1,0:T(8,128)(2,1)S(1)} collective-permute-done((bf16[512,256]{1,0:T(8,128)(2,1)S(1)}, bf16[512,256]{1,0:T(8,128)(2,1)S(1)}, u32[]{:S(2)}, u32[]{:S(2)}) %collective-permute-start.12) | collective-permute-done | bytes 262176 | tf_op jit(solution)/shard_map/ppermute | solution.py:363
  65.0 2.1 %collective-permute-start.13 = (bf16[640,256]{1,0:T(8,128)(2,1)S(1)}, bf16[640,256]{1,0:T(8,128)(2,1)S(1)}, u32[]{:S(2)}, u32[]{:S(2)}) collective-permute-start(bf16[640,256]{1,0:T(8,128)(2,1)S(1)} %get-tuple-element.60), channel_id=1, source_target_pairs={{0,12},{1,13},{2,14},{3,15},{4,8},{5,9},{6,10},{7,11},{8,4},{9,5},... | collective-permute-start | bytes 983048 | tf_op jit(solution)/shard_map/ppermute | solution.py:363
  67.1 0.0 collective-permute-done.7
  67.1 0.9 collective-permute-start.8
  67.9 1.2 %collective-permute-start.10 = (bf16[384,256]{1,0:T(8,128)(2,1)S(1)}, bf16[384,256]{1,0:T(8,128)(2,1)S(1)}, u32[]{:S(2)}, u32[]{:S(2)}) collective-permute-start(bf16[384,256]{1,0:T(8,128)(2,1)S(1)} %get-tuple-element.54), channel_id=1, source_target_pairs={{0,2},{1,3},{2,0},{3,1},{4,6},{5,7},{6,4},{7,5},{8,10},{9,11},{10,... | collective-permute-start | bytes 589832 | tf_op jit(solution)/shard_map/ppermute | solution.py:363
  69.1 1.7 %place_early.1 = (bf16[8,8,128,256]{3,2,1,0:T(8,128)(2,1)}, s32[3]{0:T(128)S(1)}) custom-call(bf16[392,256]{1,0:T(8,128)(2,1)S(1)} %collective-permute-done.1.refs_0_, bf16[520,256]{1,0:T(8,128)(2,1)S(1)} %collective-permute-done.2.refs_1_, bf16[520,256]{1,0:T(8,128)(2,1)S(1)} %collective-permute-done.4.refs_2_), custom_call_target="tpu_custom_call" | custom-call | tf_op jit(solution)/shard_map/place_early/pallas_call | solution.py:496
  70.8 30.6 %collective-permute-done.13 = bf16[640,256]{1,0:T(8,128)(2,1)S(1)} collective-permute-done((bf16[640,256]{1,0:T(8,128)(2,1)S(1)}, bf16[640,256]{1,0:T(8,128)(2,1)S(1)}, u32[]{:S(2)}, u32[]{:S(2)}) %collective-permute-start.13) | collective-permute-done | bytes 327712 | tf_op jit(solution)/shard_map/ppermute | solution.py:363
  101.4 0.0 collective-permute-done.10
  101.4 0.0 collective-permute-done.11
  101.4 0.0 collective-permute-done.8
  101.4 2.2 %place_mid.1.refs_0_ = bf16[8,8,128,256]{3,2,1,0:T(8,128)(2,1)} custom-call(bf16[8,8,128,256]{3,2,1,0:T(8,128)(2,1)} %get-tuple-element.42.refs_0_, s32[3]{0:T(128)S(1)} %get-tuple-element.43.refs_1_, bf16[8,128,256]{2,1,0:T(8,128)(2,1)S(1)} %bitcast.16, bf16[5,128,256]{2,1,0:T(8,128)(2,1)S(1)} %bitcast.21, ...), custom_call_target="tpu_custom_call", output_to_operand_aliasing={{}: (0, {})} | custom-call | tf_op jit(solution)/shard_map/place_mid/pallas_call | solution.py:523
  103.6 0.0 collective-permute-done.14
  103.6 0.9 place_last.1
  (1 shorter events, 0.0 us)
Async XLA Ops:
  0.7 3.5 %collective-permute-start = (s32[4]{0:T(128)S(1)}, s32[4]{0:T(128)S(1)}, u32[]{:S(2)}, u32[]{:S(2)}) collective-permute-start(s32[4]{0:T(128)S(1)} %bitcast_add_fusion.refs_0_.heads), channel_id=1, source_target_pairs={{0,16},{16,0},{1,17},{17,1},{2,18},{18,2},{3,19},{19,3},{4,20},{20... | collective-permute-start | bytes 56 | tf_op jit(solution)/shard_map/ppermute | solution.py:367
  3.4 11.4 %copy-start = (s32[1,4,8]{2,1,0:T(4,128)S(1)}, s32[1,4,8]{2,1,0:T(4,128)}, u32[]{:S(2)}) copy-start(s32[1,4,8]{2,1,0:T(4,128)} %param.10) | copy-start | bytes 388
  3.5 11.4 %copy-start.1 = (s32[1,4,8]{2,1,0:T(4,128)S(1)}, s32[1,4,8]{2,1,0:T(4,128)}, u32[]{:S(2)}) copy-start(s32[1,4,8]{2,1,0:T(4,128)} %param.11) | copy-start | bytes 388
  5.3 19.6 %collective-permute-start.1 = (bf16[392,256]{1,0:T(8,128)(2,1)S(1)}, bf16[392,256]{1,0:T(8,128)(2,1)S(1)}, u32[]{:S(2)}, u32[]{:S(2)}) collective-permute-start(bf16[392,256]{1,0:T(8,128)(2,1)S(1)} %get-tuple-element.36), channel_id=1, source_target_pairs={{0,12},{1,13},{2,14},{3,15},{4,8},{5,9},{6,10},{7,11},{8,4},{9,5},... | collective-permute-start | bytes 602120 | tf_op jit(solution)/shard_map/ppermute | solution.py:363
  5.9 25.7 %collective-permute-start.2 = (bf16[520,256]{1,0:T(8,128)(2,1)S(1)}, bf16[520,256]{1,0:T(8,128)(2,1)S(1)}, u32[]{:S(2)}, u32[]{:S(2)}) collective-permute-start(bf16[520,256]{1,0:T(8,128)(2,1)S(1)} %get-tuple-element.37), channel_id=1, source_target_pairs={{0,10},{1,11},{2,8},{3,9},{4,14},{5,15},{6,12},{7,13},{8,2},{9,3},... | collective-permute-start | bytes 798728 | tf_op jit(solution)/shard_map/ppermute | solution.py:363
  12.8 12.2 %collective-permute-start.5 = (bf16[128,1024]{1,0:T(8,128)(2,1)S(1)}, bf16[128,1024]{1,0:T(8,128)(2,1)S(1)}, u32[]{:S(2)}, u32[]{:S(2)}) collective-permute-start(bf16[128,1024]{1,0:T(8,128)(2,1)S(1)} %get-tuple-element.44), channel_id=1, source_target_pairs={{0,16},{16,0},{1,17},{17,1},{2,18},{18,2},{3,19},{19,3},{4,20},{20... | collective-permute-start | bytes 786440 | tf_op jit(solution)/shard_map/ppermute | solution.py:367
  14.4 10.6 %collective-permute-start.6 = (bf16[128,1024]{1,0:T(8,128)(2,1)S(1)}, bf16[128,1024]{1,0:T(8,128)(2,1)S(1)}, u32[]{:S(2)}, u32[]{:S(2)}) collective-permute-start(bf16[128,1024]{1,0:T(8,128)(2,1)S(1)} %get-tuple-element.45), channel_id=1, source_target_pairs={{0,16},{16,0},{1,17},{17,1},{2,18},{18,2},{3,19},{19,3},{4,20},{20... | collective-permute-start | bytes 786440 | tf_op jit(solution)/shard_map/ppermute | solution.py:367
  14.9 10.1 %collective-permute-start.3 = (s32[4,8]{1,0:T(4,128)S(1)}, s32[4,8]{1,0:T(4,128)S(1)}, u32[]{:S(2)}, u32[]{:S(2)}) collective-permute-start(s32[4,8]{1,0:T(4,128)S(1)} %add_bitcast_fusion.refs_2_), channel_id=1, source_target_pairs={{0,16},{16,0},{1,17},{17,1},{2,18},{18,2},{3,19},{19,3},{4,20},{20... | collective-permute-start | bytes 392 | tf_op jit(solution)/shard_map/ppermute | solution.py:367
  25.0 14.6 %collective-permute-start.4 = (bf16[520,256]{1,0:T(8,128)(2,1)S(1)}, bf16[520,256]{1,0:T(8,128)(2,1)S(1)}, u32[]{:S(2)}, u32[]{:S(2)}) collective-permute-start(bf16[520,256]{1,0:T(8,128)(2,1)S(1)} %get-tuple-element.41), channel_id=1, source_target_pairs={{0,14},{1,15},{2,12},{3,13},{4,10},{5,11},{6,8},{7,9},{8,6},{9,7},... | collective-permute-start | bytes 798728 | tf_op jit(solution)/shard_map/ppermute | solution.py:363
  31.5 35.5 %collective-permute-start.7 = (bf16[1024,256]{1,0:T(8,128)(2,1)S(1)}, bf16[1024,256]{1,0:T(8,128)(2,1)S(1)}, u32[]{:S(2)}, u32[]{:S(2)}) collective-permute-start(bf16[1024,256]{1,0:T(8,128)(2,1)S(1)} %get-tuple-element.49), channel_id=1, source_target_pairs={{0,4},{1,5},{2,6},{3,7},{4,0},{5,1},{6,2},{7,3},{8,12},{9,13},{10,... | collective-permute-start | bytes 1572872 | tf_op jit(solution)/shard_map/ppermute | solution.py:363
  39.5 17.0 %collective-permute-start.9 = (bf16[512,256]{1,0:T(8,128)(2,1)S(1)}, bf16[512,256]{1,0:T(8,128)(2,1)S(1)}, u32[]{:S(2)}, u32[]{:S(2)}) collective-permute-start(bf16[512,256]{1,0:T(8,128)(2,1)S(1)} %get-tuple-element.53), channel_id=1, source_target_pairs={{0,14},{1,15},{2,12},{3,13},{4,10},{5,11},{6,8},{7,9},{8,6},{9,7},... | collective-permute-start | bytes 786440 | tf_op jit(solution)/shard_map/ppermute | solution.py:363
  41.8 23.2 %collective-permute-start.12 = (bf16[512,256]{1,0:T(8,128)(2,1)S(1)}, bf16[512,256]{1,0:T(8,128)(2,1)S(1)}, u32[]{:S(2)}, u32[]{:S(2)}) collective-permute-start(bf16[512,256]{1,0:T(8,128)(2,1)S(1)} %get-tuple-element.58), channel_id=1, source_target_pairs={{0,10},{1,11},{2,8},{3,9},{4,14},{5,15},{6,12},{7,13},{8,2},{9,3},... | collective-permute-start | bytes 786440 | tf_op jit(solution)/shard_map/ppermute | solution.py:363
  41.8 59.6 %collective-permute-start.11 = (bf16[1024,256]{1,0:T(8,128)(2,1)S(1)}, bf16[1024,256]{1,0:T(8,128)(2,1)S(1)}, u32[]{:S(2)}, u32[]{:S(2)}) collective-permute-start(bf16[1024,256]{1,0:T(8,128)(2,1)S(1)} %get-tuple-element.56), channel_id=1, source_target_pairs={{0,6},{1,7},{2,4},{3,5},{4,2},{5,3},{6,0},{7,1},{8,14},{9,15},{10,... | collective-permute-start | bytes 1572872 | tf_op jit(solution)/shard_map/ppermute | solution.py:363
  56.5 47.1 %collective-permute-start.14 = (bf16[1024,256]{1,0:T(8,128)(2,1)S(1)}, bf16[1024,256]{1,0:T(8,128)(2,1)S(1)}, u32[]{:S(2)}, u32[]{:S(2)}) collective-permute-start(bf16[1024,256]{1,0:T(8,128)(2,1)S(1)} %get-tuple-element.62), channel_id=1, source_target_pairs={{0,8},{1,9},{2,10},{3,11},{4,12},{5,13},{6,14},{7,15},{8,0},{9,1},... | collective-permute-start | bytes 1572872 | tf_op jit(solution)/shard_map/ppermute | solution.py:363
  65.0 36.4 %collective-permute-start.13 = (bf16[640,256]{1,0:T(8,128)(2,1)S(1)}, bf16[640,256]{1,0:T(8,128)(2,1)S(1)}, u32[]{:S(2)}, u32[]{:S(2)}) collective-permute-start(bf16[640,256]{1,0:T(8,128)(2,1)S(1)} %get-tuple-element.60), channel_id=1, source_target_pairs={{0,12},{1,13},{2,14},{3,15},{4,8},{5,9},{6,10},{7,11},{8,4},{9,5},... | collective-permute-start | bytes 983048 | tf_op jit(solution)/shard_map/ppermute | solution.py:363
  67.1 34.3 %collective-permute-start.8 = (bf16[640,256]{1,0:T(8,128)(2,1)S(1)}, bf16[640,256]{1,0:T(8,128)(2,1)S(1)}, u32[]{:S(2)}, u32[]{:S(2)}) collective-permute-start(bf16[640,256]{1,0:T(8,128)(2,1)S(1)} %get-tuple-element.50), channel_id=1, source_target_pairs={{0,2},{1,3},{2,0},{3,1},{4,6},{5,7},{6,4},{7,5},{8,10},{9,11},{10,... | collective-permute-start | bytes 983048 | tf_op jit(solution)/shard_map/ppermute | solution.py:363
  67.9 33.5 %collective-permute-start.10 = (bf16[384,256]{1,0:T(8,128)(2,1)S(1)}, bf16[384,256]{1,0:T(8,128)(2,1)S(1)}, u32[]{:S(2)}, u32[]{:S(2)}) collective-permute-start(bf16[384,256]{1,0:T(8,128)(2,1)S(1)} %get-tuple-element.54), channel_id=1, source_target_pairs={{0,2},{1,3},{2,0},{3,1},{4,6},{5,7},{6,4},{7,5},{8,10},{9,11},{10,... | collective-permute-start | bytes 589832 | tf_op jit(solution)/shard_map/ppermute | solution.py:363

commit v15 on v9

--- a/solution.py
+++ b/solution.py
@@ -538,10 +538,9 @@
             )(*held, *known, *[arrived[m].reshape(-1, block, width) for m in messages])
         ]
 
-    last = [late(6), late(4)]
+    last = [late(4), late(6)]
     held = place(held, [m for m in plan.late if m not in last], "place_mid")
-    for m in last:
-        held = place(held, [m], "place_last%d" % m[0])
+    held = place(held, last, "place_last")
     return held[0].reshape(1, plan.rows * GRID_COLS * block, width)
 
 

time: 101 us -> 101 us (level)
  waiting for transfers between devices: 38.1 us -> 39.3 us
    ppermute x11, waiting for transfers between devices: 29.3 us -> 30.5 us  [across(): return lax.ppermute(value, 'wide', pairs)]
    pallas_call x3 -> x2, Pallas kernels: 4.24 us -> 3.43 us  [place(): pl.pallas_call(body, out_shape=out_shape, in_specs=[HBM] * len(held) + [A...]
  transfers between devices with their start and end apart: 15 -> 15, of which waited for: 6 -> 6; matrix products, arithmetic and copies ran while one was open for 0% -> 0% of each run, Pallas kernels for 14% -> 13%
where the time goes in v15:
time: 101 us
  starting transfers between devices  45.4 us (45%)
  waiting for transfers between devices  39.3 us (39%)
  Pallas kernels  15.7 us (16%)
    ppermute x11, starting transfers between devices, across(): return lax.ppermute(value, 'wide', pairs)  38.7 us
    ppermute x11, waiting for transfers between devices, across(): return lax.ppermute(value, 'wide', pairs)  30.5 us
    ppermute x4, waiting for transfers between devices, along(): lax.ppermute(value, 'front', [(f, (f + steps) % plan.groups) for f in ran...  8.75 us
    ppermute x4, starting transfers between devices, along(): lax.ppermute(value, 'front', [(f, (f + steps) % plan.groups) for f in ran...  6.64 us
    pallas_call x1, Pallas kernels, local(): pl.pallas_call(functools.partial(assemble_kernel, plan), out_shape=[jax.S...  5.74 us
    pallas_call x2, Pallas kernels, place(): pl.pallas_call(body, out_shape=out_shape, in_specs=[HBM] * len(held) + [A...  3.43 us
    pallas_call x1, Pallas kernels, local(): pl.pallas_call(functools.partial(bucket_kernel, plan, tail), out_shape=[j...  2.5 us
  transfers between devices with their start and end apart: 15, of which 6 were waited for; matrix products, arithmetic and copies ran while one was open for 0% of the time, Pallas kernels for 13%

profile of v15, /device:TPU:0, one launch (start us, length us, event | category | flops | bytes accessed | tf_op | source)
XLA Modules:
  0.0 101.2 jit_solution(8890025178917931755)
XLA Ops:
  0.0 0.7 bitcast_add_fusion.refs_0_.heads
  0.7 3.0 %collective-permute-start = (s32[4]{0:T(128)S(1)}, s32[4]{0:T(128)S(1)}, u32[]{:S(2)}, u32[]{:S(2)}) collective-permute-start(s32[4]{0:T(128)S(1)} %bitcast_add_fusion.refs_0_.heads), channel_id=1, source_target_pairs={{0,16},{16,0},{1,17},{17,1},{2,18},{18,2},{3,19},{19,3},{4,20},{20... | collective-permute-start | bytes 56 | tf_op jit(solution)/shard_map/ppermute | solution.py:367
  3.6 1.2 %stage.1 = (bf16[1024,256]{1,0:T(8,128)(2,1)S(1)}, bf16[1024,256]{1,0:T(8,128)(2,1)S(1)}) custom-call(bf16[1,1024,2048]{2,1,0:T(8,128)(2,1)} %refs_4_.1), custom_call_target="tpu_custom_call" | custom-call | tf_op jit(solution)/shard_map/stage/pallas_call | solution.py:391
  4.9 0.0 copy-start
  4.9 0.0 copy-start.1
  4.9 0.2 collective-permute-done.refs_1_
  5.2 1.1 %pack_early.1 = (bf16[264,256]{1,0:T(8,128)(2,1)S(1)}, bf16[520,256]{1,0:T(8,128)(2,1)S(1)}, s32[1]{0:T(128)}) custom-call(s32[4]{0:T(128)S(1)} %bitcast_add_fusion.refs_0_.heads, s32[4]{0:T(128)S(1)} %collective-permute-done.refs_1_, bf16[1024,256]{1,0:T(8,128)(2,1)S(1)} %get-tuple-element.34.refs_2_, bf16[1024,256]{1,0:T(8,128)(2,1)S(1)} %get-tuple-element.35.refs_3_), custom_call_target="tpu_custom_call" | custom-call | tf_op jit(solution)/shard_map/pack_early/pallas_call | solution.py:401
  6.3 3.2 %collective-permute-start.1 = (bf16[264,256]{1,0:T(8,128)(2,1)S(1)}, bf16[264,256]{1,0:T(8,128)(2,1)S(1)}, u32[]{:S(2)}, u32[]{:S(2)}) collective-permute-start(bf16[264,256]{1,0:T(8,128)(2,1)S(1)} %get-tuple-element.36), channel_id=1, source_target_pairs={{0,8},{1,9},{2,10},{3,11},{4,12},{5,13},{6,14},{7,15},{8,0},{9,1},... | collective-permute-start | bytes 405512 | tf_op jit(solution)/shard_map/ppermute | solution.py:363
  9.4 1.3 %collective-permute-start.2 = (bf16[520,256]{1,0:T(8,128)(2,1)S(1)}, bf16[520,256]{1,0:T(8,128)(2,1)S(1)}, u32[]{:S(2)}, u32[]{:S(2)}) collective-permute-start(bf16[520,256]{1,0:T(8,128)(2,1)S(1)} %get-tuple-element.37), channel_id=1, source_target_pairs={{0,10},{1,11},{2,8},{3,9},{4,14},{5,15},{6,12},{7,13},{8,2},{9,3},... | collective-permute-start | bytes 798728 | tf_op jit(solution)/shard_map/ppermute | solution.py:363
  10.7 2.5 %bucket.1 = (bf16[128,1024]{1,0:T(8,128)(2,1)S(1)}, bf16[128,1024]{1,0:T(8,128)(2,1)S(1)}, bf16[520,256]{1,0:T(8,128)(2,1)S(1)}) custom-call(s32[4]{0:T(128)S(1)} %bitcast_add_fusion.refs_0_.heads, s32[1]{0:T(128)} %get-tuple-element.38.refs_0_, bf16[1,512,1024]{2,1,0:T(8,128)(2,1)} %refs_5_.1, bf16[1,1024,2048]{2,1,0:T(8,128)(2,1)} %refs_4_.1), custom_call_target="tpu_custom_call" | custom-call | tf_op jit(solution)/shard_map/bucket/pallas_call | solution.py:415
  13.2 1.6 %collective-permute-start.5 = (bf16[128,1024]{1,0:T(8,128)(2,1)S(1)}, bf16[128,1024]{1,0:T(8,128)(2,1)S(1)}, u32[]{:S(2)}, u32[]{:S(2)}) collective-permute-start(bf16[128,1024]{1,0:T(8,128)(2,1)S(1)} %get-tuple-element.44), channel_id=1, source_target_pairs={{0,16},{16,0},{1,17},{17,1},{2,18},{18,2},{3,19},{19,3},{4,20},{20... | collective-permute-start | bytes 786440 | tf_op jit(solution)/shard_map/ppermute | solution.py:367
  14.8 0.5 collective-permute-start.6
  15.3 0.0 copy-done
  15.3 0.0 copy-done.1
  15.3 1.6 %collective-permute-start.3 = (s32[4,8]{1,0:T(4,128)S(1)}, s32[4,8]{1,0:T(4,128)S(1)}, u32[]{:S(2)}, u32[]{:S(2)}) collective-permute-start(s32[4,8]{1,0:T(4,128)S(1)} %add_bitcast_fusion.refs_2_), channel_id=1, source_target_pairs={{0,16},{16,0},{1,17},{17,1},{2,18},{18,2},{3,19},{19,3},{4,20},{20... | collective-permute-start | bytes 392 | tf_op jit(solution)/shard_map/ppermute | solution.py:367
  16.9 8.5 %collective-permute-done.3.refs_3_ = s32[4,8]{1,0:T(4,128)S(1)} collective-permute-done((s32[4,8]{1,0:T(4,128)S(1)}, s32[4,8]{1,0:T(4,128)S(1)}, u32[]{:S(2)}, u32[]{:S(2)}) %collective-permute-start.3) | collective-permute-done | bytes 160 | tf_op jit(solution)/shard_map/ppermute | solution.py:367
  25.4 0.0 collective-permute-done.1.refs_0_
  25.4 3.6 %collective-permute-start.4 = (bf16[520,256]{1,0:T(8,128)(2,1)S(1)}, bf16[520,256]{1,0:T(8,128)(2,1)S(1)}, u32[]{:S(2)}, u32[]{:S(2)}) collective-permute-start(bf16[520,256]{1,0:T(8,128)(2,1)S(1)} %get-tuple-element.41), channel_id=1, source_target_pairs={{0,14},{1,15},{2,12},{3,13},{4,10},{5,11},{6,8},{7,9},{8,6},{9,7},... | collective-permute-start | bytes 798728 | tf_op jit(solution)/shard_map/ppermute | solution.py:363
  29.0 0.0 collective-permute-done.5.refs_6_
  29.0 0.0 collective-permute-done.6.refs_7_
  29.0 5.7 %assemble.1 = (bf16[1024,256]{1,0:T(8,128)(2,1)S(1)}, bf16[1024,256]{1,0:T(8,128)(2,1)S(1)}, bf16[1024,256]{1,0:T(8,128)(2,1)S(1)}, bf16[512,256]{1,0:T(8,128)(2...) custom-call(s32[4]{0:T(128)S(1)} %bitcast_add_fusion.refs_0_.heads, ...), custom_call_target="tpu_custom_call" | custom-call | tf_op jit(solution)/shard_map/assemble/pallas_call | solution.py:441
  34.8 0.0 collective-permute-done.2.refs_1_
  34.8 1.5 %collective-permute-start.7 = (bf16[1024,256]{1,0:T(8,128)(2,1)S(1)}, bf16[1024,256]{1,0:T(8,128)(2,1)S(1)}, u32[]{:S(2)}, u32[]{:S(2)}) collective-permute-start(bf16[1024,256]{1,0:T(8,128)(2,1)S(1)} %get-tuple-element.48), channel_id=1, source_target_pairs={{0,2},{1,3},{2,0},{3,1},{4,6},{5,7},{6,4},{7,5},{8,10},{9,11},{10,... | collective-permute-start | bytes 1572872 | tf_op jit(solution)/shard_map/ppermute | solution.py:363
  36.2 0.0 collective-permute-start.12
  36.2 0.0 collective-permute-done.4.refs_2_
  36.2 2.8 %collective-permute-start.10 = (bf16[512,256]{1,0:T(8,128)(2,1)S(1)}, bf16[512,256]{1,0:T(8,128)(2,1)S(1)}, u32[]{:S(2)}, u32[]{:S(2)}) collective-permute-start(bf16[512,256]{1,0:T(8,128)(2,1)S(1)} %get-tuple-element.55), channel_id=1, source_target_pairs={{0,14},{1,15},{2,12},{3,13},{4,10},{5,11},{6,8},{7,9},{8,6},{9,7},... | collective-permute-start | bytes 786440 | tf_op jit(solution)/shard_map/ppermute | solution.py:363
  39.0 15.3 %collective-permute-start.8 = (bf16[1024,256]{1,0:T(8,128)(2,1)S(1)}, bf16[1024,256]{1,0:T(8,128)(2,1)S(1)}, u32[]{:S(2)}, u32[]{:S(2)}) collective-permute-start(bf16[1024,256]{1,0:T(8,128)(2,1)S(1)} %get-tuple-element.50), channel_id=1, source_target_pairs={{0,4},{1,5},{2,6},{3,7},{4,0},{5,1},{6,2},{7,3},{8,12},{9,13},{10,... | collective-permute-start | bytes 1572872 | tf_op jit(solution)/shard_map/ppermute | solution.py:363
  54.3 2.3 %collective-permute-done.12 = bf16[512,256]{1,0:T(8,128)(2,1)S(1)} collective-permute-done((bf16[512,256]{1,0:T(8,128)(2,1)S(1)}, bf16[512,256]{1,0:T(8,128)(2,1)S(1)}, u32[]{:S(2)}, u32[]{:S(2)}) %collective-permute-start.12) | collective-permute-done | bytes 262176 | tf_op jit(solution)/shard_map/ppermute | solution.py:363
  56.6 3.5 %collective-permute-start.14 = (bf16[1024,256]{1,0:T(8,128)(2,1)S(1)}, bf16[1024,256]{1,0:T(8,128)(2,1)S(1)}, u32[]{:S(2)}, u32[]{:S(2)}) collective-permute-start(bf16[1024,256]{1,0:T(8,128)(2,1)S(1)} %get-tuple-element.62), channel_id=1, source_target_pairs={{0,12},{1,13},{2,14},{3,15},{4,8},{5,9},{6,10},{7,11},{8,4},{9,5},... | collective-permute-start | bytes 1572872 | tf_op jit(solution)/shard_map/ppermute | solution.py:363
  60.1 0.0 collective-permute-done.10
  60.1 4.7 %collective-permute-start.13 = (bf16[768,256]{1,0:T(8,128)(2,1)S(1)}, bf16[768,256]{1,0:T(8,128)(2,1)S(1)}, u32[]{:S(2)}, u32[]{:S(2)}) collective-permute-start(bf16[768,256]{1,0:T(8,128)(2,1)S(1)} %get-tuple-element.60), channel_id=1, source_target_pairs={{0,8},{1,9},{2,10},{3,11},{4,12},{5,13},{6,14},{7,15},{8,0},{9,1},... | collective-permute-start | bytes 1179656 | tf_op jit(solution)/shard_map/ppermute | solution.py:363
  64.9 0.0 collective-permute-start.11
  64.9 0.0 collective-permute-done.7
  64.9 2.9 %collective-permute-start.9 = (bf16[512,256]{1,0:T(8,128)(2,1)S(1)}, bf16[512,256]{1,0:T(8,128)(2,1)S(1)}, u32[]{:S(2)}, u32[]{:S(2)}) collective-permute-start(bf16[512,256]{1,0:T(8,128)(2,1)S(1)} %get-tuple-element.52), channel_id=1, source_target_pairs={{0,6},{1,7},{2,4},{3,5},{4,2},{5,3},{6,0},{7,1},{8,14},{9,15},{10,... | collective-permute-start | bytes 786440 | tf_op jit(solution)/shard_map/ppermute | solution.py:363
  67.8 1.7 %place_early.1 = (bf16[8,8,128,256]{3,2,1,0:T(8,128)(2,1)}, s32[3]{0:T(128)S(1)}) custom-call(bf16[264,256]{1,0:T(8,128)(2,1)S(1)} %collective-permute-done.1.refs_0_, bf16[520,256]{1,0:T(8,128)(2,1)S(1)} %collective-permute-done.2.refs_1_, bf16[520,256]{1,0:T(8,128)(2,1)S(1)} %collective-permute-done.4.refs_2_), custom_call_target="tpu_custom_call" | custom-call | tf_op jit(solution)/shard_map/place_early/pallas_call | solution.py:496
  69.5 21.9 %collective-permute-done.11 = bf16[512,256]{1,0:T(8,128)(2,1)S(1)} collective-permute-done((bf16[512,256]{1,0:T(8,128)(2,1)S(1)}, bf16[512,256]{1,0:T(8,128)(2,1)S(1)}, u32[]{:S(2)}, u32[]{:S(2)}) %collective-permute-start.11) | collective-permute-done | bytes 262176 | tf_op jit(solution)/shard_map/ppermute | solution.py:363
  91.4 0.0 collective-permute-done.8
  91.4 2.8 %collective-permute-done.9 = bf16[512,256]{1,0:T(8,128)(2,1)S(1)} collective-permute-done((bf16[512,256]{1,0:T(8,128)(2,1)S(1)}, bf16[512,256]{1,0:T(8,128)(2,1)S(1)}, u32[]{:S(2)}, u32[]{:S(2)}) %collective-permute-start.9) | collective-permute-done | bytes 262176 | tf_op jit(solution)/shard_map/ppermute | solution.py:363
  94.2 2.0 %place_mid.1.refs_0_ = bf16[8,8,128,256]{3,2,1,0:T(8,128)(2,1)} custom-call(bf16[8,8,128,256]{3,2,1,0:T(8,128)(2,1)} %get-tuple-element.42.refs_0_, s32[3]{0:T(128)S(1)} %get-tuple-element.43.refs_1_, bf16[8,128,256]{2,1,0:T(8,128)(2,1)S(1)} %bitcast.16, bf16[8,128,256]{2,1,0:T(8,128)(2,1)S(1)} %bitcast.17, ...), custom_call_target="tpu_custom_call", output_to_operand_aliasing={{}: (0, {})} | custom-call | tf_op jit(solution)/shard_map/place_mid/pallas_call | solution.py:523
  96.2 0.0 collective-permute-done.14
  96.2 3.5 %collective-permute-done.13 = bf16[768,256]{1,0:T(8,128)(2,1)S(1)} collective-permute-done((bf16[768,256]{1,0:T(8,128)(2,1)S(1)}, bf16[768,256]{1,0:T(8,128)(2,1)S(1)}, u32[]{:S(2)}, u32[]{:S(2)}) %collective-permute-start.13) | collective-permute-done | bytes 393248 | tf_op jit(solution)/shard_map/ppermute | solution.py:363
  99.7 1.5 %place_last.1 = bf16[8,8,128,256]{3,2,1,0:T(8,128)(2,1)} custom-call(bf16[8,8,128,256]{3,2,1,0:T(8,128)(2,1)} %place_mid.1.refs_0_, s32[3]{0:T(128)S(1)} %get-tuple-element.43.refs_1_, bf16[6,128,256]{2,1,0:T(8,128)(2,1)S(1)} %bitcast.20, bf16[8,128,256]{2,1,0:T(8,128)(2,1)S(1)} %bitcast.18), custom_call_target="tpu_custom_call", output_to_operand_aliasing={{}: (0, {})} | custom-call | tf_op jit(solution)/shard_map/place_last/pallas_call | solution.py:523
  (1 shorter events, 0.0 us)
Async XLA Ops:
  0.7 4.5 %collective-permute-start = (s32[4]{0:T(128)S(1)}, s32[4]{0:T(128)S(1)}, u32[]{:S(2)}, u32[]{:S(2)}) collective-permute-start(s32[4]{0:T(128)S(1)} %bitcast_add_fusion.refs_0_.heads), channel_id=1, source_target_pairs={{0,16},{16,0},{1,17},{17,1},{2,18},{18,2},{3,19},{19,3},{4,20},{20... | collective-permute-start | bytes 56 | tf_op jit(solution)/shard_map/ppermute | solution.py:367
  4.9 10.4 %copy-start = (s32[1,4,8]{2,1,0:T(4,128)S(1)}, s32[1,4,8]{2,1,0:T(4,128)}, u32[]{:S(2)}) copy-start(s32[1,4,8]{2,1,0:T(4,128)} %param.10) | copy-start | bytes 388
  4.9 10.4 %copy-start.1 = (s32[1,4,8]{2,1,0:T(4,128)S(1)}, s32[1,4,8]{2,1,0:T(4,128)}, u32[]{:S(2)}) copy-start(s32[1,4,8]{2,1,0:T(4,128)} %param.11) | copy-start | bytes 388
  6.3 19.1 %collective-permute-start.1 = (bf16[264,256]{1,0:T(8,128)(2,1)S(1)}, bf16[264,256]{1,0:T(8,128)(2,1)S(1)}, u32[]{:S(2)}, u32[]{:S(2)}) collective-permute-start(bf16[264,256]{1,0:T(8,128)(2,1)S(1)} %get-tuple-element.36), channel_id=1, source_target_pairs={{0,8},{1,9},{2,10},{3,11},{4,12},{5,13},{6,14},{7,15},{8,0},{9,1},... | collective-permute-start | bytes 405512 | tf_op jit(solution)/shard_map/ppermute | solution.py:363
  9.4 25.3 %collective-permute-start.2 = (bf16[520,256]{1,0:T(8,128)(2,1)S(1)}, bf16[520,256]{1,0:T(8,128)(2,1)S(1)}, u32[]{:S(2)}, u32[]{:S(2)}) collective-permute-start(bf16[520,256]{1,0:T(8,128)(2,1)S(1)} %get-tuple-element.37), channel_id=1, source_target_pairs={{0,10},{1,11},{2,8},{3,9},{4,14},{5,15},{6,12},{7,13},{8,2},{9,3},... | collective-permute-start | bytes 798728 | tf_op jit(solution)/shard_map/ppermute | solution.py:363
  13.2 15.8 %collective-permute-start.5 = (bf16[128,1024]{1,0:T(8,128)(2,1)S(1)}, bf16[128,1024]{1,0:T(8,128)(2,1)S(1)}, u32[]{:S(2)}, u32[]{:S(2)}) collective-permute-start(bf16[128,1024]{1,0:T(8,128)(2,1)S(1)} %get-tuple-element.44), channel_id=1, source_target_pairs={{0,16},{16,0},{1,17},{17,1},{2,18},{18,2},{3,19},{19,3},{4,20},{20... | collective-permute-start | bytes 786440 | tf_op jit(solution)/shard_map/ppermute | solution.py:367
  14.8 14.2 %collective-permute-start.6 = (bf16[128,1024]{1,0:T(8,128)(2,1)S(1)}, bf16[128,1024]{1,0:T(8,128)(2,1)S(1)}, u32[]{:S(2)}, u32[]{:S(2)}) collective-permute-start(bf16[128,1024]{1,0:T(8,128)(2,1)S(1)} %get-tuple-element.45), channel_id=1, source_target_pairs={{0,16},{16,0},{1,17},{17,1},{2,18},{18,2},{3,19},{19,3},{4,20},{20... | collective-permute-start | bytes 786440 | tf_op jit(solution)/shard_map/ppermute | solution.py:367
  15.3 10.1 %collective-permute-start.3 = (s32[4,8]{1,0:T(4,128)S(1)}, s32[4,8]{1,0:T(4,128)S(1)}, u32[]{:S(2)}, u32[]{:S(2)}) collective-permute-start(s32[4,8]{1,0:T(4,128)S(1)} %add_bitcast_fusion.refs_2_), channel_id=1, source_target_pairs={{0,16},{16,0},{1,17},{17,1},{2,18},{18,2},{3,19},{19,3},{4,20},{20... | collective-permute-start | bytes 392 | tf_op jit(solution)/shard_map/ppermute | solution.py:367
  25.4 10.8 %collective-permute-start.4 = (bf16[520,256]{1,0:T(8,128)(2,1)S(1)}, bf16[520,256]{1,0:T(8,128)(2,1)S(1)}, u32[]{:S(2)}, u32[]{:S(2)}) collective-permute-start(bf16[520,256]{1,0:T(8,128)(2,1)S(1)} %get-tuple-element.41), channel_id=1, source_target_pairs={{0,14},{1,15},{2,12},{3,13},{4,10},{5,11},{6,8},{7,9},{8,6},{9,7},... | collective-permute-start | bytes 798728 | tf_op jit(solution)/shard_map/ppermute | solution.py:363
  34.8 30.1 %collective-permute-start.7 = (bf16[1024,256]{1,0:T(8,128)(2,1)S(1)}, bf16[1024,256]{1,0:T(8,128)(2,1)S(1)}, u32[]{:S(2)}, u32[]{:S(2)}) collective-permute-start(bf16[1024,256]{1,0:T(8,128)(2,1)S(1)} %get-tuple-element.48), channel_id=1, source_target_pairs={{0,2},{1,3},{2,0},{3,1},{4,6},{5,7},{6,4},{7,5},{8,10},{9,11},{10,... | collective-permute-start | bytes 1572872 | tf_op jit(solution)/shard_map/ppermute | solution.py:363
  36.2 20.4 %collective-permute-start.12 = (bf16[512,256]{1,0:T(8,128)(2,1)S(1)}, bf16[512,256]{1,0:T(8,128)(2,1)S(1)}, u32[]{:S(2)}, u32[]{:S(2)}) collective-permute-start(bf16[512,256]{1,0:T(8,128)(2,1)S(1)} %get-tuple-element.58), channel_id=1, source_target_pairs={{0,10},{1,11},{2,8},{3,9},{4,14},{5,15},{6,12},{7,13},{8,2},{9,3},... | collective-permute-start | bytes 786440 | tf_op jit(solution)/shard_map/ppermute | solution.py:363
  36.2 23.9 %collective-permute-start.10 = (bf16[512,256]{1,0:T(8,128)(2,1)S(1)}, bf16[512,256]{1,0:T(8,128)(2,1)S(1)}, u32[]{:S(2)}, u32[]{:S(2)}) collective-permute-start(bf16[512,256]{1,0:T(8,128)(2,1)S(1)} %get-tuple-element.55), channel_id=1, source_target_pairs={{0,14},{1,15},{2,12},{3,13},{4,10},{5,11},{6,8},{7,9},{8,6},{9,7},... | collective-permute-start | bytes 786440 | tf_op jit(solution)/shard_map/ppermute | solution.py:363
  39.0 52.4 %collective-permute-start.8 = (bf16[1024,256]{1,0:T(8,128)(2,1)S(1)}, bf16[1024,256]{1,0:T(8,128)(2,1)S(1)}, u32[]{:S(2)}, u32[]{:S(2)}) collective-permute-start(bf16[1024,256]{1,0:T(8,128)(2,1)S(1)} %get-tuple-element.50), channel_id=1, source_target_pairs={{0,4},{1,5},{2,6},{3,7},{4,0},{5,1},{6,2},{7,3},{8,12},{9,13},{10,... | collective-permute-start | bytes 1572872 | tf_op jit(solution)/shard_map/ppermute | solution.py:363
  56.6 39.6 %collective-permute-start.14 = (bf16[1024,256]{1,0:T(8,128)(2,1)S(1)}, bf16[1024,256]{1,0:T(8,128)(2,1)S(1)}, u32[]{:S(2)}, u32[]{:S(2)}) collective-permute-start(bf16[1024,256]{1,0:T(8,128)(2,1)S(1)} %get-tuple-element.62), channel_id=1, source_target_pairs={{0,12},{1,13},{2,14},{3,15},{4,8},{5,9},{6,10},{7,11},{8,4},{9,5},... | collective-permute-start | bytes 1572872 | tf_op jit(solution)/shard_map/ppermute | solution.py:363
  60.1 39.6 %collective-permute-start.13 = (bf16[768,256]{1,0:T(8,128)(2,1)S(1)}, bf16[768,256]{1,0:T(8,128)(2,1)S(1)}, u32[]{:S(2)}, u32[]{:S(2)}) collective-permute-start(bf16[768,256]{1,0:T(8,128)(2,1)S(1)} %get-tuple-element.60), channel_id=1, source_target_pairs={{0,8},{1,9},{2,10},{3,11},{4,12},{5,13},{6,14},{7,15},{8,0},{9,1},... | collective-permute-start | bytes 1179656 | tf_op jit(solution)/shard_map/ppermute | solution.py:363
  64.9 26.6 %collective-permute-start.11 = (bf16[512,256]{1,0:T(8,128)(2,1)S(1)}, bf16[512,256]{1,0:T(8,128)(2,1)S(1)}, u32[]{:S(2)}, u32[]{:S(2)}) collective-permute-start(bf16[512,256]{1,0:T(8,128)(2,1)S(1)} %get-tuple-element.56), channel_id=1, source_target_pairs={{0,6},{1,7},{2,4},{3,5},{4,2},{5,3},{6,0},{7,1},{8,14},{9,15},{10,... | collective-permute-start | bytes 786440 | tf_op jit(solution)/shard_map/ppermute | solution.py:363
  64.9 29.4 %collective-permute-start.9 = (bf16[512,256]{1,0:T(8,128)(2,1)S(1)}, bf16[512,256]{1,0:T(8,128)(2,1)S(1)}, u32[]{:S(2)}, u32[]{:S(2)}) collective-permute-start(bf16[512,256]{1,0:T(8,128)(2,1)S(1)} %get-tuple-element.52), channel_id=1, source_target_pairs={{0,6},{1,7},{2,4},{3,5},{4,2},{5,3},{6,0},{7,1},{8,14},{9,15},{10,... | collective-permute-start | bytes 786440 | tf_op jit(solution)/shard_map/ppermute | solution.py:363
